TPU v7x, 32 devices: a whole 2x2x4 slice. The times are simulated.
32 devices in a mesh: col: 4 (over y, x), seq: 8 (over z, core).
Axes of the slice: x: 2, y: 2, z: 4, core: 2. Of those that a mesh axis runs over, the one named last changes fastest.
Arguments:
- tokens: bfloat16 [8, 512, 768], P('seq', 'col'), may hold values from -6 to 6
- offsets: int32 [2], replicated, may hold values from 0 to 1023
- band: int32 [512, 65], P('col'), may hold values 0 or 1
- col_counts: int32 [4], P('col'), may hold values from 32 to 128, as said below
- norm1_gain: bfloat16 [768], P('seq'), may hold values from 0.5 to 1.5
- norm1_shift: bfloat16 [768], P('seq'), may hold values from -4 to 4
- norm2_gain: bfloat16 [768], P('seq'), may hold values from 0.5 to 1.5
- norm2_shift: bfloat16 [768], P('seq'), may hold values from -4 to 4
- norm3_gain: bfloat16 [768], P('seq'), may hold values from 0.5 to 1.5
- norm3_shift: bfloat16 [768], P('seq'), may hold values from -4 to 4
- row_query: bfloat16 [768, 768], P('seq'), may hold values from -0.21875 to 0.21875
- row_key: bfloat16 [768, 768], P('seq'), may hold values from -0.21875 to 0.21875
- row_value: bfloat16 [768, 768], P('seq'), may hold values from -0.21875 to 0.21875
- row_output: bfloat16 [768, 768], P('seq'), may hold values from -0.875 to 0.875
- col_query: bfloat16 [768, 768], P('seq'), may hold values from -0.21875 to 0.21875
- col_key: bfloat16 [768, 768], P('seq'), may hold values from -0.21875 to 0.21875
- col_value: bfloat16 [768, 768], P('seq'), may hold values from -0.21875 to 0.21875
- col_output: bfloat16 [768, 768], P('seq'), may hold values from -0.3125 to 0.3125
- feed_in: bfloat16 [768, 3072], P('seq'), may hold values from -0.21875 to 0.21875
- feed_out: bfloat16 [3072, 768], P('seq'), may hold values from -0.109375 to 0.109375
- cotangent: bfloat16 [8, 512, 768], P('seq', 'col'), may hold values from -6 to 6
Outputs:
- output: bfloat16 [8, 512, 768], P('seq', 'col')
- entropy: float32 [], replicated
- input_grad: bfloat16 [8, 512, 768], P('seq', 'col')
- grad_norm1_gain: float32 [768], P('seq')
- grad_norm1_shift: float32 [768], P('seq')
- grad_norm2_gain: float32 [768], P('seq')
- grad_norm2_shift: float32 [768], P('seq')
- grad_norm3_gain: float32 [768], P('seq')
- grad_norm3_shift: float32 [768], P('seq')
- grad_row_query: float32 [768, 768], P('seq')
- grad_row_key: float32 [768, 768], P('seq')
- grad_row_value: float32 [768, 768], P('seq')
- grad_row_output: float32 [768, 768], P('seq')
- grad_col_query: float32 [768, 768], P('seq')
- grad_col_key: float32 [768, 768], P('seq')
- grad_col_value: float32 [768, 768], P('seq')
- grad_col_output: float32 [768, 768], P('seq')
- grad_feed_in: float32 [768, 3072], P('seq')
- grad_feed_out: float32 [3072, 768], P('seq')
Inputs may be any that keep to these rules, and one draw needn't show every extreme that they name: `col_counts`: block 0 has 32 true columns and the last block all 128.
All inputs are finite; a program needn't handle non-finite values. No bound on the sum of `band` on one device may be relied on, other than what follows from the above.
Results may differ from a plain program's by a relative error of at most 0.035.
Values may be sent and summed in bfloat16 or wider, within the bound.
No kernel may reach another device: no remote copies, remote signals or barrier semaphores. Data moves between devices by JAX's collectives and lax.ppermute only.
A program may use at most 192 MiB of HBM per device.

v0:
```python
from functools import partial
import math

import jax
import jax.numpy as jnp
from jax import lax
from jax.sharding import PartitionSpec as P

HEADS = 12
HEAD_DIM = 64
WINDOW = 32


entropy_weight = 8192.0
norm_eps = 1e-05


def with_halo(cells, sides, width):
    for axis, dim in sides:
        count = lax.axis_size(axis)
        ends = count - 1
        head = lax.slice_in_dim(cells, 0, width, axis=dim)
        tail = lax.slice_in_dim(cells, cells.shape[dim] - width, cells.shape[dim], axis=dim)
        cells = jnp.concatenate(
            [
                lax.ppermute(tail, axis, [(i, (i + 1) % count) for i in range(ends)]),
                cells,
                lax.ppermute(head, axis, [((i + 1) % count, i) for i in range(ends)]),
            ],
            axis=dim,
        )
    return cells


def layer_norm(inputs, norm_gain, norm_shift):
    average = jnp.mean(inputs, axis=-1, keepdims=True)
    centred = inputs - average
    variance = jnp.mean(centred * centred, axis=-1, keepdims=True)
    return centred * lax.rsqrt(variance + norm_eps) * norm_gain + norm_shift


def position_table(offsets, row_first, col_first, row_count, col_count, model_width):
    half_width = model_width // 2
    frequency = jnp.exp(-math.log(1000.0) * jnp.arange(half_width, dtype=jnp.float32) / half_width)
    col_place = (jnp.arange(col_count, dtype=jnp.int32) + col_first + offsets[1]).astype(
        jnp.float32
    )
    row_place = (jnp.arange(row_count, dtype=jnp.int32) + row_first + offsets[0]).astype(
        jnp.float32
    )
    col_wave = jnp.sin(col_place[:, None] * frequency[None, :])
    row_wave = jnp.sin(row_place[:, None] * frequency[None, :])
    col_full = jnp.broadcast_to(col_wave[None, :, :], (row_count, col_count, half_width))
    row_full = jnp.broadcast_to(row_wave[:, None, :], (row_count, col_count, half_width))
    return 0.5 * jnp.concatenate([col_full, row_full], axis=-1)


def softmax_entropy(scores, allowed, valid):
    masked = jnp.where(allowed[None], scores, -1000000000.0)
    largest = jnp.max(masked, axis=-1, keepdims=True)
    powers = jnp.exp(masked - largest)
    row_total = jnp.sum(powers, axis=-1, keepdims=True)
    probs_out = powers / row_total
    log_total = largest[..., 0] + jnp.log(row_total[..., 0])
    entropies = log_total - jnp.sum(probs_out * jnp.where(allowed[None], scores, 0.0), axis=-1)
    return (probs_out, jnp.sum(entropies * valid[None, :]))


def plain_softmax(scores):
    largest = jnp.max(scores, axis=-1, keepdims=True)
    powers = jnp.exp(scores - largest)
    return powers / jnp.sum(powers, axis=-1, keepdims=True)


def project(activations, weight):
    return jnp.einsum("rci,ij->rcj", activations, weight, preferred_element_type=jnp.float32)


def project_back(gradient, weight):
    return jnp.einsum("rcj,ij->rci", gradient, weight, preferred_element_type=jnp.float32)


def weight_grad(activations, gradient):
    return jnp.einsum("rci,rcj->ij", activations, gradient, preferred_element_type=jnp.float32)


def on_device(
    tokens,
    offsets,
    band,
    col_counts,
    norm1_gain,
    norm1_shift,
    norm2_gain,
    norm2_shift,
    norm3_gain,
    norm3_shift,
    row_query,
    row_key,
    row_value,
    row_output,
    col_query,
    col_key,
    col_value,
    col_output,
    feed_in,
    feed_out,
    cotangent,
):
    rows_dev, cols_dev, model_width = tokens.shape
    total_rows = rows_dev * lax.axis_size("seq")
    total_cols = cols_dev * lax.axis_size("col")
    row_first = lax.axis_index("seq") * rows_dev
    col_first = lax.axis_index("col") * cols_dev
    count_here = col_counts[0].astype(jnp.float32)
    count_early = lax.psum(count_here, "col")
    params = (
        lax.all_gather(norm1_gain, "seq", axis=0, tiled=True),
        lax.all_gather(norm1_shift, "seq", axis=0, tiled=True),
        lax.all_gather(norm2_gain, "seq", axis=0, tiled=True),
        lax.all_gather(norm2_shift, "seq", axis=0, tiled=True),
        lax.all_gather(norm3_gain, "seq", axis=0, tiled=True),
        lax.all_gather(norm3_shift, "seq", axis=0, tiled=True),
        lax.all_gather(row_query, "seq", axis=0, tiled=True),
        lax.all_gather(row_key, "seq", axis=0, tiled=True),
        lax.all_gather(row_value, "seq", axis=0, tiled=True),
        lax.all_gather(row_output, "seq", axis=0, tiled=True),
        lax.all_gather(col_query, "seq", axis=0, tiled=True),
        lax.all_gather(col_key, "seq", axis=0, tiled=True),
        lax.all_gather(col_value, "seq", axis=0, tiled=True),
        lax.all_gather(col_output, "seq", axis=0, tiled=True),
        lax.all_gather(feed_in, "seq", axis=0, tiled=True),
        lax.all_gather(feed_out, "seq", axis=0, tiled=True),
    )
    gain_one = params[0].astype(jnp.float32)
    shift_one = params[1].astype(jnp.float32)
    gain_two = params[2].astype(jnp.float32)
    shift_two = params[3].astype(jnp.float32)
    gain_three = params[4].astype(jnp.float32)
    shift_three = params[5].astype(jnp.float32)
    query_row, key_row, value_row, output_row = (params[6], params[7], params[8], params[9])
    query_col, key_col, value_col, output_col = (params[10], params[11], params[12], params[13])
    feed_up, feed_down = (params[14], params[15])
    stream_zero = tokens.astype(jnp.float32) + position_table(
        offsets, row_first, col_first, rows_dev, cols_dev, model_width
    )
    normed_one, norm_back_one = jax.vjp(layer_norm, stream_zero, gain_one, shift_one)
    normed_one = normed_one.astype(jnp.bfloat16)
    row_queries = project(normed_one, query_row).astype(jnp.bfloat16)
    row_keys = project(normed_one, key_row).astype(jnp.bfloat16)
    row_values = project(normed_one, value_row).astype(jnp.bfloat16)
    extended = with_halo(jnp.stack([row_keys, row_values]), (("col", 2),), WINDOW)
    ext_cols = cols_dev + 2 * WINDOW
    queries_heads = row_queries.reshape(rows_dev, cols_dev, HEADS, HEAD_DIM)
    keys_ext = extended[0].reshape(rows_dev, ext_cols, HEADS, HEAD_DIM)
    values_ext = extended[1].reshape(rows_dev, ext_cols, HEADS, HEAD_DIM)
    partial_logits = jnp.einsum(
        "rchd,rehd->hce", queries_heads, keys_ext, preferred_element_type=jnp.float32
    )
    row_scale = 1.0 / math.sqrt(HEAD_DIM * total_rows)
    row_scores = lax.psum(partial_logits, "seq") * row_scale
    query_index = jnp.arange(cols_dev, dtype=jnp.int32)[:, None]
    key_index = jnp.arange(ext_cols, dtype=jnp.int32)[None, :]
    distance = key_index - query_index
    choose = jnp.arange(2 * WINDOW + 1, dtype=jnp.int32)
    matches = (distance[:, None, :] == choose[None, :, None]) & (band[:, :, None] == 1)
    key_global = col_first - WINDOW + key_index
    inside = (key_global >= 0) & (key_global < total_cols)
    allowed = (jnp.any(matches, axis=1) | (distance == WINDOW)) & inside
    valid = (jnp.arange(cols_dev, dtype=jnp.int32) < col_counts[0]).astype(jnp.float32)
    (row_probs, ent_part), ent_back = jax.vjp(
        lambda given: softmax_entropy(given, allowed, valid), row_scores
    )
    payload = ent_part[None]
    sums = lax.psum(payload, "col")
    entropy = sums[0] / (HEADS * count_early)
    row_probs_low = row_probs.astype(jnp.bfloat16)
    row_mix = jnp.einsum(
        "hce,rehd->rchd", row_probs_low, values_ext, preferred_element_type=jnp.float32
    )
    row_mix = row_mix.reshape(rows_dev, cols_dev, model_width).astype(jnp.bfloat16)
    stream_one = stream_zero + project(row_mix, output_row)
    normed_two, norm_back_two = jax.vjp(layer_norm, stream_one, gain_two, shift_two)
    normed_two = normed_two.astype(jnp.bfloat16)
    col_queries = project(normed_two, query_col).astype(jnp.bfloat16)
    col_keys = project(normed_two, key_col).astype(jnp.bfloat16)
    col_values = project(normed_two, value_col).astype(jnp.bfloat16)
    col_scale = 1.0 / math.sqrt(HEAD_DIM)
    keys_all, values_all = (
        lax.all_gather(col_keys, "seq", axis=0, tiled=True),
        lax.all_gather(col_values, "seq", axis=0, tiled=True),
    )
    col_heads_q = col_queries.reshape(rows_dev, cols_dev, HEADS, HEAD_DIM)
    keys_heads = keys_all.reshape(total_rows, cols_dev, HEADS, HEAD_DIM)
    values_heads = values_all.reshape(total_rows, cols_dev, HEADS, HEAD_DIM)
    col_raw = jnp.einsum(
        "rchd,schd->chrs", col_heads_q, keys_heads, preferred_element_type=jnp.float32
    )
    col_probs = plain_softmax(col_raw * col_scale)
    col_probs_low = col_probs.astype(jnp.bfloat16)
    col_mix = jnp.einsum(
        "chrs,schd->rchd", col_probs_low, values_heads, preferred_element_type=jnp.float32
    )
    col_mix = col_mix.reshape(rows_dev, cols_dev, model_width).astype(jnp.bfloat16)
    stream_two = stream_one + project(col_mix, output_col)
    normed_three, norm_back_three = jax.vjp(layer_norm, stream_two, gain_three, shift_three)
    normed_three = normed_three.astype(jnp.bfloat16)
    hidden_pre = project(normed_three, feed_up)
    hidden_act, gelu_back = jax.vjp(partial(jax.nn.gelu, approximate=False), hidden_pre)
    hidden_low = hidden_act.astype(jnp.bfloat16)
    output = (stream_two + project(hidden_low, feed_down)).astype(jnp.bfloat16)
    grad_feed_down = weight_grad(hidden_low, cotangent)
    grad_hidden = gelu_back(project_back(cotangent, feed_down))[0].astype(jnp.bfloat16)
    grad_feed_up = weight_grad(normed_three, grad_hidden)
    back_stream, grad_gain_three, grad_shift_three = norm_back_three(
        project_back(grad_hidden, feed_up)
    )
    grad_two = cotangent.astype(jnp.float32) + back_stream
    grad_two_low = grad_two.astype(jnp.bfloat16)
    grad_output_col = weight_grad(col_mix, grad_two_low)
    grad_mix_flat = project_back(grad_two_low, output_col).astype(jnp.bfloat16)
    grad_col_mix = grad_mix_flat.reshape(rows_dev, cols_dev, HEADS, HEAD_DIM)
    col_dprobs = jnp.einsum(
        "rchd,schd->chrs", grad_col_mix, values_heads, preferred_element_type=jnp.float32
    )
    col_dscores = col_probs * (col_dprobs - jnp.sum(col_probs * col_dprobs, axis=-1, keepdims=True))
    col_dscores = col_dscores.astype(jnp.bfloat16)
    grad_col_q = (
        jnp.einsum("chrs,schd->rchd", col_dscores, keys_heads, preferred_element_type=jnp.float32)
        * col_scale
    )
    grad_col_q = grad_col_q.reshape(rows_dev, cols_dev, model_width).astype(jnp.bfloat16)
    row_count = lax.axis_size("seq") * rows_dev
    key_part = (
        jnp.einsum("chrs,rchd->schd", col_dscores, col_heads_q, preferred_element_type=jnp.float32)
        * col_scale
    )
    value_part = jnp.einsum(
        "chrs,rchd->schd", col_probs_low, grad_col_mix, preferred_element_type=jnp.float32
    )
    key_value_grads = lax.psum_scatter(
        jnp.concatenate(
            [
                key_part.reshape(row_count, cols_dev, model_width),
                value_part.reshape(row_count, cols_dev, model_width),
            ],
            axis=-1,
        ),
        "seq",
        scatter_dimension=0,
        tiled=True,
    )
    grad_col_k = key_value_grads[..., :model_width].astype(jnp.bfloat16)
    grad_col_v = key_value_grads[..., model_width:].astype(jnp.bfloat16)
    grad_query_col = weight_grad(normed_two, grad_col_q)
    grad_key_col = weight_grad(normed_two, grad_col_k)
    grad_value_col = weight_grad(normed_two, grad_col_v)
    back_input = (
        project_back(grad_col_q, query_col)
        + project_back(grad_col_k, key_col)
        + project_back(grad_col_v, value_col)
    )
    back_stream, grad_gain_two, grad_shift_two = norm_back_two(back_input)
    grad_one = grad_two + back_stream
    grad_one_low = grad_one.astype(jnp.bfloat16)
    grad_output_row = weight_grad(row_mix, grad_one_low)
    grad_row_mix = project_back(grad_one_low, output_row).astype(jnp.bfloat16)
    grad_row_mix = grad_row_mix.reshape(rows_dev, cols_dev, HEADS, HEAD_DIM)
    dprobs_part = jnp.einsum(
        "rchd,rehd->hce", grad_row_mix, values_ext, preferred_element_type=jnp.float32
    )
    row_dprobs = lax.psum(dprobs_part.astype(jnp.bfloat16), "seq").astype(jnp.float32)
    ent_cot = jnp.asarray(entropy_weight, dtype=jnp.float32) / (HEADS * count_early)
    row_dscores = ent_back((row_dprobs, ent_cot))[0].astype(jnp.bfloat16)
    grad_row_q = (
        jnp.einsum("hce,rehd->rchd", row_dscores, keys_ext, preferred_element_type=jnp.float32)
        * row_scale
    )
    grad_row_q = grad_row_q.reshape(rows_dev, cols_dev, model_width).astype(jnp.bfloat16)
    grad_keys_ext = (
        jnp.einsum("hce,rchd->rehd", row_dscores, queries_heads, preferred_element_type=jnp.float32)
        * row_scale
    )
    grad_values_ext = jnp.einsum(
        "hce,rchd->rehd", row_probs_low, grad_row_mix, preferred_element_type=jnp.float32
    )
    grad_ext = jnp.stack([grad_keys_ext, grad_values_ext]).reshape(
        2, rows_dev, ext_cols, model_width
    )
    rims = jnp.concatenate([grad_ext[:, :, :WINDOW], grad_ext[:, :, WINDOW + cols_dev :]], axis=2)
    returned = with_halo(rims.astype(jnp.bfloat16), (("col", 2),), WINDOW).astype(rims.dtype)
    interior = grad_ext[:, :, WINDOW : WINDOW + cols_dev]
    interior = interior.at[:, :, :WINDOW].add(returned[:, :, :WINDOW])
    interior = interior.at[:, :, cols_dev - WINDOW :].add(returned[:, :, 3 * WINDOW :])
    grad_row_k = interior[0].astype(jnp.bfloat16)
    grad_row_v = interior[1].astype(jnp.bfloat16)
    grad_query_row = weight_grad(normed_one, grad_row_q)
    grad_key_row = weight_grad(normed_one, grad_row_k)
    grad_value_row = weight_grad(normed_one, grad_row_v)
    back_input = (
        project_back(grad_row_q, query_row)
        + project_back(grad_row_k, key_row)
        + project_back(grad_row_v, value_row)
    )
    back_stream, grad_gain_one, grad_shift_one = norm_back_one(back_input)
    input_grad = (grad_one + back_stream).astype(jnp.bfloat16)
    shares = (
        lax.psum_scatter(
            grad_gain_one.astype(jnp.bfloat16), "seq", scatter_dimension=0, tiled=True
        ).astype(jnp.float32),
        lax.psum_scatter(
            grad_shift_one.astype(jnp.bfloat16), "seq", scatter_dimension=0, tiled=True
        ).astype(jnp.float32),
        lax.psum_scatter(
            grad_gain_two.astype(jnp.bfloat16), "seq", scatter_dimension=0, tiled=True
        ).astype(jnp.float32),
        lax.psum_scatter(
            grad_shift_two.astype(jnp.bfloat16), "seq", scatter_dimension=0, tiled=True
        ).astype(jnp.float32),
        lax.psum_scatter(
            grad_gain_three.astype(jnp.bfloat16), "seq", scatter_dimension=0, tiled=True
        ).astype(jnp.float32),
        lax.psum_scatter(
            grad_shift_three.astype(jnp.bfloat16), "seq", scatter_dimension=0, tiled=True
        ).astype(jnp.float32),
        lax.psum_scatter(
            grad_query_row.astype(jnp.bfloat16), "seq", scatter_dimension=0, tiled=True
        ).astype(jnp.float32),
        lax.psum_scatter(
            grad_key_row.astype(jnp.bfloat16), "seq", scatter_dimension=0, tiled=True
        ).astype(jnp.float32),
        lax.psum_scatter(
            grad_value_row.astype(jnp.bfloat16), "seq", scatter_dimension=0, tiled=True
        ).astype(jnp.float32),
        lax.psum_scatter(
            grad_output_row.astype(jnp.bfloat16), "seq", scatter_dimension=0, tiled=True
        ).astype(jnp.float32),
        lax.psum_scatter(
            grad_query_col.astype(jnp.bfloat16), "seq", scatter_dimension=0, tiled=True
        ).astype(jnp.float32),
        lax.psum_scatter(
            grad_key_col.astype(jnp.bfloat16), "seq", scatter_dimension=0, tiled=True
        ).astype(jnp.float32),
        lax.psum_scatter(
            grad_value_col.astype(jnp.bfloat16), "seq", scatter_dimension=0, tiled=True
        ).astype(jnp.float32),
        lax.psum_scatter(
            grad_output_col.astype(jnp.bfloat16), "seq", scatter_dimension=0, tiled=True
        ).astype(jnp.float32),
        lax.psum_scatter(
            grad_feed_up.astype(jnp.bfloat16), "seq", scatter_dimension=0, tiled=True
        ).astype(jnp.float32),
        lax.psum_scatter(
            grad_feed_down.astype(jnp.bfloat16), "seq", scatter_dimension=0, tiled=True
        ).astype(jnp.float32),
    )
    totals = (
        lax.psum(shares[0].astype(jnp.bfloat16), "col").astype(jnp.float32),
        lax.psum(shares[1].astype(jnp.bfloat16), "col").astype(jnp.float32),
        lax.psum(shares[2].astype(jnp.bfloat16), "col").astype(jnp.float32),
        lax.psum(shares[3].astype(jnp.bfloat16), "col").astype(jnp.float32),
        lax.psum(shares[4].astype(jnp.bfloat16), "col").astype(jnp.float32),
        lax.psum(shares[5].astype(jnp.bfloat16), "col").astype(jnp.float32),
        lax.psum(shares[6].astype(jnp.bfloat16), "col").astype(jnp.float32),
        lax.psum(shares[7].astype(jnp.bfloat16), "col").astype(jnp.float32),
        lax.psum(shares[8].astype(jnp.bfloat16), "col").astype(jnp.float32),
        lax.psum(shares[9].astype(jnp.bfloat16), "col").astype(jnp.float32),
        lax.psum(shares[10].astype(jnp.bfloat16), "col").astype(jnp.float32),
        lax.psum(shares[11].astype(jnp.bfloat16), "col").astype(jnp.float32),
        lax.psum(shares[12].astype(jnp.bfloat16), "col").astype(jnp.float32),
        lax.psum(shares[13].astype(jnp.bfloat16), "col").astype(jnp.float32),
        lax.psum(shares[14].astype(jnp.bfloat16), "col").astype(jnp.float32),
        lax.psum(shares[15].astype(jnp.bfloat16), "col").astype(jnp.float32),
    )
    return (
        output,
        entropy,
        input_grad,
        totals[0],
        totals[1],
        totals[2],
        totals[3],
        totals[4],
        totals[5],
        totals[6],
        totals[7],
        totals[8],
        totals[9],
        totals[10],
        totals[11],
        totals[12],
        totals[13],
        totals[14],
        totals[15],
    )


def solution(mesh):
    return jax.shard_map(
        on_device,
        mesh=mesh,
        in_specs=(
            P("seq", "col", None),
            P(),
            P("col", None),
            P("col"),
            P("seq"),
            P("seq"),
            P("seq"),
            P("seq"),
            P("seq"),
            P("seq"),
            P("seq", None),
            P("seq", None),
            P("seq", None),
            P("seq", None),
            P("seq", None),
            P("seq", None),
            P("seq", None),
            P("seq", None),
            P("seq", None),
            P("seq", None),
            P("seq", "col", None),
        ),
        out_specs=(
            P("seq", "col", None),
            P(),
            P("seq", "col", None),
            P("seq"),
            P("seq"),
            P("seq"),
            P("seq"),
            P("seq"),
            P("seq"),
            P("seq", None),
            P("seq", None),
            P("seq", None),
            P("seq", None),
            P("seq", None),
            P("seq", None),
            P("seq", None),
            P("seq", None),
            P("seq", None),
            P("seq", None),
        ),
        check_vma=False,
    )
```

profile of v0, /device:TPU:0, one launch (start us, length us, event | category | flops | bytes accessed | tf_op | source)
XLA Modules:
  0.0 1053.9 jit_solution(9029271661781928081)
XLA Ops:
  18.5 30.5 %all-reduce.13 = (bf16[768]{0:T(1024)(128)(2,1)S(1)}, bf16[768]{0:T(1024)(128)(2,1)S(1)}, bf16[768]{0:T(1024)(128)(2,1)S(1)}, bf16[768]{0:T(1024)(128)(2,1)S(1)}...) all-reduce(bf16[768]{0:T(1024)(128)(2,1)S(1)} %dynamic-update-slice, ...), channel_id=1, replica_groups=mesh['col'=4,'seq'=8] {'seq'}, use_global_device_ids=true, to_apply=%add.1 | all-reduce | flops 4608 | bytes 18432
  65.8 17.7 %all-gather.19.cloned.1.call-done = bf16[768,768]{1,0:T(8,128)(2,1)} async-done(((bf16[96,768]{1,0:T(8,128)(2,1)}), bf16[768,768]{1,0:T(8,128)(2,1)}) %all-gather.19.cloned.1.call-update) | async-done | bytes 1179664 | tf_op jit(solution)/shard_map/all_gather | solution.py:124
  91.0 55.5 %all-reduce.20.cloned.1.call-done = f32[12,128,192]{1,2,0:T(8,128)} async-done(((f32[12,128,192]{1,2,0:T(8,128)}), f32[12,128,192]{1,2,0:T(8,128)}) %all-reduce.20.cloned.1.call-update) | async-done | bytes 1179664 | tf_op jit(solution)/shard_map/psum | solution.py:161
  148.9 20.8 %all-gather.21.cloned.1.call-done = bf16[768,768]{1,0:T(8,128)(2,1)} async-done(((bf16[96,768]{1,0:T(8,128)(2,1)}), bf16[768,768]{1,0:T(8,128)(2,1)}) %all-gather.21.cloned.1.call-update) | async-done | bytes 1179664 | tf_op jit(solution)/shard_map/all_gather | solution.py:127
  171.8 21.8 %all-gather.27.cloned.1.call-done = bf16[768,768]{1,0:T(8,128)(2,1)} async-done(((bf16[96,768]{1,0:T(8,128)(2,1)}), bf16[768,768]{1,0:T(8,128)(2,1)}) %all-gather.27.cloned.1.call-update) | async-done | bytes 1179664 | tf_op jit(solution)/shard_map/all_gather | solution.py:129
  195.9 21.7 %all-gather.23.cloned.1.call-done = bf16[768,768]{1,0:T(8,128)(2,1)} async-done(((bf16[96,768]{1,0:T(8,128)(2,1)}), bf16[768,768]{1,0:T(8,128)(2,1)}) %all-gather.23.cloned.1.call-update) | async-done | bytes 1179664 | tf_op jit(solution)/shard_map/all_gather | solution.py:130
  223.4 18.3 %all-gather.25.cloned.1.call-done = bf16[768,768]{1,0:T(8,128)(2,1)} async-done(((bf16[96,768]{1,0:T(8,128)(2,1)}), bf16[768,768]{1,0:T(8,128)(2,1)}) %all-gather.25.cloned.1.call-update) | async-done | bytes 1179664 | tf_op jit(solution)/shard_map/all_gather | solution.py:128
  243.6 25.3 %all-gather.37.cloned.1.call-done = bf16[1024,768]{1,0:T(8,128)(2,1)} async-done(((bf16[128,768]{1,0:T(8,128)(2,1)}), bf16[1024,768]{1,0:T(8,128)(2,1)}) %all-gather.37.cloned.1.call-update) | async-done | bytes 1572880 | tf_op jit(solution)/shard_map/all_gather | solution.py:190
  275.7 19.8 %all-gather.35.cloned.1.call-done = bf16[1024,768]{1,0:T(8,128)(2,1)} async-done(((bf16[128,768]{1,0:T(8,128)(2,1)}), bf16[1024,768]{1,0:T(8,128)(2,1)}) %all-gather.35.cloned.1.call-update) | async-done | bytes 1572880 | tf_op jit(solution)/shard_map/all_gather | solution.py:191
  301.6 17.8 %all-gather.29.cloned.1.call-done = bf16[768,768]{1,0:T(8,128)(2,1)} async-done(((bf16[96,768]{1,0:T(8,128)(2,1)}), bf16[768,768]{1,0:T(8,128)(2,1)}) %all-gather.29.cloned.1.call-update) | async-done | bytes 1179664 | tf_op jit(solution)/shard_map/all_gather | solution.py:131
  323.0 49.4 %all-gather.31.cloned.1.call-done = bf16[768,3072]{1,0:T(8,128)(2,1)} async-done(((bf16[96,3072]{1,0:T(8,128)(2,1)}), bf16[768,3072]{1,0:T(8,128)(2,1)}) %all-gather.31.cloned.1.call-update) | async-done | bytes 4718608 | tf_op jit(solution)/shard_map/all_gather | solution.py:132
  372.4 8.4 multiply_convert_fusion
  380.8 43.8 %all-gather.33.cloned.1.call-done = bf16[3072,768]{1,0:T(8,128)(2,1)} async-done(((bf16[384,768]{1,0:T(8,128)(2,1)}), bf16[3072,768]{1,0:T(8,128)(2,1)}) %all-gather.33.cloned.1.call-update) | async-done | bytes 4718608 | tf_op jit(solution)/shard_map/all_gather | solution.py:133
  448.3 64.4 %reduce-scatter.12.cloned.1.call-done = f32[1,128,1536]{1,2,0:T(8,128)} async-done(((f32[8,128,1536]{1,2,0:T(8,128)}), f32[1,128,1536]{1,2,0:T(8,128)}) %reduce-scatter.12.cloned.1.call-update) | async-done | bytes 786448 | tf_op jit(solution)/shard_map/reduce_scatter | solution.py:241
  538.3 10.4 psum.142
  551.2 25.1 %all-reduce.22.cloned.1.call-done = bf16[12,128,192]{1,2,0:T(8,128)(2,1)} async-done(((bf16[12,128,192]{1,2,0:T(8,128)(2,1)}), bf16[12,128,192]{1,2,0:T(8,128)(2,1)}) %all-reduce.22.cloned.1.call-update) | async-done | bytes 589840 | tf_op jit(solution)/shard_map/psum | solution.py:272
  594.4 10.3 collective-permute-done.3
  606.2 6.8 scatter-add.6
  614.4 7.8 scatter-add.9
  626.2 17.1 %reduce-scatter.22.cloned.1.call-done = bf16[96,768]{1,0:T(8,128)(2,1)} async-done(((bf16[768,768]{1,0:T(8,128)(2,1)}), bf16[96,768]{1,0:T(8,128)(2,1)}) %reduce-scatter.22.cloned.1.call-update) | async-done | bytes 147472 | tf_op jit(solution)/shard_map/reduce_scatter | solution.py:338
  643.4 55.2 %reduce-scatter.30.cloned.1.call-done = bf16[96,3072]{1,0:T(8,128)(2,1)} async-done(((bf16[768,3072]{1,0:T(8,128)(2,1)}), bf16[96,3072]{1,0:T(8,128)(2,1)}) %reduce-scatter.30.cloned.1.call-update) | async-done | bytes 589840 | tf_op jit(solution)/shard_map/reduce_scatter | solution.py:350
  698.6 55.7 %reduce-scatter.32.cloned.1.call-done = bf16[384,768]{1,0:T(8,128)(2,1)} async-done(((bf16[3072,768]{1,0:T(8,128)(2,1)}), bf16[384,768]{1,0:T(8,128)(2,1)}) %reduce-scatter.32.cloned.1.call-update) | async-done | bytes 589840 | tf_op jit(solution)/shard_map/reduce_scatter | solution.py:353
  754.3 33.4 %reduce-scatter.20.cloned.1.call-done = bf16[96,768]{1,0:T(8,128)(2,1)} async-done(((bf16[768,768]{1,0:T(8,128)(2,1)}), bf16[96,768]{1,0:T(8,128)(2,1)}) %reduce-scatter.20.cloned.1.call-update) | async-done | bytes 147472 | tf_op jit(solution)/shard_map/reduce_scatter | solution.py:335
  787.7 33.1 %reduce-scatter.26.cloned.1.call-done = bf16[96,768]{1,0:T(8,128)(2,1)} async-done(((bf16[768,768]{1,0:T(8,128)(2,1)}), bf16[96,768]{1,0:T(8,128)(2,1)}) %reduce-scatter.26.cloned.1.call-update) | async-done | bytes 147472 | tf_op jit(solution)/shard_map/reduce_scatter | solution.py:344
  820.8 33.4 %reduce-scatter.24.cloned.1.call-done = bf16[96,768]{1,0:T(8,128)(2,1)} async-done(((bf16[768,768]{1,0:T(8,128)(2,1)}), bf16[96,768]{1,0:T(8,128)(2,1)}) %reduce-scatter.24.cloned.1.call-update) | async-done | bytes 147472 | tf_op jit(solution)/shard_map/reduce_scatter | solution.py:341
  854.1 33.9 %reduce-scatter.14.cloned.1.call-done = bf16[96,768]{1,0:T(8,128)(2,1)} async-done(((bf16[768,768]{1,0:T(8,128)(2,1)}), bf16[96,768]{1,0:T(8,128)(2,1)}) %reduce-scatter.14.cloned.1.call-update) | async-done | bytes 147472 | tf_op jit(solution)/shard_map/reduce_scatter | solution.py:326
  888.1 34.0 %reduce-scatter.16.cloned.1.call-done = bf16[96,768]{1,0:T(8,128)(2,1)} async-done(((bf16[768,768]{1,0:T(8,128)(2,1)}), bf16[96,768]{1,0:T(8,128)(2,1)}) %reduce-scatter.16.cloned.1.call-update) | async-done | bytes 147472 | tf_op jit(solution)/shard_map/reduce_scatter | solution.py:329
  922.1 33.4 %reduce-scatter.18.cloned.1.call-done = bf16[96,768]{1,0:T(8,128)(2,1)} async-done(((bf16[768,768]{1,0:T(8,128)(2,1)}), bf16[96,768]{1,0:T(8,128)(2,1)}) %reduce-scatter.18.cloned.1.call-update) | async-done | bytes 147472 | tf_op jit(solution)/shard_map/reduce_scatter | solution.py:332
  960.1 10.5 psum.141
  975.4 25.9 %all-reduce.12 = (bf16[768]{0:T(1024)(128)(2,1)S(1)}, bf16[768]{0:T(1024)(128)(2,1)S(1)}, bf16[768]{0:T(1024)(128)(2,1)S(1)}, bf16[768]{0:T(1024)(128)(2,1)S(1)}...) all-reduce(bf16[768]{0:T(1024)(128)(2,1)S(1)} %get-tuple-element.45, ...), channel_id=5, replica_groups=mesh['col'=4,'seq'=8] {'seq'}, use_global_device_ids=true, to_apply=%region_29.30.clone | all-reduce | flops 4608 | bytes 18432
  1001.8 8.2 all-reduce.14
  1014.1 19.8 %all-reduce.24.cloned.1.call-done = (bf16[96,768]{1,0:T(8,128)(2,1)}, bf16[96,768]{1,0:T(8,128)(2,1)}, bf16[96,768]{1,0:T(8,128)(2,1)}, bf16[96,768]{1,0:T(8,128...) async-done(((bf16[96,768]{1,0:T(8,128)(2,1)}, ...) | async-done | bytes 2359312 | tf_op jit(solution)/shard_map/psum | solution.py:364
  (420 shorter events, 163.6 us)
Async XLA Ops:
  7.2 46.1 %all-gather.17.cloned.1.call-start = ((), (), s32[]{:S(2)}) async-start(), calls=%async_computation.12 | async-start | bytes 1327104 | tf_op jit(solution)/shard_map/all_gather | solution.py:126
  7.9 51.5 %all-gather.15.cloned.1.call-start = ((), (), s32[]{:S(2)}) async-start(), calls=%async_computation.11 | async-start | bytes 1327104 | tf_op jit(solution)/shard_map/all_gather | solution.py:125
  8.7 74.8 %all-gather.19.cloned.1.call-start = ((), (), s32[]{:S(2)}) async-start(), calls=%async_computation.13 | async-start | bytes 1327104 | tf_op jit(solution)/shard_map/all_gather | solution.py:124
  9.4 137.0 %all-reduce.20.cloned.1.call-start = ((), (), s32[]{:S(2)}) async-start(), calls=%async_computation.14 | async-start | bytes 2359296 | tf_op jit(solution)/shard_map/psum | solution.py:161
  61.1 24.2 %collective-permute-start = (bf16[2,1,32,768]{3,2,1,0:T(8,128)(2,1)S(1)}, bf16[2,1,32,768]{3,2,1,0:T(8,128)(2,1)S(1)}, u32[]{:S(2)}, u32[]{:S(2)}) collective-permute-start(bf16[2,1,32,768]{3,2,1,0:T(8,128)(2,1)S(1)} %get-tuple-element.94), channel_id=1, source_target_pairs={{0,8},{8,16},{16,24},{1,9},{9,17},{17,25},{2,10},{10,18},{18,26},{... | collective-permute-start | bytes 294920 | tf_op jit(solution)/shard_map/ppermute | solution.py:26
  64.5 20.8 %collective-permute-start.1 = (bf16[2,1,32,768]{3,2,1,0:T(8,128)(2,1)S(1)}, bf16[2,1,32,768]{3,2,1,0:T(8,128)(2,1)S(1)}, u32[]{:S(2)}, u32[]{:S(2)}) collective-permute-start(bf16[2,1,32,768]{3,2,1,0:T(8,128)(2,1)S(1)} %get-tuple-element.95), channel_id=1, source_target_pairs={{8,0},{16,8},{24,16},{9,1},{17,9},{25,17},{10,2},{18,10},{26,18},{... | collective-permute-start | bytes 294920 | tf_op jit(solution)/shard_map/ppermute | solution.py:28
  87.0 82.6 %all-gather.21.cloned.1.call-start = ((), (), s32[]{:S(2)}) async-start(), calls=%async_computation.15 | async-start | bytes 1327104 | tf_op jit(solution)/shard_map/all_gather | solution.py:127
  87.6 106.0 %all-gather.27.cloned.1.call-start = ((), (), s32[]{:S(2)}) async-start(), calls=%async_computation.18 | async-start | bytes 1327104 | tf_op jit(solution)/shard_map/all_gather | solution.py:129
  88.2 129.5 %all-gather.23.cloned.1.call-start = ((), (), s32[]{:S(2)}) async-start(), calls=%async_computation.16 | async-start | bytes 1327104 | tf_op jit(solution)/shard_map/all_gather | solution.py:130
  88.9 152.8 %all-gather.25.cloned.1.call-start = ((), (), s32[]{:S(2)}) async-start(), calls=%async_computation.17 | async-start | bytes 1327104 | tf_op jit(solution)/shard_map/all_gather | solution.py:128
  89.7 179.2 %all-gather.37.cloned.1.call-start = ((), (), s32[]{:S(2)}) async-start(), calls=%async_computation.35 | async-start | bytes 1769472 | tf_op jit(solution)/shard_map/all_gather | solution.py:190
  195.9 99.7 %all-gather.35.cloned.1.call-start = ((), (), s32[]{:S(2)}) async-start(), calls=%async_computation.34 | async-start | bytes 1769472 | tf_op jit(solution)/shard_map/all_gather | solution.py:191
  220.0 99.4 %all-gather.29.cloned.1.call-start = ((), (), s32[]{:S(2)}) async-start(), calls=%async_computation.19 | async-start | bytes 1327104 | tf_op jit(solution)/shard_map/all_gather | solution.py:131
  220.7 151.7 %all-gather.31.cloned.1.call-start = ((), (), s32[]{:S(2)}) async-start(), calls=%async_computation.20 | async-start | bytes 5308416 | tf_op jit(solution)/shard_map/all_gather | solution.py:132
  221.3 203.3 %all-gather.33.cloned.1.call-start = ((), (), s32[]{:S(2)}) async-start(), calls=%async_computation.21 | async-start | bytes 5308416 | tf_op jit(solution)/shard_map/all_gather | solution.py:133
  222.0 290.6 %reduce-scatter.12.cloned.1.call-start = ((), (), s32[]{:S(2)}) async-start(), calls=%async_computation.22 | async-start | bytes 7077888 | tf_op jit(solution)/shard_map/reduce_scatter | solution.py:241
  443.9 132.4 %all-reduce.22.cloned.1.call-start = ((), (), s32[]{:S(2)}) async-start(), calls=%async_computation.23 | async-start | bytes 1179648 | tf_op jit(solution)/shard_map/psum | solution.py:272
  521.2 105.1 %reduce-scatter.28.cloned.1.call-start = ((), (), s32[]{:S(2)}) async-start(), calls=%async_computation.31 | async-start | bytes 1327104 | tf_op jit(solution)/shard_map/reduce_scatter | solution.py:347
  522.8 120.6 %reduce-scatter.22.cloned.1.call-start = ((), (), s32[]{:S(2)}) async-start(), calls=%async_computation.28 | async-start | bytes 1327104 | tf_op jit(solution)/shard_map/reduce_scatter | solution.py:338
  524.4 174.2 %reduce-scatter.30.cloned.1.call-start = ((), (), s32[]{:S(2)}) async-start(), calls=%async_computation.32 | async-start | bytes 5308416 | tf_op jit(solution)/shard_map/reduce_scatter | solution.py:350
  528.8 225.4 %reduce-scatter.32.cloned.1.call-start = ((), (), s32[]{:S(2)}) async-start(), calls=%async_computation.33 | async-start | bytes 5308416 | tf_op jit(solution)/shard_map/reduce_scatter | solution.py:353
  533.6 254.1 %reduce-scatter.20.cloned.1.call-start = ((), (), s32[]{:S(2)}) async-start(), calls=%async_computation.27 | async-start | bytes 1327104 | tf_op jit(solution)/shard_map/reduce_scatter | solution.py:335
  535.9 284.8 %reduce-scatter.26.cloned.1.call-start = ((), (), s32[]{:S(2)}) async-start(), calls=%async_computation.30 | async-start | bytes 1327104 | tf_op jit(solution)/shard_map/reduce_scatter | solution.py:344
  537.6 316.6 %reduce-scatter.24.cloned.1.call-start = ((), (), s32[]{:S(2)}) async-start(), calls=%async_computation.29 | async-start | bytes 1327104 | tf_op jit(solution)/shard_map/reduce_scatter | solution.py:341
  550.9 337.2 %reduce-scatter.14.cloned.1.call-start = ((), (), s32[]{:S(2)}) async-start(), calls=%async_computation.24 | async-start | bytes 1327104 | tf_op jit(solution)/shard_map/reduce_scatter | solution.py:326
  582.4 339.7 %reduce-scatter.16.cloned.1.call-start = ((), (), s32[]{:S(2)}) async-start(), calls=%async_computation.25 | async-start | bytes 1327104 | tf_op jit(solution)/shard_map/reduce_scatter | solution.py:329
  584.4 10.0 collective-permute-start.2
  587.8 16.9 %collective-permute-start.3 = (bf16[2,1,32,768]{2,3,1,0:T(8,128)(2,1)S(1)}, bf16[2,1,32,768]{2,3,1,0:T(8,128)(2,1)S(1)}, u32[]{:S(2)}, u32[]{:S(2)}) collective-permute-start(bf16[2,1,32,768]{2,3,1,0:T(8,128)(2,1)S(1)} %fusion.17), channel_id=1, source_target_pairs={{8,0},{16,8},{24,16},{9,1},{17,9},{25,17},{10,2},{18,10},{26,18},{... | collective-permute-start | bytes 294920 | tf_op jit(solution)/shard_map/ppermute | solution.py:28
  623.7 331.7 %reduce-scatter.18.cloned.1.call-start = ((), (), s32[]{:S(2)}) async-start(), calls=%async_computation.26 | async-start | bytes 1327104 | tf_op jit(solution)/shard_map/reduce_scatter | solution.py:332
  625.4 330.1 %copy-start.25 = (f32[128,768]{1,0:T(8,128)S(1)}, f32[128,768]{1,0:T(8,128)}, u32[]{:S(2)}) copy-start(f32[128,768]{1,0:T(8,128)} %copy-done.24) | copy-start | bytes 1179652
  625.4 330.1 %copy-start.12 = (bf16[128,3072]{1,0:T(8,128)(2,1)S(1)}, bf16[128,3072]{1,0:T(8,128)(2,1)}, u32[]{:S(2)}) copy-start(bf16[128,3072]{1,0:T(8,128)(2,1)} %get-tuple-element.89) | copy-start | bytes 2359300
  625.4 408.4 %all-reduce.24.cloned.1.call-start = ((), (), s32[]{:S(2)}) async-start(), calls=%async_computation.36 | async-start | bytes 4718592 | tf_op jit(solution)/shard_map/psum | solution.py:364
  (94 other events, 1143.2 us)
Sparse Core Ops, SparseCore 0:
  9.7 25.5 all-gather.16
  36.9 22.4 all-gather.14
  61.1 22.3 all-gather.18
  87.1 59.2 all-reduce.19
  147.9 21.6 all-gather.20
  171.1 22.4 all-gather.26
  195.2 22.4 all-gather.22
  219.3 22.4 all-gather.24
  244.0 24.8 all-gather.36
  270.9 24.5 all-gather.34
  297.2 22.1 all-gather.28
  320.9 51.4 all-gather.30
  374.0 50.5 all-gather.32
  444.0 68.6 reduce-scatter.11
  521.3 54.9 all-reduce.21
  578.4 31.6 reduce-scatter.27
  612.3 31.0 reduce-scatter.21
  645.5 53.0 reduce-scatter.29
  700.9 53.3 reduce-scatter.31
  756.4 31.2 reduce-scatter.19
  790.0 30.7 reduce-scatter.25
  823.1 31.0 reduce-scatter.23
  857.0 31.0 reduce-scatter.13
  890.8 31.2 reduce-scatter.15
  924.4 31.0 reduce-scatter.17
  959.5 74.3 all-reduce.23
where the time goes:
time: 1060 us; the launch traced here: 1050 us
  waiting for transfers between devices  777 us (73%)
  blocking collectives  85.5 us (8%)
  matrix products  68.7 us (6%)
  local copies, waits for them, and re-layouts  47.4 us (4%)
  other arithmetic  43.4 us (4%)
  between operations  21.2 us (2%)
  starting transfers between devices  11 us (1%)
    reduce_scatter x1, waiting for transfers between devices, on_device(): lax.psum_scatter(jnp.concatenate([key_part.reshape(row_count, cols_dev, m...  64.4 us
    unnamed x2, blocking collectives  56.4 us
    reduce_scatter x1, waiting for transfers between devices, on_device(): lax.psum_scatter(grad_feed_down.astype(jnp.bfloat16), 'seq', scatter_dime...  55.7 us
    psum x1, waiting for transfers between devices, on_device(): row_scores = lax.psum(partial_logits, 'seq') * row_scale  55.5 us
    reduce_scatter x1, waiting for transfers between devices, on_device(): lax.psum_scatter(grad_feed_up.astype(jnp.bfloat16), 'seq', scatter_dimens...  55.2 us
    all_gather x1, waiting for transfers between devices, on_device(): lax.all_gather(feed_in, 'seq', axis=0, tiled=True)  49.4 us
    all_gather x1, waiting for transfers between devices, on_device(): lax.all_gather(feed_out, 'seq', axis=0, tiled=True)  43.8 us
    reduce_scatter x1, waiting for transfers between devices, on_device(): lax.psum_scatter(grad_key_row.astype(jnp.bfloat16), 'seq', scatter_dimens...  34 us
  transfers between devices with their start and end apart: 30, of which 26 were waited for; matrix products, arithmetic and copies ran while one was open for 11% of the time, Pallas kernels for 0%

commit v1 on v0

--- a/solution.py
+++ b/solution.py
@@ -4,6 +4,8 @@
 import jax
 import jax.numpy as jnp
 from jax import lax
+from jax.experimental import pallas as pl
+from jax.experimental.pallas import tpu as pltpu
 from jax.sharding import PartitionSpec as P
 
 HEADS = 12
@@ -84,7 +86,7 @@
     return jnp.einsum("rci,rcj->ij", activations, gradient, preferred_element_type=jnp.float32)
 
 
-def on_device(
+def general_plan(
     tokens,
     offsets,
     band,
@@ -395,6 +397,1056 @@
     )
 
 
+def kernel_call(body, outs, args, smem=(), anywhere=(), scratch=(), flops=0):
+    out_shapes = [jax.ShapeDtypeStruct(shape, kind) for shape, kind in outs]
+    moved = sum(item.size * item.dtype.itemsize for item in args) + sum(
+        item.size * item.dtype.itemsize for item in out_shapes
+    )
+    in_specs = []
+    for place in range(len(args)):
+        if place in smem:
+            in_specs.append(pl.BlockSpec(memory_space=pltpu.SMEM))
+        elif place in anywhere:
+            in_specs.append(pl.BlockSpec(memory_space=pl.ANY))
+        else:
+            in_specs.append(pl.BlockSpec(memory_space=pltpu.VMEM))
+    return pl.pallas_call(
+        body,
+        out_shape=out_shapes,
+        in_specs=in_specs,
+        out_specs=[pl.BlockSpec(memory_space=pltpu.VMEM)] * len(outs),
+        scratch_shapes=list(scratch),
+        compiler_params=pltpu.CompilerParams(vmem_limit_bytes=48 << 20),
+        cost_estimate=pl.CostEstimate(
+            flops=int(flops), bytes_accessed=int(moved), transcendentals=0
+        ),
+    )(*args)
+
+
+def dot(left, right):
+    return jnp.dot(left, right, preferred_element_type=jnp.float32)
+
+
+def dot_back(left, right):
+    return lax.dot_general(
+        left, right, (((1,), (1,)), ((), ())), preferred_element_type=jnp.float32
+    )
+
+
+def dot_tokens(left, right):
+    return lax.dot_general(
+        left, right, (((0,), (0,)), ((), ())), preferred_element_type=jnp.float32
+    )
+
+
+def unit_norm(inputs):
+    centred = inputs - jnp.mean(inputs, axis=-1, keepdims=True)
+    scale = lax.rsqrt(jnp.mean(centred * centred, axis=-1, keepdims=True) + norm_eps)
+    return centred * scale, scale
+
+
+def unit_norm_back(given, unit, scale, gain):
+    scaled = given * gain
+    first = jnp.mean(scaled, axis=-1, keepdims=True)
+    second = jnp.mean(scaled * unit, axis=-1, keepdims=True)
+    return scale * (scaled - first - unit * second)
+
+
+def norm_sums(given, unit):
+    return jnp.concatenate(
+        [
+            jnp.sum(given * unit, axis=0, keepdims=True),
+            jnp.sum(given, axis=0, keepdims=True),
+        ],
+        axis=0,
+    )
+
+
+def head_mask(width, model_width):
+    rows = lax.broadcasted_iota(jnp.int32, (HEADS * width, model_width), 0) // width
+    lanes = lax.broadcasted_iota(jnp.int32, (HEADS * width, model_width), 1) // HEAD_DIM
+    return rows == lanes
+
+
+def spread_heads(block, mask):
+    tiled = jnp.concatenate([block] * HEADS, axis=0)
+    return jnp.where(mask, tiled, jnp.zeros_like(tiled))
+
+
+def fold_heads(product, mask, width):
+    kept = jnp.where(mask, product, 0.0)
+    total = kept[:width]
+    for head in range(1, HEADS):
+        total = total + kept[head * width : (head + 1) * width]
+    return total
+
+
+def head_of_lane(model_width):
+    rows = lax.broadcasted_iota(jnp.int32, (model_width, 128), 0) // HEAD_DIM
+    lanes = lax.broadcasted_iota(jnp.int32, (model_width, 128), 1)
+    return (rows == lanes).astype(jnp.bfloat16)
+
+
+def per_head_sum(product, lane_heads):
+    high = product.astype(jnp.bfloat16)
+    rest = (product - high.astype(jnp.float32)).astype(jnp.bfloat16)
+    return dot(high, lane_heads) + dot(rest, lane_heads)
+
+
+def slot_span(spot_ref, side, slot, width):
+    return pl.ds(pl.multiple_of((slot ^ spot_ref[side]) * width, width), width)
+
+
+def window_rows(spot_ref, near_ref, left_ref, right_ref, which, slot, width):
+    return jnp.concatenate(
+        [
+            left_ref[which, slot_span(spot_ref, 5, slot, width)],
+            near_ref[which, slot * width : (slot + 1) * width],
+            right_ref[which, slot_span(spot_ref, 6, slot, width)],
+        ],
+        axis=0,
+    )
+
+
+def half_of(values, core, width):
+    return jnp.where(core == 0, values[:, :width], values[:, width:])
+
+
+def fast_plan(
+    tokens,
+    offsets,
+    band,
+    col_counts,
+    norms,
+    row_weights,
+    col_weights,
+    feed_in,
+    feed_out,
+    cotangent,
+):
+    f32, bf16 = jnp.float32, jnp.bfloat16
+    cols_dev, model = tokens.shape[1:]
+    cols_axis, seqs = lax.axis_size("col"), lax.axis_size("seq")
+    chips = seqs // 2
+    width = cols_dev // chips
+    toks = chips * width
+    shard = model // seqs
+    half = model // 2
+    hidden = feed_out.shape[0] * seqs // cols_axis
+    fold = HEADS * width
+    span = 3 * width
+    col_at = lax.axis_index("col")
+    seq_at = lax.axis_index("seq")
+    chip, core = seq_at // 2, seq_at % 2
+    flip = col_at % 2
+
+    def chunk_of(chip_index):
+        return jnp.where(flip == 0, chip_index, chips - 1 - chip_index)
+
+    chunk = chunk_of(chip)
+    piece = col_at * chips + chunk
+
+    def along_chips(values, step):
+        return lax.ppermute(values, "seq", [(i, i ^ (2 * step)) for i in range(seqs)])
+
+    def along_core(values):
+        return lax.ppermute(values, "seq", [(i, i ^ 1) for i in range(seqs)])
+
+    def along_cols(values, step):
+        return lax.ppermute(values, "col", [(i, i ^ step) for i in range(cols_axis)])
+
+    def place_of(piece_index, core_index):
+        block, part = divmod(piece_index, chips)
+        chip_index = part if block % 2 == 0 else chips - 1 - part
+        return block * seqs + chip_index * 2 + core_index
+
+    rightward = [
+        (place_of(i, k), place_of(i + 1, k)) for i in range(cols_axis * chips - 1) for k in (0, 1)
+    ]
+    leftward = [(target, source) for source, target in rightward]
+
+    def to_right(values):
+        return lax.ppermute(values, ("col", "seq"), rightward)
+
+    def to_left(values):
+        return lax.ppermute(values, ("col", "seq"), leftward)
+
+    steps = range(1, chips)
+    col_steps = range(1, cols_axis)
+
+    def turn_to(other):
+        block, rest = other // chips, other % chips
+        return chip ^ jnp.where(block % 2 == 0, rest, chips - 1 - rest)
+
+    to_left_turn = turn_to(jnp.maximum(piece - 1, 0))
+    to_right_turn = turn_to(jnp.minimum(piece + 1, cols_axis * chips - 1))
+    spot = jnp.stack(
+        [col_at, chip, core, chunk, col_counts[0], to_left_turn, to_right_turn]
+    ).astype(jnp.int32)
+
+    both = jnp.concatenate([tokens, cotangent], axis=0)
+
+    def chunk_rows(values, index):
+        return lax.dynamic_slice_in_dim(values, chunk_of(index) * width, width, axis=1)
+
+    got = [chunk_rows(both, chip)] + [
+        along_chips(chunk_rows(both, chip ^ step), step) for step in steps
+    ]
+    stream_in = jnp.concatenate([item[0] for item in got], axis=0)
+    given_out = jnp.concatenate([item[1] for item in got], axis=0)
+
+    norm_line = jnp.concatenate(
+        list(norms)
+        + [
+            col_counts.astype(bf16),
+            jnp.zeros((model - 6 * shard - 1,), bf16),
+        ]
+    )
+    norm_tile = jnp.broadcast_to(norm_line[None, None], (cols_axis, 8, model))
+
+    def gather_layer(weights, extra):
+        own = jnp.stack(weights)
+        if extra is not None:
+            own = jnp.concatenate([own, extra], axis=1)
+        mine = lax.dynamic_index_in_dim(own, col_at, axis=0, keepdims=False)
+        rows = jnp.stack([along_chips(mine, step) for step in steps])
+        near = [rows] + [along_cols(rows, step) for step in col_steps]
+        own_pair = (own, along_core(own))
+        near_pair = (near, [along_core(item) for item in near])
+        return own_pair, near_pair
+
+    def assemble_layer(own_pair, near_pair):
+        def body(spot_ref, *refs):
+            count = 2 * (1 + cols_axis)
+            pieces, out_ref, sems = refs[:count], refs[count], refs[count + 1]
+            at_col, at_chip, at_core = spot_ref[0], spot_ref[1], spot_ref[2]
+            copies = []
+
+            def move(source, matrix, from_chip, from_core):
+                row = pl.multiple_of((from_chip * 2 + from_core) * shard, shard)
+                copies.append(
+                    pltpu.make_async_copy(
+                        source, out_ref.at[matrix, pl.ds(row, shard)], sems.at[len(copies)]
+                    )
+                )
+                copies[-1].start()
+
+            for other in (0, 1):
+                base = other * (1 + cols_axis)
+                from_core = at_core ^ other
+                for matrix in range(cols_axis):
+                    move(pieces[base].at[matrix, pl.ds(0, shard)], matrix, at_chip, from_core)
+                for step in range(cols_axis):
+                    for hop in steps:
+                        move(
+                            pieces[base + 1 + step].at[hop - 1, pl.ds(0, shard)],
+                            at_col ^ step,
+                            at_chip ^ hop,
+                            from_core,
+                        )
+            for copy in copies:
+                copy.wait()
+
+        args = [spot, own_pair[0], *near_pair[0], own_pair[1], *near_pair[1]]
+        total = 2 * cols_axis * chips
+        return kernel_call(
+            body,
+            [((cols_axis, model, model), bf16)],
+            args,
+            smem=(0,),
+            anywhere=tuple(range(1, len(args))),
+            scratch=[pltpu.SemaphoreType.DMA((total,))],
+        )[0]
+
+    row_own, row_near = gather_layer(row_weights, norm_tile)
+    weights_row = assemble_layer(row_own, row_near)
+    lines = jnp.stack(
+        [
+            line
+            for side in (0, 1)
+            for line in [row_own[side][0, shard]]
+            + [row_near[side][0][step - 1, shard] for step in steps]
+        ]
+    )
+    line_shard = jnp.stack(
+        [(chip ^ step) * 2 + (core ^ side) for side in (0, 1) for step in range(chips)]
+    )
+    order = (jnp.arange(seqs)[:, None] == line_shard[None, :]).astype(bf16)
+    ordered = jnp.dot(order, lines, preferred_element_type=f32)
+    norm_rows = ordered[:, : 6 * shard].reshape(seqs, 6, shard).transpose(1, 0, 2)
+    norm_rows = jnp.pad(norm_rows.reshape(6, model), ((0, 2), (0, 0)))
+    count_total = col_counts[0].astype(f32)
+    for step in col_steps:
+        count_total = count_total + row_near[0][step][0, shard, 6 * shard].astype(f32)
+    entropy_scale = jnp.reshape(entropy_weight / (HEADS * count_total), (1,))
+
+    col_own, col_near = gather_layer(col_weights, None)
+    weights_col = assemble_layer(col_own, col_near)
+
+    part = feed_out.shape[0] // cols_axis
+    feed_cols = lax.dynamic_slice_in_dim(
+        feed_in.reshape(shard, seqs, feed_out.shape[0]), col_at * part, part, axis=2
+    ).reshape(shard, hidden)
+    feed_rows = lax.dynamic_slice_in_dim(feed_out, col_at * part, part, axis=0)
+    feed_own = jnp.stack([feed_cols, feed_rows])
+    feed_all = jnp.stack([feed_own] + [along_chips(feed_own, step) for step in steps])
+    feed_other = along_core(feed_all)
+
+    def assemble_feed():
+        def body(spot_ref, near_ref, far_ref, out_ref, sems):
+            at_chip, at_core = spot_ref[1], spot_ref[2]
+            copies = []
+            for other, ref in enumerate((near_ref, far_ref)):
+                for hop in range(chips):
+                    row = ((at_chip ^ hop) * 2 + (at_core ^ other)) * shard
+                    for matrix in (0, 1):
+                        copies.append(
+                            pltpu.make_async_copy(
+                                ref.at[hop, matrix],
+                                out_ref.at[matrix, pl.ds(pl.multiple_of(row, shard), shard)],
+                                sems.at[len(copies)],
+                            )
+                        )
+                        copies[-1].start()
+            for copy in copies:
+                copy.wait()
+
+        return kernel_call(
+            body,
+            [((2, model, hidden), bf16)],
+            [spot, feed_all, feed_other],
+            smem=(0,),
+            anywhere=(1, 2),
+            scratch=[pltpu.SemaphoreType.DMA((4 * chips,))],
+        )[0]
+
+    weights_feed = assemble_feed()
+    given_near = [given_out] + [along_cols(given_out, step) for step in col_steps]
+
+    half_width = model // 2
+    frequency = jnp.exp(-math.log(1000.0) * jnp.arange(half_width, dtype=f32) / half_width)
+    col_place = (jnp.arange(width, dtype=jnp.int32) + piece * width + offsets[1]).astype(f32)
+    seq_slots = jnp.stack([(chip ^ step) * 2 + core for step in range(chips)])
+    row_place = (seq_slots + offsets[0]).astype(f32)
+    waves = 0.5 * jnp.sin(
+        jnp.concatenate([col_place, row_place])[:, None] * frequency[None, :]
+    )
+    band_here = lax.dynamic_slice_in_dim(band, chunk * width, width, axis=0)
+    query_index = jnp.arange(width, dtype=jnp.int32)[:, None]
+    key_index = jnp.arange(span, dtype=jnp.int32)[None, :]
+    distance = key_index - query_index
+    choose = jnp.arange(2 * WINDOW + 1, dtype=jnp.int32)
+    matches = (distance[:, None, :] == choose[None, :, None]) & (band_here[:, :, None] == 1)
+    key_global = (piece - 1) * width + key_index
+    inside = (key_global >= 0) & (key_global < cols_axis * cols_dev)
+    allowed = ((jnp.any(matches, axis=1) | (distance == WINDOW)) & inside).astype(f32)
+
+    def project_row(stream_ref, waves_ref, norm_ref, weight_ref, zero_ref, low_ref, q_ref, kv_ref):
+        for slot in range(chips):
+            rows = slice(slot * width, (slot + 1) * width)
+            zero_ref[rows, :half] = stream_ref[rows, :half].astype(f32) + waves_ref[:width]
+            zero_ref[rows, half:] = (
+                stream_ref[rows, half:].astype(f32) + waves_ref[width + slot : width + slot + 1]
+            )
+        unit, _ = unit_norm(zero_ref[...])
+        low = (unit * norm_ref[0:1] + norm_ref[1:2]).astype(bf16)
+        low_ref[...] = low
+        q_ref[...] = dot(low, weight_ref[0]).astype(bf16)
+        kv_ref[0] = dot(low, weight_ref[1]).astype(bf16)
+        kv_ref[1] = dot(low, weight_ref[2]).astype(bf16)
+
+    big = 2.0 * toks * model * model
+    stream_zero, normed_one, row_q, row_kv = kernel_call(
+        project_row,
+        [
+            ((toks, model), f32),
+            ((toks, model), bf16),
+            ((toks, model), bf16),
+            ((2, toks, model), bf16),
+        ],
+        [stream_in, waves, norm_rows, weights_row],
+        flops=3 * big,
+    )
+    kv_left = to_right(row_kv)
+    kv_right = to_left(row_kv)
+
+    def tied_logits(spot_ref, q_ref, near_ref, left_ref, right_ref, out_ref):
+        mask = head_mask(width, model)
+        total = None
+        for slot in range(chips):
+            keys = window_rows(spot_ref, near_ref, left_ref, right_ref, 0, slot, width)
+            spread = spread_heads(q_ref[slot * width : (slot + 1) * width], mask)
+            term = dot_back(spread, keys)
+            total = term if total is None else total + term
+        out_ref[...] = total
+
+    logits = kernel_call(
+        tied_logits,
+        [((fold, span), f32)],
+        [spot, row_q, row_kv, kv_left, kv_right],
+        smem=(0,),
+        flops=chips * 2.0 * fold * model * span,
+    )[0]
+    logits_other = along_core(logits)
+    row_scale = 1.0 / math.sqrt(HEAD_DIM * seqs)
+    col_scale = 1.0 / math.sqrt(HEAD_DIM)
+
+    def attend_row(
+        spot_ref,
+        logits_ref,
+        other_ref,
+        allowed_ref,
+        near_ref,
+        left_ref,
+        right_ref,
+        zero_ref,
+        norm_ref,
+        weight_ref,
+        scores_ref,
+        probs_ref,
+        mix_ref,
+        stream_ref,
+        low_ref,
+        entropy_ref,
+    ):
+        mask = head_mask(width, model)
+        scores = (logits_ref[...] + other_ref[...]) * row_scale
+        open_here = jnp.concatenate([allowed_ref[...]] * HEADS, axis=0) > 0.5
+        masked = jnp.where(open_here, scores, -1000000000.0)
+        largest = jnp.max(masked, axis=-1, keepdims=True)
+        powers = jnp.exp(masked - largest)
+        total = jnp.sum(powers, axis=-1, keepdims=True)
+        probs = powers / total
+        kept = jnp.where(open_here, scores, 0.0)
+        entropies = largest + jnp.log(total) - jnp.sum(probs * kept, axis=-1, keepdims=True)
+        rows = lax.broadcasted_iota(jnp.int32, (fold, 1), 0) % width
+        entropies = jnp.where(rows + spot_ref[3] * width < spot_ref[4], entropies, 0.0)
+        lanes = lax.broadcasted_iota(jnp.int32, (1, model), 1)
+        found = jnp.sum(entropies, axis=0, keepdims=True)
+        entropy_ref[...] = jnp.where((lanes == 0) & (spot_ref[2] == 0), found, 0.0)
+        scores_ref[...] = kept
+        probs_ref[...] = probs
+        low_probs = probs.astype(bf16)
+        for slot in range(chips):
+            values = window_rows(spot_ref, near_ref, left_ref, right_ref, 1, slot, width)
+            mix_ref[slot * width : (slot + 1) * width] = fold_heads(
+                dot(low_probs, values), mask, width
+            ).astype(bf16)
+        stream = zero_ref[...] + dot(mix_ref[...], weight_ref[3])
+        stream_ref[...] = stream
+        unit, _ = unit_norm(stream)
+        low_ref[...] = (unit * norm_ref[2:3] + norm_ref[3:4]).astype(bf16)
+
+    scores, probs, row_mix, stream_one, normed_two, entropy_row = kernel_call(
+        attend_row,
+        [
+            ((fold, span), f32),
+            ((fold, span), f32),
+            ((toks, model), bf16),
+            ((toks, model), f32),
+            ((toks, model), bf16),
+            ((1, model), f32),
+        ],
+        [
+            spot,
+            logits,
+            logits_other,
+            allowed,
+            row_kv,
+            kv_left,
+            kv_right,
+            stream_zero,
+            norm_rows,
+            weights_row,
+        ],
+        smem=(0,),
+        flops=chips * 2.0 * fold * model * span + big,
+    )
+
+    def project_col(low_ref, weight_ref, q_ref, kv_ref):
+        low = low_ref[...]
+        q_ref[...] = dot(low, weight_ref[0]).astype(bf16)
+        kv_ref[0] = dot(low, weight_ref[1]).astype(bf16)
+        kv_ref[1] = dot(low, weight_ref[2]).astype(bf16)
+
+    col_q, col_kv = kernel_call(
+        project_col,
+        [((toks, model), bf16), ((2, toks, model), bf16)],
+        [normed_two, weights_col],
+        flops=3 * big,
+    )
+    kv_other = along_core(col_kv)
+
+    def slot_rows(slot):
+        return slice(slot * width, (slot + 1) * width)
+
+    def attend_col(
+        q_ref,
+        near_ref,
+        far_ref,
+        one_ref,
+        norm_ref,
+        weight_ref,
+        probs_ref,
+        mix_ref,
+        stream_ref,
+        low_ref,
+    ):
+        lane_heads = head_of_lane(model)
+        sides = (near_ref, far_ref)
+        for slot in range(chips):
+            query = q_ref[slot_rows(slot)].astype(f32)
+            products = jnp.concatenate(
+                [
+                    query * sides[s // chips][0, slot_rows(s % chips)].astype(f32)
+                    for s in range(seqs)
+                ],
+                axis=0,
+            )
+            found = per_head_sum(products, lane_heads) * col_scale
+            parts = [found[s * width : (s + 1) * width] for s in range(seqs)]
+            largest = parts[0]
+            for item in parts[1:]:
+                largest = jnp.maximum(largest, item)
+            powers = [jnp.exp(item - largest) for item in parts]
+            total = powers[0]
+            for item in powers[1:]:
+                total = total + item
+            weights = jnp.concatenate([item / total for item in powers], axis=0)
+            probs_ref[slot] = weights
+            wide = dot_back(weights.astype(bf16), lane_heads)
+            mixed = None
+            for s in range(seqs):
+                term = wide[s * width : (s + 1) * width] * sides[s // chips][
+                    1, slot_rows(s % chips)
+                ].astype(f32)
+                mixed = term if mixed is None else mixed + term
+            mix_ref[slot_rows(slot)] = mixed.astype(bf16)
+        stream = one_ref[...] + dot(mix_ref[...], weight_ref[3])
+        stream_ref[...] = stream
+        unit, _ = unit_norm(stream)
+        low_ref[...] = (unit * norm_ref[4:5] + norm_ref[5:6]).astype(bf16)
+
+    col_probs, col_mix, stream_two, normed_three = kernel_call(
+        attend_col,
+        [
+            ((chips, seqs * width, 128), f32),
+            ((toks, model), bf16),
+            ((toks, model), f32),
+            ((toks, model), bf16),
+        ],
+        [col_q, col_kv, kv_other, stream_one, norm_rows, weights_col],
+        flops=big + 6.0 * chips * seqs * width * model * 128,
+    )
+    low_near = [normed_three] + [along_cols(normed_three, step) for step in col_steps]
+
+    def feed_main(a0, a1, a2, a3, d0, d1, d2, d3, weight_ref, act_ref, grad_ref, *back_refs):
+        up, down = weight_ref[0], weight_ref[1]
+        for step, (low_ref, given_ref) in enumerate(((a0, d0), (a1, d1), (a2, d2), (a3, d3))):
+            pre = dot(low_ref[...], up)
+            bell = 0.5 * (1.0 + lax.erf(pre * (0.5**0.5)))
+            slope = bell + pre * jnp.exp(-0.5 * pre * pre) * ((0.5 / math.pi) ** 0.5)
+            act_ref[step] = (pre * bell).astype(bf16)
+            grad = (slope * dot_back(given_ref[...], down)).astype(bf16)
+            grad_ref[step] = grad
+            back_refs[step][...] = dot_back(grad, up).astype(bf16)
+
+    feed_big = 2.0 * toks * cols_axis * model * hidden
+    feed_results = kernel_call(
+        feed_main,
+        [((cols_axis, toks, hidden), bf16)] * 2 + [((toks, model), bf16)] * cols_axis,
+        [*low_near, *given_near, weights_feed],
+        flops=3 * feed_big,
+    )
+    act, grad_hidden, back_parts = feed_results[0], feed_results[1], feed_results[2:]
+    back_near = [back_parts[0]] + [along_cols(back_parts[step], step) for step in col_steps]
+
+    def feed_weights(
+        spot_ref, a0, a1, a2, a3, d0, d1, d2, d3, act_ref, grad_ref, weight_ref, mine_ref, give_ref, *outs
+    ):
+        at_core = spot_ref[2]
+        low = jnp.concatenate([a0[...], a1[...], a2[...], a3[...]], axis=0)
+        given = jnp.concatenate([d0[...], d1[...], d2[...], d3[...]], axis=0)
+        rows = cols_axis * toks
+        acts = act_ref[...].reshape(rows, hidden)
+        grads = grad_ref[...].reshape(rows, hidden)
+        for step in range(cols_axis):
+            outs[step][...] = dot(act_ref[step], weight_ref[1]).astype(bf16)
+        for ref, at in ((mine_ref, at_core), (give_ref, 1 - at_core)):
+            ref[0] = dot_tokens(low, half_of(grads, at, half)).astype(bf16)
+            ref[1] = dot_tokens(acts, half_of(given, at, half)).astype(bf16)
+
+    feed_grads = kernel_call(
+        feed_weights,
+        [((2, model, half), bf16)] * 2 + [((toks, model), bf16)] * cols_axis,
+        [spot, *low_near, *given_near, act, grad_hidden, weights_feed],
+        smem=(0,),
+        flops=3 * feed_big,
+    )
+    feed_mine, feed_give, out_parts = feed_grads[0], feed_grads[1], feed_grads[2:]
+    out_near = [out_parts[0]] + [along_cols(out_parts[step], step) for step in col_steps]
+    feed_got = along_core(feed_give)
+
+    def attend_col_back(
+        spot_ref,
+        b0,
+        b1,
+        b2,
+        b3,
+        given_ref,
+        two_ref,
+        norm_ref,
+        weight_ref,
+        q_ref,
+        near_ref,
+        far_ref,
+        probs_ref,
+        dtwo_ref,
+        low_ref,
+        dq_ref,
+        dkv_ref,
+        send_ref,
+        sums_ref,
+        wide_ref,
+    ):
+        lane_heads = head_of_lane(model)
+        back = b0[...].astype(f32) + b1[...].astype(f32) + b2[...].astype(f32) + b3[...].astype(f32)
+        unit, scale = unit_norm(two_ref[...])
+        sums_ref[...] = norm_sums(back, unit)
+        dtwo = given_ref[...].astype(f32) + unit_norm_back(back, unit, scale, norm_ref[4:5])
+        dtwo_ref[...] = dtwo
+        low = dtwo.astype(bf16)
+        low_ref[...] = low
+        dmix = dot_back(low, weight_ref[3]).astype(bf16).astype(f32)
+        wide_ref[...] = jnp.zeros_like(wide_ref)
+        sides = (near_ref, far_ref)
+        for slot in range(chips):
+            dout = dmix[slot_rows(slot)]
+            query = q_ref[slot_rows(slot)].astype(f32)
+            products = jnp.concatenate(
+                [
+                    dout * sides[s // chips][1, slot_rows(s % chips)].astype(f32)
+                    for s in range(seqs)
+                ],
+                axis=0,
+            )
+            found = per_head_sum(products, lane_heads)
+            weights = probs_ref[slot]
+            mean = None
+            for s in range(seqs):
+                rows = slice(s * width, (s + 1) * width)
+                term = weights[rows] * found[rows]
+                mean = term if mean is None else mean + term
+            dscores = (weights * (found - jnp.concatenate([mean] * seqs, axis=0))).astype(bf16)
+            wide_d = dot_back(dscores, lane_heads)
+            wide_p = dot_back(weights.astype(bf16), lane_heads)
+            dquery = None
+            for s in range(seqs):
+                rows = slice(s * width, (s + 1) * width)
+                term = wide_d[rows] * sides[s // chips][0, slot_rows(s % chips)].astype(f32)
+                dquery = term if dquery is None else dquery + term
+                wide_ref[0, rows] += wide_d[rows] * query
+                wide_ref[1, rows] += wide_p[rows] * dout
+            dq_ref[slot_rows(slot)] = (dquery * col_scale).astype(bf16)
+        dkv_ref[0] = wide_ref[0, :toks] * col_scale
+        dkv_ref[1] = wide_ref[1, :toks]
+        send_ref[0] = (wide_ref[0, toks:] * col_scale).astype(bf16)
+        send_ref[1] = wide_ref[1, toks:].astype(bf16)
+
+    grad_two, grad_two_low, col_dq, col_dkv, col_send, sums_three = kernel_call(
+        attend_col_back,
+        [
+            ((toks, model), f32),
+            ((toks, model), bf16),
+            ((toks, model), bf16),
+            ((2, toks, model), f32),
+            ((2, toks, model), bf16),
+            ((2, model), f32),
+        ],
+        [
+            spot,
+            *back_near,
+            given_out,
+            stream_two,
+            norm_rows,
+            weights_col,
+            col_q,
+            col_kv,
+            kv_other,
+            col_probs,
+        ],
+        smem=(0,),
+        scratch=[pltpu.VMEM((2, 2 * toks, model), f32)],
+        flops=big + 10.0 * chips * seqs * width * model * 128,
+    )
+    col_got = along_core(col_send)
+
+    def row_entry_back(
+        spot_ref,
+        dq_ref,
+        dkv_ref,
+        got_ref,
+        low_two_ref,
+        dtwo_ref,
+        one_ref,
+        norm_ref,
+        col_ref,
+        row_ref,
+        near_ref,
+        left_ref,
+        right_ref,
+        mine_ref,
+        give_ref,
+        done_ref,
+        low_ref,
+        dmix_ref,
+        dprobs_ref,
+        sums_ref,
+    ):
+        at_core = spot_ref[2]
+        dq = dq_ref[...]
+        dk = (dkv_ref[0] + got_ref[0].astype(f32)).astype(bf16)
+        dv = (dkv_ref[1] + got_ref[1].astype(f32)).astype(bf16)
+        for index, item in enumerate((dq, dk, dv, low_two_ref[...])):
+            mine_ref[index] = half_of(item, at_core, half)
+            give_ref[index] = half_of(item, 1 - at_core, half)
+        back = dot_back(dq, col_ref[0]) + dot_back(dk, col_ref[1]) + dot_back(dv, col_ref[2])
+        unit, scale = unit_norm(one_ref[...])
+        sums_ref[...] = norm_sums(back, unit)
+        done = dtwo_ref[...] + unit_norm_back(back, unit, scale, norm_ref[2:3])
+        done_ref[...] = done
+        low = done.astype(bf16)
+        low_ref[...] = low
+        dmix = dot_back(low, row_ref[3]).astype(bf16)
+        dmix_ref[...] = dmix
+        mask = head_mask(width, model)
+        total = None
+        for slot in range(chips):
+            values = window_rows(spot_ref, near_ref, left_ref, right_ref, 1, slot, width)
+            term = dot_back(spread_heads(dmix[slot_rows(slot)], mask), values)
+            total = term if total is None else total + term
+        dprobs_ref[...] = total
+
+    (
+        col_mine,
+        col_give,
+        grad_one,
+        grad_one_low,
+        row_dmix,
+        dprobs,
+        sums_two,
+    ) = kernel_call(
+        row_entry_back,
+        [
+            ((4, toks, half), bf16),
+            ((4, toks, half), bf16),
+            ((toks, model), f32),
+            ((toks, model), bf16),
+            ((toks, model), bf16),
+            ((fold, span), f32),
+            ((2, model), f32),
+        ],
+        [
+            spot,
+            col_dq,
+            col_dkv,
+            col_got,
+            grad_two_low,
+            grad_two,
+            stream_one,
+            norm_rows,
+            weights_col,
+            weights_row,
+            row_kv,
+            kv_left,
+            kv_right,
+        ],
+        smem=(0,),
+        flops=4 * big + chips * 2.0 * fold * model * span,
+    )
+    dprobs_other = along_core(dprobs)
+
+    def attend_row_back(
+        spot_ref,
+        weight_ref,
+        dprobs_ref,
+        other_ref,
+        scores_ref,
+        probs_ref,
+        q_ref,
+        near_ref,
+        left_ref,
+        right_ref,
+        dmix_ref,
+        dq_ref,
+        dkv_ref,
+        to_left_ref,
+        to_right_ref,
+    ):
+        mask = head_mask(width, model)
+        dprob = dprobs_ref[...] + other_ref[...]
+        probs_here, scores_here = probs_ref[...], scores_ref[...]
+        rows = lax.broadcasted_iota(jnp.int32, (fold, 1), 0) % width
+        weight = jnp.where(rows + spot_ref[3] * width < spot_ref[4], weight_ref[0], 0.0)
+        first = dprob - jnp.sum(probs_here * dprob, axis=-1, keepdims=True)
+        second = scores_here - jnp.sum(probs_here * scores_here, axis=-1, keepdims=True)
+        dscores = (probs_here * (first - weight * second)).astype(bf16)
+        low_probs = probs_here.astype(bf16)
+        for slot in range(chips):
+            at = slot_rows(slot)
+            keys = window_rows(spot_ref, near_ref, left_ref, right_ref, 0, slot, width)
+            dq_ref[at] = (
+                fold_heads(dot(dscores, keys), mask, width) * row_scale
+            ).astype(bf16)
+            dkeys = dot_tokens(dscores, spread_heads(q_ref[at], mask)) * row_scale
+            dvalues = dot_tokens(low_probs, spread_heads(dmix_ref[at], mask))
+            for index, item in enumerate((dkeys, dvalues)):
+                to_left_ref[index, at] = item[:width].astype(bf16)
+                dkv_ref[index, at] = item[width : 2 * width]
+                to_right_ref[index, at] = item[2 * width :].astype(bf16)
+
+    row_dq, row_dkv, edge_left, edge_right = kernel_call(
+        attend_row_back,
+        [
+            ((toks, model), bf16),
+            ((2, toks, model), f32),
+            ((2, toks, model), bf16),
+            ((2, toks, model), bf16),
+        ],
+        [
+            spot,
+            entropy_scale,
+            dprobs,
+            dprobs_other,
+            scores,
+            probs,
+            row_q,
+            row_kv,
+            kv_left,
+            kv_right,
+            row_dmix,
+        ],
+        smem=(0, 1),
+        flops=3 * chips * 2.0 * fold * model * span,
+    )
+    edge_from_right = to_left(edge_left)
+    edge_from_left = to_right(edge_right)
+
+    def input_back(
+        spot_ref,
+        dq_ref,
+        dkv_ref,
+        from_right_ref,
+        from_left_ref,
+        low_one_ref,
+        done_ref,
+        zero_ref,
+        norm_ref,
+        row_ref,
+        mine_ref,
+        give_ref,
+        out_ref,
+        sums_ref,
+    ):
+        at_core = spot_ref[2]
+        dq = dq_ref[...]
+        dk, dv = (
+            jnp.concatenate(
+                [
+                    (
+                        dkv_ref[index, slot_rows(slot)]
+                        + from_left_ref[index, slot_span(spot_ref, 5, slot, width)].astype(f32)
+                        + from_right_ref[index, slot_span(spot_ref, 6, slot, width)].astype(f32)
+                    ).astype(bf16)
+                    for slot in range(chips)
+                ],
+                axis=0,
+            )
+            for index in (0, 1)
+        )
+        for index, item in enumerate((dq, dk, dv, low_one_ref[...])):
+            mine_ref[index] = half_of(item, at_core, half)
+            give_ref[index] = half_of(item, 1 - at_core, half)
+        back = dot_back(dq, row_ref[0]) + dot_back(dk, row_ref[1]) + dot_back(dv, row_ref[2])
+        unit, scale = unit_norm(zero_ref[...])
+        sums_ref[...] = norm_sums(back, unit)
+        out_ref[...] = (done_ref[...] + unit_norm_back(back, unit, scale, norm_ref[0:1])).astype(
+            bf16
+        )
+
+    row_mine, row_give, grad_in, sums_one = kernel_call(
+        input_back,
+        [
+            ((4, toks, half), bf16),
+            ((4, toks, half), bf16),
+            ((toks, model), bf16),
+            ((2, model), f32),
+        ],
+        [
+            spot,
+            row_dq,
+            row_dkv,
+            edge_from_right,
+            edge_from_left,
+            grad_one_low,
+            grad_one,
+            stream_zero,
+            norm_rows,
+            weights_row,
+        ],
+        smem=(0,),
+        flops=3 * big,
+    )
+
+    def layer_grads(low, mix, low_other, mix_other, mine, given):
+        def body(
+            spot_ref, low_ref, mix_ref, low2_ref, mix2_ref, mine_ref, given_ref, *outs_and_scratch
+        ):
+            outs, (left_ref, right_ref) = outs_and_scratch[:cols_axis], outs_and_scratch[cols_axis:]
+            at_col = spot_ref[0]
+            left_ref[0, :toks] = low_ref[...]
+            left_ref[0, toks:] = low2_ref[...]
+            left_ref[1, :toks] = mix_ref[...]
+            left_ref[1, toks:] = mix2_ref[...]
+            right_ref[:, :toks] = mine_ref[...]
+            right_ref[:, toks:] = given_ref[...]
+            for step in range(cols_axis):
+                matrix = at_col ^ step
+                left = left_ref[matrix // 3]
+                outs[step][...] = dot_tokens(left, right_ref[matrix]).astype(bf16)
+
+        return kernel_call(
+            body,
+            [((model, half), bf16)] * cols_axis,
+            [spot, low, mix, low_other, mix_other, mine, given],
+            smem=(0,),
+            scratch=[
+                pltpu.VMEM((2, 2 * toks, model), bf16),
+                pltpu.VMEM((4, 2 * toks, half), bf16),
+            ],
+            flops=4 * big,
+        )
+
+    def add_parts(items):
+        total = items[0].astype(f32)
+        for item in items[1:]:
+            total = total + item.astype(f32)
+        return total.astype(bf16)
+
+    def settle(items):
+        def rows_for(index):
+            return add_parts(
+                [
+                    lax.dynamic_slice_in_dim(item, index * 2 * shard, 2 * shard, axis=1)
+                    for item in items
+                ]
+            )
+
+        total = add_parts(
+            [rows_for(chip)] + [along_chips(rows_for(chip ^ step), step) for step in steps]
+        )
+        keep = lax.dynamic_slice_in_dim(total, core * shard, shard, axis=1)
+        other = along_core(lax.dynamic_slice_in_dim(total, (1 - core) * shard, shard, axis=1))
+        sides = jnp.where(
+            core == 0,
+            jnp.concatenate([keep, other], axis=2),
+            jnp.concatenate([other, keep], axis=2),
+        )
+        near = [sides] + [along_cols(sides, step) for step in col_steps]
+        stacked = jnp.stack(near)
+        return [
+            lax.dynamic_index_in_dim(stacked, col_at ^ block, axis=0, keepdims=False)
+            for block in range(cols_axis)
+        ]
+
+    def layer_settle(low, mix, mine, give):
+        low_other, mix_other = along_core(low), along_core(mix)
+        partial_sums = layer_grads(low, mix, low_other, mix_other, mine, along_core(give))
+        near = [partial_sums[0]] + [
+            along_cols(partial_sums[step], step) for step in col_steps
+        ]
+        return [item[0].astype(f32) for item in settle([item[None] for item in near])]
+
+    feed_parts = settle([feed_mine, feed_got])
+    grad_feed_in = jnp.stack([item[0].reshape(shard, seqs, part) for item in feed_parts], axis=2)
+    grad_feed_in = grad_feed_in.reshape(shard, feed_in.shape[1]).astype(f32)
+    grad_feed_out = jnp.concatenate([item[1] for item in feed_parts], axis=0).astype(f32)
+    col_grads = layer_settle(normed_two, col_mix, col_mine, col_give)
+    row_grads = layer_settle(normed_one, row_mix, row_mine, row_give)
+
+    small = jnp.concatenate(
+        [sums_one, sums_two, sums_three, entropy_row, jnp.zeros((1, model), f32)], axis=0
+    )
+    small = small + along_core(small)
+    step = 1
+    while step < chips:
+        small = small + along_chips(small, step)
+        step *= 2
+    step = 1
+    while step < cols_axis:
+        small = small + along_cols(small, step)
+        step *= 2
+    entropy = small[6, 0] / (HEADS * count_total)
+    norm_here = lax.dynamic_slice_in_dim(small, seq_at * shard, shard, axis=1)
+
+    result = stream_two
+    for item in out_near:
+        result = result + item.astype(f32)
+    result = result.astype(bf16)
+
+    def to_sequence(values):
+        slots = [values[slot_rows(slot)] for slot in range(chips)]
+        arrived = [slots[0]] + [along_chips(slots[step], step) for step in steps]
+        whole = jnp.stack(arrived)
+        return jnp.concatenate(
+            [
+                lax.dynamic_index_in_dim(whole, chunk_of(index) ^ chip, axis=0, keepdims=False)
+                for index in range(chips)
+            ],
+            axis=0,
+        )[None]
+
+    return (
+        to_sequence(result),
+        entropy,
+        to_sequence(grad_in),
+        *[norm_here[index] for index in range(6)],
+        *row_grads,
+        *col_grads,
+        grad_feed_in,
+        grad_feed_out,
+    )
+
+
+def fits_fast(tokens, feed_out):
+    chips = lax.axis_size("seq") // 2
+    return (
+        lax.axis_size("col") == 4
+        and lax.axis_size("seq") == 8
+        and tokens.shape[0] == 1
+        and tokens.shape[1] == chips * WINDOW
+        and tokens.shape[2] == HEADS * HEAD_DIM
+        and feed_out.shape[0] * 2 == tokens.shape[2]
+    )
+
+
+def on_device(tokens, offsets, band, col_counts, *rest):
+    if not fits_fast(tokens, rest[15]):
+        return general_plan(tokens, offsets, band, col_counts, *rest)
+    return fast_plan(
+        tokens,
+        offsets,
+        band,
+        col_counts,
+        rest[0:6],
+        rest[6:10],
+        rest[10:14],
+        rest[14],
+        rest[15],
+        rest[16],
+    )
+
+
 def solution(mesh):
     return jax.shard_map(
         on_device,

time: 1060 us -> 426 us (0.40)
  waiting for transfers between devices: 777 us -> 152 us
  starting transfers between devices: 11 us -> 103 us
  blocking collectives: 85.5 us -> 0 us
  Pallas kernels: 0 us -> 77.4 us
  matrix products: 68.7 us -> 0.12 us
  other arithmetic: 43.4 us -> 24.1 us
  between operations: 21.2 us -> 6.71 us
    reduce_scatter x11 -> x0, waiting for transfers between devices: 394 us -> none  [the longest x1 64.4 us: on_device(): lax.psum_scatter(jnp.concatenate([key_part.reshape(row_count, cols_dev, m...]
    all_gather x12 -> x0, waiting for transfers between devices: 261 us -> none  [the longest x1 49.4 us: on_device(): lax.all_gather(feed_in, 'seq', axis=0, tiled=True)]
    ppermute x4 -> x94, waiting for transfers between devices: 15.1 us -> 152 us  [the longest x35 72.3 us: along_cols(): lax.ppermute(values, 'col', [(i, i ^ step) for i in range(cols_axis)])]
    psum x3 -> x0, waiting for transfers between devices: 100 us -> none  [the longest x1 55.5 us: on_device(): row_scores = lax.psum(partial_logits, 'seq') * row_scale]
    ppermute x4 -> x94, starting transfers between devices: 9.37 us -> 103 us  [the longest x29 46.2 us: along_chips(): return lax.ppermute(values, 'seq', [(i, i ^ 2 * step) for i in range(seqs)])]
    pallas_call x0 -> x16, Pallas kernels: none -> 77.4 us  [kernel_call(): pl.pallas_call(body, out_shape=out_shapes, in_specs=in_specs, out_specs=[...]
    dot_general x36 -> x1, matrix products: 68.7 us -> 0.12 us  [fast_plan(): ordered = jnp.dot(order, lines, preferred_element_type=f32)]
    unnamed x2 -> x0, blocking collectives: 56.4 us -> none
  transfers between devices with their start and end apart: 30 -> 94, of which waited for: 26 -> 27; matrix products, arithmetic and copies ran while one was open for 11% -> 10% of each run, Pallas kernels for 0% -> 16%
where the time goes in v1:
time: 426 us; the launch traced here: 420 us
  waiting for transfers between devices  152 us (36%)
  starting transfers between devices  103 us (24%)
  Pallas kernels  77.4 us (18%)
  local copies, waits for them, and re-layouts  56.4 us (13%)
  other arithmetic  24.1 us (6%)
  between operations  6.71 us (2%)
    pallas_call x16, Pallas kernels, kernel_call(): pl.pallas_call(body, out_shape=out_shapes, in_specs=in_specs, out_specs=[...  77.4 us
    ppermute x35, waiting for transfers between devices, along_cols(): lax.ppermute(values, 'col', [(i, i ^ step) for i in range(cols_axis)])  72.3 us
    ppermute x29, waiting for transfers between devices, along_chips(): return lax.ppermute(values, 'seq', [(i, i ^ 2 * step) for i in range(seqs)])  69.9 us
    ppermute x29, starting transfers between devices, along_chips(): return lax.ppermute(values, 'seq', [(i, i ^ 2 * step) for i in range(seqs)])  46.2 us
    ppermute x35, starting transfers between devices, along_cols(): lax.ppermute(values, 'col', [(i, i ^ step) for i in range(cols_axis)])  41.6 us
    unnamed x168, local copies, waits for them, and re-layouts  30.9 us
  transfers between devices with their start and end apart: 94, of which 27 were waited for; matrix products, arithmetic and copies ran while one was open for 10% of the time, Pallas kernels for 16%

profile of v1, /device:TPU:0, one launch (start us, length us, event | category | flops | bytes accessed | tf_op | source)
XLA Modules:
  0.0 420.2 jit_solution(12011785016741831250)
XLA Ops:
  1.4 4.1 concatenate.149
  7.5 5.0 %collective-permute-start.5 = (bf16[104,768]{1,0:T(8,128)(2,1)}, bf16[104,768]{1,0:T(8,128)(2,1)}, u32[]{:S(2)}, u32[]{:S(2)}) collective-permute-start(bf16[104,768]{1,0:T(8,128)(2,1)} %dynamic-slice_bitcast_fusion), channel_id=1, source_target_pairs={{0,6},{1,7},{2,4},{3,5},{4,2},{5,3},{6,0},{7,1},{8,14},{9,15},{10,... | collective-permute-start | bytes 479240 | tf_op jit(solution)/shard_map/ppermute | solution.py:550
  13.9 3.8 collective-permute-start.2
  31.5 6.4 %collective-permute-done.1 = bf16[2,32,768]{2,1,0:T(8,128)(2,1)} collective-permute-done((bf16[2,32,768]{2,1,0:T(8,128)(2,1)}, bf16[2,32,768]{2,1,0:T(8,128)(2,1)}, u32[]{:S(2)}, u32[]{:S(2)}) %collective-permute-start.1) | collective-permute-done | bytes 98336 | tf_op jit(solution)/shard_map/ppermute | solution.py:550
  46.3 3.9 collective-permute-done
  56.6 4.8 %collective-permute-done.37 = bf16[2,96,768]{2,1,0:T(8,128)(2,1)S(1)} collective-permute-done((bf16[2,96,768]{2,1,0:T(8,128)(2,1)}, bf16[2,96,768]{2,1,0:T(8,128)(2,1)S(1)}, u32[]{:S(2)}, u32[]{:S(2)}) %collective-permute-start.37) | collective-permute-done | bytes 294944 | tf_op jit(solution)/shard_map/ppermute | solution.py:550
  62.6 8.0 %collective-permute-done.9.refs_3_ = bf16[3,104,768]{2,1,0:T(8,128)(2,1)S(1)} collective-permute-done((bf16[3,104,768]{2,1,0:T(8,128)(2,1)S(1)}, bf16[3,104,768]{2,1,0:T(8,128)(2,1)S(1)}, u32[]{:S(2)}, u32[]{:S(2)}) %collective-permute-start.9) | collective-permute-done | bytes 479264 | tf_op jit(solution)/shard_map/ppermute | solution.py:556
  73.5 14.7 %collective-permute-done.36 = bf16[2,96,768]{2,1,0:T(8,128)(2,1)S(1)} collective-permute-done((bf16[2,96,768]{2,1,0:T(8,128)(2,1)}, bf16[2,96,768]{2,1,0:T(8,128)(2,1)S(1)}, u32[]{:S(2)}, u32[]{:S(2)}) %collective-permute-start.36) | collective-permute-done | bytes 294944 | tf_op jit(solution)/shard_map/ppermute | solution.py:550
  99.8 9.2 %shard_map.348.weight_ref.row_ref = bf16[4,768,768]{2,1,0:T(8,128)(2,1)} custom-call(s32[7]{0:T(128)S(1)} %stack.211.spot_ref, bf16[4,104,768]{2,1,0:T(8,128)(2,1)S(1)} %pad_maximum_fusion.2.refs_0_, bf16[3,104,768]{2,1,0:T(8,128)(2,1)S(1)} %pad_maximum_fusion.6.refs_1_, bf16[3,104,768]{2,1,0:T(8,128)(2,1)S(1)} %copy-done.13, ...), custom_call_target="tpu_custom_call" | custom-call | bytes 9830428 | tf_op jit(solution)/shard_map/pallas_call | solution.py:413
  112.9 3.9 collective-permute-start.14
  120.2 5.5 %collective-permute-done.14.left_ref = bf16[2,128,768]{2,1,0:T(8,128)(2,1)S(1)} collective-permute-done((bf16[2,128,768]{2,1,0:T(8,128)(2,1)S(1)}, bf16[2,128,768]{2,1,0:T(8,128)(2,1)S(1)}, u32[]{:S(2)}, u32[]{:S(2)}) %collective-permute-start.14) | collective-permute-done | bytes 393248 | tf_op jit(solution)/shard_map/ppermute | solution.py:569
  125.7 4.1 collective-permute-done.15.right_ref
  133.1 6.5 %shard_map.352.weight_ref.col_ref = bf16[4,768,768]{2,1,0:T(8,128)(2,1)} custom-call(s32[7]{0:T(128)S(1)} %stack.211.spot_ref, bf16[4,96,768]{2,1,0:T(8,128)(2,1)S(1)} %pad_maximum_fusion.3.refs_0_, bf16[3,96,768]{2,1,0:T(8,128)(2,1)S(1)} %pad_maximum_fusion.7.refs_1_, bf16[3,96,768]{2,1,0:T(8,128)(2,1)} %collective-permute-done.20.refs_2_, ...), custom_call_target="tpu_custom_call" | custom-call | bytes 9437212 | tf_op jit(solution)/shard_map/pallas_call | solution.py:413
  139.6 3.9 shard_map.351
  148.1 5.1 %shard_map.354 = (f32[4,256,128]{2,1,0:T(8,128)S(1)}, bf16[128,768]{1,0:T(8,128)(2,1)S(1)}, f32[128,768]{1,0:T(8,128)S(1)}, bf16[128,768]{1,0:T(8,128)(2,1)S(1)}) custom-call(bf16[128,768]{1,0:T(8,128)(2,1)S(1)} %get-tuple-element.80.q_ref, bf16[2,128,768]{2,1,0:T(8,128)(2,1)S(1)} %get-tuple-element.81.near_ref, ...), custom_call_target="tpu_custom_call" | custom-call | flops 754974720 | bytes 7430144 | tf_op jit(solution)/shard_map/pallas_call | solution.py:413
  162.1 4.1 collective-permute-done.30.a2
  166.1 5.3 %shard_map.356 = (bf16[4,128,768]{2,1,0:T(8,128)(2,1)S(1)}, bf16[4,128,768]{2,1,0:T(8,128)(2,1)S(1)}, bf16[128,768]{1,0:T(8,128)(2,1)S(1)}, bf16[128,768]{1,0:T(...) custom-call(bf16[128,768]{1,0:T(8,128)(2,1)S(1)} %get-tuple-element.84.a0, ...), custom_call_target="tpu_custom_call" | custom-call | flops 1811939328 | bytes 6291456 | tf_op jit(solution)/shard_map/pallas_call | solution.py:413
  175.0 4.1 collective-permute-done.45.b1
  181.7 6.6 %shard_map.358 = (f32[128,768]{1,0:T(8,128)S(1)}, bf16[128,768]{1,0:T(8,128)(2,1)S(1)}, bf16[128,768]{1,0:T(8,128)(2,1)S(1)}, f32[2,128,768]{2,1,0:T(8,128)S(1)}...) custom-call(s32[7]{0:T(128)S(1)} %stack.211.spot_ref, bf16[128,768]{1,0:T(8,128)(2,1)S(1)} %get-tuple-element.91.b0, ...), custom_call_target="tpu_custom_call" | custom-call | flops 1157627904 | bytes 9599004 | tf_op jit(solution)/shard_map/pallas_call | solution.py:413
  189.7 5.1 %shard_map.357 = (bf16[2,768,384]{2,1,0:T(8,128)(2,1)S(1)}, bf16[2,768,384]{2,1,0:T(8,128)(2,1)}, bf16[128,768]{1,0:T(8,128)(2,1)S(1)}, bf16[128,768]{1,0:T(8,12...) custom-call(s32[7]{0:T(128)S(1)} %stack.211.spot_ref, bf16[128,768]{1,0:T(8,128)(2,1)S(1)} %get-tuple-element.84.a0, ...), custom_call_target="tpu_custom_call" | custom-call | flops 1811939328 | bytes 8650780 | tf_op jit(solution)/shard_map/pallas_call | solution.py:413
  207.6 7.5 %shard_map.359 = (bf16[4,128,384]{2,1,0:T(8,128)(2,1)S(1)}, bf16[4,128,384]{2,1,0:T(8,128)(2,1)}, f32[128,768]{1,0:T(8,128)S(1)}, bf16[128,768]{1,0:T(8,128)(2,1...) custom-call(s32[7]{0:T(128)S(1)} %stack.211.spot_ref, ...), custom_call_target="tpu_custom_call" | custom-call | flops 830472192 | bytes 14727196 | tf_op jit(solution)/shard_map/pallas_call | solution.py:413
  217.1 13.1 %shard_map.360 = (bf16[128,768]{1,0:T(8,128)(2,1)S(1)}, f32[2,128,768]{2,1,0:T(8,128)S(1)}, bf16[2,128,768]{2,1,0:T(8,128)(2,1)}, bf16[2,128,768]{2,1,0:T(8,128)(2,1)S(1)}) custom-call(s32[7]{0:T(128)S(1)} %stack.211.spot_ref, f32[1]{0:T(128)} %bitcast.66.weight_ref, f32[384,96]{1,0:T(8,128)S(1)} %get-tuple-element.101.dprobs_ref, ...), custom_call_target="tpu_custom_call" | custom-call | flops 679477248 | bytes 3932192 | tf_op jit(solution)/shard_map/pallas_call | solution.py:413
  232.4 4.6 %collective-permute-start.51 = (bf16[2,128,768]{2,1,0:T(8,128)(2,1)S(1)}, bf16[2,128,768]{2,1,0:T(8,128)(2,1)S(1)}, u32[]{:S(2)}, u32[]{:S(2)}) collective-permute-start(bf16[2,128,768]{2,1,0:T(8,128)(2,1)S(1)} %get-tuple-element.108), channel_id=1, source_target_pairs={{0,2},{1,3},{2,4},{3,5},{4,6},{5,7},{6,14},{7,15},{14,12},{15,13},... | collective-permute-start | bytes 1179656 | tf_op jit(solution)/shard_map/ppermute | solution.py:569
  239.3 8.4 %collective-permute-done.44 = bf16[32,768]{1,0:T(8,128)(2,1)S(1)} collective-permute-done((bf16[32,768]{1,0:T(8,128)(2,1)S(1)}, bf16[32,768]{1,0:T(8,128)(2,1)S(1)}, u32[]{:S(2)}, u32[]{:S(2)}) %collective-permute-start.44) | collective-permute-done | bytes 49184 | tf_op jit(solution)/shard_map/ppermute | solution.py:550
  257.1 3.9 shard_map.361
  278.7 11.5 %collective-permute-done.54 = f32[8,768]{1,0:T(8,128)S(1)} collective-permute-done((f32[8,768]{1,0:T(8,128)S(1)}, f32[8,768]{1,0:T(8,128)S(1)}, u32[]{:S(2)}, u32[]{:S(2)}) %collective-permute-start.54) | collective-permute-done | bytes 24608 | tf_op jit(solution)/shard_map/ppermute | solution.py:550
  295.2 10.0 %collective-permute-done.55 = f32[8,768]{1,0:T(8,128)S(1)} collective-permute-done((f32[8,768]{1,0:T(8,128)S(1)}, f32[8,768]{1,0:T(8,128)S(1)}, u32[]{:S(2)}, u32[]{:S(2)}) %collective-permute-start.55) | collective-permute-done | bytes 24608 | tf_op jit(solution)/shard_map/ppermute | solution.py:556
  315.0 6.2 %collective-permute-done.77 = bf16[768,384]{1,0:T(8,128)(2,1)S(1)} collective-permute-done((bf16[768,384]{1,0:T(8,128)(2,1)S(1)}, bf16[768,384]{1,0:T(8,128)(2,1)S(1)}, u32[]{:S(2)}, u32[]{:S(2)}) %collective-permute-start.77) | collective-permute-done | bytes 589856 | tf_op jit(solution)/shard_map/ppermute | solution.py:556
  329.2 3.9 collective-permute-done.80
  351.5 27.9 %collective-permute-done.92 = bf16[2,96,768]{2,1,0:T(8,128)(2,1)S(1)} collective-permute-done((bf16[2,96,768]{2,1,0:T(8,128)(2,1)}, bf16[2,96,768]{2,1,0:T(8,128)(2,1)S(1)}, u32[]{:S(2)}, u32[]{:S(2)}) %collective-permute-start.92) | collective-permute-done | bytes 294944 | tf_op jit(solution)/shard_map/ppermute | solution.py:556
  392.1 3.9 collective-permute-done.68
  397.0 3.8 collective-permute-done.67
  (436 shorter events, 194.6 us)
Async XLA Ops:
  7.5 33.7 %collective-permute-start.5 = (bf16[104,768]{1,0:T(8,128)(2,1)}, bf16[104,768]{1,0:T(8,128)(2,1)}, u32[]{:S(2)}, u32[]{:S(2)}) collective-permute-start(bf16[104,768]{1,0:T(8,128)(2,1)} %dynamic-slice_bitcast_fusion), channel_id=1, source_target_pairs={{0,6},{1,7},{2,4},{3,5},{4,2},{5,3},{6,0},{7,1},{8,14},{9,15},{10,... | collective-permute-start | bytes 479240 | tf_op jit(solution)/shard_map/ppermute | solution.py:550
  12.5 31.1 %collective-permute-start.4 = (bf16[104,768]{1,0:T(8,128)(2,1)}, bf16[104,768]{1,0:T(8,128)(2,1)}, u32[]{:S(2)}, u32[]{:S(2)}) collective-permute-start(bf16[104,768]{1,0:T(8,128)(2,1)} %dynamic-slice_bitcast_fusion), channel_id=1, source_target_pairs={{0,4},{1,5},{2,6},{3,7},{4,0},{5,1},{6,2},{7,3},{8,12},{9,13},{10,... | collective-permute-start | bytes 479240 | tf_op jit(solution)/shard_map/ppermute | solution.py:550
  12.5 31.1 %collective-permute-start.3 = (bf16[104,768]{1,0:T(8,128)(2,1)}, bf16[104,768]{1,0:T(8,128)(2,1)}, u32[]{:S(2)}, u32[]{:S(2)}) collective-permute-start(bf16[104,768]{1,0:T(8,128)(2,1)} %dynamic-slice_bitcast_fusion), channel_id=1, source_target_pairs={{0,2},{1,3},{2,0},{3,1},{4,6},{5,7},{6,4},{7,5},{8,10},{9,11},{10,... | collective-permute-start | bytes 479240 | tf_op jit(solution)/shard_map/ppermute | solution.py:550
  26.9 25.5 %collective-permute-start.19 = (bf16[96,768]{1,0:T(8,128)(2,1)}, bf16[96,768]{1,0:T(8,128)(2,1)S(1)}, u32[]{:S(2)}, u32[]{:S(2)}) collective-permute-start(bf16[96,768]{1,0:T(8,128)(2,1)} %dynamic-slice_bitcast_fusion.6), channel_id=1, source_target_pairs={{0,6},{1,7},{2,4},{3,5},{4,2},{5,3},{6,0},{7,1},{8,14},{9,15},{10,... | collective-permute-start | bytes 442376 | tf_op jit(solution)/shard_map/ppermute | solution.py:550
  61.3 26.9 %collective-permute-start.6 = (bf16[4,104,768]{2,1,0:T(8,128)(2,1)S(1)}, bf16[4,104,768]{2,1,0:T(8,128)(2,1)S(1)}, u32[]{:S(2)}, u32[]{:S(2)}) collective-permute-start(bf16[4,104,768]{2,1,0:T(8,128)(2,1)S(1)} %pad_maximum_fusion.2.refs_0_), channel_id=1, source_target_pairs={{0,1},{1,0},{2,3},{3,2},{4,5},{5,4},{6,7},{7,6},{8,9},{9,8},{10,11... | collective-permute-start | bytes 1916936 | tf_op jit(solution)/shard_map/ppermute | solution.py:553
  61.3 28.4 %collective-permute-start.11 = (bf16[3,104,768]{2,1,0:T(8,128)(2,1)S(1)}, bf16[3,104,768]{2,1,0:T(8,128)(2,1)S(1)}, u32[]{:S(2)}, u32[]{:S(2)}) collective-permute-start(bf16[3,104,768]{2,1,0:T(8,128)(2,1)S(1)} %collective-permute-done.8.refs_2_), channel_id=1, source_target_pairs={{0,1},{1,0},{2,3},{3,2},{4,5},{5,4},{6,7},{7,6},{8,9},{9,8},{10,11... | collective-permute-start | bytes 1437704 | tf_op jit(solution)/shard_map/ppermute | solution.py:553
  70.6 21.4 %collective-permute-start.12 = (bf16[3,104,768]{2,1,0:T(8,128)(2,1)S(1)}, bf16[3,104,768]{2,1,0:T(8,128)(2,1)S(1)}, u32[]{:S(2)}, u32[]{:S(2)}) collective-permute-start(bf16[3,104,768]{2,1,0:T(8,128)(2,1)S(1)} %collective-permute-done.9.refs_3_), channel_id=1, source_target_pairs={{0,1},{1,0},{2,3},{3,2},{4,5},{5,4},{6,7},{7,6},{8,9},{9,8},{10,11... | collective-permute-start | bytes 1437704 | tf_op jit(solution)/shard_map/ppermute | solution.py:553
  72.6 21.7 %collective-permute-start.13 = (bf16[3,104,768]{2,1,0:T(8,128)(2,1)}, bf16[3,104,768]{2,1,0:T(8,128)(2,1)}, u32[]{:S(2)}, u32[]{:S(2)}) collective-permute-start(bf16[3,104,768]{2,1,0:T(8,128)(2,1)} %collective-permute-done.10.refs_4_), channel_id=1, source_target_pairs={{0,1},{1,0},{2,3},{3,2},{4,5},{5,4},{6,7},{7,6},{8,9},{9,8},{10,11... | collective-permute-start | bytes 1437704 | tf_op jit(solution)/shard_map/ppermute | solution.py:553
  88.2 24.7 %collective-permute-start.35 = (bf16[2,96,768]{2,1,0:T(8,128)(2,1)}, bf16[2,96,768]{2,1,0:T(8,128)(2,1)}, u32[]{:S(2)}, u32[]{:S(2)}) collective-permute-start(bf16[2,96,768]{2,1,0:T(8,128)(2,1)} %get-tuple-element.169), channel_id=1, source_target_pairs={{0,2},{1,3},{2,0},{3,1},{4,6},{5,7},{6,4},{7,5},{8,10},{9,11},{10,... | collective-permute-start | bytes 884744 | tf_op jit(solution)/shard_map/ppermute | solution.py:550
  88.2 28.6 %collective-permute-start.20 = (bf16[3,96,768]{2,1,0:T(8,128)(2,1)S(1)}, bf16[3,96,768]{2,1,0:T(8,128)(2,1)}, u32[]{:S(2)}, u32[]{:S(2)}) collective-permute-start(bf16[3,96,768]{2,1,0:T(8,128)(2,1)S(1)} %pad_maximum_fusion.7.refs_1_), channel_id=1, source_target_pairs={{0,8},{8,0},{16,24},{24,16},{1,9},{9,1},{17,25},{25,17},{2,10},{10... | collective-permute-start | bytes 1327112 | tf_op jit(solution)/shard_map/ppermute | solution.py:556
  90.5 28.7 %collective-permute-start.21 = (bf16[3,96,768]{2,1,0:T(8,128)(2,1)S(1)}, bf16[3,96,768]{2,1,0:T(8,128)(2,1)}, u32[]{:S(2)}, u32[]{:S(2)}) collective-permute-start(bf16[3,96,768]{2,1,0:T(8,128)(2,1)S(1)} %pad_maximum_fusion.7.refs_1_), channel_id=1, source_target_pairs={{0,16},{8,24},{16,0},{24,8},{1,17},{9,25},{17,1},{25,9},{2,18},{10... | collective-permute-start | bytes 1327112 | tf_op jit(solution)/shard_map/ppermute | solution.py:556
  92.9 26.7 %collective-permute-start.22 = (bf16[3,96,768]{2,1,0:T(8,128)(2,1)S(1)}, bf16[3,96,768]{2,1,0:T(8,128)(2,1)}, u32[]{:S(2)}, u32[]{:S(2)}) collective-permute-start(bf16[3,96,768]{2,1,0:T(8,128)(2,1)S(1)} %pad_maximum_fusion.7.refs_1_), channel_id=1, source_target_pairs={{0,24},{8,16},{16,8},{24,0},{1,25},{9,17},{17,9},{25,1},{2,26},{10... | collective-permute-start | bytes 1327112 | tf_op jit(solution)/shard_map/ppermute | solution.py:556
  94.2 25.7 %collective-permute-start.23 = (bf16[4,96,768]{2,1,0:T(8,128)(2,1)S(1)}, bf16[4,96,768]{2,1,0:T(8,128)(2,1)}, u32[]{:S(2)}, u32[]{:S(2)}) collective-permute-start(bf16[4,96,768]{2,1,0:T(8,128)(2,1)S(1)} %pad_maximum_fusion.3.refs_0_), channel_id=1, source_target_pairs={{0,1},{1,0},{2,3},{3,2},{4,5},{5,4},{6,7},{7,6},{8,9},{9,8},{10,11... | collective-permute-start | bytes 1769480 | tf_op jit(solution)/shard_map/ppermute | solution.py:553
  119.5 35.7 %collective-permute-start.38 = (bf16[4,2,96,768]{3,2,1,0:T(8,128)(2,1)S(1)}, bf16[4,2,96,768]{3,2,1,0:T(8,128)(2,1)}, u32[]{:S(2)}, u32[]{:S(2)}) collective-permute-start(bf16[4,2,96,768]{3,2,1,0:T(8,128)(2,1)S(1)} %pad_maximum_fusion.near_ref), channel_id=1, source_target_pairs={{0,1},{1,0},{2,3},{3,2},{4,5},{5,4},{6,7},{7,6},{8,9},{9,8},{10,11... | collective-permute-start | bytes 3538952 | tf_op jit(solution)/shard_map/ppermute | solution.py:553
  200.0 68.0 %collective-permute-start.86 = (bf16[2,768,384]{2,1,0:T(8,128)(2,1)}, bf16[2,768,384]{2,1,0:T(8,128)(2,1)}, u32[]{:S(2)}, u32[]{:S(2)}) collective-permute-start(bf16[2,768,384]{2,1,0:T(8,128)(2,1)} %get-tuple-element.132), channel_id=1, source_target_pairs={{0,1},{1,0},{2,3},{3,2},{4,5},{5,4},{6,7},{7,6},{8,9},{9,8},{10,11... | collective-permute-start | bytes 3538952 | tf_op jit(solution)/shard_map/ppermute | solution.py:553
  230.9 22.1 %collective-permute-start.50 = (bf16[2,128,768]{2,1,0:T(8,128)(2,1)}, bf16[2,128,768]{2,1,0:T(8,128)(2,1)S(1)}, u32[]{:S(2)}, u32[]{:S(2)}) collective-permute-start(bf16[2,128,768]{2,1,0:T(8,128)(2,1)} %get-tuple-element.107), channel_id=1, source_target_pairs={{2,0},{3,1},{4,2},{5,3},{6,4},{7,5},{14,6},{15,7},{12,14},{13,15},... | collective-permute-start | bytes 1179656 | tf_op jit(solution)/shard_map/ppermute | solution.py:572
  232.4 21.1 %collective-permute-start.51 = (bf16[2,128,768]{2,1,0:T(8,128)(2,1)S(1)}, bf16[2,128,768]{2,1,0:T(8,128)(2,1)S(1)}, u32[]{:S(2)}, u32[]{:S(2)}) collective-permute-start(bf16[2,128,768]{2,1,0:T(8,128)(2,1)S(1)} %get-tuple-element.108), channel_id=1, source_target_pairs={{0,2},{1,3},{2,4},{3,5},{4,6},{5,7},{6,14},{7,15},{14,12},{15,13},... | collective-permute-start | bytes 1179656 | tf_op jit(solution)/shard_map/ppermute | solution.py:569
  250.2 22.2 %collective-permute-start.73 = (bf16[128,768]{1,0:T(8,128)(2,1)S(1)}, bf16[128,768]{1,0:T(8,128)(2,1)}, u32[]{:S(2)}, u32[]{:S(2)}) collective-permute-start(bf16[128,768]{1,0:T(8,128)(2,1)S(1)} %copy-done.25), channel_id=1, source_target_pairs={{0,1},{1,0},{2,3},{3,2},{4,5},{5,4},{6,7},{7,6},{8,9},{9,8},{10,11... | collective-permute-start | bytes 589832 | tf_op jit(solution)/shard_map/ppermute | solution.py:553
  253.0 23.3 %collective-permute-start.75 = (bf16[4,128,384]{2,1,0:T(8,128)(2,1)}, bf16[4,128,384]{2,1,0:T(8,128)(2,1)}, u32[]{:S(2)}, u32[]{:S(2)}) collective-permute-start(bf16[4,128,384]{2,1,0:T(8,128)(2,1)} %get-tuple-element.126), channel_id=1, source_target_pairs={{0,1},{1,0},{2,3},{3,2},{4,5},{5,4},{6,7},{7,6},{8,9},{9,8},{10,11... | collective-permute-start | bytes 1179656 | tf_op jit(solution)/shard_map/ppermute | solution.py:553
  264.5 27.7 %collective-permute-start.59 = (bf16[32,768]{1,0:T(8,128)(2,1)S(1)}, bf16[32,768]{1,0:T(8,128)(2,1)S(1)}, u32[]{:S(2)}, u32[]{:S(2)}) collective-permute-start(bf16[32,768]{1,0:T(8,128)(2,1)S(1)} %get-tuple-element.175), channel_id=1, source_target_pairs={{0,6},{1,7},{2,4},{3,5},{4,2},{5,3},{6,0},{7,1},{8,14},{9,15},{10,... | collective-permute-start | bytes 147464 | tf_op jit(solution)/shard_map/ppermute | solution.py:550
  272.4 22.7 %collective-permute-start.57 = (bf16[32,768]{1,0:T(8,128)(2,1)S(1)}, bf16[32,768]{1,0:T(8,128)(2,1)S(1)}, u32[]{:S(2)}, u32[]{:S(2)}) collective-permute-start(bf16[32,768]{1,0:T(8,128)(2,1)S(1)} %get-tuple-element.177), channel_id=1, source_target_pairs={{0,2},{1,3},{2,0},{3,1},{4,6},{5,7},{6,4},{7,5},{8,10},{9,11},{10,... | collective-permute-start | bytes 147464 | tf_op jit(solution)/shard_map/ppermute | solution.py:550
  273.0 37.0 %collective-permute-start.89 = (bf16[2,192,384]{2,1,0:T(8,128)(2,1)S(1)}, bf16[2,192,384]{2,1,0:T(8,128)(2,1)S(1)}, u32[]{:S(2)}, u32[]{:S(2)}) collective-permute-start(bf16[2,192,384]{2,1,0:T(8,128)(2,1)S(1)} %get-tuple-element.134), channel_id=1, source_target_pairs={{0,6},{1,7},{2,4},{3,5},{4,2},{5,3},{6,0},{7,1},{8,14},{9,15},{10,... | collective-permute-start | bytes 884744 | tf_op jit(solution)/shard_map/ppermute | solution.py:550
  290.2 24.7 %collective-permute-start.78 = (bf16[768,384]{1,0:T(8,128)(2,1)S(1)}, bf16[768,384]{1,0:T(8,128)(2,1)S(1)}, u32[]{:S(2)}, u32[]{:S(2)}) collective-permute-start(bf16[768,384]{1,0:T(8,128)(2,1)S(1)} %get-tuple-element.130), channel_id=1, source_target_pairs={{0,24},{8,16},{16,8},{24,0},{1,25},{9,17},{17,9},{25,1},{2,26},{10... | collective-permute-start | bytes 1769480 | tf_op jit(solution)/shard_map/ppermute | solution.py:556
  292.4 20.8 %collective-permute-start.87 = (bf16[2,192,384]{2,1,0:T(8,128)(2,1)S(1)}, bf16[2,192,384]{2,1,0:T(8,128)(2,1)S(1)}, u32[]{:S(2)}, u32[]{:S(2)}) collective-permute-start(bf16[2,192,384]{2,1,0:T(8,128)(2,1)S(1)} %get-tuple-element.133), channel_id=1, source_target_pairs={{0,2},{1,3},{2,0},{3,1},{4,6},{5,7},{6,4},{7,5},{8,10},{9,11},{10,... | collective-permute-start | bytes 884744 | tf_op jit(solution)/shard_map/ppermute | solution.py:550
  313.1 24.8 %collective-permute-start.60 = (bf16[128,768]{1,0:T(8,128)(2,1)S(1)}, bf16[128,768]{1,0:T(8,128)(2,1)}, u32[]{:S(2)}, u32[]{:S(2)}) collective-permute-start(bf16[128,768]{1,0:T(8,128)(2,1)S(1)} %copy-done.49), channel_id=1, source_target_pairs={{0,1},{1,0},{2,3},{3,2},{4,5},{5,4},{6,7},{7,6},{8,9},{9,8},{10,11... | collective-permute-start | bytes 589832 | tf_op jit(solution)/shard_map/ppermute | solution.py:553
  344.3 41.4 %collective-permute-start.65 = (bf16[768,384]{1,0:T(8,128)(2,1)S(1)}, bf16[768,384]{1,0:T(8,128)(2,1)}, u32[]{:S(2)}, u32[]{:S(2)}) collective-permute-start(bf16[768,384]{1,0:T(8,128)(2,1)S(1)} %get-tuple-element.123), channel_id=1, source_target_pairs={{0,24},{8,16},{16,8},{24,0},{1,25},{9,17},{17,9},{25,1},{2,26},{10... | collective-permute-start | bytes 1769480 | tf_op jit(solution)/shard_map/ppermute | solution.py:556
  345.0 40.7 %collective-permute-start.64 = (bf16[768,384]{1,0:T(8,128)(2,1)S(1)}, bf16[768,384]{1,0:T(8,128)(2,1)}, u32[]{:S(2)}, u32[]{:S(2)}) collective-permute-start(bf16[768,384]{1,0:T(8,128)(2,1)S(1)} %get-tuple-element.122), channel_id=1, source_target_pairs={{0,16},{8,24},{16,0},{24,8},{1,17},{9,25},{17,1},{25,9},{2,18},{10... | collective-permute-start | bytes 1769480 | tf_op jit(solution)/shard_map/ppermute | solution.py:556
  346.3 39.4 %collective-permute-start.63 = (bf16[768,384]{1,0:T(8,128)(2,1)S(1)}, bf16[768,384]{1,0:T(8,128)(2,1)}, u32[]{:S(2)}, u32[]{:S(2)}) collective-permute-start(bf16[768,384]{1,0:T(8,128)(2,1)S(1)} %get-tuple-element.121), channel_id=1, source_target_pairs={{0,8},{8,0},{16,24},{24,16},{1,9},{9,1},{17,25},{25,17},{2,10},{10... | collective-permute-start | bytes 1769480 | tf_op jit(solution)/shard_map/ppermute | solution.py:556
  347.9 31.6 %collective-permute-start.92 = (bf16[2,96,768]{2,1,0:T(8,128)(2,1)}, bf16[2,96,768]{2,1,0:T(8,128)(2,1)S(1)}, u32[]{:S(2)}, u32[]{:S(2)}) collective-permute-start(bf16[2,96,768]{2,1,0:T(8,128)(2,1)} %maximum_select_fusion.1), channel_id=1, source_target_pairs={{0,16},{8,24},{16,0},{24,8},{1,17},{9,25},{17,1},{25,9},{2,18},{10... | collective-permute-start | bytes 884744 | tf_op jit(solution)/shard_map/ppermute | solution.py:556
  348.9 31.6 %collective-permute-start.91 = (bf16[2,96,768]{2,1,0:T(8,128)(2,1)}, bf16[2,96,768]{2,1,0:T(8,128)(2,1)S(1)}, u32[]{:S(2)}, u32[]{:S(2)}) collective-permute-start(bf16[2,96,768]{2,1,0:T(8,128)(2,1)} %maximum_select_fusion.1), channel_id=1, source_target_pairs={{0,8},{8,0},{16,24},{24,16},{1,9},{9,1},{17,25},{25,17},{2,10},{10... | collective-permute-start | bytes 884744 | tf_op jit(solution)/shard_map/ppermute | solution.py:556
  379.4 30.3 %collective-permute-start.85 = (bf16[1,96,768]{2,1,0:T(8,128)(2,1)}, bf16[1,96,768]{2,1,0:T(8,128)(2,1)}, u32[]{:S(2)}, u32[]{:S(2)}) collective-permute-start(bf16[1,96,768]{2,1,0:T(8,128)(2,1)} %maximum_select_fusion.5), channel_id=1, source_target_pairs={{0,24},{8,16},{16,8},{24,0},{1,25},{9,17},{17,9},{25,1},{2,26},{10... | collective-permute-start | bytes 442376 | tf_op jit(solution)/shard_map/ppermute | solution.py:556
  380.6 30.1 %collective-permute-start.84 = (bf16[1,96,768]{2,1,0:T(8,128)(2,1)}, bf16[1,96,768]{2,1,0:T(8,128)(2,1)}, u32[]{:S(2)}, u32[]{:S(2)}) collective-permute-start(bf16[1,96,768]{2,1,0:T(8,128)(2,1)} %maximum_select_fusion.5), channel_id=1, source_target_pairs={{0,16},{8,24},{16,0},{24,8},{1,17},{9,25},{17,1},{25,9},{2,18},{10... | collective-permute-start | bytes 442376 | tf_op jit(solution)/shard_map/ppermute | solution.py:556
  (145 other events, 1312.3 us)

commit v2 on v1

--- a/solution.py
+++ b/solution.py
@@ -397,29 +397,36 @@
     )
 
 
-def kernel_call(body, outs, args, smem=(), anywhere=(), scratch=(), flops=0):
+def after(values, *needed):
+    return lax.optimization_barrier((values, needed))[0]
+
+
+def kernel_call(
+    body, outs, args, smem=(), scratch=(), flops=1, moved=1, stream=False, room=16
+):
     out_shapes = [jax.ShapeDtypeStruct(shape, kind) for shape, kind in outs]
-    moved = sum(item.size * item.dtype.itemsize for item in args) + sum(
-        item.size * item.dtype.itemsize for item in out_shapes
-    )
-    in_specs = []
-    for place in range(len(args)):
-        if place in smem:
-            in_specs.append(pl.BlockSpec(memory_space=pltpu.SMEM))
-        elif place in anywhere:
-            in_specs.append(pl.BlockSpec(memory_space=pl.ANY))
-        else:
-            in_specs.append(pl.BlockSpec(memory_space=pltpu.VMEM))
+
+    def whole(item):
+        if not stream:
+            return pl.BlockSpec(memory_space=pltpu.VMEM)
+        rank = len(item.shape)
+        return pl.BlockSpec(item.shape, lambda step: (0,) * rank, pipeline_mode=pl.Buffered(1))
+
     return pl.pallas_call(
         body,
+        grid=(1,) if stream else (),
         out_shape=out_shapes,
-        in_specs=in_specs,
-        out_specs=[pl.BlockSpec(memory_space=pltpu.VMEM)] * len(outs),
+        in_specs=[
+            pl.BlockSpec(memory_space=pltpu.SMEM) if place in smem else whole(item)
+            for place, item in enumerate(args)
+        ],
+        out_specs=[whole(item) for item in out_shapes],
         scratch_shapes=list(scratch),
-        compiler_params=pltpu.CompilerParams(vmem_limit_bytes=48 << 20),
+        compiler_params=pltpu.CompilerParams(vmem_limit_bytes=(56 if stream else room) << 20),
         cost_estimate=pl.CostEstimate(
             flops=int(flops), bytes_accessed=int(moved), transcendentals=0
         ),
+        name=body.__name__,
     )(*args)
 
 
@@ -555,6 +562,18 @@
     def along_cols(values, step):
         return lax.ppermute(values, "col", [(i, i ^ step) for i in range(cols_axis)])
 
+    def pair_cols(values):
+        pairs = [
+            (c * seqs + i, (c ^ (1 + i % 2)) * seqs + i)
+            for c in range(cols_axis)
+            for i in range(seqs)
+        ]
+        return lax.ppermute(values, ("col", "seq"), pairs)
+
+    def pair_chips(values):
+        pairs = [(i, (i // 2 ^ (1 + i % 2)) * 2 + i % 2) for i in range(seqs)]
+        return lax.ppermute(values, "seq", pairs)
+
     def place_of(piece_index, core_index):
         block, part = divmod(piece_index, chips)
         chip_index = part if block % 2 == 0 else chips - 1 - part
@@ -583,145 +602,6 @@
     spot = jnp.stack(
         [col_at, chip, core, chunk, col_counts[0], to_left_turn, to_right_turn]
     ).astype(jnp.int32)
-
-    both = jnp.concatenate([tokens, cotangent], axis=0)
-
-    def chunk_rows(values, index):
-        return lax.dynamic_slice_in_dim(values, chunk_of(index) * width, width, axis=1)
-
-    got = [chunk_rows(both, chip)] + [
-        along_chips(chunk_rows(both, chip ^ step), step) for step in steps
-    ]
-    stream_in = jnp.concatenate([item[0] for item in got], axis=0)
-    given_out = jnp.concatenate([item[1] for item in got], axis=0)
-
-    norm_line = jnp.concatenate(
-        list(norms)
-        + [
-            col_counts.astype(bf16),
-            jnp.zeros((model - 6 * shard - 1,), bf16),
-        ]
-    )
-    norm_tile = jnp.broadcast_to(norm_line[None, None], (cols_axis, 8, model))
-
-    def gather_layer(weights, extra):
-        own = jnp.stack(weights)
-        if extra is not None:
-            own = jnp.concatenate([own, extra], axis=1)
-        mine = lax.dynamic_index_in_dim(own, col_at, axis=0, keepdims=False)
-        rows = jnp.stack([along_chips(mine, step) for step in steps])
-        near = [rows] + [along_cols(rows, step) for step in col_steps]
-        own_pair = (own, along_core(own))
-        near_pair = (near, [along_core(item) for item in near])
-        return own_pair, near_pair
-
-    def assemble_layer(own_pair, near_pair):
-        def body(spot_ref, *refs):
-            count = 2 * (1 + cols_axis)
-            pieces, out_ref, sems = refs[:count], refs[count], refs[count + 1]
-            at_col, at_chip, at_core = spot_ref[0], spot_ref[1], spot_ref[2]
-            copies = []
-
-            def move(source, matrix, from_chip, from_core):
-                row = pl.multiple_of((from_chip * 2 + from_core) * shard, shard)
-                copies.append(
-                    pltpu.make_async_copy(
-                        source, out_ref.at[matrix, pl.ds(row, shard)], sems.at[len(copies)]
-                    )
-                )
-                copies[-1].start()
-
-            for other in (0, 1):
-                base = other * (1 + cols_axis)
-                from_core = at_core ^ other
-                for matrix in range(cols_axis):
-                    move(pieces[base].at[matrix, pl.ds(0, shard)], matrix, at_chip, from_core)
-                for step in range(cols_axis):
-                    for hop in steps:
-                        move(
-                            pieces[base + 1 + step].at[hop - 1, pl.ds(0, shard)],
-                            at_col ^ step,
-                            at_chip ^ hop,
-                            from_core,
-                        )
-            for copy in copies:
-                copy.wait()
-
-        args = [spot, own_pair[0], *near_pair[0], own_pair[1], *near_pair[1]]
-        total = 2 * cols_axis * chips
-        return kernel_call(
-            body,
-            [((cols_axis, model, model), bf16)],
-            args,
-            smem=(0,),
-            anywhere=tuple(range(1, len(args))),
-            scratch=[pltpu.SemaphoreType.DMA((total,))],
-        )[0]
-
-    row_own, row_near = gather_layer(row_weights, norm_tile)
-    weights_row = assemble_layer(row_own, row_near)
-    lines = jnp.stack(
-        [
-            line
-            for side in (0, 1)
-            for line in [row_own[side][0, shard]]
-            + [row_near[side][0][step - 1, shard] for step in steps]
-        ]
-    )
-    line_shard = jnp.stack(
-        [(chip ^ step) * 2 + (core ^ side) for side in (0, 1) for step in range(chips)]
-    )
-    order = (jnp.arange(seqs)[:, None] == line_shard[None, :]).astype(bf16)
-    ordered = jnp.dot(order, lines, preferred_element_type=f32)
-    norm_rows = ordered[:, : 6 * shard].reshape(seqs, 6, shard).transpose(1, 0, 2)
-    norm_rows = jnp.pad(norm_rows.reshape(6, model), ((0, 2), (0, 0)))
-    count_total = col_counts[0].astype(f32)
-    for step in col_steps:
-        count_total = count_total + row_near[0][step][0, shard, 6 * shard].astype(f32)
-    entropy_scale = jnp.reshape(entropy_weight / (HEADS * count_total), (1,))
-
-    col_own, col_near = gather_layer(col_weights, None)
-    weights_col = assemble_layer(col_own, col_near)
-
-    part = feed_out.shape[0] // cols_axis
-    feed_cols = lax.dynamic_slice_in_dim(
-        feed_in.reshape(shard, seqs, feed_out.shape[0]), col_at * part, part, axis=2
-    ).reshape(shard, hidden)
-    feed_rows = lax.dynamic_slice_in_dim(feed_out, col_at * part, part, axis=0)
-    feed_own = jnp.stack([feed_cols, feed_rows])
-    feed_all = jnp.stack([feed_own] + [along_chips(feed_own, step) for step in steps])
-    feed_other = along_core(feed_all)
-
-    def assemble_feed():
-        def body(spot_ref, near_ref, far_ref, out_ref, sems):
-            at_chip, at_core = spot_ref[1], spot_ref[2]
-            copies = []
-            for other, ref in enumerate((near_ref, far_ref)):
-                for hop in range(chips):
-                    row = ((at_chip ^ hop) * 2 + (at_core ^ other)) * shard
-                    for matrix in (0, 1):
-                        copies.append(
-                            pltpu.make_async_copy(
-                                ref.at[hop, matrix],
-                                out_ref.at[matrix, pl.ds(pl.multiple_of(row, shard), shard)],
-                                sems.at[len(copies)],
-                            )
-                        )
-                        copies[-1].start()
-            for copy in copies:
-                copy.wait()
-
-        return kernel_call(
-            body,
-            [((2, model, hidden), bf16)],
-            [spot, feed_all, feed_other],
-            smem=(0,),
-            anywhere=(1, 2),
-            scratch=[pltpu.SemaphoreType.DMA((4 * chips,))],
-        )[0]
-
-    weights_feed = assemble_feed()
-    given_near = [given_out] + [along_cols(given_out, step) for step in col_steps]
 
     half_width = model // 2
     frequency = jnp.exp(-math.log(1000.0) * jnp.arange(half_width, dtype=f32) / half_width)
@@ -741,7 +621,183 @@
     inside = (key_global >= 0) & (key_global < cols_axis * cols_dev)
     allowed = ((jnp.any(matches, axis=1) | (distance == WINDOW)) & inside).astype(f32)
 
-    def project_row(stream_ref, waves_ref, norm_ref, weight_ref, zero_ref, low_ref, q_ref, kv_ref):
+    quarter = shard // cols_axis
+    lines = 8
+    hops = chips - 1
+    col_rows = cols_axis * quarter
+    row_rows = col_rows + lines
+
+    def chunk_at(spot_ref, chip_index):
+        at = jnp.where(spot_ref[0] % 2 == 0, chip_index, chips - 1 - chip_index)
+        return pl.ds(pl.multiple_of(at * width, width), width)
+
+    def pack(spot_ref, weights, token_ref, own_ref, chunk_ref, send_refs, block):
+        at = pl.multiple_of(spot_ref[0] * quarter, quarter)
+        size = len(weights) * quarter
+        for index, ref in enumerate(weights):
+            own_ref[index * shard : (index + 1) * shard] = ref[...]
+            for send_ref in send_refs:
+                send_ref[index * quarter : (index + 1) * quarter] = ref[pl.ds(at, quarter)]
+        if block is not None:
+            for ref, row in [(own_ref, len(weights) * shard)] + [
+                (ref, size) for ref in send_refs
+            ]:
+                ref[row : row + lines] = jnp.zeros((lines, model), bf16)
+                ref[row : row + lines, :128] = block
+            size = size + lines
+        chunk_ref[...] = token_ref[0, chunk_at(spot_ref, spot_ref[1])]
+        for hop, ref in enumerate(send_refs):
+            ref[size:] = token_ref[0, chunk_at(spot_ref, spot_ref[1] ^ (hop + 1))]
+
+    def pack_row(spot_ref, *refs):
+        norm_refs, token_ref, own_ref, chunk_ref = refs[4:10], refs[10], refs[11], refs[12]
+        block = jnp.zeros((lines, 128), f32)
+        rows = lax.broadcasted_iota(jnp.int32, (lines, 128), 0)
+        for index, ref in enumerate(norm_refs):
+            line = jnp.pad(ref[...].astype(f32), ((0, 0), (0, 128 - shard)))
+            block = jnp.where(rows == index, line, block)
+        block = jnp.where(rows == 6, spot_ref[4].astype(f32), block).astype(bf16)
+        pack(spot_ref, refs[:4], token_ref, own_ref, chunk_ref, refs[13:], block)
+
+    part = feed_out.shape[0] // cols_axis
+    block_cols = feed_out.shape[0]
+
+    def pack_rest(spot_ref, *refs):
+        in_ref, out_ref, own_ref = refs[5], refs[6], refs[7]
+        pack(spot_ref, refs[:4], refs[4], refs[8], refs[9], refs[10:], None)
+        first = lax.broadcasted_iota(jnp.int32, (block_cols, 128), 0)
+        lanes = lax.broadcasted_iota(jnp.int32, (block_cols, 128), 1)
+        chosen = ((first == lanes + spot_ref[0] * part) & (lanes < part)).astype(bf16)
+        for index in range(seqs):
+            block = in_ref[:, index * block_cols : (index + 1) * block_cols]
+            own_ref[0, :, index * part : (index + 1) * part] = dot(block, chosen)[
+                :, :part
+            ].astype(bf16)
+        own_ref[1] = out_ref[pl.ds(pl.multiple_of(spot_ref[0] * part, part), part)]
+
+    def split_got(own_ref, *refs):
+        rows = refs[0].shape[0] - width
+        ins, (hops_ref, stream_ref) = refs[:-2], refs[-2:]
+        stream_ref[:width] = own_ref[...]
+        for hop, ref in enumerate(ins):
+            hops_ref[hop * rows : (hop + 1) * rows] = ref[:rows]
+            stream_ref[(hop + 1) * width : (hop + 2) * width] = ref[rows:]
+
+    def spread_plane(near, far):
+        def join_cores(near_ref, far_ref, out_ref):
+            rows = near_ref.shape[0]
+            out_ref[:rows] = near_ref[...]
+            out_ref[rows:] = far_ref[...]
+
+        both_cores = kernel_call(join_cores, [((2 * near.shape[0], model), bf16)], [near, far])[0]
+        return both_cores, pair_cols(both_cores), along_cols(near, cols_axis - 1)
+
+    def place_rows(spot_ref, refs, outs, rows, unit):
+        at_col, at_chip, at_core = spot_ref[0], spot_ref[1], spot_ref[2]
+        other = 1 - at_core
+
+        def row_of(from_chip, from_core, offset, size):
+            return pl.ds(
+                pl.multiple_of((from_chip * 2 + from_core) * shard + offset, quarter), size
+            )
+
+        pieces = (
+            (refs[2], at_col, at_core, 2),
+            (refs[3], at_col ^ (1 + at_core), at_core, 2),
+            (refs[4], at_col ^ 3, at_core, 1),
+            (refs[5], at_col ^ (1 + other), other, 2),
+            (refs[6], at_col ^ 3, other, 1),
+        )
+        for index, (out_ref, lead) in enumerate(outs):
+            for ref, core_at in ((refs[0], at_core), (refs[1], other)):
+                out_ref[lead + (row_of(at_chip, core_at, 0, shard),)] = ref[
+                    index * shard : (index + 1) * shard
+                ]
+            for ref, col, core_at, sides in pieces:
+                for side in range(sides):
+                    for hop in steps:
+                        at = row_of(at_chip ^ hop, core_at ^ side, col * quarter, quarter)
+                        start = side * unit + (hop - 1) * rows + index * quarter
+                        out_ref[lead + (at,)] = ref[start : start + quarter]
+
+    row_own, stream_own, *row_sends = kernel_call(
+        pack_row,
+        [((cols_axis * shard + lines, model), bf16), ((width, model), bf16)]
+        + [((row_rows + width, model), bf16)] * hops,
+        [spot, *row_weights, *[item[None] for item in norms], tokens],
+        smem=(0,),
+        stream=True,
+    )
+    row_got = [along_chips(row_sends[step - 1], step) for step in steps]
+    feed_own, col_own, given_own, *col_sends = kernel_call(
+        pack_rest,
+        [
+            ((2, shard, hidden), bf16),
+            ((cols_axis * shard, model), bf16),
+            ((width, model), bf16),
+        ]
+        + [((col_rows + width, model), bf16)] * hops,
+        [spot, *col_weights, cotangent, feed_in, feed_out],
+        smem=(0,),
+        stream=True,
+    )
+    row_got = after(row_got, waves, allowed, col_sends)
+    row_hops, stream_in = kernel_call(
+        split_got,
+        [((hops * row_rows, model), bf16), ((toks, model), bf16)],
+        [stream_own, *row_got],
+    )
+    row_far_own = along_core(row_own)
+    row_plane, row_pair, row_diagonal = spread_plane(row_hops, along_core(row_hops))
+    col_sends = after(col_sends, row_plane)
+    col_got = [along_chips(col_sends[step - 1], step) for step in steps]
+    row_last = after((row_pair, row_diagonal), row_pair, row_diagonal, col_got)
+    row_pieces = [row_own, row_far_own, row_plane, row_pair, row_diagonal] + [
+        along_core(item) for item in row_last
+    ]
+
+    def stack_got(own_ref, *refs):
+        rows = refs[0].shape[0] - width
+        ins, out_ref = refs[:-1], refs[-1]
+        at = hops * rows
+        out_ref[at : at + width] = own_ref[...]
+        for hop, ref in enumerate(ins):
+            out_ref[hop * rows : (hop + 1) * rows] = ref[:rows]
+            out_ref[at + (hop + 1) * width : at + (hop + 2) * width] = ref[rows:]
+
+    col_unit = hops * col_rows + toks
+    col_hops = kernel_call(stack_got, [((col_unit, model), bf16)], [given_own, *col_got])[0]
+    col_far_own = along_core(col_own)
+    col_plane, col_pair, col_diagonal = spread_plane(col_hops, along_core(col_hops))
+
+    def project_row(spot_ref, stream_ref, waves_ref, *refs):
+        pieces, outs = refs[:7], refs[7:]
+        zero_ref, low_ref, q_ref, kv_ref, weight_ref, last_ref, norm_ref = outs
+        place_rows(
+            spot_ref,
+            pieces,
+            [(weight_ref, (index,)) for index in range(3)] + [(last_ref, ())],
+            row_rows,
+            hops * row_rows,
+        )
+        first = lax.broadcasted_iota(jnp.int32, (128, model), 0)
+        lanes = lax.broadcasted_iota(jnp.int32, (128, model), 1)
+        total = jnp.zeros((lines, model), f32)
+        for side in (0, 1):
+            for hop in range(chips):
+                if hop == 0:
+                    block = pieces[side][cols_axis * shard : cols_axis * shard + lines, :128]
+                else:
+                    at = (side * hops + hop) * row_rows - lines
+                    block = pieces[2][at : at + lines, :128]
+                start = ((spot_ref[1] ^ hop) * 2 + (spot_ref[2] ^ side)) * shard
+                chosen = ((lanes == first + start) & (first < shard)).astype(bf16)
+                total = total + dot(block, chosen)
+        count = spot_ref[4].astype(f32)
+        for ref in pieces[3:6]:
+            count = count + ref[row_rows - lines : row_rows, :128][6:7, 0:1].astype(f32)
+        rows = lax.broadcasted_iota(jnp.int32, (lines, model), 0)
+        norm_ref[...] = jnp.where(rows == 6, count, total)
         for slot in range(chips):
             rows = slice(slot * width, (slot + 1) * width)
             zero_ref[rows, :half] = stream_ref[rows, :half].astype(f32) + waves_ref[:width]
@@ -756,19 +812,34 @@
         kv_ref[1] = dot(low, weight_ref[2]).astype(bf16)
 
     big = 2.0 * toks * model * model
-    stream_zero, normed_one, row_q, row_kv = kernel_call(
+    stream_zero, normed_one, row_q, row_kv, weights_row, weights_out, norm_rows = kernel_call(
         project_row,
         [
             ((toks, model), f32),
             ((toks, model), bf16),
             ((toks, model), bf16),
             ((2, toks, model), bf16),
+            ((3, model, model), bf16),
+            ((model, model), bf16),
+            ((lines, model), f32),
         ],
-        [stream_in, waves, norm_rows, weights_row],
-        flops=3 * big,
+        [spot, stream_in, waves, *row_pieces],
+        smem=(0,),
     )
     kv_left = to_right(row_kv)
     kv_right = to_left(row_kv)
+
+    feed_own = after(feed_own, kv_left, kv_right)
+    feed_other = along_core(feed_own)
+
+    def pair_feed(own_ref, other_ref, out_ref):
+        out_ref[0] = own_ref[...]
+        out_ref[1] = other_ref[...]
+
+    feed_both = kernel_call(
+        pair_feed, [((2, 2, shard, hidden), bf16)], [feed_own, feed_other]
+    )[0]
+    feed_pair, feed_diagonal = pair_chips(feed_both), along_chips(feed_own, chips - 1)
 
     def tied_logits(spot_ref, q_ref, near_ref, left_ref, right_ref, out_ref):
         mask = head_mask(width, model)
@@ -785,9 +856,8 @@
         [((fold, span), f32)],
         [spot, row_q, row_kv, kv_left, kv_right],
         smem=(0,),
-        flops=chips * 2.0 * fold * model * span,
     )[0]
-    logits_other = along_core(logits)
+    logits_other = after(along_core(logits), col_pair, col_diagonal)
     row_scale = 1.0 / math.sqrt(HEAD_DIM * seqs)
     col_scale = 1.0 / math.sqrt(HEAD_DIM)
 
@@ -832,7 +902,7 @@
             mix_ref[slot * width : (slot + 1) * width] = fold_heads(
                 dot(low_probs, values), mask, width
             ).astype(bf16)
-        stream = zero_ref[...] + dot(mix_ref[...], weight_ref[3])
+        stream = zero_ref[...] + dot(mix_ref[...], weight_ref[...])
         stream_ref[...] = stream
         unit, _ = unit_norm(stream)
         low_ref[...] = (unit * norm_ref[2:3] + norm_ref[3:4]).astype(bf16)
@@ -857,10 +927,36 @@
             kv_right,
             stream_zero,
             norm_rows,
-            weights_row,
+            weights_out,
         ],
         smem=(0,),
-        flops=chips * 2.0 * fold * model * span + big,
+    )
+
+    col_last = after((col_pair, col_diagonal), normed_two)
+    col_pieces = [col_own, col_far_own, col_plane, col_pair, col_diagonal] + [
+        along_core(item) for item in col_last
+    ]
+
+    def assemble_col(spot_ref, *refs):
+        three_ref, last_ref, given_ref = refs[7:]
+        outs = [(three_ref, (index,)) for index in range(3)] + [(last_ref, ())]
+        place_rows(spot_ref, refs[:7], outs, col_rows, col_unit)
+        at_core = spot_ref[2]
+        start = hops * col_rows
+        given_ref[0] = refs[2][start:col_unit]
+        given_ref[1 + at_core] = refs[3][start:col_unit]
+        given_ref[2 - at_core] = refs[5][col_unit + start :]
+        given_ref[3] = refs[4][start:]
+
+    weights_three, weights_last, given_all = kernel_call(
+        assemble_col,
+        [
+            ((3, model, model), bf16),
+            ((model, model), bf16),
+            ((cols_axis, toks, model), bf16),
+        ],
+        [spot, *col_pieces],
+        smem=(0,),
     )
 
     def project_col(low_ref, weight_ref, q_ref, kv_ref):
@@ -872,8 +968,7 @@
     col_q, col_kv = kernel_call(
         project_col,
         [((toks, model), bf16), ((2, toks, model), bf16)],
-        [normed_two, weights_col],
-        flops=3 * big,
+        [normed_two, weights_three],
     )
     kv_other = along_core(col_kv)
 
@@ -922,7 +1017,7 @@
                 ].astype(f32)
                 mixed = term if mixed is None else mixed + term
             mix_ref[slot_rows(slot)] = mixed.astype(bf16)
-        stream = one_ref[...] + dot(mix_ref[...], weight_ref[3])
+        stream = one_ref[...] + dot(mix_ref[...], weight_ref[...])
         stream_ref[...] = stream
         unit, _ = unit_norm(stream)
         low_ref[...] = (unit * norm_ref[4:5] + norm_ref[5:6]).astype(bf16)
@@ -935,19 +1030,43 @@
             ((toks, model), f32),
             ((toks, model), bf16),
         ],
-        [col_q, col_kv, kv_other, stream_one, norm_rows, weights_col],
-        flops=big + 6.0 * chips * seqs * width * model * 128,
+        [col_q, col_kv, kv_other, stream_one, norm_rows, weights_last],
     )
     low_near = [normed_three] + [along_cols(normed_three, step) for step in col_steps]
 
-    def feed_main(a0, a1, a2, a3, d0, d1, d2, d3, weight_ref, act_ref, grad_ref, *back_refs):
+    feed_last = after((feed_pair, feed_diagonal), low_near)
+    feed_far = [along_core(item) for item in feed_last]
+
+    def assemble_feed(spot_ref, both_ref, pair_ref, last_ref, pair2_ref, last2_ref, out_ref):
+        at_chip, at_core = spot_ref[1], spot_ref[2]
+        other = 1 - at_core
+
+        def move(rows, from_chip, from_core):
+            at = pl.multiple_of((from_chip * 2 + from_core) * shard, shard)
+            out_ref[:, pl.ds(at, shard)] = rows
+
+        for side in (0, 1):
+            move(both_ref[side], at_chip, at_core ^ side)
+            move(pair_ref[side], at_chip ^ (1 + at_core), at_core ^ side)
+            move(pair2_ref[side], at_chip ^ (1 + other), other ^ side)
+        move(last_ref[...], at_chip ^ 3, at_core)
+        move(last2_ref[...], at_chip ^ 3, other)
+
+    weights_feed = kernel_call(
+        assemble_feed,
+        [((2, model, hidden), bf16)],
+        [spot, feed_both, feed_pair, feed_diagonal, *feed_far],
+        smem=(0,),
+    )[0]
+
+    def feed_main(a0, a1, a2, a3, given_ref, weight_ref, act_ref, grad_ref, *back_refs):
         up, down = weight_ref[0], weight_ref[1]
-        for step, (low_ref, given_ref) in enumerate(((a0, d0), (a1, d1), (a2, d2), (a3, d3))):
+        for step, low_ref in enumerate((a0, a1, a2, a3)):
             pre = dot(low_ref[...], up)
             bell = 0.5 * (1.0 + lax.erf(pre * (0.5**0.5)))
             slope = bell + pre * jnp.exp(-0.5 * pre * pre) * ((0.5 / math.pi) ** 0.5)
             act_ref[step] = (pre * bell).astype(bf16)
-            grad = (slope * dot_back(given_ref[...], down)).astype(bf16)
+            grad = (slope * dot_back(given_ref[step], down)).astype(bf16)
             grad_ref[step] = grad
             back_refs[step][...] = dot_back(grad, up).astype(bf16)
 
@@ -955,37 +1074,156 @@
     feed_results = kernel_call(
         feed_main,
         [((cols_axis, toks, hidden), bf16)] * 2 + [((toks, model), bf16)] * cols_axis,
-        [*low_near, *given_near, weights_feed],
-        flops=3 * feed_big,
+        [*low_near, given_all, weights_feed],
     )
     act, grad_hidden, back_parts = feed_results[0], feed_results[1], feed_results[2:]
     back_near = [back_parts[0]] + [along_cols(back_parts[step], step) for step in col_steps]
 
     def feed_weights(
-        spot_ref, a0, a1, a2, a3, d0, d1, d2, d3, act_ref, grad_ref, weight_ref, mine_ref, give_ref, *outs
+        spot_ref, a0, a1, a2, a3, given_ref, act_ref, grad_ref, weight_ref, mine_ref, give_ref, *outs
     ):
         at_core = spot_ref[2]
         low = jnp.concatenate([a0[...], a1[...], a2[...], a3[...]], axis=0)
-        given = jnp.concatenate([d0[...], d1[...], d2[...], d3[...]], axis=0)
+        given = given_ref[...].reshape(cols_axis * toks, model)
         rows = cols_axis * toks
         acts = act_ref[...].reshape(rows, hidden)
         grads = grad_ref[...].reshape(rows, hidden)
         for step in range(cols_axis):
             outs[step][...] = dot(act_ref[step], weight_ref[1]).astype(bf16)
         for ref, at in ((mine_ref, at_core), (give_ref, 1 - at_core)):
-            ref[0] = dot_tokens(low, half_of(grads, at, half)).astype(bf16)
-            ref[1] = dot_tokens(acts, half_of(given, at, half)).astype(bf16)
+            ref[:model] = dot_tokens(low, half_of(grads, at, half)).astype(bf16)
+            ref[model:] = dot_tokens(acts, half_of(given, at, half)).astype(bf16)
 
     feed_grads = kernel_call(
         feed_weights,
-        [((2, model, half), bf16)] * 2 + [((toks, model), bf16)] * cols_axis,
-        [spot, *low_near, *given_near, act, grad_hidden, weights_feed],
+        [((2 * model, half), bf16)] * 2 + [((toks, model), bf16)] * cols_axis,
+        [spot, *low_near, given_all, act, grad_hidden, weights_feed],
         smem=(0,),
-        flops=3 * feed_big,
+        flops=6.0 * toks * cols_axis * model * hidden,
+        moved=16 << 20,
+        room=24,
     )
     feed_mine, feed_give, out_parts = feed_grads[0], feed_grads[1], feed_grads[2:]
-    out_near = [out_parts[0]] + [along_cols(out_parts[step], step) for step in col_steps]
-    feed_got = along_core(feed_give)
+    feed_back_in = along_core(feed_give)
+
+    block = 2 * shard
+    extra = 2 * lines
+
+    def renew(total, at):
+        line = total[at : at + 1]
+        whole = line[:, 0:1] + line[:, 1:2]
+        high = whole.astype(bf16).astype(f32)
+        lanes = lax.broadcasted_iota(jnp.int32, total.shape, 1)
+        rows = lax.broadcasted_iota(jnp.int32, total.shape, 0)
+        total = jnp.where((rows == at) & (lanes == 0), high, total)
+        return jnp.where((rows == at) & (lanes == 1), whole - high, total)
+
+    def layer_grads(low, mix, low_far, mix_far, mine, got, more):
+        rows = model + (extra if len(more) == 1 else 2 * toks)
+
+        def weight_sums(spot_ref, low_ref, mix_ref, low2_ref, mix2_ref, mine_ref, got_ref, *refs):
+            more_refs, outs = refs[: len(more)], refs[len(more) : -2]
+            left_ref, right_ref = refs[-2:]
+            left_ref[0, :toks] = low_ref[...]
+            left_ref[0, toks:] = low2_ref[...]
+            left_ref[1, :toks] = mix_ref[...]
+            left_ref[1, toks:] = mix2_ref[...]
+            right_ref[:, :toks] = mine_ref[...]
+            right_ref[:, toks:] = got_ref[...]
+            for step in range(cols_axis):
+                matrix = spot_ref[0] ^ step
+                left = left_ref[matrix // 3]
+                outs[step][:model] = dot_tokens(left, right_ref[matrix]).astype(bf16)
+                if len(more) == 1:
+                    sums_ref = more_refs[0]
+                    tail = jnp.concatenate([sums_ref[:, :half], sums_ref[:, half:]], axis=0)
+                    outs[step][model:] = renew(tail, 6).astype(bf16)
+                else:
+                    outs[step][model : model + toks] = more_refs[step][:, :half]
+                    outs[step][model + toks :] = more_refs[step][:, half:]
+
+        return kernel_call(
+            weight_sums,
+            [((rows, half), bf16)] * cols_axis,
+            [spot, low, mix, low_far, mix_far, mine, got, *more],
+            smem=(0,),
+            scratch=[
+                pltpu.VMEM((2, 2 * toks, model), bf16),
+                pltpu.VMEM((4, 2 * toks, half), bf16),
+            ],
+        )
+
+    def split_chips(items, count, tail, stream=None, slots=()):
+        slot_rows_out = 2 * width if stream is not None or slots else 0
+
+        def chip_parts(spot_ref, *refs):
+            ins, outs, total_ref = refs[: len(items)], refs[-chips - 1 : -1], refs[-1]
+            more = refs[len(items) : -chips - 1]
+            total = ins[0][...].astype(f32)
+            for ref in ins[1:]:
+                total = total + ref[...].astype(f32)
+            total_ref[...] = total.astype(bf16)
+            if stream is not None:
+                result = more[0][...] + jnp.concatenate(
+                    [total[model : model + toks], total[model + toks :]], axis=1
+                )
+            for hop in range(chips):
+                at = pl.multiple_of((spot_ref[1] ^ hop) * block, block)
+                for index in range(count):
+                    outs[hop][index * block : (index + 1) * block] = total_ref[
+                        pl.ds(index * model + at, block)
+                    ]
+                row = count * block
+                if tail:
+                    outs[hop][row : row + tail] = renew(total[count * model :], 6).astype(bf16)
+                    row = row + tail
+                if slot_rows_out:
+                    if stream is not None:
+                        slot = result[slot_rows(hop)].astype(bf16)
+                    else:
+                        slot = more[hop][...]
+                    outs[hop][row : row + width] = slot[:, :half]
+                    outs[hop][row + width :] = slot[:, half:]
+
+        size = count * block + tail + slot_rows_out
+        return kernel_call(
+            chip_parts,
+            [((size, half), bf16)] * chips,
+            [spot, *items] + ([] if stream is None else [stream]) + list(slots),
+            smem=(0,),
+            scratch=[pltpu.VMEM(items[0].shape, bf16)],
+        )
+
+    def split_cores(items, count, tail):
+        rows_in = count * block + tail
+
+        def core_parts(spot_ref, *refs):
+            ins, (keep_ref, give_ref, total_ref) = refs[: len(items)], refs[len(items) :]
+            total = ins[0][:rows_in].astype(f32)
+            for ref in ins[1:]:
+                total = total + ref[:rows_in].astype(f32)
+            total_ref[...] = total.astype(bf16)
+            for ref, at in ((keep_ref, spot_ref[2]), (give_ref, 1 - spot_ref[2])):
+                for index in range(count):
+                    row = pl.multiple_of(index * block + at * shard, shard)
+                    ref[index * shard : (index + 1) * shard] = total_ref[pl.ds(row, shard)]
+                if tail:
+                    ref[count * shard :] = renew(total[count * block :], 6).astype(bf16)
+
+        size = count * shard + tail
+        return kernel_call(
+            core_parts,
+            [((size, half), bf16)] * 2,
+            [spot, *items],
+            smem=(0,),
+            scratch=[pltpu.VMEM((rows_in, half), bf16)],
+        )
+
+    def over_chips(parts):
+        return [parts[0]] + [along_chips(parts[step], step) for step in steps]
+
+    feed_slices = split_chips([feed_mine, feed_back_in], 2, 0)
+    back_near = after(back_near, feed_slices)
 
     def attend_col_back(
         spot_ref,
@@ -1013,11 +1251,11 @@
         back = b0[...].astype(f32) + b1[...].astype(f32) + b2[...].astype(f32) + b3[...].astype(f32)
         unit, scale = unit_norm(two_ref[...])
         sums_ref[...] = norm_sums(back, unit)
-        dtwo = given_ref[...].astype(f32) + unit_norm_back(back, unit, scale, norm_ref[4:5])
+        dtwo = given_ref[0].astype(f32) + unit_norm_back(back, unit, scale, norm_ref[4:5])
         dtwo_ref[...] = dtwo
         low = dtwo.astype(bf16)
         low_ref[...] = low
-        dmix = dot_back(low, weight_ref[3]).astype(bf16).astype(f32)
+        dmix = dot_back(low, weight_ref[...]).astype(bf16).astype(f32)
         wide_ref[...] = jnp.zeros_like(wide_ref)
         sides = (near_ref, far_ref)
         for slot in range(chips):
@@ -1066,10 +1304,10 @@
         [
             spot,
             *back_near,
-            given_out,
+            given_all,
             stream_two,
             norm_rows,
-            weights_col,
+            weights_last,
             col_q,
             col_kv,
             kv_other,
@@ -1077,9 +1315,8 @@
         ],
         smem=(0,),
         scratch=[pltpu.VMEM((2, 2 * toks, model), f32)],
-        flops=big + 10.0 * chips * seqs * width * model * 128,
-    )
-    col_got = along_core(col_send)
+    )
+    dkv_got = along_core(col_send)
 
     def row_entry_back(
         spot_ref,
@@ -1117,7 +1354,7 @@
         done_ref[...] = done
         low = done.astype(bf16)
         low_ref[...] = low
-        dmix = dot_back(low, row_ref[3]).astype(bf16)
+        dmix = dot_back(low, row_ref[...]).astype(bf16)
         dmix_ref[...] = dmix
         mask = head_mask(width, model)
         total = None
@@ -1150,21 +1387,30 @@
             spot,
             col_dq,
             col_dkv,
-            col_got,
+            dkv_got,
             grad_two_low,
             grad_two,
             stream_one,
             norm_rows,
-            weights_col,
-            weights_row,
+            weights_three,
+            weights_out,
             row_kv,
             kv_left,
             kv_right,
         ],
         smem=(0,),
-        flops=4 * big + chips * 2.0 * fold * model * span,
     )
     dprobs_other = along_core(dprobs)
+    col_sums = layer_grads(
+        normed_two,
+        col_mix,
+        along_core(normed_two),
+        along_core(col_mix),
+        col_mine,
+        along_core(col_give),
+        out_parts,
+    )
+    dprobs_other = after(dprobs_other, col_sums)
 
     def attend_row_back(
         spot_ref,
@@ -1187,7 +1433,7 @@
         dprob = dprobs_ref[...] + other_ref[...]
         probs_here, scores_here = probs_ref[...], scores_ref[...]
         rows = lax.broadcasted_iota(jnp.int32, (fold, 1), 0) % width
-        weight = jnp.where(rows + spot_ref[3] * width < spot_ref[4], weight_ref[0], 0.0)
+        weight = jnp.where(rows + spot_ref[3] * width < spot_ref[4], entropy_weight / (HEADS * weight_ref[6:7, 0:1]), 0.0)
         first = dprob - jnp.sum(probs_here * dprob, axis=-1, keepdims=True)
         second = scores_here - jnp.sum(probs_here * scores_here, axis=-1, keepdims=True)
         dscores = (probs_here * (first - weight * second)).astype(bf16)
@@ -1215,7 +1461,7 @@
         ],
         [
             spot,
-            entropy_scale,
+            norm_rows,
             dprobs,
             dprobs_other,
             scores,
@@ -1226,11 +1472,12 @@
             kv_right,
             row_dmix,
         ],
-        smem=(0, 1),
-        flops=3 * chips * 2.0 * fold * model * span,
+        smem=(0,),
     )
     edge_from_right = to_left(edge_left)
     edge_from_left = to_right(edge_right)
+    feed_keep, feed_swap = split_cores(over_chips(feed_slices), 2, 0)
+    edge_from_left = after(edge_from_left, feed_keep)
 
     def input_back(
         spot_ref,
@@ -1243,10 +1490,13 @@
         zero_ref,
         norm_ref,
         row_ref,
+        two_ref,
+        three_ref,
+        entropy_ref,
         mine_ref,
         give_ref,
-        out_ref,
         sums_ref,
+        *slot_refs,
     ):
         at_core = spot_ref[2]
         dq = dq_ref[...]
@@ -1269,19 +1519,23 @@
             give_ref[index] = half_of(item, 1 - at_core, half)
         back = dot_back(dq, row_ref[0]) + dot_back(dk, row_ref[1]) + dot_back(dv, row_ref[2])
         unit, scale = unit_norm(zero_ref[...])
-        sums_ref[...] = norm_sums(back, unit)
-        out_ref[...] = (done_ref[...] + unit_norm_back(back, unit, scale, norm_ref[0:1])).astype(
-            bf16
-        )
-
-    row_mine, row_give, grad_in, sums_one = kernel_call(
+        sums_ref[0:2] = norm_sums(back, unit)
+        sums_ref[2:4] = two_ref[...]
+        sums_ref[4:6] = three_ref[...]
+        sums_ref[6:7] = entropy_ref[...]
+        sums_ref[7:8] = jnp.zeros((1, model), f32)
+        result = (done_ref[...] + unit_norm_back(back, unit, scale, norm_ref[0:1])).astype(bf16)
+        for slot in range(chips):
+            slot_refs[slot][...] = result[slot_rows(slot)]
+
+    row_mine, row_give, sums, *grad_slots = kernel_call(
         input_back,
         [
             ((4, toks, half), bf16),
             ((4, toks, half), bf16),
-            ((toks, model), bf16),
-            ((2, model), f32),
-        ],
+            ((lines, model), f32),
+        ]
+        + [((width, model), bf16)] * chips,
         [
             spot,
             row_dq,
@@ -1293,123 +1547,129 @@
             stream_zero,
             norm_rows,
             weights_row,
+            sums_two,
+            sums_three,
+            entropy_row,
         ],
         smem=(0,),
-        flops=3 * big,
-    )
-
-    def layer_grads(low, mix, low_other, mix_other, mine, given):
-        def body(
-            spot_ref, low_ref, mix_ref, low2_ref, mix2_ref, mine_ref, given_ref, *outs_and_scratch
-        ):
-            outs, (left_ref, right_ref) = outs_and_scratch[:cols_axis], outs_and_scratch[cols_axis:]
-            at_col = spot_ref[0]
-            left_ref[0, :toks] = low_ref[...]
-            left_ref[0, toks:] = low2_ref[...]
-            left_ref[1, :toks] = mix_ref[...]
-            left_ref[1, toks:] = mix2_ref[...]
-            right_ref[:, :toks] = mine_ref[...]
-            right_ref[:, toks:] = given_ref[...]
-            for step in range(cols_axis):
-                matrix = at_col ^ step
-                left = left_ref[matrix // 3]
-                outs[step][...] = dot_tokens(left, right_ref[matrix]).astype(bf16)
-
-        return kernel_call(
-            body,
-            [((model, half), bf16)] * cols_axis,
-            [spot, low, mix, low_other, mix_other, mine, given],
-            smem=(0,),
-            scratch=[
-                pltpu.VMEM((2, 2 * toks, model), bf16),
-                pltpu.VMEM((4, 2 * toks, half), bf16),
-            ],
-            flops=4 * big,
+    )
+
+    def join_halves(spot_ref, keep_rows, got_rows):
+        first = spot_ref[2] == 0
+        return jnp.concatenate(
+            [jnp.where(first, keep_rows, got_rows), jnp.where(first, got_rows, keep_rows)], axis=1
         )
 
-    def add_parts(items):
-        total = items[0].astype(f32)
-        for item in items[1:]:
-            total = total + item.astype(f32)
-        return total.astype(bf16)
-
-    def settle(items):
-        def rows_for(index):
-            return add_parts(
-                [
-                    lax.dynamic_slice_in_dim(item, index * 2 * shard, 2 * shard, axis=1)
-                    for item in items
-                ]
-            )
-
-        total = add_parts(
-            [rows_for(chip)] + [along_chips(rows_for(chip ^ step), step) for step in steps]
-        )
-        keep = lax.dynamic_slice_in_dim(total, core * shard, shard, axis=1)
-        other = along_core(lax.dynamic_slice_in_dim(total, (1 - core) * shard, shard, axis=1))
-        sides = jnp.where(
-            core == 0,
-            jnp.concatenate([keep, other], axis=2),
-            jnp.concatenate([other, keep], axis=2),
-        )
-        near = [sides] + [along_cols(sides, step) for step in col_steps]
-        stacked = jnp.stack(near)
-        return [
-            lax.dynamic_index_in_dim(stacked, col_at ^ block, axis=0, keepdims=False)
-            for block in range(cols_axis)
-        ]
-
-    def layer_settle(low, mix, mine, give):
-        low_other, mix_other = along_core(low), along_core(mix)
-        partial_sums = layer_grads(low, mix, low_other, mix_other, mine, along_core(give))
-        near = [partial_sums[0]] + [
-            along_cols(partial_sums[step], step) for step in col_steps
-        ]
-        return [item[0].astype(f32) for item in settle([item[None] for item in near])]
-
-    feed_parts = settle([feed_mine, feed_got])
-    grad_feed_in = jnp.stack([item[0].reshape(shard, seqs, part) for item in feed_parts], axis=2)
-    grad_feed_in = grad_feed_in.reshape(shard, feed_in.shape[1]).astype(f32)
-    grad_feed_out = jnp.concatenate([item[1] for item in feed_parts], axis=0).astype(f32)
-    col_grads = layer_settle(normed_two, col_mix, col_mine, col_give)
-    row_grads = layer_settle(normed_one, row_mix, row_mine, row_give)
-
-    small = jnp.concatenate(
-        [sums_one, sums_two, sums_three, entropy_row, jnp.zeros((1, model), f32)], axis=0
-    )
-    small = small + along_core(small)
-    step = 1
-    while step < chips:
-        small = small + along_chips(small, step)
-        step *= 2
-    step = 1
-    while step < cols_axis:
-        small = small + along_cols(small, step)
-        step *= 2
-    entropy = small[6, 0] / (HEADS * count_total)
-    norm_here = lax.dynamic_slice_in_dim(small, seq_at * shard, shard, axis=1)
-
-    result = stream_two
-    for item in out_near:
-        result = result + item.astype(f32)
-    result = result.astype(bf16)
-
-    def to_sequence(values):
-        slots = [values[slot_rows(slot)] for slot in range(chips)]
-        arrived = [slots[0]] + [along_chips(slots[step], step) for step in steps]
-        whole = jnp.stack(arrived)
-        return jnp.concatenate(
-            [
-                lax.dynamic_index_in_dim(whole, chunk_of(index) ^ chip, axis=0, keepdims=False)
-                for index in range(chips)
-            ],
-            axis=0,
-        )[None]
+    def over_cols(whole):
+        return [whole] + [along_cols(whole, step) for step in col_steps]
+
+    def order_rows(slices, at):
+        def order_slots(spot_ref, *refs):
+            for hop, ref in enumerate(refs[:-1]):
+                refs[-1][0, chunk_at(spot_ref, spot_ref[1] ^ hop)] = jnp.concatenate(
+                    [ref[at : at + width], ref[at + width : at + 2 * width]], axis=1
+                )
+
+        return kernel_call(order_slots, [(tokens.shape, bf16)], [spot, *slices], smem=(0,))[0]
+
+    feed_back = along_core(feed_swap)
+    col_parts = [col_sums[0]] + [along_cols(col_sums[step], step) for step in col_steps]
+    col_slices = split_chips(col_parts, 1, 0, stream=stream_two)
+    col_slices = after(col_slices, sums)
+    col_reached = over_chips(col_slices)
+    col_keep, col_swap = split_cores(col_reached, 1, 0)
+
+    def join_two(spot_ref, keep_ref, got_ref, keep2_ref, got2_ref, out_ref):
+        rows = 2 * shard
+        out_ref[:rows] = join_halves(spot_ref, keep_ref[...], got_ref[...])
+        out_ref[rows:] = join_halves(spot_ref, keep2_ref[...], got2_ref[...])
+
+    (pair,) = kernel_call(
+        join_two,
+        [((3 * shard, model), bf16)],
+        [spot, feed_keep, feed_back, col_keep, along_core(col_swap)],
+        smem=(0,),
+    )
+    pair_ends = over_cols(pair)
+    result = order_rows(col_reached, block)
+
+    def spread_pair(spot_ref, u0, u1, u2, u3, in_ref, out_ref, g0, g1, g2, g3, all_ref):
+        for step, ref in enumerate((u0, u1, u2, u3)):
+            all_ref[spot_ref[0] ^ step] = ref[...]
+        for source, grad_ref in enumerate((g0, g1, g2, g3)):
+            wide = all_ref[source, :shard].astype(f32)
+            for index in range(seqs):
+                at = index * block_cols + source * part
+                in_ref[:, at : at + part] = wide[:, index * part : (index + 1) * part]
+            out_ref[source * part : (source + 1) * part] = all_ref[
+                source, shard : 2 * shard
+            ].astype(f32)
+            grad_ref[...] = all_ref[source, 2 * shard :].astype(f32)
+
+    row_parts = layer_grads(
+        normed_one,
+        row_mix,
+        along_core(normed_one),
+        along_core(row_mix),
+        row_mine,
+        along_core(row_give),
+        [sums],
+    )
+    row_parts = [row_parts[0]] + [along_cols(row_parts[step], step) for step in col_steps]
+    row_slices = split_chips(row_parts, 1, extra, slots=grad_slots)
+    row_reached = over_chips(row_slices)
+    row_keep, row_swap = split_cores(row_reached, 1, extra)
+
+    def join_row(spot_ref, keep_ref, got_ref, out_ref, norm_ref, entropy_ref):
+        out_ref[...] = join_halves(spot_ref, keep_ref[:shard], got_ref[:shard])
+        total = keep_ref[shard:].astype(f32) + got_ref[shard:].astype(f32)
+        line = total[6:7]
+        entropy_ref[...] = line[:, 0:1] + line[:, 1:2]
+        wide = jnp.concatenate([total[:lines], total[lines:]], axis=1)
+        at = spot_ref[1] * 2 + spot_ref[2]
+        found = wide[:, :shard]
+        for index in range(1, seqs):
+            here = wide[:, index * shard : (index + 1) * shard]
+            found = jnp.where(at == index, here, found)
+        norm_ref[...] = found
+
+    row_join, norm_here, entropy_sum = kernel_call(
+        join_row,
+        [((shard, model), bf16), ((lines, shard), f32), ((1, 1), f32)],
+        [spot, row_keep, along_core(row_swap)],
+        smem=(0,),
+    )
+    row_ends = over_cols(row_join)
+    grad_in = order_rows(row_reached, block + extra)
+    grad_feed_in, grad_feed_out, *col_grads = kernel_call(
+        spread_pair,
+        [(feed_in.shape, f32), (feed_out.shape, f32)] + [((shard, model), f32)] * cols_axis,
+        [spot, *pair_ends],
+        smem=(0,),
+        scratch=[pltpu.VMEM((cols_axis, 3 * shard, model), bf16)],
+        room=24,
+    )
+
+    def spread_row(spot_ref, *refs):
+        ins, outs, all_ref = refs[:cols_axis], refs[cols_axis:-1], refs[-1]
+        for step, ref in enumerate(ins):
+            all_ref[spot_ref[0] ^ step] = ref[...]
+        for matrix in range(cols_axis):
+            outs[matrix][...] = all_ref[matrix].astype(f32)
+
+    row_grads = kernel_call(
+        spread_row,
+        [((shard, model), f32)] * cols_axis,
+        [spot, *row_ends],
+        smem=(0,),
+        scratch=[pltpu.VMEM((cols_axis, shard, model), bf16)],
+    )
+    entropy = entropy_sum[0, 0] / (HEADS * norm_rows[6, 0])
 
     return (
-        to_sequence(result),
+        result,
         entropy,
-        to_sequence(grad_in),
+        grad_in,
         *[norm_here[index] for index in range(6)],
         *row_grads,
         *col_grads,

time: 426 us -> 294 us (0.69); the launches traced: 420 us -> 293 us
  local copies, waits for them, and re-layouts: 56.4 us -> 3.02 us
  Pallas kernels: 77.4 us -> 53.2 us
  other arithmetic: 24.1 us -> 2.2 us
  starting transfers between devices: 103 us -> 86.7 us
  waiting for transfers between devices: 152 us -> 143 us
    unnamed x168 -> x20, local copies, waits for them, and re-layouts: 30.9 us -> 0.05 us
    ppermute x35 -> x20, waiting for transfers between devices: 72.3 us -> 47.4 us  [along_cols(): lax.ppermute(values, 'col', [(i, i ^ step) for i in range(cols_axis)])]
    pallas_call x16 -> x34, Pallas kernels: 77.4 us -> 53.2 us  [kernel_call(): pl.pallas_call(body, grid=(1,) if stream else (), out_shape=out_shapes, i...]
    ppermute x35 -> x20, starting transfers between devices: 41.6 us -> 28.1 us  [along_cols(): lax.ppermute(values, 'col', [(i, i ^ step) for i in range(cols_axis)])]
    ppermute x26 -> x25, waiting for transfers between devices: 0.36 us -> 11.7 us  [along_core(): return lax.ppermute(values, 'seq', [(i, i ^ 1) for i in range(seqs)])]
    convert_element_type x10 -> x0, other arithmetic: 9.83 us -> none  [the longest x6 5.77 us: add_parts(): return total.astype(bf16)]
    ppermute x29 -> x16, starting transfers between devices: 46.2 us -> 37.2 us  [along_chips(): return lax.ppermute(values, 'seq', [(i, i ^ 2 * step) for i in range(seqs)])]
    ppermute x0 -> x3, starting transfers between devices: none -> 6.65 us  [the longest x1 3.53 us: pair_chips(): return lax.ppermute(values, 'seq', pairs)]
  transfers between devices with their start and end apart: 94 -> 68, of which waited for: 27 -> 31; matrix products, arithmetic and copies ran while one was open for 10% -> 2% of each run, Pallas kernels for 16% -> 10%
where the time goes in v2:
time: 294 us; the launch traced here: 293 us
  waiting for transfers between devices  143 us (49%)
  starting transfers between devices  86.7 us (29%)
  Pallas kernels  53.2 us (18%)
  between operations  4.42 us (2%)
  local copies, waits for them, and re-layouts  3.02 us (1%)
    ppermute x16, waiting for transfers between devices, along_chips(): return lax.ppermute(values, 'seq', [(i, i ^ 2 * step) for i in range(seqs)])  69.5 us
    pallas_call x34, Pallas kernels, kernel_call(): pl.pallas_call(body, grid=(1,) if stream else (), out_shape=out_shapes, i...  53.2 us
    ppermute x20, waiting for transfers between devices, along_cols(): lax.ppermute(values, 'col', [(i, i ^ step) for i in range(cols_axis)])  47.4 us
    ppermute x16, starting transfers between devices, along_chips(): return lax.ppermute(values, 'seq', [(i, i ^ 2 * step) for i in range(seqs)])  37.2 us
    ppermute x20, starting transfers between devices, along_cols(): lax.ppermute(values, 'col', [(i, i ^ step) for i in range(cols_axis)])  28.1 us
    ppermute x25, waiting for transfers between devices, along_core(): return lax.ppermute(values, 'seq', [(i, i ^ 1) for i in range(seqs)])  11.7 us
    ppermute x2, waiting for transfers between devices, to_right(): return lax.ppermute(values, ('col', 'seq'), rightward)  8.97 us
    ppermute x2, starting transfers between devices, to_right(): return lax.ppermute(values, ('col', 'seq'), rightward)  7.32 us
  transfers between devices with their start and end apart: 68, of which 31 were waited for; matrix products, arithmetic and copies ran while one was open for 2% of the time, Pallas kernels for 10%

profile of v2, /device:TPU:0, one launch (start us, length us, event | category | flops | bytes accessed | tf_op | source)
XLA Modules:
  0.0 292.9 jit_solution(33325768258988858)
XLA Ops:
  4.4 3.0 %collective-permute-start = (bf16[136,768]{1,0:T(8,128)(2,1)}, bf16[136,768]{1,0:T(8,128)(2,1)S(1)}, u32[]{:S(2)}, u32[]{:S(2)}) collective-permute-start(bf16[136,768]{1,0:T(8,128)(2,1)} %get-tuple-element.154), channel_id=1, source_target_pairs={{0,2},{1,3},{2,0},{3,1},{4,6},{5,7},{6,4},{7,5},{8,10},{9,11},{10,... | collective-permute-start | bytes 626696 | tf_op jit(solution)/shard_map/ppermute | solution.py:557
  13.6 3.0 %pack_rest.1 = (bf16[2,96,768]{2,1,0:T(8,128)(2,1)}, bf16[384,768]{1,0:T(8,128)(2,1)}, bf16[32,768]{1,0:T(8,128)(2,1)}, bf16[128,768]{1,0:T(8,128)(2,1)}, bf16[1...) custom-call(s32[7]{0:T(128)} %stack.42.spot_ref, bf16[96,768]{1,0:T(8,128)(2,1)} %refs_0_.3, bf16[96,768]{1,0:T(8,128)(2,1)} %refs_1_.3, ...), custom_call_target="tpu_custom_call" | custom-call | flops 1 | bytes 1 | tf_op jit(solution)/shard_map/pack_rest/pallas_call | solution.py:415
  16.7 8.9 %collective-permute-done.1.refs_1_ = bf16[136,768]{1,0:T(8,128)(2,1)S(1)} collective-permute-done((bf16[136,768]{1,0:T(8,128)(2,1)}, bf16[136,768]{1,0:T(8,128)(2,1)S(1)}, u32[]{:S(2)}, u32[]{:S(2)}) %collective-permute-start.1) | collective-permute-done | bytes 208928 | tf_op jit(solution)/shard_map/ppermute | solution.py:557
  29.3 3.6 %collective-permute-start.7 = (bf16[128,768]{1,0:T(8,128)(2,1)S(1)}, bf16[128,768]{1,0:T(8,128)(2,1)S(1)}, u32[]{:S(2)}, u32[]{:S(2)}) collective-permute-start(bf16[128,768]{1,0:T(8,128)(2,1)S(1)} %copy-done.9), channel_id=1, source_target_pairs={{0,2},{1,3},{2,0},{3,1},{4,6},{5,7},{6,4},{7,5},{8,10},{9,11},{10,... | collective-permute-start | bytes 589832 | tf_op jit(solution)/shard_map/ppermute | solution.py:557
  36.9 4.4 %collective-permute-done.7.refs_0_ = bf16[128,768]{1,0:T(8,128)(2,1)S(1)} collective-permute-done((bf16[128,768]{1,0:T(8,128)(2,1)S(1)}, bf16[128,768]{1,0:T(8,128)(2,1)S(1)}, u32[]{:S(2)}, u32[]{:S(2)}) %collective-permute-start.7) | collective-permute-done | bytes 196640 | tf_op jit(solution)/shard_map/ppermute | solution.py:557
  41.3 8.7 %collective-permute-done.8.refs_1_ = bf16[128,768]{1,0:T(8,128)(2,1)S(1)} collective-permute-done((bf16[128,768]{1,0:T(8,128)(2,1)S(1)}, bf16[128,768]{1,0:T(8,128)(2,1)S(1)}, u32[]{:S(2)}, u32[]{:S(2)}) %collective-permute-start.8) | collective-permute-done | bytes 196640 | tf_op jit(solution)/shard_map/ppermute | solution.py:557
  59.1 5.5 %collective-permute-start.12 = (bf16[2,128,768]{2,1,0:T(8,128)(2,1)S(1)}, bf16[2,128,768]{2,1,0:T(8,128)(2,1)S(1)}, u32[]{:S(2)}, u32[]{:S(2)}) collective-permute-start(bf16[2,128,768]{2,1,0:T(8,128)(2,1)S(1)} %get-tuple-element.172.near_ref), channel_id=1, source_target_pairs={{0,2},{1,3},{2,4},{3,5},{4,6},{5,7},{6,14},{7,15},{14,12},{15,13},... | collective-permute-start | bytes 1179656 | tf_op jit(solution)/shard_map/ppermute | solution.py:588
  66.1 7.1 %collective-permute-done.12.left_ref = bf16[2,128,768]{2,1,0:T(8,128)(2,1)S(1)} collective-permute-done((bf16[2,128,768]{2,1,0:T(8,128)(2,1)S(1)}, bf16[2,128,768]{2,1,0:T(8,128)(2,1)S(1)}, u32[]{:S(2)}, u32[]{:S(2)}) %collective-permute-start.12) | collective-permute-done | bytes 393248 | tf_op jit(solution)/shard_map/ppermute | solution.py:588
  73.2 4.1 %collective-permute-done.13.right_ref = bf16[2,128,768]{2,1,0:T(8,128)(2,1)S(1)} collective-permute-done((bf16[2,128,768]{2,1,0:T(8,128)(2,1)S(1)}, bf16[2,128,768]{2,1,0:T(8,128)(2,1)S(1)}, u32[]{:S(2)}, u32[]{:S(2)}) %collective-permute-start.13) | collective-permute-done | bytes 393248 | tf_op jit(solution)/shard_map/ppermute | solution.py:591
  78.8 5.3 %collective-permute-done.17.refs_4_ = bf16[416,768]{1,0:T(8,128)(2,1)S(1)} collective-permute-done((bf16[416,768]{1,0:T(8,128)(2,1)S(1)}, bf16[416,768]{1,0:T(8,128)(2,1)S(1)}, u32[]{:S(2)}, u32[]{:S(2)}) %collective-permute-start.17) | collective-permute-done | bytes 639008 | tf_op jit(solution)/shard_map/ppermute | solution.py:563
  87.1 3.7 %collective-permute-done.18.refs_1_ = bf16[384,768]{1,0:T(8,128)(2,1)S(1)} collective-permute-done((bf16[384,768]{1,0:T(8,128)(2,1)S(1)}, bf16[384,768]{1,0:T(8,128)(2,1)S(1)}, u32[]{:S(2)}, u32[]{:S(2)}) %collective-permute-start.18) | collective-permute-done | bytes 589856 | tf_op jit(solution)/shard_map/ppermute | solution.py:560
  92.7 3.5 %collective-permute-start.28 = (bf16[2,2,96,768]{3,2,1,0:T(8,128)(2,1)S(1)}, bf16[2,2,96,768]{3,2,1,0:T(8,128)(2,1)S(1)}, u32[]{:S(2)}, u32[]{:S(2)}) collective-permute-start(bf16[2,2,96,768]{3,2,1,0:T(8,128)(2,1)S(1)} %pair_feed.1.both_ref), channel_id=1, source_target_pairs={{0,2},{1,5},{2,0},{3,7},{4,6},{5,1},{6,4},{7,3},{8,10},{9,13},{10,... | collective-permute-start | bytes 1769480 | tf_op jit(solution)/shard_map/ppermute | solution.py:575
  96.2 10.2 %collective-permute-start.29 = (bf16[2,96,768]{2,1,0:T(8,128)(2,1)S(1)}, bf16[2,96,768]{2,1,0:T(8,128)(2,1)S(1)}, u32[]{:S(2)}, u32[]{:S(2)}) collective-permute-start(bf16[2,96,768]{2,1,0:T(8,128)(2,1)S(1)} %copy-done.3), channel_id=1, source_target_pairs={{0,6},{1,7},{2,4},{3,5},{4,2},{5,3},{6,0},{7,1},{8,14},{9,15},{10,... | collective-permute-start | bytes 884744 | tf_op jit(solution)/shard_map/ppermute | solution.py:557
  106.5 2.8 attend_col.1
  112.9 13.8 %collective-permute-done.29.last_ref = bf16[2,96,768]{2,1,0:T(8,128)(2,1)S(1)} collective-permute-done((bf16[2,96,768]{2,1,0:T(8,128)(2,1)S(1)}, bf16[2,96,768]{2,1,0:T(8,128)(2,1)S(1)}, u32[]{:S(2)}, u32[]{:S(2)}) %collective-permute-start.29) | collective-permute-done | bytes 294944 | tf_op jit(solution)/shard_map/ppermute | solution.py:557
  129.9 3.7 %feed_main.1 = (bf16[4,128,768]{2,1,0:T(8,128)(2,1)S(1)}, bf16[4,128,768]{2,1,0:T(8,128)(2,1)S(1)}, bf16[128,768]{1,0:T(8,128)(2,1)S(1)}, bf16[128,768]{1,0:T(8,...) custom-call(bf16[128,768]{1,0:T(8,128)(2,1)S(1)} %get-tuple-element.188.a0, ...), custom_call_target="tpu_custom_call" | custom-call | flops 1 | bytes 1 | tf_op jit(solution)/shard_map/feed_main/pallas_call | solution.py:415
  133.6 3.0 %feed_weights.1 = (bf16[1536,384]{1,0:T(8,128)(2,1)S(1)}, bf16[1536,384]{1,0:T(8,128)(2,1)S(1)}, bf16[128,768]{1,0:T(8,128)(2,1)S(1)}, bf16[128,768]{1,0:T(8,128...) custom-call(s32[7]{0:T(128)S(1)} %copy-done.2, bf16[128,768]{1,0:T(8,128)(2,1)S(1)} %get-tuple-element.188.a0, ...), custom_call_target="tpu_custom_call" | custom-call | flops 1811939328 | bytes 16777216 | tf_op jit(solution)/shard_map/feed_weights/pallas_call | solution.py:415
  136.8 4.2 %collective-permute-start.32 = (bf16[128,768]{1,0:T(8,128)(2,1)S(1)}, bf16[128,768]{1,0:T(8,128)(2,1)S(1)}, u32[]{:S(2)}, u32[]{:S(2)}) collective-permute-start(bf16[128,768]{1,0:T(8,128)(2,1)S(1)} %get-tuple-element.195), channel_id=1, source_target_pairs={{0,8},{8,0},{16,24},{24,16},{1,9},{9,1},{17,25},{25,17},{2,10},{10... | collective-permute-start | bytes 589832 | tf_op jit(solution)/shard_map/ppermute | solution.py:563
  143.9 2.8 collective-permute-done.32.b1
  146.7 5.2 %collective-permute-done.33.b2 = bf16[128,768]{1,0:T(8,128)(2,1)S(1)} collective-permute-done((bf16[128,768]{1,0:T(8,128)(2,1)S(1)}, bf16[128,768]{1,0:T(8,128)(2,1)S(1)}, u32[]{:S(2)}, u32[]{:S(2)}) %collective-permute-start.33) | collective-permute-done | bytes 196640 | tf_op jit(solution)/shard_map/ppermute | solution.py:563
  151.9 4.1 %attend_col_back.1 = (f32[128,768]{1,0:T(8,128)S(1)}, bf16[128,768]{1,0:T(8,128)(2,1)S(1)}, bf16[128,768]{1,0:T(8,128)(2,1)S(1)}, f32[2,128,768]{2,1,0:T(8,128)S...) custom-call(s32[7]{0:T(128)S(1)} %copy-done.2, bf16[128,768]{1,0:T(8,128)(2,1)S(1)} %get-tuple-element.206.b0, ...), custom_call_target="tpu_custom_call" | custom-call | flops 1 | bytes 1 | tf_op jit(solution)/shard_map/attend_col_back/pallas_call | solution.py:415
  157.8 3.6 %row_entry_back.1 = (bf16[4,128,384]{2,1,0:T(8,128)(2,1)S(1)}, bf16[4,128,384]{2,1,0:T(8,128)(2,1)S(1)}, f32[128,768]{1,0:T(8,128)S(1)}, bf16[128,768]{1,0:T(8,1...) custom-call(s32[7]{0:T(128)S(1)} %copy-done.2, ...), custom_call_target="tpu_custom_call" | custom-call | flops 1 | bytes 1 | tf_op jit(solution)/shard_map/row_entry_back/pallas_call | solution.py:415
  162.1 3.8 %collective-permute-start.44 = (bf16[384,384]{1,0:T(8,128)(2,1)S(1)}, bf16[384,384]{1,0:T(8,128)(2,1)S(1)}, u32[]{:S(2)}, u32[]{:S(2)}) collective-permute-start(bf16[384,384]{1,0:T(8,128)(2,1)S(1)} %get-tuple-element.203), channel_id=1, source_target_pairs={{0,2},{1,3},{2,0},{3,1},{4,6},{5,7},{6,4},{7,5},{8,10},{9,11},{10,... | collective-permute-start | bytes 884744 | tf_op jit(solution)/shard_map/ppermute | solution.py:557
  180.0 9.4 %collective-permute-done.45.refs_2_ = bf16[384,384]{1,0:T(8,128)(2,1)S(1)} collective-permute-done((bf16[384,384]{1,0:T(8,128)(2,1)S(1)}, bf16[384,384]{1,0:T(8,128)(2,1)S(1)}, u32[]{:S(2)}, u32[]{:S(2)}) %collective-permute-start.45) | collective-permute-done | bytes 294944 | tf_op jit(solution)/shard_map/ppermute | solution.py:557
  204.0 4.9 %collective-permute-start.55 = (bf16[784,384]{1,0:T(8,128)(2,1)S(1)}, bf16[784,384]{1,0:T(8,128)(2,1)S(1)}, u32[]{:S(2)}, u32[]{:S(2)}) collective-permute-start(bf16[784,384]{1,0:T(8,128)(2,1)S(1)} %get-tuple-element.260), channel_id=1, source_target_pairs={{0,24},{8,16},{16,8},{24,0},{1,25},{9,17},{17,9},{25,1},{2,26},{10... | collective-permute-start | bytes 1806344 | tf_op jit(solution)/shard_map/ppermute | solution.py:563
  208.8 18.0 %collective-permute-done.39.refs_2_ = bf16[1024,384]{1,0:T(8,128)(2,1)S(1)} collective-permute-done((bf16[1024,384]{1,0:T(8,128)(2,1)S(1)}, bf16[1024,384]{1,0:T(8,128)(2,1)S(1)}, u32[]{:S(2)}, u32[]{:S(2)}) %collective-permute-start.39) | collective-permute-done | bytes 786464 | tf_op jit(solution)/shard_map/ppermute | solution.py:563
  230.6 4.9 %collective-permute-done.47.refs_1_ = bf16[256,384]{1,0:T(8,128)(2,1)S(1)} collective-permute-done((bf16[256,384]{1,0:T(8,128)(2,1)S(1)}, bf16[256,384]{1,0:T(8,128)(2,1)S(1)}, u32[]{:S(2)}, u32[]{:S(2)}) %collective-permute-start.47) | collective-permute-done | bytes 196640 | tf_op jit(solution)/shard_map/ppermute | solution.py:557
  236.8 4.0 %collective-permute-done.48.refs_2_ = bf16[256,384]{1,0:T(8,128)(2,1)S(1)} collective-permute-done((bf16[256,384]{1,0:T(8,128)(2,1)S(1)}, bf16[256,384]{1,0:T(8,128)(2,1)S(1)}, u32[]{:S(2)}, u32[]{:S(2)}) %collective-permute-start.48) | collective-permute-done | bytes 196640 | tf_op jit(solution)/shard_map/ppermute | solution.py:557
  243.8 6.8 %collective-permute-done.54.refs_2_ = bf16[784,384]{1,0:T(8,128)(2,1)S(1)} collective-permute-done((bf16[784,384]{1,0:T(8,128)(2,1)S(1)}, bf16[784,384]{1,0:T(8,128)(2,1)S(1)}, u32[]{:S(2)}, u32[]{:S(2)}) %collective-permute-start.54) | collective-permute-done | bytes 602144 | tf_op jit(solution)/shard_map/ppermute | solution.py:563
  260.8 11.0 %collective-permute-done.57.refs_2_ = bf16[272,384]{1,0:T(8,128)(2,1)S(1)} collective-permute-done((bf16[272,384]{1,0:T(8,128)(2,1)S(1)}, bf16[272,384]{1,0:T(8,128)(2,1)S(1)}, u32[]{:S(2)}, u32[]{:S(2)}) %collective-permute-start.57) | collective-permute-done | bytes 208928 | tf_op jit(solution)/shard_map/ppermute | solution.py:557
  275.1 2.8 spread_pair.1
  287.3 2.8 collective-permute-done.61.refs_2_
  (172 shorter events, 105.5 us)
Async XLA Ops:
  7.5 18.2 %collective-permute-start.1 = (bf16[136,768]{1,0:T(8,128)(2,1)}, bf16[136,768]{1,0:T(8,128)(2,1)S(1)}, u32[]{:S(2)}, u32[]{:S(2)}) collective-permute-start(bf16[136,768]{1,0:T(8,128)(2,1)} %get-tuple-element.155), channel_id=1, source_target_pairs={{0,4},{1,5},{2,6},{3,7},{4,0},{5,1},{6,2},{7,3},{8,12},{9,13},{10,... | collective-permute-start | bytes 626696 | tf_op jit(solution)/shard_map/ppermute | solution.py:557
  10.1 15.6 %collective-permute-start.2 = (bf16[136,768]{1,0:T(8,128)(2,1)}, bf16[136,768]{1,0:T(8,128)(2,1)S(1)}, u32[]{:S(2)}, u32[]{:S(2)}) collective-permute-start(bf16[136,768]{1,0:T(8,128)(2,1)} %get-tuple-element.156), channel_id=1, source_target_pairs={{0,6},{1,7},{2,4},{3,5},{4,2},{5,3},{6,0},{7,1},{8,14},{9,15},{10,... | collective-permute-start | bytes 626696 | tf_op jit(solution)/shard_map/ppermute | solution.py:557
  27.7 25.1 %collective-permute-start.5 = (bf16[624,768]{1,0:T(8,128)(2,1)S(1)}, bf16[624,768]{1,0:T(8,128)(2,1)S(1)}, u32[]{:S(2)}, u32[]{:S(2)}) collective-permute-start(bf16[624,768]{1,0:T(8,128)(2,1)S(1)} %join_cores.2.refs_2_), channel_id=1, source_target_pairs={{0,8},{1,17},{2,10},{3,19},{4,12},{5,21},{6,14},{7,23},{8,0},{9,25... | collective-permute-start | bytes 2875400 | tf_op jit(solution)/shard_map/ppermute | solution.py:571
  32.9 17.1 %collective-permute-start.8 = (bf16[128,768]{1,0:T(8,128)(2,1)S(1)}, bf16[128,768]{1,0:T(8,128)(2,1)S(1)}, u32[]{:S(2)}, u32[]{:S(2)}) collective-permute-start(bf16[128,768]{1,0:T(8,128)(2,1)S(1)} %copy-done.8), channel_id=1, source_target_pairs={{0,4},{1,5},{2,6},{3,7},{4,0},{5,1},{6,2},{7,3},{8,12},{9,13},{10,... | collective-permute-start | bytes 589832 | tf_op jit(solution)/shard_map/ppermute | solution.py:557
  33.9 16.1 %collective-permute-start.9 = (bf16[128,768]{1,0:T(8,128)(2,1)S(1)}, bf16[128,768]{1,0:T(8,128)(2,1)S(1)}, u32[]{:S(2)}, u32[]{:S(2)}) collective-permute-start(bf16[128,768]{1,0:T(8,128)(2,1)S(1)} %copy-done.7), channel_id=1, source_target_pairs={{0,6},{1,7},{2,4},{3,5},{4,2},{5,3},{6,0},{7,1},{8,14},{9,15},{10,... | collective-permute-start | bytes 589832 | tf_op jit(solution)/shard_map/ppermute | solution.py:557
  35.4 17.4 %collective-permute-start.6 = (bf16[312,768]{1,0:T(8,128)(2,1)S(1)}, bf16[312,768]{1,0:T(8,128)(2,1)S(1)}, u32[]{:S(2)}, u32[]{:S(2)}) collective-permute-start(bf16[312,768]{1,0:T(8,128)(2,1)S(1)} %get-tuple-element.165.near_ref), channel_id=1, source_target_pairs={{0,24},{8,16},{16,8},{24,0},{1,25},{9,17},{17,9},{25,1},{2,26},{10... | collective-permute-start | bytes 1437704 | tf_op jit(solution)/shard_map/ppermute | solution.py:563
  52.9 31.1 %collective-permute-start.16 = (bf16[832,768]{1,0:T(8,128)(2,1)S(1)}, bf16[832,768]{1,0:T(8,128)(2,1)S(1)}, u32[]{:S(2)}, u32[]{:S(2)}) collective-permute-start(bf16[832,768]{1,0:T(8,128)(2,1)S(1)} %join_cores.3.refs_2_), channel_id=1, source_target_pairs={{0,8},{1,17},{2,10},{3,19},{4,12},{5,21},{6,14},{7,23},{8,0},{9,25... | collective-permute-start | bytes 3833864 | tf_op jit(solution)/shard_map/ppermute | solution.py:571
  55.0 29.0 %collective-permute-start.17 = (bf16[416,768]{1,0:T(8,128)(2,1)S(1)}, bf16[416,768]{1,0:T(8,128)(2,1)S(1)}, u32[]{:S(2)}, u32[]{:S(2)}) collective-permute-start(bf16[416,768]{1,0:T(8,128)(2,1)S(1)} %stack_got.1.near_ref), channel_id=1, source_target_pairs={{0,24},{8,16},{16,8},{24,0},{1,25},{9,17},{17,9},{25,1},{2,26},{10... | collective-permute-start | bytes 1916936 | tf_op jit(solution)/shard_map/ppermute | solution.py:563
  59.1 14.2 %collective-permute-start.12 = (bf16[2,128,768]{2,1,0:T(8,128)(2,1)S(1)}, bf16[2,128,768]{2,1,0:T(8,128)(2,1)S(1)}, u32[]{:S(2)}, u32[]{:S(2)}) collective-permute-start(bf16[2,128,768]{2,1,0:T(8,128)(2,1)S(1)} %get-tuple-element.172.near_ref), channel_id=1, source_target_pairs={{0,2},{1,3},{2,4},{3,5},{4,6},{5,7},{6,14},{7,15},{14,12},{15,13},... | collective-permute-start | bytes 1179656 | tf_op jit(solution)/shard_map/ppermute | solution.py:588
  64.6 12.8 %collective-permute-start.13 = (bf16[2,128,768]{2,1,0:T(8,128)(2,1)S(1)}, bf16[2,128,768]{2,1,0:T(8,128)(2,1)S(1)}, u32[]{:S(2)}, u32[]{:S(2)}) collective-permute-start(bf16[2,128,768]{2,1,0:T(8,128)(2,1)S(1)} %get-tuple-element.172.near_ref), channel_id=1, source_target_pairs={{2,0},{3,1},{4,2},{5,3},{6,4},{7,5},{14,6},{15,7},{12,14},{13,15},... | collective-permute-start | bytes 1179656 | tf_op jit(solution)/shard_map/ppermute | solution.py:591
  92.4 14.0 %collective-permute-start.21 = (bf16[2,128,768]{2,1,0:T(8,128)(2,1)S(1)}, bf16[2,128,768]{2,1,0:T(8,128)(2,1)S(1)}, u32[]{:S(2)}, u32[]{:S(2)}) collective-permute-start(bf16[2,128,768]{2,1,0:T(8,128)(2,1)S(1)} %get-tuple-element.184.near_ref), channel_id=1, source_target_pairs={{0,1},{1,0},{2,3},{3,2},{4,5},{5,4},{6,7},{7,6},{8,9},{9,8},{10,11... | collective-permute-start | bytes 1179656 | tf_op jit(solution)/shard_map/ppermute | solution.py:560
  92.7 34.0 %collective-permute-start.28 = (bf16[2,2,96,768]{3,2,1,0:T(8,128)(2,1)S(1)}, bf16[2,2,96,768]{3,2,1,0:T(8,128)(2,1)S(1)}, u32[]{:S(2)}, u32[]{:S(2)}) collective-permute-start(bf16[2,2,96,768]{3,2,1,0:T(8,128)(2,1)S(1)} %pair_feed.1.both_ref), channel_id=1, source_target_pairs={{0,2},{1,5},{2,0},{3,7},{4,6},{5,1},{6,4},{7,3},{8,10},{9,13},{10,... | collective-permute-start | bytes 1769480 | tf_op jit(solution)/shard_map/ppermute | solution.py:575
  96.2 30.4 %collective-permute-start.29 = (bf16[2,96,768]{2,1,0:T(8,128)(2,1)S(1)}, bf16[2,96,768]{2,1,0:T(8,128)(2,1)S(1)}, u32[]{:S(2)}, u32[]{:S(2)}) collective-permute-start(bf16[2,96,768]{2,1,0:T(8,128)(2,1)S(1)} %copy-done.3), channel_id=1, source_target_pairs={{0,6},{1,7},{2,4},{3,5},{4,2},{5,3},{6,0},{7,1},{8,14},{9,15},{10,... | collective-permute-start | bytes 884744 | tf_op jit(solution)/shard_map/ppermute | solution.py:557
  109.3 17.4 %collective-permute-start.24 = (bf16[128,768]{1,0:T(8,128)(2,1)S(1)}, bf16[128,768]{1,0:T(8,128)(2,1)S(1)}, u32[]{:S(2)}, u32[]{:S(2)}) collective-permute-start(bf16[128,768]{1,0:T(8,128)(2,1)S(1)} %get-tuple-element.188.a0), channel_id=1, source_target_pairs={{0,8},{8,0},{16,24},{24,16},{1,9},{9,1},{17,25},{25,17},{2,10},{10... | collective-permute-start | bytes 589832 | tf_op jit(solution)/shard_map/ppermute | solution.py:563
  110.9 15.8 %collective-permute-start.25 = (bf16[128,768]{1,0:T(8,128)(2,1)S(1)}, bf16[128,768]{1,0:T(8,128)(2,1)S(1)}, u32[]{:S(2)}, u32[]{:S(2)}) collective-permute-start(bf16[128,768]{1,0:T(8,128)(2,1)S(1)} %get-tuple-element.188.a0), channel_id=1, source_target_pairs={{0,16},{8,24},{16,0},{24,8},{1,17},{9,25},{17,1},{25,9},{2,18},{10... | collective-permute-start | bytes 589832 | tf_op jit(solution)/shard_map/ppermute | solution.py:563
  111.4 15.3 %collective-permute-start.26 = (bf16[128,768]{1,0:T(8,128)(2,1)S(1)}, bf16[128,768]{1,0:T(8,128)(2,1)S(1)}, u32[]{:S(2)}, u32[]{:S(2)}) collective-permute-start(bf16[128,768]{1,0:T(8,128)(2,1)S(1)} %get-tuple-element.188.a0), channel_id=1, source_target_pairs={{0,24},{8,16},{16,8},{24,0},{1,25},{9,17},{17,9},{25,1},{2,26},{10... | collective-permute-start | bytes 589832 | tf_op jit(solution)/shard_map/ppermute | solution.py:563
  162.1 16.4 %collective-permute-start.44 = (bf16[384,384]{1,0:T(8,128)(2,1)S(1)}, bf16[384,384]{1,0:T(8,128)(2,1)S(1)}, u32[]{:S(2)}, u32[]{:S(2)}) collective-permute-start(bf16[384,384]{1,0:T(8,128)(2,1)S(1)} %get-tuple-element.203), channel_id=1, source_target_pairs={{0,2},{1,3},{2,0},{3,1},{4,6},{5,7},{6,4},{7,5},{8,10},{9,11},{10,... | collective-permute-start | bytes 884744 | tf_op jit(solution)/shard_map/ppermute | solution.py:557
  165.9 23.5 %collective-permute-start.45 = (bf16[384,384]{1,0:T(8,128)(2,1)S(1)}, bf16[384,384]{1,0:T(8,128)(2,1)S(1)}, u32[]{:S(2)}, u32[]{:S(2)}) collective-permute-start(bf16[384,384]{1,0:T(8,128)(2,1)S(1)} %get-tuple-element.204), channel_id=1, source_target_pairs={{0,4},{1,5},{2,6},{3,7},{4,0},{5,1},{6,2},{7,3},{8,12},{9,13},{10,... | collective-permute-start | bytes 884744 | tf_op jit(solution)/shard_map/ppermute | solution.py:557
  167.5 22.1 %collective-permute-start.46 = (bf16[384,384]{1,0:T(8,128)(2,1)S(1)}, bf16[384,384]{1,0:T(8,128)(2,1)S(1)}, u32[]{:S(2)}, u32[]{:S(2)}) collective-permute-start(bf16[384,384]{1,0:T(8,128)(2,1)S(1)} %get-tuple-element.205), channel_id=1, source_target_pairs={{0,6},{1,7},{2,4},{3,5},{4,2},{5,3},{6,0},{7,1},{8,14},{9,15},{10,... | collective-permute-start | bytes 884744 | tf_op jit(solution)/shard_map/ppermute | solution.py:557
  173.5 20.3 %collective-permute-start.43 = (bf16[2,128,768]{2,1,0:T(8,128)(2,1)S(1)}, bf16[2,128,768]{2,1,0:T(8,128)(2,1)S(1)}, u32[]{:S(2)}, u32[]{:S(2)}) collective-permute-start(bf16[2,128,768]{2,1,0:T(8,128)(2,1)S(1)} %get-tuple-element.239), channel_id=1, source_target_pairs={{0,2},{1,3},{2,4},{3,5},{4,6},{5,7},{6,14},{7,15},{14,12},{15,13},... | collective-permute-start | bytes 1179656 | tf_op jit(solution)/shard_map/ppermute | solution.py:588
  175.3 20.1 %collective-permute-start.42 = (bf16[2,128,768]{2,1,0:T(8,128)(2,1)S(1)}, bf16[2,128,768]{2,1,0:T(8,128)(2,1)S(1)}, u32[]{:S(2)}, u32[]{:S(2)}) collective-permute-start(bf16[2,128,768]{2,1,0:T(8,128)(2,1)S(1)} %get-tuple-element.238), channel_id=1, source_target_pairs={{2,0},{3,1},{4,2},{5,3},{6,4},{7,5},{14,6},{15,7},{12,14},{13,15},... | collective-permute-start | bytes 1179656 | tf_op jit(solution)/shard_map/ppermute | solution.py:591
  178.4 25.6 %collective-permute-start.38 = (bf16[1024,384]{1,0:T(8,128)(2,1)S(1)}, bf16[1024,384]{1,0:T(8,128)(2,1)S(1)}, u32[]{:S(2)}, u32[]{:S(2)}) collective-permute-start(bf16[1024,384]{1,0:T(8,128)(2,1)S(1)} %get-tuple-element.224), channel_id=1, source_target_pairs={{0,8},{8,0},{16,24},{24,16},{1,9},{9,1},{17,25},{25,17},{2,10},{10... | collective-permute-start | bytes 2359304 | tf_op jit(solution)/shard_map/ppermute | solution.py:563
  189.4 37.5 %collective-permute-start.39 = (bf16[1024,384]{1,0:T(8,128)(2,1)S(1)}, bf16[1024,384]{1,0:T(8,128)(2,1)S(1)}, u32[]{:S(2)}, u32[]{:S(2)}) collective-permute-start(bf16[1024,384]{1,0:T(8,128)(2,1)S(1)} %get-tuple-element.225), channel_id=1, source_target_pairs={{0,16},{8,24},{16,0},{24,8},{1,17},{9,25},{17,1},{25,9},{2,18},{10... | collective-permute-start | bytes 2359304 | tf_op jit(solution)/shard_map/ppermute | solution.py:563
  189.6 37.2 %collective-permute-start.40 = (bf16[1024,384]{1,0:T(8,128)(2,1)S(1)}, bf16[1024,384]{1,0:T(8,128)(2,1)S(1)}, u32[]{:S(2)}, u32[]{:S(2)}) collective-permute-start(bf16[1024,384]{1,0:T(8,128)(2,1)S(1)} %get-tuple-element.226), channel_id=1, source_target_pairs={{0,24},{8,16},{16,8},{24,0},{1,25},{9,17},{17,9},{25,1},{2,26},{10... | collective-permute-start | bytes 2359304 | tf_op jit(solution)/shard_map/ppermute | solution.py:563
  201.2 42.6 %collective-permute-start.53 = (bf16[784,384]{1,0:T(8,128)(2,1)S(1)}, bf16[784,384]{1,0:T(8,128)(2,1)S(1)}, u32[]{:S(2)}, u32[]{:S(2)}) collective-permute-start(bf16[784,384]{1,0:T(8,128)(2,1)S(1)} %get-tuple-element.258), channel_id=1, source_target_pairs={{0,8},{8,0},{16,24},{24,16},{1,9},{9,1},{17,25},{25,17},{2,10},{10... | collective-permute-start | bytes 1806344 | tf_op jit(solution)/shard_map/ppermute | solution.py:563
  201.3 49.4 %collective-permute-start.54 = (bf16[784,384]{1,0:T(8,128)(2,1)S(1)}, bf16[784,384]{1,0:T(8,128)(2,1)S(1)}, u32[]{:S(2)}, u32[]{:S(2)}) collective-permute-start(bf16[784,384]{1,0:T(8,128)(2,1)S(1)} %get-tuple-element.259), channel_id=1, source_target_pairs={{0,16},{8,24},{16,0},{24,8},{1,17},{9,25},{17,1},{25,9},{2,18},{10... | collective-permute-start | bytes 1806344 | tf_op jit(solution)/shard_map/ppermute | solution.py:563
  204.0 46.7 %collective-permute-start.55 = (bf16[784,384]{1,0:T(8,128)(2,1)S(1)}, bf16[784,384]{1,0:T(8,128)(2,1)S(1)}, u32[]{:S(2)}, u32[]{:S(2)}) collective-permute-start(bf16[784,384]{1,0:T(8,128)(2,1)S(1)} %get-tuple-element.260), channel_id=1, source_target_pairs={{0,24},{8,16},{16,8},{24,0},{1,25},{9,17},{17,9},{25,1},{2,26},{10... | collective-permute-start | bytes 1806344 | tf_op jit(solution)/shard_map/ppermute | solution.py:563
  252.6 22.5 %collective-permute-start.65 = (bf16[288,768]{1,0:T(8,128)(2,1)S(1)}, bf16[288,768]{1,0:T(8,128)(2,1)S(1)}, u32[]{:S(2)}, u32[]{:S(2)}) collective-permute-start(bf16[288,768]{1,0:T(8,128)(2,1)S(1)} %join_two.1.u0), channel_id=1, source_target_pairs={{0,8},{8,0},{16,24},{24,16},{1,9},{9,1},{17,25},{25,17},{2,10},{10... | collective-permute-start | bytes 1327112 | tf_op jit(solution)/shard_map/ppermute | solution.py:563
  253.2 21.8 %collective-permute-start.66 = (bf16[288,768]{1,0:T(8,128)(2,1)S(1)}, bf16[288,768]{1,0:T(8,128)(2,1)S(1)}, u32[]{:S(2)}, u32[]{:S(2)}) collective-permute-start(bf16[288,768]{1,0:T(8,128)(2,1)S(1)} %join_two.1.u0), channel_id=1, source_target_pairs={{0,16},{8,24},{16,0},{24,8},{1,17},{9,25},{17,1},{25,9},{2,18},{10... | collective-permute-start | bytes 1327112 | tf_op jit(solution)/shard_map/ppermute | solution.py:563
  254.4 20.7 %collective-permute-start.67 = (bf16[288,768]{1,0:T(8,128)(2,1)S(1)}, bf16[288,768]{1,0:T(8,128)(2,1)S(1)}, u32[]{:S(2)}, u32[]{:S(2)}) collective-permute-start(bf16[288,768]{1,0:T(8,128)(2,1)S(1)} %join_two.1.u0), channel_id=1, source_target_pairs={{0,24},{8,16},{16,8},{24,0},{1,25},{9,17},{17,9},{25,1},{2,26},{10... | collective-permute-start | bytes 1327112 | tf_op jit(solution)/shard_map/ppermute | solution.py:563
  256.1 15.7 %collective-permute-start.57 = (bf16[272,384]{1,0:T(8,128)(2,1)S(1)}, bf16[272,384]{1,0:T(8,128)(2,1)S(1)}, u32[]{:S(2)}, u32[]{:S(2)}) collective-permute-start(bf16[272,384]{1,0:T(8,128)(2,1)S(1)} %get-tuple-element.267), channel_id=1, source_target_pairs={{0,4},{1,5},{2,6},{3,7},{4,0},{5,1},{6,2},{7,3},{8,12},{9,13},{10,... | collective-permute-start | bytes 626696 | tf_op jit(solution)/shard_map/ppermute | solution.py:557
  259.0 12.8 %collective-permute-start.58 = (bf16[272,384]{1,0:T(8,128)(2,1)S(1)}, bf16[272,384]{1,0:T(8,128)(2,1)S(1)}, u32[]{:S(2)}, u32[]{:S(2)}) collective-permute-start(bf16[272,384]{1,0:T(8,128)(2,1)S(1)} %get-tuple-element.268), channel_id=1, source_target_pairs={{0,6},{1,7},{2,4},{3,5},{4,2},{5,3},{6,0},{7,1},{8,14},{9,15},{10,... | collective-permute-start | bytes 626696 | tf_op jit(solution)/shard_map/ppermute | solution.py:557
  (46 other events, 316.5 us)

commit v3 on v2

--- a/solution.py
+++ b/solution.py
@@ -495,9 +495,7 @@
 
 
 def per_head_sum(product, lane_heads):
-    high = product.astype(jnp.bfloat16)
-    rest = (product - high.astype(jnp.float32)).astype(jnp.bfloat16)
-    return dot(high, lane_heads) + dot(rest, lane_heads)
+    return dot(product.astype(jnp.bfloat16), lane_heads)
 
 
 def slot_span(spot_ref, side, slot, width):
@@ -631,7 +629,7 @@
         at = jnp.where(spot_ref[0] % 2 == 0, chip_index, chips - 1 - chip_index)
         return pl.ds(pl.multiple_of(at * width, width), width)
 
-    def pack(spot_ref, weights, token_ref, own_ref, chunk_ref, send_refs, block):
+    def pack(spot_ref, weights, own_ref, send_refs, block):
         at = pl.multiple_of(spot_ref[0] * quarter, quarter)
         size = len(weights) * quarter
         for index, ref in enumerate(weights):
@@ -644,27 +642,29 @@
             ]:
                 ref[row : row + lines] = jnp.zeros((lines, model), bf16)
                 ref[row : row + lines, :128] = block
-            size = size + lines
-        chunk_ref[...] = token_ref[0, chunk_at(spot_ref, spot_ref[1])]
-        for hop, ref in enumerate(send_refs):
-            ref[size:] = token_ref[0, chunk_at(spot_ref, spot_ref[1] ^ (hop + 1))]
 
     def pack_row(spot_ref, *refs):
-        norm_refs, token_ref, own_ref, chunk_ref = refs[4:10], refs[10], refs[11], refs[12]
+        norm_refs, own_ref, send_ref = refs[4:10], refs[10], refs[11]
         block = jnp.zeros((lines, 128), f32)
         rows = lax.broadcasted_iota(jnp.int32, (lines, 128), 0)
         for index, ref in enumerate(norm_refs):
             line = jnp.pad(ref[...].astype(f32), ((0, 0), (0, 128 - shard)))
             block = jnp.where(rows == index, line, block)
         block = jnp.where(rows == 6, spot_ref[4].astype(f32), block).astype(bf16)
-        pack(spot_ref, refs[:4], token_ref, own_ref, chunk_ref, refs[13:], block)
+        pack(spot_ref, refs[:4], own_ref, [send_ref], block)
 
     part = feed_out.shape[0] // cols_axis
     block_cols = feed_out.shape[0]
 
     def pack_rest(spot_ref, *refs):
-        in_ref, out_ref, own_ref = refs[5], refs[6], refs[7]
-        pack(spot_ref, refs[:4], refs[4], refs[8], refs[9], refs[10:], None)
+        token_refs, in_ref, out_ref = refs[4:6], refs[6], refs[7]
+        own_ref, chunk_ref, send_refs = refs[8], refs[10], refs[11:]
+        pack(spot_ref, refs[:4], refs[9], send_refs, None)
+        for index, ref in enumerate(token_refs):
+            chunk_ref[index * width : (index + 1) * width] = ref[0, chunk_at(spot_ref, spot_ref[1])]
+            for hop, send_ref in enumerate(send_refs):
+                at = col_rows + index * width
+                send_ref[at : at + width] = ref[0, chunk_at(spot_ref, spot_ref[1] ^ (hop + 1))]
         first = lax.broadcasted_iota(jnp.int32, (block_cols, 128), 0)
         lanes = lax.broadcasted_iota(jnp.int32, (block_cols, 128), 1)
         chosen = ((first == lanes + spot_ref[0] * part) & (lanes < part)).astype(bf16)
@@ -675,13 +675,17 @@
             ].astype(bf16)
         own_ref[1] = out_ref[pl.ds(pl.multiple_of(spot_ref[0] * part, part), part)]
 
-    def split_got(own_ref, *refs):
-        rows = refs[0].shape[0] - width
-        ins, (hops_ref, stream_ref) = refs[:-2], refs[-2:]
-        stream_ref[:width] = own_ref[...]
-        for hop, ref in enumerate(ins):
-            hops_ref[hop * rows : (hop + 1) * rows] = ref[:rows]
-            stream_ref[(hop + 1) * width : (hop + 2) * width] = ref[rows:]
+    def stack_row(*refs):
+        for hop, ref in enumerate(refs[:-1]):
+            refs[-1][hop * row_rows : (hop + 1) * row_rows] = ref[...]
+
+    def stack_col(own_ref, *refs):
+        ins, (out_ref, given_ref) = refs[:-2], refs[-2:]
+        for slot, ref in enumerate((own_ref, *ins)):
+            at = 0 if slot == 0 else col_rows
+            given_ref[slot * width : (slot + 1) * width] = ref[at + width : at + 2 * width]
+            if slot:
+                out_ref[(slot - 1) * col_rows : slot * col_rows] = ref[:col_rows]
 
     def spread_plane(near, far):
         def join_cores(near_ref, far_ref, out_ref):
@@ -720,58 +724,47 @@
                         start = side * unit + (hop - 1) * rows + index * quarter
                         out_ref[lead + (at,)] = ref[start : start + quarter]
 
-    row_own, stream_own, *row_sends = kernel_call(
+    row_own, row_send = kernel_call(
         pack_row,
-        [((cols_axis * shard + lines, model), bf16), ((width, model), bf16)]
-        + [((row_rows + width, model), bf16)] * hops,
-        [spot, *row_weights, *[item[None] for item in norms], tokens],
+        [((cols_axis * shard + lines, model), bf16), ((row_rows, model), bf16)],
+        [spot, *row_weights, *[item[None] for item in norms]],
         smem=(0,),
         stream=True,
     )
-    row_got = [along_chips(row_sends[step - 1], step) for step in steps]
-    feed_own, col_own, given_own, *col_sends = kernel_call(
+    row_got = [along_chips(row_send, step) for step in steps]
+    feed_own, col_own, chunks_own, *col_sends = kernel_call(
         pack_rest,
         [
             ((2, shard, hidden), bf16),
             ((cols_axis * shard, model), bf16),
-            ((width, model), bf16),
+            ((2 * width, model), bf16),
         ]
-        + [((col_rows + width, model), bf16)] * hops,
-        [spot, *col_weights, cotangent, feed_in, feed_out],
+        + [((col_rows + 2 * width, model), bf16)] * hops,
+        [spot, *col_weights, tokens, cotangent, feed_in, feed_out],
         smem=(0,),
         stream=True,
     )
     row_got = after(row_got, waves, allowed, col_sends)
-    row_hops, stream_in = kernel_call(
-        split_got,
-        [((hops * row_rows, model), bf16), ((toks, model), bf16)],
-        [stream_own, *row_got],
-    )
+    feed_other = along_core(feed_own)
+    row_hops = kernel_call(stack_row, [((hops * row_rows, model), bf16)], row_got)[0]
     row_far_own = along_core(row_own)
     row_plane, row_pair, row_diagonal = spread_plane(row_hops, along_core(row_hops))
     col_sends = after(col_sends, row_plane)
     col_got = [along_chips(col_sends[step - 1], step) for step in steps]
-    row_last = after((row_pair, row_diagonal), row_pair, row_diagonal, col_got)
+
+    def pair_feed(own_ref, other_ref, out_ref):
+        out_ref[0] = own_ref[...]
+        out_ref[1] = other_ref[...]
+
+    feed_both = kernel_call(
+        pair_feed, [((2, 2, shard, hidden), bf16)], [feed_own, after(feed_other, row_plane)]
+    )[0]
+    row_last = after((row_pair, row_diagonal), row_pair, row_diagonal, col_got, feed_both)
     row_pieces = [row_own, row_far_own, row_plane, row_pair, row_diagonal] + [
         along_core(item) for item in row_last
     ]
-
-    def stack_got(own_ref, *refs):
-        rows = refs[0].shape[0] - width
-        ins, out_ref = refs[:-1], refs[-1]
-        at = hops * rows
-        out_ref[at : at + width] = own_ref[...]
-        for hop, ref in enumerate(ins):
-            out_ref[hop * rows : (hop + 1) * rows] = ref[:rows]
-            out_ref[at + (hop + 1) * width : at + (hop + 2) * width] = ref[rows:]
-
-    col_unit = hops * col_rows + toks
-    col_hops = kernel_call(stack_got, [((col_unit, model), bf16)], [given_own, *col_got])[0]
-    col_far_own = along_core(col_own)
-    col_plane, col_pair, col_diagonal = spread_plane(col_hops, along_core(col_hops))
-
-    def project_row(spot_ref, stream_ref, waves_ref, *refs):
-        pieces, outs = refs[:7], refs[7:]
+    def project_row(spot_ref, waves_ref, *refs):
+        token_refs, pieces, outs = refs[:chips], refs[chips : chips + 7], refs[chips + 7 :]
         zero_ref, low_ref, q_ref, kv_ref, weight_ref, last_ref, norm_ref = outs
         place_rows(
             spot_ref,
@@ -800,10 +793,10 @@
         norm_ref[...] = jnp.where(rows == 6, count, total)
         for slot in range(chips):
             rows = slice(slot * width, (slot + 1) * width)
-            zero_ref[rows, :half] = stream_ref[rows, :half].astype(f32) + waves_ref[:width]
-            zero_ref[rows, half:] = (
-                stream_ref[rows, half:].astype(f32) + waves_ref[width + slot : width + slot + 1]
-            )
+            at = 0 if slot == 0 else col_rows
+            stream = token_refs[slot][at : at + width].astype(f32)
+            zero_ref[rows, :half] = stream[:, :half] + waves_ref[:width]
+            zero_ref[rows, half:] = stream[:, half:] + waves_ref[width + slot : width + slot + 1]
         unit, _ = unit_norm(zero_ref[...])
         low = (unit * norm_ref[0:1] + norm_ref[1:2]).astype(bf16)
         low_ref[...] = low
@@ -823,23 +816,22 @@
             ((model, model), bf16),
             ((lines, model), f32),
         ],
-        [spot, stream_in, waves, *row_pieces],
+        [spot, waves, chunks_own, *col_got, *row_pieces],
         smem=(0,),
     )
     kv_left = to_right(row_kv)
     kv_right = to_left(row_kv)
-
-    feed_own = after(feed_own, kv_left, kv_right)
-    feed_other = along_core(feed_own)
-
-    def pair_feed(own_ref, other_ref, out_ref):
-        out_ref[0] = own_ref[...]
-        out_ref[1] = other_ref[...]
-
-    feed_both = kernel_call(
-        pair_feed, [((2, 2, shard, hidden), bf16)], [feed_own, feed_other]
-    )[0]
-    feed_pair, feed_diagonal = pair_chips(feed_both), along_chips(feed_own, chips - 1)
+    col_unit = hops * col_rows
+    col_hops, given_out = kernel_call(
+        stack_col,
+        [((col_unit, model), bf16), ((toks, model), bf16)],
+        [after(chunks_own, row_q), *col_got],
+    )
+    col_far_own = along_core(col_own)
+    col_plane, col_pair, col_diagonal = spread_plane(col_hops, along_core(col_hops))
+
+    feed_pair = pair_chips(after(feed_both, row_q))
+    kv_left = after(kv_left, feed_pair, col_pair, col_diagonal)
 
     def tied_logits(spot_ref, q_ref, near_ref, left_ref, right_ref, out_ref):
         mask = head_mask(width, model)
@@ -857,7 +849,9 @@
         [spot, row_q, row_kv, kv_left, kv_right],
         smem=(0,),
     )[0]
-    logits_other = after(along_core(logits), col_pair, col_diagonal)
+    logits_other = along_core(logits)
+    feed_diagonal = along_chips(after(feed_own, logits), chips - 1)
+    given_far = after(along_core(given_out), logits)
     row_scale = 1.0 / math.sqrt(HEAD_DIM * seqs)
     col_scale = 1.0 / math.sqrt(HEAD_DIM)
 
@@ -938,23 +932,13 @@
     ]
 
     def assemble_col(spot_ref, *refs):
-        three_ref, last_ref, given_ref = refs[7:]
+        three_ref, last_ref = refs[7:]
         outs = [(three_ref, (index,)) for index in range(3)] + [(last_ref, ())]
         place_rows(spot_ref, refs[:7], outs, col_rows, col_unit)
-        at_core = spot_ref[2]
-        start = hops * col_rows
-        given_ref[0] = refs[2][start:col_unit]
-        given_ref[1 + at_core] = refs[3][start:col_unit]
-        given_ref[2 - at_core] = refs[5][col_unit + start :]
-        given_ref[3] = refs[4][start:]
-
-    weights_three, weights_last, given_all = kernel_call(
+
+    weights_three, weights_last = kernel_call(
         assemble_col,
-        [
-            ((3, model, model), bf16),
-            ((model, model), bf16),
-            ((cols_axis, toks, model), bf16),
-        ],
+        [((3, model, model), bf16), ((model, model), bf16)],
         [spot, *col_pieces],
         smem=(0,),
     )
@@ -971,6 +955,13 @@
         [normed_two, weights_three],
     )
     kv_other = along_core(col_kv)
+
+    def join_given(near_ref, far_ref, out_ref):
+        out_ref[:toks] = near_ref[...]
+        out_ref[toks:] = far_ref[...]
+
+    given_both = kernel_call(join_given, [((2 * toks, model), bf16)], [given_out, given_far])[0]
+    given_pair = pair_cols(given_both)
 
     def slot_rows(slot):
         return slice(slot * width, (slot + 1) * width)
@@ -982,10 +973,12 @@
         one_ref,
         norm_ref,
         weight_ref,
+        given_ref,
         probs_ref,
         mix_ref,
         stream_ref,
         low_ref,
+        message_ref,
     ):
         lane_heads = head_of_lane(model)
         sides = (near_ref, far_ref)
@@ -1020,24 +1013,46 @@
         stream = one_ref[...] + dot(mix_ref[...], weight_ref[...])
         stream_ref[...] = stream
         unit, _ = unit_norm(stream)
-        low_ref[...] = (unit * norm_ref[4:5] + norm_ref[5:6]).astype(bf16)
-
-    col_probs, col_mix, stream_two, normed_three = kernel_call(
+        low = (unit * norm_ref[4:5] + norm_ref[5:6]).astype(bf16)
+        low_ref[...] = low
+        message_ref[:toks] = low
+        message_ref[toks:] = given_ref[...]
+
+    col_probs, col_mix, stream_two, normed_three, message = kernel_call(
         attend_col,
         [
             ((chips, seqs * width, 128), f32),
             ((toks, model), bf16),
             ((toks, model), f32),
             ((toks, model), bf16),
+            ((2 * toks, model), bf16),
         ],
-        [col_q, col_kv, kv_other, stream_one, norm_rows, weights_last],
-    )
-    low_near = [normed_three] + [along_cols(normed_three, step) for step in col_steps]
-
-    feed_last = after((feed_pair, feed_diagonal), low_near)
+        [col_q, col_kv, kv_other, stream_one, norm_rows, weights_last, given_out],
+    )
+    low_near = [
+        normed_three,
+        along_cols(normed_three, 1),
+        along_cols(normed_three, 2),
+        along_cols(message, 3),
+    ]
+
+    feed_last = after((feed_pair, feed_diagonal, given_pair), low_near)
     feed_far = [along_core(item) for item in feed_last]
 
-    def assemble_feed(spot_ref, both_ref, pair_ref, last_ref, pair2_ref, last2_ref, out_ref):
+    def assemble_feed(
+        spot_ref,
+        both_ref,
+        pair_ref,
+        last_ref,
+        pair2_ref,
+        last2_ref,
+        d0_ref,
+        d1_ref,
+        d2_ref,
+        d3_ref,
+        out_ref,
+        given_ref,
+    ):
         at_chip, at_core = spot_ref[1], spot_ref[2]
         other = 1 - at_core
 
@@ -1051,18 +1066,33 @@
             move(pair2_ref[side], at_chip ^ (1 + other), other ^ side)
         move(last_ref[...], at_chip ^ 3, at_core)
         move(last2_ref[...], at_chip ^ 3, other)
-
-    weights_feed = kernel_call(
+        given_ref[0] = d0_ref[...]
+        given_ref[1 + at_core] = d1_ref[:toks]
+        given_ref[2 - at_core] = d2_ref[toks:]
+        given_ref[3] = d3_ref[toks:]
+
+    weights_feed, given_all = kernel_call(
         assemble_feed,
-        [((2, model, hidden), bf16)],
-        [spot, feed_both, feed_pair, feed_diagonal, *feed_far],
+        [((2, model, hidden), bf16), ((cols_axis, toks, model), bf16)],
+        [
+            spot,
+            feed_both,
+            feed_pair,
+            feed_diagonal,
+            feed_far[0],
+            feed_far[1],
+            given_out,
+            given_pair,
+            feed_far[2],
+            low_near[3],
+        ],
         smem=(0,),
-    )[0]
+    )
 
     def feed_main(a0, a1, a2, a3, given_ref, weight_ref, act_ref, grad_ref, *back_refs):
         up, down = weight_ref[0], weight_ref[1]
         for step, low_ref in enumerate((a0, a1, a2, a3)):
-            pre = dot(low_ref[...], up)
+            pre = dot(low_ref[:toks], up)
             bell = 0.5 * (1.0 + lax.erf(pre * (0.5**0.5)))
             slope = bell + pre * jnp.exp(-0.5 * pre * pre) * ((0.5 / math.pi) ** 0.5)
             act_ref[step] = (pre * bell).astype(bf16)
@@ -1083,7 +1113,7 @@
         spot_ref, a0, a1, a2, a3, given_ref, act_ref, grad_ref, weight_ref, mine_ref, give_ref, *outs
     ):
         at_core = spot_ref[2]
-        low = jnp.concatenate([a0[...], a1[...], a2[...], a3[...]], axis=0)
+        low = jnp.concatenate([a0[...], a1[...], a2[...], a3[:toks]], axis=0)
         given = given_ref[...].reshape(cols_axis * toks, model)
         rows = cols_axis * toks
         acts = act_ref[...].reshape(rows, hidden)
@@ -1104,7 +1134,6 @@
         room=24,
     )
     feed_mine, feed_give, out_parts = feed_grads[0], feed_grads[1], feed_grads[2:]
-    feed_back_in = along_core(feed_give)
 
     block = 2 * shard
     extra = 2 * lines
@@ -1154,7 +1183,7 @@
         )
 
     def split_chips(items, count, tail, stream=None, slots=()):
-        slot_rows_out = 2 * width if stream is not None or slots else 0
+        slot_rows_out = 2 * width * ((stream is not None) + bool(slots))
 
         def chip_parts(spot_ref, *refs):
             ins, outs, total_ref = refs[: len(items)], refs[-chips - 1 : -1], refs[-1]
@@ -1177,13 +1206,15 @@
                 if tail:
                     outs[hop][row : row + tail] = renew(total[count * model :], 6).astype(bf16)
                     row = row + tail
-                if slot_rows_out:
-                    if stream is not None:
-                        slot = result[slot_rows(hop)].astype(bf16)
-                    else:
-                        slot = more[hop][...]
+                sent = []
+                if stream is not None:
+                    sent.append(result[slot_rows(hop)].astype(bf16))
+                if slots:
+                    sent.append(more[hop - chips][...])
+                for slot in sent:
                     outs[hop][row : row + width] = slot[:, :half]
-                    outs[hop][row + width :] = slot[:, half:]
+                    outs[hop][row + width : row + 2 * width] = slot[:, half:]
+                    row = row + 2 * width
 
         size = count * block + tail + slot_rows_out
         return kernel_call(
@@ -1222,8 +1253,7 @@
     def over_chips(parts):
         return [parts[0]] + [along_chips(parts[step], step) for step in steps]
 
-    feed_slices = split_chips([feed_mine, feed_back_in], 2, 0)
-    back_near = after(back_near, feed_slices)
+    back_near = after(back_near, feed_mine)
 
     def attend_col_back(
         spot_ref,
@@ -1316,7 +1346,9 @@
         smem=(0,),
         scratch=[pltpu.VMEM((2, 2 * toks, model), f32)],
     )
-    dkv_got = along_core(col_send)
+    row_low_far, row_mix_far = along_core(normed_one), along_core(row_mix)
+    col_low_far, col_mix_far = along_core(normed_two), along_core(col_mix)
+    dkv_got = after(along_core(col_send), row_low_far, row_mix_far)
 
     def row_entry_back(
         spot_ref,
@@ -1404,8 +1436,8 @@
     col_sums = layer_grads(
         normed_two,
         col_mix,
-        along_core(normed_two),
-        along_core(col_mix),
+        col_low_far,
+        col_mix_far,
         col_mine,
         along_core(col_give),
         out_parts,
@@ -1476,8 +1508,8 @@
     )
     edge_from_right = to_left(edge_left)
     edge_from_left = to_right(edge_right)
+    feed_slices = split_chips([feed_mine, along_core(after(feed_give, edge_left))], 2, 0)
     feed_keep, feed_swap = split_cores(over_chips(feed_slices), 2, 0)
-    edge_from_left = after(edge_from_left, feed_keep)
 
     def input_back(
         spot_ref,
@@ -1574,8 +1606,7 @@
 
     feed_back = along_core(feed_swap)
     col_parts = [col_sums[0]] + [along_cols(col_sums[step], step) for step in col_steps]
-    col_slices = split_chips(col_parts, 1, 0, stream=stream_two)
-    col_slices = after(col_slices, sums)
+    col_slices = split_chips(col_parts, 1, 0, stream=stream_two, slots=grad_slots)
     col_reached = over_chips(col_slices)
     col_keep, col_swap = split_cores(col_reached, 1, 0)
 
@@ -1591,7 +1622,6 @@
         smem=(0,),
     )
     pair_ends = over_cols(pair)
-    result = order_rows(col_reached, block)
 
     def spread_pair(spot_ref, u0, u1, u2, u3, in_ref, out_ref, g0, g1, g2, g3, all_ref):
         for step, ref in enumerate((u0, u1, u2, u3)):
@@ -1609,14 +1639,15 @@
     row_parts = layer_grads(
         normed_one,
         row_mix,
-        along_core(normed_one),
-        along_core(row_mix),
+        row_low_far,
+        row_mix_far,
         row_mine,
         along_core(row_give),
         [sums],
     )
-    row_parts = [row_parts[0]] + [along_cols(row_parts[step], step) for step in col_steps]
-    row_slices = split_chips(row_parts, 1, extra, slots=grad_slots)
+    row_sends = after(row_parts, col_parts, feed_keep)
+    row_parts = [row_parts[0]] + [along_cols(row_sends[step], step) for step in col_steps]
+    row_slices = split_chips(row_parts, 1, extra)
     row_reached = over_chips(row_slices)
     row_keep, row_swap = split_cores(row_reached, 1, extra)
 
@@ -1640,11 +1671,12 @@
         smem=(0,),
     )
     row_ends = over_cols(row_join)
-    grad_in = order_rows(row_reached, block + extra)
+    result = order_rows(after(col_reached, row_join), block)
+    grad_in = order_rows(after(col_reached, row_join), block + 2 * width)
     grad_feed_in, grad_feed_out, *col_grads = kernel_call(
         spread_pair,
         [(feed_in.shape, f32), (feed_out.shape, f32)] + [((shard, model), f32)] * cols_axis,
-        [spot, *pair_ends],
+        [spot, *after(pair_ends, row_join)],
         smem=(0,),
         scratch=[pltpu.VMEM((cols_axis, 3 * shard, model), bf16)],
         room=24,

time: 294 us -> 278 us (0.946)
  waiting for transfers between devices: 143 us -> 129 us
    ppermute x20, waiting for transfers between devices: 47.4 us -> 28.8 us  [along_cols(): lax.ppermute(values, 'col', [(i, i ^ step) for i in range(cols_axis)])]
    ppermute x16, waiting for transfers between devices: 69.5 us -> 56.6 us  [along_chips(): return lax.ppermute(values, 'seq', [(i, i ^ 2 * step) for i in range(seqs)])]
    ppermute x2, waiting for transfers between devices: 8.97 us -> 18.3 us  [to_right(): return lax.ppermute(values, ('col', 'seq'), rightward)]
    ppermute x25 -> x27, waiting for transfers between devices: 11.7 us -> 19.6 us  [along_core(): return lax.ppermute(values, 'seq', [(i, i ^ 1) for i in range(seqs)])]
    ppermute x16, starting transfers between devices: 37.2 us -> 31.2 us  [along_chips(): return lax.ppermute(values, 'seq', [(i, i ^ 2 * step) for i in range(seqs)])]
    ppermute x2 -> x3, starting transfers between devices: 3.11 us -> 7.1 us  [pair_cols(): return lax.ppermute(values, ('col', 'seq'), pairs)]
    pallas_call x34 -> x35, Pallas kernels: 53.2 us -> 52 us  [kernel_call(): pl.pallas_call(body, grid=(1,) if stream else (), out_shape=out_shapes, i...]
  transfers between devices with their start and end apart: 68 -> 71, of which waited for: 31 -> 34; matrix products, arithmetic and copies ran while one was open for 2% -> 2% of each run, Pallas kernels for 10% -> 10%
where the time goes in v3:
time: 278 us
  waiting for transfers between devices  129 us (46%)
  starting transfers between devices  86.3 us (31%)
  Pallas kernels  52 us (19%)
  between operations  4.37 us (2%)
  local copies, waits for them, and re-layouts  3.01 us (1%)
  other arithmetic  2.96 us (1%)
    ppermute x16, waiting for transfers between devices, along_chips(): return lax.ppermute(values, 'seq', [(i, i ^ 2 * step) for i in range(seqs)])  56.6 us
    pallas_call x35, Pallas kernels, kernel_call(): pl.pallas_call(body, grid=(1,) if stream else (), out_shape=out_shapes, i...  52 us
    ppermute x16, starting transfers between devices, along_chips(): return lax.ppermute(values, 'seq', [(i, i ^ 2 * step) for i in range(seqs)])  31.2 us
    ppermute x20, waiting for transfers between devices, along_cols(): lax.ppermute(values, 'col', [(i, i ^ step) for i in range(cols_axis)])  28.8 us
    ppermute x20, starting transfers between devices, along_cols(): lax.ppermute(values, 'col', [(i, i ^ step) for i in range(cols_axis)])  28.3 us
    ppermute x27, waiting for transfers between devices, along_core(): return lax.ppermute(values, 'seq', [(i, i ^ 1) for i in range(seqs)])  19.6 us
    ppermute x2, waiting for transfers between devices, to_right(): return lax.ppermute(values, ('col', 'seq'), rightward)  18.3 us
    ppermute x3, starting transfers between devices, pair_cols(): return lax.ppermute(values, ('col', 'seq'), pairs)  7.1 us
  transfers between devices with their start and end apart: 71, of which 34 were waited for; matrix products, arithmetic and copies ran while one was open for 2% of the time, Pallas kernels for 10%

profile of v3, /device:TPU:0, one launch (start us, length us, event | category | flops | bytes accessed | tf_op | source)
XLA Modules:
  0.0 277.6 jit_solution(16071511399699954026)
XLA Ops:
  4.1 3.0 %collective-permute-start = (bf16[104,768]{1,0:T(8,128)(2,1)}, bf16[104,768]{1,0:T(8,128)(2,1)S(1)}, u32[]{:S(2)}, u32[]{:S(2)}) collective-permute-start(bf16[104,768]{1,0:T(8,128)(2,1)} %get-tuple-element.169), channel_id=1, source_target_pairs={{0,2},{1,3},{2,0},{3,1},{4,6},{5,7},{6,4},{7,5},{8,10},{9,11},{10,... | collective-permute-start | bytes 479240 | tf_op jit(solution)/shard_map/ppermute | solution.py:555
  7.1 2.6 collective-permute-start.1
  14.1 3.2 %pack_rest.1 = (bf16[2,96,768]{2,1,0:T(8,128)(2,1)}, bf16[384,768]{1,0:T(8,128)(2,1)}, bf16[64,768]{1,0:T(8,128)(2,1)}, bf16[160,768]{1,0:T(8,128)(2,1)}, bf16[1...) custom-call(s32[7]{0:T(128)} %stack.42.spot_ref, bf16[96,768]{1,0:T(8,128)(2,1)} %refs_0_.2, bf16[96,768]{1,0:T(8,128)(2,1)} %refs_1_.2, ...), custom_call_target="tpu_custom_call" | custom-call | flops 1 | bytes 1 | tf_op jit(solution)/shard_map/pack_rest/pallas_call | solution.py:415
  17.3 4.8 %collective-permute-done.1.refs_1_ = bf16[104,768]{1,0:T(8,128)(2,1)S(1)} collective-permute-done((bf16[104,768]{1,0:T(8,128)(2,1)}, bf16[104,768]{1,0:T(8,128)(2,1)S(1)}, u32[]{:S(2)}, u32[]{:S(2)}) %collective-permute-start.1) | collective-permute-done | bytes 159776 | tf_op jit(solution)/shard_map/ppermute | solution.py:555
  27.3 2.6 collective-permute-start.4
  32.5 16.9 %collective-permute-done.9.refs_8_ = bf16[312,768]{1,0:T(8,128)(2,1)S(1)} collective-permute-done((bf16[312,768]{1,0:T(8,128)(2,1)S(1)}, bf16[312,768]{1,0:T(8,128)(2,1)S(1)}, u32[]{:S(2)}, u32[]{:S(2)}) %collective-permute-start.9) | collective-permute-done | bytes 479264 | tf_op jit(solution)/shard_map/ppermute | solution.py:561
  50.7 2.8 %collective-permute-done.7.refs_5_ = bf16[392,768]{1,0:T(8,128)(2,1)S(1)} collective-permute-done((bf16[392,768]{1,0:T(8,128)(2,1)S(1)}, bf16[392,768]{1,0:T(8,128)(2,1)S(1)}, u32[]{:S(2)}, u32[]{:S(2)}) %collective-permute-start.7) | collective-permute-done | bytes 602144 | tf_op jit(solution)/shard_map/ppermute | solution.py:558
  59.7 4.9 %collective-permute-start.14 = (bf16[2,2,96,768]{3,2,1,0:T(8,128)(2,1)S(1)}, bf16[2,2,96,768]{3,2,1,0:T(8,128)(2,1)S(1)}, u32[]{:S(2)}, u32[]{:S(2)}) collective-permute-start(bf16[2,2,96,768]{3,2,1,0:T(8,128)(2,1)S(1)} %pair_feed.1.both_ref), channel_id=1, source_target_pairs={{0,2},{1,5},{2,0},{3,7},{4,6},{5,1},{6,4},{7,3},{8,10},{9,13},{10,... | collective-permute-start | bytes 1769480 | tf_op jit(solution)/shard_map/ppermute | solution.py:573
  68.7 17.2 %collective-permute-done.13.left_ref = bf16[2,128,768]{2,1,0:T(8,128)(2,1)S(1)} collective-permute-done((bf16[2,128,768]{2,1,0:T(8,128)(2,1)S(1)}, bf16[2,128,768]{2,1,0:T(8,128)(2,1)S(1)}, u32[]{:S(2)}, u32[]{:S(2)}) %collective-permute-start.13) | collective-permute-done | bytes 393248 | tf_op jit(solution)/shard_map/ppermute | solution.py:586
  92.2 2.6 collective-permute-done.20.refs_1_
  99.0 4.0 %collective-permute-start.31 = (bf16[256,768]{1,0:T(8,128)(2,1)S(1)}, bf16[256,768]{1,0:T(8,128)(2,1)S(1)}, u32[]{:S(2)}, u32[]{:S(2)}) collective-permute-start(bf16[256,768]{1,0:T(8,128)(2,1)S(1)} %join_given.1), channel_id=1, source_target_pairs={{0,8},{1,17},{2,10},{3,19},{4,12},{5,21},{6,14},{7,23},{8,0},{9,25... | collective-permute-start | bytes 1179656 | tf_op jit(solution)/shard_map/ppermute | solution.py:569
  111.3 5.8 %collective-permute-done.29.last_ref = bf16[2,96,768]{2,1,0:T(8,128)(2,1)S(1)} collective-permute-done((bf16[2,96,768]{2,1,0:T(8,128)(2,1)S(1)}, bf16[2,96,768]{2,1,0:T(8,128)(2,1)S(1)}, u32[]{:S(2)}, u32[]{:S(2)}) %collective-permute-start.29) | collective-permute-done | bytes 294944 | tf_op jit(solution)/shard_map/ppermute | solution.py:555
  117.1 4.3 %collective-permute-done.26.a1 = bf16[128,768]{1,0:T(8,128)(2,1)S(1)} collective-permute-done((bf16[128,768]{1,0:T(8,128)(2,1)S(1)}, bf16[128,768]{1,0:T(8,128)(2,1)S(1)}, u32[]{:S(2)}, u32[]{:S(2)}) %collective-permute-start.26) | collective-permute-done | bytes 196640 | tf_op jit(solution)/shard_map/ppermute | solution.py:561
  123.2 2.5 collective-permute-done.33.last2_ref
  126.5 3.7 %feed_main.1 = (bf16[4,128,768]{2,1,0:T(8,128)(2,1)S(1)}, bf16[4,128,768]{2,1,0:T(8,128)(2,1)S(1)}, bf16[128,768]{1,0:T(8,128)(2,1)S(1)}, bf16[128,768]{1,0:T(8,...) custom-call(bf16[128,768]{1,0:T(8,128)(2,1)S(1)} %get-tuple-element.201.a0, ...), custom_call_target="tpu_custom_call" | custom-call | flops 1 | bytes 1 | tf_op jit(solution)/shard_map/feed_main/pallas_call | solution.py:415
  133.7 3.0 %feed_weights.1 = (bf16[1536,384]{1,0:T(8,128)(2,1)S(1)}, bf16[1536,384]{1,0:T(8,128)(2,1)S(1)}, bf16[128,768]{1,0:T(8,128)(2,1)S(1)}, bf16[128,768]{1,0:T(8,128...) custom-call(s32[7]{0:T(128)S(1)} %copy-done.3, bf16[128,768]{1,0:T(8,128)(2,1)S(1)} %get-tuple-element.201.a0, ...), custom_call_target="tpu_custom_call" | custom-call | flops 1811939328 | bytes 16777216 | tf_op jit(solution)/shard_map/feed_weights/pallas_call | solution.py:415
  138.0 3.9 %collective-permute-done.36.b2 = bf16[128,768]{1,0:T(8,128)(2,1)S(1)} collective-permute-done((bf16[128,768]{1,0:T(8,128)(2,1)S(1)}, bf16[128,768]{1,0:T(8,128)(2,1)S(1)}, u32[]{:S(2)}, u32[]{:S(2)}) %collective-permute-start.36) | collective-permute-done | bytes 196640 | tf_op jit(solution)/shard_map/ppermute | solution.py:561
  141.9 3.8 %attend_col_back.1 = (f32[128,768]{1,0:T(8,128)S(1)}, bf16[128,768]{1,0:T(8,128)(2,1)S(1)}, bf16[128,768]{1,0:T(8,128)(2,1)S(1)}, f32[2,128,768]{2,1,0:T(8,128)S...) custom-call(s32[7]{0:T(128)S(1)} %copy-done.3, bf16[128,768]{1,0:T(8,128)(2,1)S(1)} %get-tuple-element.217.b0, ...), custom_call_target="tpu_custom_call" | custom-call | flops 1 | bytes 1 | tf_op jit(solution)/shard_map/attend_col_back/pallas_call | solution.py:415
  148.0 3.6 %row_entry_back.1 = (bf16[4,128,384]{2,1,0:T(8,128)(2,1)S(1)}, bf16[4,128,384]{2,1,0:T(8,128)(2,1)S(1)}, f32[128,768]{1,0:T(8,128)S(1)}, bf16[128,768]{1,0:T(8,1...) custom-call(s32[7]{0:T(128)S(1)} %copy-done.3, ...), custom_call_target="tpu_custom_call" | custom-call | flops 1 | bytes 1 | tf_op jit(solution)/shard_map/row_entry_back/pallas_call | solution.py:415
  159.4 4.8 %collective-permute-start.47 = (bf16[2,128,768]{2,1,0:T(8,128)(2,1)S(1)}, bf16[2,128,768]{2,1,0:T(8,128)(2,1)S(1)}, u32[]{:S(2)}, u32[]{:S(2)}) collective-permute-start(bf16[2,128,768]{2,1,0:T(8,128)(2,1)S(1)} %get-tuple-element.249), channel_id=1, source_target_pairs={{0,2},{1,3},{2,4},{3,5},{4,6},{5,7},{6,14},{7,15},{14,12},{15,13},... | collective-permute-start | bytes 1179656 | tf_op jit(solution)/shard_map/ppermute | solution.py:586
  166.5 4.9 %collective-permute-done.46.from_right_ref = bf16[2,128,768]{2,1,0:T(8,128)(2,1)S(1)} collective-permute-done((bf16[2,128,768]{2,1,0:T(8,128)(2,1)S(1)}, bf16[2,128,768]{2,1,0:T(8,128)(2,1)S(1)}, u32[]{:S(2)}, u32[]{:S(2)}) %collective-permute-start.46) | collective-permute-done | bytes 393248 | tf_op jit(solution)/shard_map/ppermute | solution.py:589
  175.9 2.5 collective-permute-start.53
  180.0 11.1 %collective-permute-done.53.refs_1_ = bf16[384,384]{1,0:T(8,128)(2,1)S(1)} collective-permute-done((bf16[384,384]{1,0:T(8,128)(2,1)S(1)}, bf16[384,384]{1,0:T(8,128)(2,1)S(1)}, u32[]{:S(2)}, u32[]{:S(2)}) %collective-permute-start.53) | collective-permute-done | bytes 294944 | tf_op jit(solution)/shard_map/ppermute | solution.py:555
  191.1 3.9 %collective-permute-start.55 = (bf16[384,384]{1,0:T(8,128)(2,1)S(1)}, bf16[384,384]{1,0:T(8,128)(2,1)S(1)}, u32[]{:S(2)}, u32[]{:S(2)}) collective-permute-start(bf16[384,384]{1,0:T(8,128)(2,1)S(1)} %get-tuple-element.276), channel_id=1, source_target_pairs={{0,6},{1,7},{2,4},{3,5},{4,2},{5,3},{6,0},{7,1},{8,14},{9,15},{10,... | collective-permute-start | bytes 884744 | tf_op jit(solution)/shard_map/ppermute | solution.py:555
  196.7 5.3 %collective-permute-done.55.refs_3_ = bf16[384,384]{1,0:T(8,128)(2,1)S(1)} collective-permute-done((bf16[384,384]{1,0:T(8,128)(2,1)S(1)}, bf16[384,384]{1,0:T(8,128)(2,1)S(1)}, u32[]{:S(2)}, u32[]{:S(2)}) %collective-permute-start.55) | collective-permute-done | bytes 294944 | tf_op jit(solution)/shard_map/ppermute | solution.py:555
  202.9 5.9 %collective-permute-start.56 = (bf16[784,384]{1,0:T(8,128)(2,1)S(1)}, bf16[784,384]{1,0:T(8,128)(2,1)S(1)}, u32[]{:S(2)}, u32[]{:S(2)}) collective-permute-start(bf16[784,384]{1,0:T(8,128)(2,1)S(1)} %get-tuple-element.278), channel_id=1, source_target_pairs={{0,8},{8,0},{16,24},{24,16},{1,9},{9,1},{17,25},{25,17},{2,10},{10... | collective-permute-start | bytes 1806344 | tf_op jit(solution)/shard_map/ppermute | solution.py:561
  214.9 9.5 %collective-permute-done.48.refs_1_ = bf16[320,384]{1,0:T(8,128)(2,1)S(1)} collective-permute-done((bf16[320,384]{1,0:T(8,128)(2,1)S(1)}, bf16[320,384]{1,0:T(8,128)(2,1)S(1)}, u32[]{:S(2)}, u32[]{:S(2)}) %collective-permute-start.48) | collective-permute-done | bytes 245792 | tf_op jit(solution)/shard_map/ppermute | solution.py:555
  226.1 7.6 %collective-permute-done.49.refs_2_ = bf16[320,384]{1,0:T(8,128)(2,1)S(1)} collective-permute-done((bf16[320,384]{1,0:T(8,128)(2,1)S(1)}, bf16[320,384]{1,0:T(8,128)(2,1)S(1)}, u32[]{:S(2)}, u32[]{:S(2)}) %collective-permute-start.49) | collective-permute-done | bytes 245792 | tf_op jit(solution)/shard_map/ppermute | solution.py:555
  241.3 4.6 %collective-permute-start.59 = (bf16[208,384]{1,0:T(8,128)(2,1)S(1)}, bf16[208,384]{1,0:T(8,128)(2,1)S(1)}, u32[]{:S(2)}, u32[]{:S(2)}) collective-permute-start(bf16[208,384]{1,0:T(8,128)(2,1)S(1)} %get-tuple-element.282), channel_id=1, source_target_pairs={{0,2},{1,3},{2,0},{3,1},{4,6},{5,7},{6,4},{7,5},{8,10},{9,11},{10,... | collective-permute-start | bytes 479240 | tf_op jit(solution)/shard_map/ppermute | solution.py:555
  246.5 5.0 %collective-permute-done.59.refs_1_ = bf16[208,384]{1,0:T(8,128)(2,1)S(1)} collective-permute-done((bf16[208,384]{1,0:T(8,128)(2,1)S(1)}, bf16[208,384]{1,0:T(8,128)(2,1)S(1)}, u32[]{:S(2)}, u32[]{:S(2)}) %collective-permute-start.59) | collective-permute-done | bytes 159776 | tf_op jit(solution)/shard_map/ppermute | solution.py:555
  253.5 6.6 %collective-permute-done.60.refs_2_ = bf16[208,384]{1,0:T(8,128)(2,1)S(1)} collective-permute-done((bf16[208,384]{1,0:T(8,128)(2,1)S(1)}, bf16[208,384]{1,0:T(8,128)(2,1)S(1)}, u32[]{:S(2)}, u32[]{:S(2)}) %collective-permute-start.60) | collective-permute-done | bytes 159776 | tf_op jit(solution)/shard_map/ppermute | solution.py:555
  270.4 2.8 %spread_pair.1 = (f32[96,3072]{1,0:T(8,128)}, f32[384,768]{1,0:T(8,128)}, f32[96,768]{1,0:T(8,128)}, f32[96,768]{1,0:T(8,128)}, f32[96,768]{1,0:T(8,128)}, /*index=5*/f32[96,768]{1,0:T(8,128)}) custom-call(s32[7]{0:T(128)S(1)} %copy-done.3, bf16[288,768]{1,0:T(8,128)(2,1)S(1)} %join_two.1.u0, bf16[288,768]{1,0:T(8,128)(2,1)S(1)} %collective-permute-done.68.u1, ...), custom_call_target="tpu_custom_call" | custom-call | flops 1 | bytes 1 | tf_op jit(solution)/shard_map/spread_pair/pallas_call | solution.py:415
  (175 shorter events, 103.3 us)
Async XLA Ops:
  4.1 13.2 %collective-permute-start = (bf16[104,768]{1,0:T(8,128)(2,1)}, bf16[104,768]{1,0:T(8,128)(2,1)S(1)}, u32[]{:S(2)}, u32[]{:S(2)}) collective-permute-start(bf16[104,768]{1,0:T(8,128)(2,1)} %get-tuple-element.169), channel_id=1, source_target_pairs={{0,2},{1,3},{2,0},{3,1},{4,6},{5,7},{6,4},{7,5},{8,10},{9,11},{10,... | collective-permute-start | bytes 479240 | tf_op jit(solution)/shard_map/ppermute | solution.py:555
  7.1 15.0 %collective-permute-start.1 = (bf16[104,768]{1,0:T(8,128)(2,1)}, bf16[104,768]{1,0:T(8,128)(2,1)S(1)}, u32[]{:S(2)}, u32[]{:S(2)}) collective-permute-start(bf16[104,768]{1,0:T(8,128)(2,1)} %get-tuple-element.169), channel_id=1, source_target_pairs={{0,4},{1,5},{2,6},{3,7},{4,0},{5,1},{6,2},{7,3},{8,12},{9,13},{10,... | collective-permute-start | bytes 479240 | tf_op jit(solution)/shard_map/ppermute | solution.py:555
  9.7 12.4 %collective-permute-start.2 = (bf16[104,768]{1,0:T(8,128)(2,1)}, bf16[104,768]{1,0:T(8,128)(2,1)S(1)}, u32[]{:S(2)}, u32[]{:S(2)}) collective-permute-start(bf16[104,768]{1,0:T(8,128)(2,1)} %get-tuple-element.169), channel_id=1, source_target_pairs={{0,6},{1,7},{2,4},{3,5},{4,2},{5,3},{6,0},{7,1},{8,14},{9,15},{10,... | collective-permute-start | bytes 479240 | tf_op jit(solution)/shard_map/ppermute | solution.py:555
  24.2 25.9 %collective-permute-start.8 = (bf16[624,768]{1,0:T(8,128)(2,1)S(1)}, bf16[624,768]{1,0:T(8,128)(2,1)S(1)}, u32[]{:S(2)}, u32[]{:S(2)}) collective-permute-start(bf16[624,768]{1,0:T(8,128)(2,1)S(1)} %join_cores.2.refs_6_), channel_id=1, source_target_pairs={{0,8},{1,17},{2,10},{3,19},{4,12},{5,21},{6,14},{7,23},{8,0},{9,25... | collective-permute-start | bytes 2875400 | tf_op jit(solution)/shard_map/ppermute | solution.py:569
  25.8 23.6 %collective-permute-start.9 = (bf16[312,768]{1,0:T(8,128)(2,1)S(1)}, bf16[312,768]{1,0:T(8,128)(2,1)S(1)}, u32[]{:S(2)}, u32[]{:S(2)}) collective-permute-start(bf16[312,768]{1,0:T(8,128)(2,1)S(1)} %stack_row.1.near_ref), channel_id=1, source_target_pairs={{0,24},{8,16},{16,8},{24,0},{1,25},{9,17},{17,9},{25,1},{2,26},{10... | collective-permute-start | bytes 1437704 | tf_op jit(solution)/shard_map/ppermute | solution.py:561
  27.3 22.1 %collective-permute-start.4 = (bf16[160,768]{1,0:T(8,128)(2,1)S(1)}, bf16[160,768]{1,0:T(8,128)(2,1)S(1)}, u32[]{:S(2)}, u32[]{:S(2)}) collective-permute-start(bf16[160,768]{1,0:T(8,128)(2,1)S(1)} %copy-done.7), channel_id=1, source_target_pairs={{0,2},{1,3},{2,0},{3,1},{4,6},{5,7},{6,4},{7,5},{8,10},{9,11},{10,... | collective-permute-start | bytes 737288 | tf_op jit(solution)/shard_map/ppermute | solution.py:555
  29.9 20.3 %collective-permute-start.5 = (bf16[160,768]{1,0:T(8,128)(2,1)S(1)}, bf16[160,768]{1,0:T(8,128)(2,1)S(1)}, u32[]{:S(2)}, u32[]{:S(2)}) collective-permute-start(bf16[160,768]{1,0:T(8,128)(2,1)S(1)} %copy-done.6), channel_id=1, source_target_pairs={{0,4},{1,5},{2,6},{3,7},{4,0},{5,1},{6,2},{7,3},{8,12},{9,13},{10,... | collective-permute-start | bytes 737288 | tf_op jit(solution)/shard_map/ppermute | solution.py:555
  31.0 19.2 %collective-permute-start.6 = (bf16[160,768]{1,0:T(8,128)(2,1)S(1)}, bf16[160,768]{1,0:T(8,128)(2,1)S(1)}, u32[]{:S(2)}, u32[]{:S(2)}) collective-permute-start(bf16[160,768]{1,0:T(8,128)(2,1)S(1)} %copy-done.5), channel_id=1, source_target_pairs={{0,6},{1,7},{2,4},{3,5},{4,2},{5,3},{6,0},{7,1},{8,14},{9,15},{10,... | collective-permute-start | bytes 737288 | tf_op jit(solution)/shard_map/ppermute | solution.py:555
  58.1 27.8 %collective-permute-start.16 = (bf16[576,768]{1,0:T(8,128)(2,1)S(1)}, bf16[576,768]{1,0:T(8,128)(2,1)S(1)}, u32[]{:S(2)}, u32[]{:S(2)}) collective-permute-start(bf16[576,768]{1,0:T(8,128)(2,1)S(1)} %join_cores.3.refs_2_), channel_id=1, source_target_pairs={{0,8},{1,17},{2,10},{3,19},{4,12},{5,21},{6,14},{7,23},{8,0},{9,25... | collective-permute-start | bytes 2654216 | tf_op jit(solution)/shard_map/ppermute | solution.py:569
  59.7 26.2 %collective-permute-start.14 = (bf16[2,2,96,768]{3,2,1,0:T(8,128)(2,1)S(1)}, bf16[2,2,96,768]{3,2,1,0:T(8,128)(2,1)S(1)}, u32[]{:S(2)}, u32[]{:S(2)}) collective-permute-start(bf16[2,2,96,768]{3,2,1,0:T(8,128)(2,1)S(1)} %pair_feed.1.both_ref), channel_id=1, source_target_pairs={{0,2},{1,5},{2,0},{3,7},{4,6},{5,1},{6,4},{7,3},{8,10},{9,13},{10,... | collective-permute-start | bytes 1769480 | tf_op jit(solution)/shard_map/ppermute | solution.py:573
  64.5 21.4 %collective-permute-start.17 = (bf16[288,768]{1,0:T(8,128)(2,1)S(1)}, bf16[288,768]{1,0:T(8,128)(2,1)S(1)}, u32[]{:S(2)}, u32[]{:S(2)}) collective-permute-start(bf16[288,768]{1,0:T(8,128)(2,1)S(1)} %get-tuple-element.185.near_ref), channel_id=1, source_target_pairs={{0,24},{8,16},{16,8},{24,0},{1,25},{9,17},{17,9},{25,1},{2,26},{10... | collective-permute-start | bytes 1327112 | tf_op jit(solution)/shard_map/ppermute | solution.py:561
  65.3 20.6 %collective-permute-start.13 = (bf16[2,128,768]{2,1,0:T(8,128)(2,1)S(1)}, bf16[2,128,768]{2,1,0:T(8,128)(2,1)S(1)}, u32[]{:S(2)}, u32[]{:S(2)}) collective-permute-start(bf16[2,128,768]{2,1,0:T(8,128)(2,1)S(1)} %get-tuple-element.182.near_ref), channel_id=1, source_target_pairs={{0,2},{1,3},{2,4},{3,5},{4,6},{5,7},{6,14},{7,15},{14,12},{15,13},... | collective-permute-start | bytes 1179656 | tf_op jit(solution)/shard_map/ppermute | solution.py:586
  67.3 19.4 %collective-permute-start.18 = (bf16[2,128,768]{2,1,0:T(8,128)(2,1)S(1)}, bf16[2,128,768]{2,1,0:T(8,128)(2,1)S(1)}, u32[]{:S(2)}, u32[]{:S(2)}) collective-permute-start(bf16[2,128,768]{2,1,0:T(8,128)(2,1)S(1)} %get-tuple-element.182.near_ref), channel_id=1, source_target_pairs={{2,0},{3,1},{4,2},{5,3},{6,4},{7,5},{14,6},{15,7},{12,14},{13,15},... | collective-permute-start | bytes 1179656 | tf_op jit(solution)/shard_map/ppermute | solution.py:589
  99.0 18.1 %collective-permute-start.31 = (bf16[256,768]{1,0:T(8,128)(2,1)S(1)}, bf16[256,768]{1,0:T(8,128)(2,1)S(1)}, u32[]{:S(2)}, u32[]{:S(2)}) collective-permute-start(bf16[256,768]{1,0:T(8,128)(2,1)S(1)} %join_given.1), channel_id=1, source_target_pairs={{0,8},{1,17},{2,10},{3,19},{4,12},{5,21},{6,14},{7,23},{8,0},{9,25... | collective-permute-start | bytes 1179656 | tf_op jit(solution)/shard_map/ppermute | solution.py:569
  105.2 17.5 %collective-permute-start.28 = (bf16[256,768]{1,0:T(8,128)(2,1)S(1)}, bf16[256,768]{1,0:T(8,128)(2,1)S(1)}, u32[]{:S(2)}, u32[]{:S(2)}) collective-permute-start(bf16[256,768]{1,0:T(8,128)(2,1)S(1)} %get-tuple-element.202), channel_id=1, source_target_pairs={{0,24},{8,16},{16,8},{24,0},{1,25},{9,17},{17,9},{25,1},{2,26},{10... | collective-permute-start | bytes 1179656 | tf_op jit(solution)/shard_map/ppermute | solution.py:561
  109.8 12.9 %collective-permute-start.27 = (bf16[128,768]{1,0:T(8,128)(2,1)S(1)}, bf16[128,768]{1,0:T(8,128)(2,1)S(1)}, u32[]{:S(2)}, u32[]{:S(2)}) collective-permute-start(bf16[128,768]{1,0:T(8,128)(2,1)S(1)} %get-tuple-element.201.a0), channel_id=1, source_target_pairs={{0,16},{8,24},{16,0},{24,8},{1,17},{9,25},{17,1},{25,9},{2,18},{10... | collective-permute-start | bytes 589832 | tf_op jit(solution)/shard_map/ppermute | solution.py:561
  157.9 16.8 %collective-permute-start.52 = (bf16[1536,384]{1,0:T(8,128)(2,1)S(1)}, bf16[1536,384]{1,0:T(8,128)(2,1)S(1)}, u32[]{:S(2)}, u32[]{:S(2)}) collective-permute-start(bf16[1536,384]{1,0:T(8,128)(2,1)S(1)} %get-tuple-element.272), channel_id=1, source_target_pairs={{0,1},{1,0},{2,3},{3,2},{4,5},{5,4},{6,7},{7,6},{8,9},{9,8},{10,11... | collective-permute-start | bytes 3538952 | tf_op jit(solution)/shard_map/ppermute | solution.py:558
  158.1 13.3 %collective-permute-start.46 = (bf16[2,128,768]{2,1,0:T(8,128)(2,1)S(1)}, bf16[2,128,768]{2,1,0:T(8,128)(2,1)S(1)}, u32[]{:S(2)}, u32[]{:S(2)}) collective-permute-start(bf16[2,128,768]{2,1,0:T(8,128)(2,1)S(1)} %get-tuple-element.248), channel_id=1, source_target_pairs={{2,0},{3,1},{4,2},{5,3},{6,4},{7,5},{14,6},{15,7},{12,14},{13,15},... | collective-permute-start | bytes 1179656 | tf_op jit(solution)/shard_map/ppermute | solution.py:589
  159.4 13.2 %collective-permute-start.47 = (bf16[2,128,768]{2,1,0:T(8,128)(2,1)S(1)}, bf16[2,128,768]{2,1,0:T(8,128)(2,1)S(1)}, u32[]{:S(2)}, u32[]{:S(2)}) collective-permute-start(bf16[2,128,768]{2,1,0:T(8,128)(2,1)S(1)} %get-tuple-element.249), channel_id=1, source_target_pairs={{0,2},{1,3},{2,4},{3,5},{4,6},{5,7},{6,14},{7,15},{14,12},{15,13},... | collective-permute-start | bytes 1179656 | tf_op jit(solution)/shard_map/ppermute | solution.py:586
  164.3 38.6 %collective-permute-start.42 = (bf16[1024,384]{1,0:T(8,128)(2,1)S(1)}, bf16[1024,384]{1,0:T(8,128)(2,1)S(1)}, u32[]{:S(2)}, u32[]{:S(2)}) collective-permute-start(bf16[1024,384]{1,0:T(8,128)(2,1)S(1)} %get-tuple-element.238), channel_id=1, source_target_pairs={{0,8},{8,0},{16,24},{24,16},{1,9},{9,1},{17,25},{25,17},{2,10},{10... | collective-permute-start | bytes 2359304 | tf_op jit(solution)/shard_map/ppermute | solution.py:561
  166.5 36.4 %collective-permute-start.43 = (bf16[1024,384]{1,0:T(8,128)(2,1)S(1)}, bf16[1024,384]{1,0:T(8,128)(2,1)S(1)}, u32[]{:S(2)}, u32[]{:S(2)}) collective-permute-start(bf16[1024,384]{1,0:T(8,128)(2,1)S(1)} %get-tuple-element.239), channel_id=1, source_target_pairs={{0,16},{8,24},{16,0},{24,8},{1,17},{9,25},{17,1},{25,9},{2,18},{10... | collective-permute-start | bytes 2359304 | tf_op jit(solution)/shard_map/ppermute | solution.py:561
  171.4 31.5 %collective-permute-start.44 = (bf16[1024,384]{1,0:T(8,128)(2,1)S(1)}, bf16[1024,384]{1,0:T(8,128)(2,1)S(1)}, u32[]{:S(2)}, u32[]{:S(2)}) collective-permute-start(bf16[1024,384]{1,0:T(8,128)(2,1)S(1)} %get-tuple-element.240), channel_id=1, source_target_pairs={{0,24},{8,16},{16,8},{24,0},{1,25},{9,17},{17,9},{25,1},{2,26},{10... | collective-permute-start | bytes 2359304 | tf_op jit(solution)/shard_map/ppermute | solution.py:561
  175.9 15.2 %collective-permute-start.53 = (bf16[384,384]{1,0:T(8,128)(2,1)S(1)}, bf16[384,384]{1,0:T(8,128)(2,1)S(1)}, u32[]{:S(2)}, u32[]{:S(2)}) collective-permute-start(bf16[384,384]{1,0:T(8,128)(2,1)S(1)} %get-tuple-element.274), channel_id=1, source_target_pairs={{0,2},{1,3},{2,0},{3,1},{4,6},{5,7},{6,4},{7,5},{8,10},{9,11},{10,... | collective-permute-start | bytes 884744 | tf_op jit(solution)/shard_map/ppermute | solution.py:555
  178.5 18.2 %collective-permute-start.54 = (bf16[384,384]{1,0:T(8,128)(2,1)S(1)}, bf16[384,384]{1,0:T(8,128)(2,1)S(1)}, u32[]{:S(2)}, u32[]{:S(2)}) collective-permute-start(bf16[384,384]{1,0:T(8,128)(2,1)S(1)} %get-tuple-element.275), channel_id=1, source_target_pairs={{0,4},{1,5},{2,6},{3,7},{4,0},{5,1},{6,2},{7,3},{8,12},{9,13},{10,... | collective-permute-start | bytes 884744 | tf_op jit(solution)/shard_map/ppermute | solution.py:555
  202.9 36.0 %collective-permute-start.56 = (bf16[784,384]{1,0:T(8,128)(2,1)S(1)}, bf16[784,384]{1,0:T(8,128)(2,1)S(1)}, u32[]{:S(2)}, u32[]{:S(2)}) collective-permute-start(bf16[784,384]{1,0:T(8,128)(2,1)S(1)} %get-tuple-element.278), channel_id=1, source_target_pairs={{0,8},{8,0},{16,24},{24,16},{1,9},{9,1},{17,25},{25,17},{2,10},{10... | collective-permute-start | bytes 1806344 | tf_op jit(solution)/shard_map/ppermute | solution.py:561
  208.8 31.3 %collective-permute-start.57 = (bf16[784,384]{1,0:T(8,128)(2,1)S(1)}, bf16[784,384]{1,0:T(8,128)(2,1)S(1)}, u32[]{:S(2)}, u32[]{:S(2)}) collective-permute-start(bf16[784,384]{1,0:T(8,128)(2,1)S(1)} %get-tuple-element.279), channel_id=1, source_target_pairs={{0,16},{8,24},{16,0},{24,8},{1,17},{9,25},{17,1},{25,9},{2,18},{10... | collective-permute-start | bytes 1806344 | tf_op jit(solution)/shard_map/ppermute | solution.py:561
  210.7 29.4 %collective-permute-start.58 = (bf16[784,384]{1,0:T(8,128)(2,1)S(1)}, bf16[784,384]{1,0:T(8,128)(2,1)S(1)}, u32[]{:S(2)}, u32[]{:S(2)}) collective-permute-start(bf16[784,384]{1,0:T(8,128)(2,1)S(1)} %get-tuple-element.280), channel_id=1, source_target_pairs={{0,24},{8,16},{16,8},{24,0},{1,25},{9,17},{17,9},{25,1},{2,26},{10... | collective-permute-start | bytes 1806344 | tf_op jit(solution)/shard_map/ppermute | solution.py:561
  214.9 18.8 %collective-permute-start.49 = (bf16[320,384]{1,0:T(8,128)(2,1)S(1)}, bf16[320,384]{1,0:T(8,128)(2,1)S(1)}, u32[]{:S(2)}, u32[]{:S(2)}) collective-permute-start(bf16[320,384]{1,0:T(8,128)(2,1)S(1)} %get-tuple-element.262), channel_id=1, source_target_pairs={{0,4},{1,5},{2,6},{3,7},{4,0},{5,1},{6,2},{7,3},{8,12},{9,13},{10,... | collective-permute-start | bytes 737288 | tf_op jit(solution)/shard_map/ppermute | solution.py:555
  236.4 32.0 %collective-permute-start.68 = (bf16[288,768]{1,0:T(8,128)(2,1)S(1)}, bf16[288,768]{1,0:T(8,128)(2,1)S(1)}, u32[]{:S(2)}, u32[]{:S(2)}) collective-permute-start(bf16[288,768]{1,0:T(8,128)(2,1)S(1)} %join_two.1.u0), channel_id=1, source_target_pairs={{0,8},{8,0},{16,24},{24,16},{1,9},{9,1},{17,25},{25,17},{2,10},{10... | collective-permute-start | bytes 1327112 | tf_op jit(solution)/shard_map/ppermute | solution.py:561
  237.8 31.9 %collective-permute-start.69 = (bf16[288,768]{1,0:T(8,128)(2,1)S(1)}, bf16[288,768]{1,0:T(8,128)(2,1)S(1)}, u32[]{:S(2)}, u32[]{:S(2)}) collective-permute-start(bf16[288,768]{1,0:T(8,128)(2,1)S(1)} %join_two.1.u0), channel_id=1, source_target_pairs={{0,16},{8,24},{16,0},{24,8},{1,17},{9,25},{17,1},{25,9},{2,18},{10... | collective-permute-start | bytes 1327112 | tf_op jit(solution)/shard_map/ppermute | solution.py:561
  238.9 30.9 %collective-permute-start.70 = (bf16[288,768]{1,0:T(8,128)(2,1)S(1)}, bf16[288,768]{1,0:T(8,128)(2,1)S(1)}, u32[]{:S(2)}, u32[]{:S(2)}) collective-permute-start(bf16[288,768]{1,0:T(8,128)(2,1)S(1)} %join_two.1.u0), channel_id=1, source_target_pairs={{0,24},{8,16},{16,8},{24,0},{1,25},{9,17},{17,9},{25,1},{2,26},{10... | collective-permute-start | bytes 1327112 | tf_op jit(solution)/shard_map/ppermute | solution.py:561
  245.9 14.2 %collective-permute-start.60 = (bf16[208,384]{1,0:T(8,128)(2,1)S(1)}, bf16[208,384]{1,0:T(8,128)(2,1)S(1)}, u32[]{:S(2)}, u32[]{:S(2)}) collective-permute-start(bf16[208,384]{1,0:T(8,128)(2,1)S(1)} %get-tuple-element.283), channel_id=1, source_target_pairs={{0,4},{1,5},{2,6},{3,7},{4,0},{5,1},{6,2},{7,3},{8,12},{9,13},{10,... | collective-permute-start | bytes 479240 | tf_op jit(solution)/shard_map/ppermute | solution.py:555
  (47 other events, 318.5 us)

commit v4 on v3

--- a/solution.py
+++ b/solution.py
@@ -831,7 +831,6 @@
     col_plane, col_pair, col_diagonal = spread_plane(col_hops, along_core(col_hops))
 
     feed_pair = pair_chips(after(feed_both, row_q))
-    kv_left = after(kv_left, feed_pair, col_pair, col_diagonal)
 
     def tied_logits(spot_ref, q_ref, near_ref, left_ref, right_ref, out_ref):
         mask = head_mask(width, model)
@@ -926,7 +925,7 @@
         smem=(0,),
     )
 
-    col_last = after((col_pair, col_diagonal), normed_two)
+    col_last = after((col_pair, col_diagonal), normed_two, feed_pair)
     col_pieces = [col_own, col_far_own, col_plane, col_pair, col_diagonal] + [
         along_core(item) for item in col_last
     ]
@@ -943,18 +942,18 @@
         smem=(0,),
     )
 
-    def project_col(low_ref, weight_ref, q_ref, kv_ref):
+    def project_col(low_ref, weight_ref, q_ref, k_ref, v_ref):
         low = low_ref[...]
         q_ref[...] = dot(low, weight_ref[0]).astype(bf16)
-        kv_ref[0] = dot(low, weight_ref[1]).astype(bf16)
-        kv_ref[1] = dot(low, weight_ref[2]).astype(bf16)
-
-    col_q, col_kv = kernel_call(
+        k_ref[...] = dot(low, weight_ref[1]).astype(bf16)
+        v_ref[...] = dot(low, weight_ref[2]).astype(bf16)
+
+    col_q, col_k, col_v = kernel_call(
         project_col,
-        [((toks, model), bf16), ((2, toks, model), bf16)],
+        [((toks, model), bf16)] * 3,
         [normed_two, weights_three],
     )
-    kv_other = along_core(col_kv)
+    k_other, v_other = along_core(col_k), along_core(col_v)
 
     def join_given(near_ref, far_ref, out_ref):
         out_ref[:toks] = near_ref[...]
@@ -968,8 +967,10 @@
 
     def attend_col(
         q_ref,
-        near_ref,
-        far_ref,
+        k_ref,
+        v_ref,
+        k2_ref,
+        v2_ref,
         one_ref,
         norm_ref,
         weight_ref,
@@ -981,12 +982,12 @@
         message_ref,
     ):
         lane_heads = head_of_lane(model)
-        sides = (near_ref, far_ref)
+        sides = ((k_ref, v_ref), (k2_ref, v2_ref))
         for slot in range(chips):
             query = q_ref[slot_rows(slot)].astype(f32)
             products = jnp.concatenate(
                 [
-                    query * sides[s // chips][0, slot_rows(s % chips)].astype(f32)
+                    query * sides[s // chips][0][slot_rows(s % chips)].astype(f32)
                     for s in range(seqs)
                 ],
                 axis=0,
@@ -1005,8 +1006,8 @@
             wide = dot_back(weights.astype(bf16), lane_heads)
             mixed = None
             for s in range(seqs):
-                term = wide[s * width : (s + 1) * width] * sides[s // chips][
-                    1, slot_rows(s % chips)
+                term = wide[s * width : (s + 1) * width] * sides[s // chips][1][
+                    slot_rows(s % chips)
                 ].astype(f32)
                 mixed = term if mixed is None else mixed + term
             mix_ref[slot_rows(slot)] = mixed.astype(bf16)
@@ -1027,7 +1028,7 @@
             ((toks, model), bf16),
             ((2 * toks, model), bf16),
         ],
-        [col_q, col_kv, kv_other, stream_one, norm_rows, weights_last, given_out],
+        [col_q, col_k, col_v, k_other, v_other, stream_one, norm_rows, weights_last, given_out],
     )
     low_near = [
         normed_three,
@@ -1266,8 +1267,10 @@
         norm_ref,
         weight_ref,
         q_ref,
-        near_ref,
-        far_ref,
+        k_ref,
+        v_ref,
+        k2_ref,
+        v2_ref,
         probs_ref,
         dtwo_ref,
         low_ref,
@@ -1287,13 +1290,13 @@
         low_ref[...] = low
         dmix = dot_back(low, weight_ref[...]).astype(bf16).astype(f32)
         wide_ref[...] = jnp.zeros_like(wide_ref)
-        sides = (near_ref, far_ref)
+        sides = ((k_ref, v_ref), (k2_ref, v2_ref))
         for slot in range(chips):
             dout = dmix[slot_rows(slot)]
             query = q_ref[slot_rows(slot)].astype(f32)
             products = jnp.concatenate(
                 [
-                    dout * sides[s // chips][1, slot_rows(s % chips)].astype(f32)
+                    dout * sides[s // chips][1][slot_rows(s % chips)].astype(f32)
                     for s in range(seqs)
                 ],
                 axis=0,
@@ -1311,7 +1314,7 @@
             dquery = None
             for s in range(seqs):
                 rows = slice(s * width, (s + 1) * width)
-                term = wide_d[rows] * sides[s // chips][0, slot_rows(s % chips)].astype(f32)
+                term = wide_d[rows] * sides[s // chips][0][slot_rows(s % chips)].astype(f32)
                 dquery = term if dquery is None else dquery + term
                 wide_ref[0, rows] += wide_d[rows] * query
                 wide_ref[1, rows] += wide_p[rows] * dout
@@ -1339,8 +1342,10 @@
             norm_rows,
             weights_last,
             col_q,
-            col_kv,
-            kv_other,
+            col_k,
+            col_v,
+            k_other,
+            v_other,
             col_probs,
         ],
         smem=(0,),
@@ -1433,16 +1438,6 @@
         smem=(0,),
     )
     dprobs_other = along_core(dprobs)
-    col_sums = layer_grads(
-        normed_two,
-        col_mix,
-        col_low_far,
-        col_mix_far,
-        col_mine,
-        along_core(col_give),
-        out_parts,
-    )
-    dprobs_other = after(dprobs_other, col_sums)
 
     def attend_row_back(
         spot_ref,
@@ -1505,6 +1500,15 @@
             row_dmix,
         ],
         smem=(0,),
+    )
+    col_sums = layer_grads(
+        normed_two,
+        col_mix,
+        col_low_far,
+        col_mix_far,
+        col_mine,
+        after(along_core(col_give), edge_left),
+        out_parts,
     )
     edge_from_right = to_left(edge_left)
     edge_from_left = to_right(edge_right)
@@ -1670,7 +1674,7 @@
         [spot, row_keep, along_core(row_swap)],
         smem=(0,),
     )
-    row_ends = over_cols(row_join)
+    row_ends = over_cols(after(row_join, pair_ends))
     result = order_rows(after(col_reached, row_join), block)
     grad_in = order_rows(after(col_reached, row_join), block + 2 * width)
     grad_feed_in, grad_feed_out, *col_grads = kernel_call(

time: 278 us -> 271 us (0.975)
  starting transfers between devices: 86.3 us -> 81.1 us
    ppermute x16, waiting for transfers between devices: 56.6 us -> 60.8 us  [along_chips(): return lax.ppermute(values, 'seq', [(i, i ^ 2 * step) for i in range(seqs)])]
    ppermute x2, waiting for transfers between devices: 18.3 us -> 15 us  [to_right(): return lax.ppermute(values, ('col', 'seq'), rightward)]
    ppermute x2, waiting for transfers between devices: 5.66 us -> 2.35 us  [to_left(): return lax.ppermute(values, ('col', 'seq'), leftward)]
    ppermute x3, starting transfers between devices: 7.1 us -> 4.21 us  [pair_cols(): return lax.ppermute(values, ('col', 'seq'), pairs)]
    ppermute x27 -> x28, waiting for transfers between devices: 19.6 us -> 19.1 us  [along_core(): return lax.ppermute(values, 'seq', [(i, i ^ 1) for i in range(seqs)])]
    ppermute x27 -> x28, starting transfers between devices: 5.36 us -> 5.82 us  [along_core(): return lax.ppermute(values, 'seq', [(i, i ^ 1) for i in range(seqs)])]
  transfers between devices with their start and end apart: 71 -> 72, of which waited for: 34 -> 36; matrix products, arithmetic and copies ran while one was open for 2% -> 2% of each run, Pallas kernels for 10% -> 12%
where the time goes in v4:
time: 271 us
  waiting for transfers between devices  127 us (47%)
  starting transfers between devices  81.1 us (30%)
  Pallas kernels  52 us (19%)
  between operations  4.38 us (2%)
  local copies, waits for them, and re-layouts  3.01 us (1%)
  other arithmetic  2.96 us (1%)
    ppermute x16, waiting for transfers between devices, along_chips(): return lax.ppermute(values, 'seq', [(i, i ^ 2 * step) for i in range(seqs)])  60.8 us
    pallas_call x35, Pallas kernels, kernel_call(): pl.pallas_call(body, grid=(1,) if stream else (), out_shape=out_shapes, i...  52 us
    ppermute x20, waiting for transfers between devices, along_cols(): lax.ppermute(values, 'col', [(i, i ^ step) for i in range(cols_axis)])  30.2 us
    ppermute x16, starting transfers between devices, along_chips(): return lax.ppermute(values, 'seq', [(i, i ^ 2 * step) for i in range(seqs)])  29 us
    ppermute x20, starting transfers between devices, along_cols(): lax.ppermute(values, 'col', [(i, i ^ step) for i in range(cols_axis)])  27.9 us
    ppermute x28, waiting for transfers between devices, along_core(): return lax.ppermute(values, 'seq', [(i, i ^ 1) for i in range(seqs)])  19.1 us
    ppermute x2, waiting for transfers between devices, to_right(): return lax.ppermute(values, ('col', 'seq'), rightward)  15 us
    ppermute x2, starting transfers between devices, to_right(): return lax.ppermute(values, ('col', 'seq'), rightward)  6.49 us
  transfers between devices with their start and end apart: 72, of which 36 were waited for; matrix products, arithmetic and copies ran while one was open for 2% of the time, Pallas kernels for 12%

profile of v4, /device:TPU:0, one launch (start us, length us, event | category | flops | bytes accessed | tf_op | source)
XLA Modules:
  0.0 270.8 jit_solution(6566731438128046355)
XLA Ops:
  4.1 3.0 %collective-permute-start = (bf16[104,768]{1,0:T(8,128)(2,1)}, bf16[104,768]{1,0:T(8,128)(2,1)S(1)}, u32[]{:S(2)}, u32[]{:S(2)}) collective-permute-start(bf16[104,768]{1,0:T(8,128)(2,1)} %get-tuple-element.170), channel_id=1, source_target_pairs={{0,2},{1,3},{2,0},{3,1},{4,6},{5,7},{6,4},{7,5},{8,10},{9,11},{10,... | collective-permute-start | bytes 479240 | tf_op jit(solution)/shard_map/ppermute | solution.py:555
  7.1 2.6 collective-permute-start.1
  14.1 3.2 %pack_rest.1 = (bf16[2,96,768]{2,1,0:T(8,128)(2,1)}, bf16[384,768]{1,0:T(8,128)(2,1)}, bf16[64,768]{1,0:T(8,128)(2,1)}, bf16[160,768]{1,0:T(8,128)(2,1)}, bf16[1...) custom-call(s32[7]{0:T(128)} %stack.42.spot_ref, bf16[96,768]{1,0:T(8,128)(2,1)} %refs_0_.2, bf16[96,768]{1,0:T(8,128)(2,1)} %refs_1_.2, ...), custom_call_target="tpu_custom_call" | custom-call | flops 1 | bytes 1 | tf_op jit(solution)/shard_map/pack_rest/pallas_call | solution.py:415
  17.3 4.8 %collective-permute-done.1.refs_1_ = bf16[104,768]{1,0:T(8,128)(2,1)S(1)} collective-permute-done((bf16[104,768]{1,0:T(8,128)(2,1)}, bf16[104,768]{1,0:T(8,128)(2,1)S(1)}, u32[]{:S(2)}, u32[]{:S(2)}) %collective-permute-start.1) | collective-permute-done | bytes 159776 | tf_op jit(solution)/shard_map/ppermute | solution.py:555
  27.3 2.6 collective-permute-start.4
  32.5 16.9 %collective-permute-done.9.refs_8_ = bf16[312,768]{1,0:T(8,128)(2,1)S(1)} collective-permute-done((bf16[312,768]{1,0:T(8,128)(2,1)S(1)}, bf16[312,768]{1,0:T(8,128)(2,1)S(1)}, u32[]{:S(2)}, u32[]{:S(2)}) %collective-permute-start.9) | collective-permute-done | bytes 479264 | tf_op jit(solution)/shard_map/ppermute | solution.py:561
  50.7 2.8 %collective-permute-done.7.refs_5_ = bf16[392,768]{1,0:T(8,128)(2,1)S(1)} collective-permute-done((bf16[392,768]{1,0:T(8,128)(2,1)S(1)}, bf16[392,768]{1,0:T(8,128)(2,1)S(1)}, u32[]{:S(2)}, u32[]{:S(2)}) %collective-permute-start.7) | collective-permute-done | bytes 602144 | tf_op jit(solution)/shard_map/ppermute | solution.py:558
  59.7 4.9 %collective-permute-start.20 = (bf16[2,2,96,768]{3,2,1,0:T(8,128)(2,1)S(1)}, bf16[2,2,96,768]{3,2,1,0:T(8,128)(2,1)S(1)}, u32[]{:S(2)}, u32[]{:S(2)}) collective-permute-start(bf16[2,2,96,768]{3,2,1,0:T(8,128)(2,1)S(1)} %pair_feed.1.both_ref), channel_id=1, source_target_pairs={{0,2},{1,5},{2,0},{3,7},{4,6},{5,1},{6,4},{7,3},{8,10},{9,13},{10,... | collective-permute-start | bytes 1769480 | tf_op jit(solution)/shard_map/ppermute | solution.py:573
  67.9 3.5 %collective-permute-start.19 = (bf16[288,768]{1,0:T(8,128)(2,1)S(1)}, bf16[288,768]{1,0:T(8,128)(2,1)S(1)}, u32[]{:S(2)}, u32[]{:S(2)}) collective-permute-start(bf16[288,768]{1,0:T(8,128)(2,1)S(1)} %get-tuple-element.190.near_ref), channel_id=1, source_target_pairs={{0,24},{8,16},{16,8},{24,0},{1,25},{9,17},{17,9},{25,1},{2,26},{10... | collective-permute-start | bytes 1327112 | tf_op jit(solution)/shard_map/ppermute | solution.py:561
  71.4 14.5 %collective-permute-done.13.left_ref = bf16[2,128,768]{2,1,0:T(8,128)(2,1)S(1)} collective-permute-done((bf16[2,128,768]{2,1,0:T(8,128)(2,1)S(1)}, bf16[2,128,768]{2,1,0:T(8,128)(2,1)S(1)}, u32[]{:S(2)}, u32[]{:S(2)}) %collective-permute-start.13) | collective-permute-done | bytes 393248 | tf_op jit(solution)/shard_map/ppermute | solution.py:586
  92.6 2.2 collective-permute-done.16.refs_1_
  98.8 2.2 attend_col.1
  105.9 7.2 %collective-permute-done.30.last_ref = bf16[2,96,768]{2,1,0:T(8,128)(2,1)S(1)} collective-permute-done((bf16[2,96,768]{2,1,0:T(8,128)(2,1)S(1)}, bf16[2,96,768]{2,1,0:T(8,128)(2,1)S(1)}, u32[]{:S(2)}, u32[]{:S(2)}) %collective-permute-start.30) | collective-permute-done | bytes 294944 | tf_op jit(solution)/shard_map/ppermute | solution.py:555
  113.1 5.0 %collective-permute-done.27.a1 = bf16[128,768]{1,0:T(8,128)(2,1)S(1)} collective-permute-done((bf16[128,768]{1,0:T(8,128)(2,1)S(1)}, bf16[128,768]{1,0:T(8,128)(2,1)S(1)}, u32[]{:S(2)}, u32[]{:S(2)}) %collective-permute-start.27) | collective-permute-done | bytes 196640 | tf_op jit(solution)/shard_map/ppermute | solution.py:561
  119.0 2.5 collective-permute-done.34.last2_ref
  122.3 3.7 %feed_main.1 = (bf16[4,128,768]{2,1,0:T(8,128)(2,1)S(1)}, bf16[4,128,768]{2,1,0:T(8,128)(2,1)S(1)}, bf16[128,768]{1,0:T(8,128)(2,1)S(1)}, bf16[128,768]{1,0:T(8,...) custom-call(bf16[128,768]{1,0:T(8,128)(2,1)S(1)} %get-tuple-element.202.a0, ...), custom_call_target="tpu_custom_call" | custom-call | flops 1 | bytes 1 | tf_op jit(solution)/shard_map/feed_main/pallas_call | solution.py:415
  129.5 3.0 %feed_weights.1 = (bf16[1536,384]{1,0:T(8,128)(2,1)S(1)}, bf16[1536,384]{1,0:T(8,128)(2,1)S(1)}, bf16[128,768]{1,0:T(8,128)(2,1)S(1)}, bf16[128,768]{1,0:T(8,128...) custom-call(s32[7]{0:T(128)S(1)} %copy-done.3, bf16[128,768]{1,0:T(8,128)(2,1)S(1)} %get-tuple-element.202.a0, ...), custom_call_target="tpu_custom_call" | custom-call | flops 1811939328 | bytes 16777216 | tf_op jit(solution)/shard_map/feed_weights/pallas_call | solution.py:415
  133.8 4.0 %collective-permute-done.37.b2 = bf16[128,768]{1,0:T(8,128)(2,1)S(1)} collective-permute-done((bf16[128,768]{1,0:T(8,128)(2,1)S(1)}, bf16[128,768]{1,0:T(8,128)(2,1)S(1)}, u32[]{:S(2)}, u32[]{:S(2)}) %collective-permute-start.37) | collective-permute-done | bytes 196640 | tf_op jit(solution)/shard_map/ppermute | solution.py:561
  137.8 3.8 %attend_col_back.1 = (f32[128,768]{1,0:T(8,128)S(1)}, bf16[128,768]{1,0:T(8,128)(2,1)S(1)}, bf16[128,768]{1,0:T(8,128)(2,1)S(1)}, f32[2,128,768]{2,1,0:T(8,128)S...) custom-call(s32[7]{0:T(128)S(1)} %copy-done.3, bf16[128,768]{1,0:T(8,128)(2,1)S(1)} %get-tuple-element.218.b0, ...), custom_call_target="tpu_custom_call" | custom-call | flops 1 | bytes 1 | tf_op jit(solution)/shard_map/attend_col_back/pallas_call | solution.py:415
  144.0 3.6 %row_entry_back.1 = (bf16[4,128,384]{2,1,0:T(8,128)(2,1)S(1)}, bf16[4,128,384]{2,1,0:T(8,128)(2,1)S(1)}, f32[128,768]{1,0:T(8,128)S(1)}, bf16[128,768]{1,0:T(8,1...) custom-call(s32[7]{0:T(128)S(1)} %copy-done.3, ...), custom_call_target="tpu_custom_call" | custom-call | flops 1 | bytes 1 | tf_op jit(solution)/shard_map/row_entry_back/pallas_call | solution.py:415
  149.0 2.2 attend_row_back.1
  153.2 4.6 %collective-permute-start.48 = (bf16[2,128,768]{2,1,0:T(8,128)(2,1)S(1)}, bf16[2,128,768]{2,1,0:T(8,128)(2,1)S(1)}, u32[]{:S(2)}, u32[]{:S(2)}) collective-permute-start(bf16[2,128,768]{2,1,0:T(8,128)(2,1)S(1)} %get-tuple-element.250), channel_id=1, source_target_pairs={{0,2},{1,3},{2,4},{3,5},{4,6},{5,7},{6,14},{7,15},{14,12},{15,13},... | collective-permute-start | bytes 1179656 | tf_op jit(solution)/shard_map/ppermute | solution.py:586
  169.4 2.5 collective-permute-start.54
  173.8 12.1 %collective-permute-done.54.refs_1_ = bf16[384,384]{1,0:T(8,128)(2,1)S(1)} collective-permute-done((bf16[384,384]{1,0:T(8,128)(2,1)S(1)}, bf16[384,384]{1,0:T(8,128)(2,1)S(1)}, u32[]{:S(2)}, u32[]{:S(2)}) %collective-permute-start.54) | collective-permute-done | bytes 294944 | tf_op jit(solution)/shard_map/ppermute | solution.py:555
  189.3 7.3 %collective-permute-done.56.refs_3_ = bf16[384,384]{1,0:T(8,128)(2,1)S(1)} collective-permute-done((bf16[384,384]{1,0:T(8,128)(2,1)S(1)}, bf16[384,384]{1,0:T(8,128)(2,1)S(1)}, u32[]{:S(2)}, u32[]{:S(2)}) %collective-permute-start.56) | collective-permute-done | bytes 294944 | tf_op jit(solution)/shard_map/ppermute | solution.py:555
  199.6 2.9 %collective-permute-start.57 = (bf16[784,384]{1,0:T(8,128)(2,1)S(1)}, bf16[784,384]{1,0:T(8,128)(2,1)S(1)}, u32[]{:S(2)}, u32[]{:S(2)}) collective-permute-start(bf16[784,384]{1,0:T(8,128)(2,1)S(1)} %get-tuple-element.279), channel_id=1, source_target_pairs={{0,8},{8,0},{16,24},{24,16},{1,9},{9,1},{17,25},{25,17},{2,10},{10... | collective-permute-start | bytes 1806344 | tf_op jit(solution)/shard_map/ppermute | solution.py:561
  208.6 9.3 %collective-permute-done.49.refs_1_ = bf16[320,384]{1,0:T(8,128)(2,1)S(1)} collective-permute-done((bf16[320,384]{1,0:T(8,128)(2,1)S(1)}, bf16[320,384]{1,0:T(8,128)(2,1)S(1)}, u32[]{:S(2)}, u32[]{:S(2)}) %collective-permute-start.49) | collective-permute-done | bytes 245792 | tf_op jit(solution)/shard_map/ppermute | solution.py:555
  219.8 7.6 %collective-permute-done.50.refs_2_ = bf16[320,384]{1,0:T(8,128)(2,1)S(1)} collective-permute-done((bf16[320,384]{1,0:T(8,128)(2,1)S(1)}, bf16[320,384]{1,0:T(8,128)(2,1)S(1)}, u32[]{:S(2)}, u32[]{:S(2)}) %collective-permute-start.50) | collective-permute-done | bytes 245792 | tf_op jit(solution)/shard_map/ppermute | solution.py:555
  235.2 4.5 %collective-permute-start.60 = (bf16[208,384]{1,0:T(8,128)(2,1)S(1)}, bf16[208,384]{1,0:T(8,128)(2,1)S(1)}, u32[]{:S(2)}, u32[]{:S(2)}) collective-permute-start(bf16[208,384]{1,0:T(8,128)(2,1)S(1)} %get-tuple-element.283), channel_id=1, source_target_pairs={{0,2},{1,3},{2,0},{3,1},{4,6},{5,7},{6,4},{7,5},{8,10},{9,11},{10,... | collective-permute-start | bytes 479240 | tf_op jit(solution)/shard_map/ppermute | solution.py:555
  240.3 5.0 %collective-permute-done.60.refs_1_ = bf16[208,384]{1,0:T(8,128)(2,1)S(1)} collective-permute-done((bf16[208,384]{1,0:T(8,128)(2,1)S(1)}, bf16[208,384]{1,0:T(8,128)(2,1)S(1)}, u32[]{:S(2)}, u32[]{:S(2)}) %collective-permute-start.60) | collective-permute-done | bytes 159776 | tf_op jit(solution)/shard_map/ppermute | solution.py:555
  247.2 6.6 %collective-permute-done.61.refs_2_ = bf16[208,384]{1,0:T(8,128)(2,1)S(1)} collective-permute-done((bf16[208,384]{1,0:T(8,128)(2,1)S(1)}, bf16[208,384]{1,0:T(8,128)(2,1)S(1)}, u32[]{:S(2)}, u32[]{:S(2)}) %collective-permute-start.61) | collective-permute-done | bytes 159776 | tf_op jit(solution)/shard_map/ppermute | solution.py:555
  264.2 2.8 %spread_pair.1 = (f32[96,3072]{1,0:T(8,128)}, f32[384,768]{1,0:T(8,128)}, f32[96,768]{1,0:T(8,128)}, f32[96,768]{1,0:T(8,128)}, f32[96,768]{1,0:T(8,128)}, /*index=5*/f32[96,768]{1,0:T(8,128)}) custom-call(s32[7]{0:T(128)S(1)} %copy-done.3, bf16[288,768]{1,0:T(8,128)(2,1)S(1)} %join_two.1.u0, bf16[288,768]{1,0:T(8,128)(2,1)S(1)} %collective-permute-done.66.u1, ...), custom_call_target="tpu_custom_call" | custom-call | flops 1 | bytes 1 | tf_op jit(solution)/shard_map/spread_pair/pallas_call | solution.py:415
  (177 shorter events, 102.9 us)
Async XLA Ops:
  4.1 13.2 %collective-permute-start = (bf16[104,768]{1,0:T(8,128)(2,1)}, bf16[104,768]{1,0:T(8,128)(2,1)S(1)}, u32[]{:S(2)}, u32[]{:S(2)}) collective-permute-start(bf16[104,768]{1,0:T(8,128)(2,1)} %get-tuple-element.170), channel_id=1, source_target_pairs={{0,2},{1,3},{2,0},{3,1},{4,6},{5,7},{6,4},{7,5},{8,10},{9,11},{10,... | collective-permute-start | bytes 479240 | tf_op jit(solution)/shard_map/ppermute | solution.py:555
  7.1 15.0 %collective-permute-start.1 = (bf16[104,768]{1,0:T(8,128)(2,1)}, bf16[104,768]{1,0:T(8,128)(2,1)S(1)}, u32[]{:S(2)}, u32[]{:S(2)}) collective-permute-start(bf16[104,768]{1,0:T(8,128)(2,1)} %get-tuple-element.170), channel_id=1, source_target_pairs={{0,4},{1,5},{2,6},{3,7},{4,0},{5,1},{6,2},{7,3},{8,12},{9,13},{10,... | collective-permute-start | bytes 479240 | tf_op jit(solution)/shard_map/ppermute | solution.py:555
  24.2 25.9 %collective-permute-start.8 = (bf16[624,768]{1,0:T(8,128)(2,1)S(1)}, bf16[624,768]{1,0:T(8,128)(2,1)S(1)}, u32[]{:S(2)}, u32[]{:S(2)}) collective-permute-start(bf16[624,768]{1,0:T(8,128)(2,1)S(1)} %join_cores.2.refs_6_), channel_id=1, source_target_pairs={{0,8},{1,17},{2,10},{3,19},{4,12},{5,21},{6,14},{7,23},{8,0},{9,25... | collective-permute-start | bytes 2875400 | tf_op jit(solution)/shard_map/ppermute | solution.py:569
  25.8 23.6 %collective-permute-start.9 = (bf16[312,768]{1,0:T(8,128)(2,1)S(1)}, bf16[312,768]{1,0:T(8,128)(2,1)S(1)}, u32[]{:S(2)}, u32[]{:S(2)}) collective-permute-start(bf16[312,768]{1,0:T(8,128)(2,1)S(1)} %stack_row.1.near_ref), channel_id=1, source_target_pairs={{0,24},{8,16},{16,8},{24,0},{1,25},{9,17},{17,9},{25,1},{2,26},{10... | collective-permute-start | bytes 1437704 | tf_op jit(solution)/shard_map/ppermute | solution.py:561
  27.3 22.1 %collective-permute-start.4 = (bf16[160,768]{1,0:T(8,128)(2,1)S(1)}, bf16[160,768]{1,0:T(8,128)(2,1)S(1)}, u32[]{:S(2)}, u32[]{:S(2)}) collective-permute-start(bf16[160,768]{1,0:T(8,128)(2,1)S(1)} %copy-done.7), channel_id=1, source_target_pairs={{0,2},{1,3},{2,0},{3,1},{4,6},{5,7},{6,4},{7,5},{8,10},{9,11},{10,... | collective-permute-start | bytes 737288 | tf_op jit(solution)/shard_map/ppermute | solution.py:555
  29.9 20.3 %collective-permute-start.5 = (bf16[160,768]{1,0:T(8,128)(2,1)S(1)}, bf16[160,768]{1,0:T(8,128)(2,1)S(1)}, u32[]{:S(2)}, u32[]{:S(2)}) collective-permute-start(bf16[160,768]{1,0:T(8,128)(2,1)S(1)} %copy-done.6), channel_id=1, source_target_pairs={{0,4},{1,5},{2,6},{3,7},{4,0},{5,1},{6,2},{7,3},{8,12},{9,13},{10,... | collective-permute-start | bytes 737288 | tf_op jit(solution)/shard_map/ppermute | solution.py:555
  31.0 19.2 %collective-permute-start.6 = (bf16[160,768]{1,0:T(8,128)(2,1)S(1)}, bf16[160,768]{1,0:T(8,128)(2,1)S(1)}, u32[]{:S(2)}, u32[]{:S(2)}) collective-permute-start(bf16[160,768]{1,0:T(8,128)(2,1)S(1)} %copy-done.5), channel_id=1, source_target_pairs={{0,6},{1,7},{2,4},{3,5},{4,2},{5,3},{6,0},{7,1},{8,14},{9,15},{10,... | collective-permute-start | bytes 737288 | tf_op jit(solution)/shard_map/ppermute | solution.py:555
  58.1 33.4 %collective-permute-start.18 = (bf16[576,768]{1,0:T(8,128)(2,1)S(1)}, bf16[576,768]{1,0:T(8,128)(2,1)S(1)}, u32[]{:S(2)}, u32[]{:S(2)}) collective-permute-start(bf16[576,768]{1,0:T(8,128)(2,1)S(1)} %join_cores.3.refs_2_), channel_id=1, source_target_pairs={{0,8},{1,17},{2,10},{3,19},{4,12},{5,21},{6,14},{7,23},{8,0},{9,25... | collective-permute-start | bytes 2654216 | tf_op jit(solution)/shard_map/ppermute | solution.py:569
  59.7 31.8 %collective-permute-start.20 = (bf16[2,2,96,768]{3,2,1,0:T(8,128)(2,1)S(1)}, bf16[2,2,96,768]{3,2,1,0:T(8,128)(2,1)S(1)}, u32[]{:S(2)}, u32[]{:S(2)}) collective-permute-start(bf16[2,2,96,768]{3,2,1,0:T(8,128)(2,1)S(1)} %pair_feed.1.both_ref), channel_id=1, source_target_pairs={{0,2},{1,5},{2,0},{3,7},{4,6},{5,1},{6,4},{7,3},{8,10},{9,13},{10,... | collective-permute-start | bytes 1769480 | tf_op jit(solution)/shard_map/ppermute | solution.py:573
  64.5 21.4 %collective-permute-start.13 = (bf16[2,128,768]{2,1,0:T(8,128)(2,1)S(1)}, bf16[2,128,768]{2,1,0:T(8,128)(2,1)S(1)}, u32[]{:S(2)}, u32[]{:S(2)}) collective-permute-start(bf16[2,128,768]{2,1,0:T(8,128)(2,1)S(1)} %get-tuple-element.183.near_ref), channel_id=1, source_target_pairs={{0,2},{1,3},{2,4},{3,5},{4,6},{5,7},{6,14},{7,15},{14,12},{15,13},... | collective-permute-start | bytes 1179656 | tf_op jit(solution)/shard_map/ppermute | solution.py:586
  66.4 20.2 %collective-permute-start.14 = (bf16[2,128,768]{2,1,0:T(8,128)(2,1)S(1)}, bf16[2,128,768]{2,1,0:T(8,128)(2,1)S(1)}, u32[]{:S(2)}, u32[]{:S(2)}) collective-permute-start(bf16[2,128,768]{2,1,0:T(8,128)(2,1)S(1)} %get-tuple-element.183.near_ref), channel_id=1, source_target_pairs={{2,0},{3,1},{4,2},{5,3},{6,4},{7,5},{14,6},{15,7},{12,14},{13,15},... | collective-permute-start | bytes 1179656 | tf_op jit(solution)/shard_map/ppermute | solution.py:589
  67.9 23.5 %collective-permute-start.19 = (bf16[288,768]{1,0:T(8,128)(2,1)S(1)}, bf16[288,768]{1,0:T(8,128)(2,1)S(1)}, u32[]{:S(2)}, u32[]{:S(2)}) collective-permute-start(bf16[288,768]{1,0:T(8,128)(2,1)S(1)} %get-tuple-element.190.near_ref), channel_id=1, source_target_pairs={{0,24},{8,16},{16,8},{24,0},{1,25},{9,17},{17,9},{25,1},{2,26},{10... | collective-permute-start | bytes 1327112 | tf_op jit(solution)/shard_map/ppermute | solution.py:561
  97.6 15.5 %collective-permute-start.32 = (bf16[256,768]{1,0:T(8,128)(2,1)S(1)}, bf16[256,768]{1,0:T(8,128)(2,1)S(1)}, u32[]{:S(2)}, u32[]{:S(2)}) collective-permute-start(bf16[256,768]{1,0:T(8,128)(2,1)S(1)} %join_given.1), channel_id=1, source_target_pairs={{0,8},{1,17},{2,10},{3,19},{4,12},{5,21},{6,14},{7,23},{8,0},{9,25... | collective-permute-start | bytes 1179656 | tf_op jit(solution)/shard_map/ppermute | solution.py:569
  101.0 17.6 %collective-permute-start.29 = (bf16[256,768]{1,0:T(8,128)(2,1)S(1)}, bf16[256,768]{1,0:T(8,128)(2,1)S(1)}, u32[]{:S(2)}, u32[]{:S(2)}) collective-permute-start(bf16[256,768]{1,0:T(8,128)(2,1)S(1)} %get-tuple-element.203), channel_id=1, source_target_pairs={{0,24},{8,16},{16,8},{24,0},{1,25},{9,17},{17,9},{25,1},{2,26},{10... | collective-permute-start | bytes 1179656 | tf_op jit(solution)/shard_map/ppermute | solution.py:561
  104.5 13.6 %collective-permute-start.27 = (bf16[128,768]{1,0:T(8,128)(2,1)S(1)}, bf16[128,768]{1,0:T(8,128)(2,1)S(1)}, u32[]{:S(2)}, u32[]{:S(2)}) collective-permute-start(bf16[128,768]{1,0:T(8,128)(2,1)S(1)} %get-tuple-element.202.a0), channel_id=1, source_target_pairs={{0,8},{8,0},{16,24},{24,16},{1,9},{9,1},{17,25},{25,17},{2,10},{10... | collective-permute-start | bytes 589832 | tf_op jit(solution)/shard_map/ppermute | solution.py:561
  105.4 13.1 %collective-permute-start.28 = (bf16[128,768]{1,0:T(8,128)(2,1)S(1)}, bf16[128,768]{1,0:T(8,128)(2,1)S(1)}, u32[]{:S(2)}, u32[]{:S(2)}) collective-permute-start(bf16[128,768]{1,0:T(8,128)(2,1)S(1)} %get-tuple-element.202.a0), channel_id=1, source_target_pairs={{0,16},{8,24},{16,0},{24,8},{1,17},{9,25},{17,1},{25,9},{2,18},{10... | collective-permute-start | bytes 589832 | tf_op jit(solution)/shard_map/ppermute | solution.py:561
  151.3 17.0 %collective-permute-start.53 = (bf16[1536,384]{1,0:T(8,128)(2,1)S(1)}, bf16[1536,384]{1,0:T(8,128)(2,1)S(1)}, u32[]{:S(2)}, u32[]{:S(2)}) collective-permute-start(bf16[1536,384]{1,0:T(8,128)(2,1)S(1)} %get-tuple-element.273), channel_id=1, source_target_pairs={{0,1},{1,0},{2,3},{3,2},{4,5},{5,4},{6,7},{7,6},{8,9},{9,8},{10,11... | collective-permute-start | bytes 3538952 | tf_op jit(solution)/shard_map/ppermute | solution.py:558
  151.9 13.0 %collective-permute-start.47 = (bf16[2,128,768]{2,1,0:T(8,128)(2,1)S(1)}, bf16[2,128,768]{2,1,0:T(8,128)(2,1)S(1)}, u32[]{:S(2)}, u32[]{:S(2)}) collective-permute-start(bf16[2,128,768]{2,1,0:T(8,128)(2,1)S(1)} %get-tuple-element.238), channel_id=1, source_target_pairs={{2,0},{3,1},{4,2},{5,3},{6,4},{7,5},{14,6},{15,7},{12,14},{13,15},... | collective-permute-start | bytes 1179656 | tf_op jit(solution)/shard_map/ppermute | solution.py:589
  153.2 12.9 %collective-permute-start.48 = (bf16[2,128,768]{2,1,0:T(8,128)(2,1)S(1)}, bf16[2,128,768]{2,1,0:T(8,128)(2,1)S(1)}, u32[]{:S(2)}, u32[]{:S(2)}) collective-permute-start(bf16[2,128,768]{2,1,0:T(8,128)(2,1)S(1)} %get-tuple-element.250), channel_id=1, source_target_pairs={{0,2},{1,3},{2,4},{3,5},{4,6},{5,7},{6,14},{7,15},{14,12},{15,13},... | collective-permute-start | bytes 1179656 | tf_op jit(solution)/shard_map/ppermute | solution.py:586
  161.2 36.3 %collective-permute-start.44 = (bf16[1024,384]{1,0:T(8,128)(2,1)S(1)}, bf16[1024,384]{1,0:T(8,128)(2,1)S(1)}, u32[]{:S(2)}, u32[]{:S(2)}) collective-permute-start(bf16[1024,384]{1,0:T(8,128)(2,1)S(1)} %get-tuple-element.245), channel_id=1, source_target_pairs={{0,8},{8,0},{16,24},{24,16},{1,9},{9,1},{17,25},{25,17},{2,10},{10... | collective-permute-start | bytes 2359304 | tf_op jit(solution)/shard_map/ppermute | solution.py:561
  163.3 36.3 %collective-permute-start.45 = (bf16[1024,384]{1,0:T(8,128)(2,1)S(1)}, bf16[1024,384]{1,0:T(8,128)(2,1)S(1)}, u32[]{:S(2)}, u32[]{:S(2)}) collective-permute-start(bf16[1024,384]{1,0:T(8,128)(2,1)S(1)} %get-tuple-element.246), channel_id=1, source_target_pairs={{0,16},{8,24},{16,0},{24,8},{1,17},{9,25},{17,1},{25,9},{2,18},{10... | collective-permute-start | bytes 2359304 | tf_op jit(solution)/shard_map/ppermute | solution.py:561
  164.9 34.6 %collective-permute-start.46 = (bf16[1024,384]{1,0:T(8,128)(2,1)S(1)}, bf16[1024,384]{1,0:T(8,128)(2,1)S(1)}, u32[]{:S(2)}, u32[]{:S(2)}) collective-permute-start(bf16[1024,384]{1,0:T(8,128)(2,1)S(1)} %get-tuple-element.247), channel_id=1, source_target_pairs={{0,24},{8,16},{16,8},{24,0},{1,25},{9,17},{17,9},{25,1},{2,26},{10... | collective-permute-start | bytes 2359304 | tf_op jit(solution)/shard_map/ppermute | solution.py:561
  169.4 16.5 %collective-permute-start.54 = (bf16[384,384]{1,0:T(8,128)(2,1)S(1)}, bf16[384,384]{1,0:T(8,128)(2,1)S(1)}, u32[]{:S(2)}, u32[]{:S(2)}) collective-permute-start(bf16[384,384]{1,0:T(8,128)(2,1)S(1)} %get-tuple-element.275), channel_id=1, source_target_pairs={{0,2},{1,3},{2,0},{3,1},{4,6},{5,7},{6,4},{7,5},{8,10},{9,11},{10,... | collective-permute-start | bytes 884744 | tf_op jit(solution)/shard_map/ppermute | solution.py:555
  172.0 17.3 %collective-permute-start.55 = (bf16[384,384]{1,0:T(8,128)(2,1)S(1)}, bf16[384,384]{1,0:T(8,128)(2,1)S(1)}, u32[]{:S(2)}, u32[]{:S(2)}) collective-permute-start(bf16[384,384]{1,0:T(8,128)(2,1)S(1)} %get-tuple-element.276), channel_id=1, source_target_pairs={{0,4},{1,5},{2,6},{3,7},{4,0},{5,1},{6,2},{7,3},{8,12},{9,13},{10,... | collective-permute-start | bytes 884744 | tf_op jit(solution)/shard_map/ppermute | solution.py:555
  199.6 33.1 %collective-permute-start.57 = (bf16[784,384]{1,0:T(8,128)(2,1)S(1)}, bf16[784,384]{1,0:T(8,128)(2,1)S(1)}, u32[]{:S(2)}, u32[]{:S(2)}) collective-permute-start(bf16[784,384]{1,0:T(8,128)(2,1)S(1)} %get-tuple-element.279), channel_id=1, source_target_pairs={{0,8},{8,0},{16,24},{24,16},{1,9},{9,1},{17,25},{25,17},{2,10},{10... | collective-permute-start | bytes 1806344 | tf_op jit(solution)/shard_map/ppermute | solution.py:561
  203.9 30.1 %collective-permute-start.58 = (bf16[784,384]{1,0:T(8,128)(2,1)S(1)}, bf16[784,384]{1,0:T(8,128)(2,1)S(1)}, u32[]{:S(2)}, u32[]{:S(2)}) collective-permute-start(bf16[784,384]{1,0:T(8,128)(2,1)S(1)} %get-tuple-element.280), channel_id=1, source_target_pairs={{0,16},{8,24},{16,0},{24,8},{1,17},{9,25},{17,1},{25,9},{2,18},{10... | collective-permute-start | bytes 1806344 | tf_op jit(solution)/shard_map/ppermute | solution.py:561
  205.9 28.1 %collective-permute-start.59 = (bf16[784,384]{1,0:T(8,128)(2,1)S(1)}, bf16[784,384]{1,0:T(8,128)(2,1)S(1)}, u32[]{:S(2)}, u32[]{:S(2)}) collective-permute-start(bf16[784,384]{1,0:T(8,128)(2,1)S(1)} %get-tuple-element.281), channel_id=1, source_target_pairs={{0,24},{8,16},{16,8},{24,0},{1,25},{9,17},{17,9},{25,1},{2,26},{10... | collective-permute-start | bytes 1806344 | tf_op jit(solution)/shard_map/ppermute | solution.py:561
  208.6 18.8 %collective-permute-start.50 = (bf16[320,384]{1,0:T(8,128)(2,1)S(1)}, bf16[320,384]{1,0:T(8,128)(2,1)S(1)}, u32[]{:S(2)}, u32[]{:S(2)}) collective-permute-start(bf16[320,384]{1,0:T(8,128)(2,1)S(1)} %get-tuple-element.263), channel_id=1, source_target_pairs={{0,4},{1,5},{2,6},{3,7},{4,0},{5,1},{6,2},{7,3},{8,12},{9,13},{10,... | collective-permute-start | bytes 737288 | tf_op jit(solution)/shard_map/ppermute | solution.py:555
  230.2 27.3 %collective-permute-start.66 = (bf16[288,768]{1,0:T(8,128)(2,1)S(1)}, bf16[288,768]{1,0:T(8,128)(2,1)S(1)}, u32[]{:S(2)}, u32[]{:S(2)}) collective-permute-start(bf16[288,768]{1,0:T(8,128)(2,1)S(1)} %join_two.1.u0), channel_id=1, source_target_pairs={{0,8},{8,0},{16,24},{24,16},{1,9},{9,1},{17,25},{25,17},{2,10},{10... | collective-permute-start | bytes 1327112 | tf_op jit(solution)/shard_map/ppermute | solution.py:561
  231.5 25.9 %collective-permute-start.67 = (bf16[288,768]{1,0:T(8,128)(2,1)S(1)}, bf16[288,768]{1,0:T(8,128)(2,1)S(1)}, u32[]{:S(2)}, u32[]{:S(2)}) collective-permute-start(bf16[288,768]{1,0:T(8,128)(2,1)S(1)} %join_two.1.u0), channel_id=1, source_target_pairs={{0,16},{8,24},{16,0},{24,8},{1,17},{9,25},{17,1},{25,9},{2,18},{10... | collective-permute-start | bytes 1327112 | tf_op jit(solution)/shard_map/ppermute | solution.py:561
  232.7 24.8 %collective-permute-start.68 = (bf16[288,768]{1,0:T(8,128)(2,1)S(1)}, bf16[288,768]{1,0:T(8,128)(2,1)S(1)}, u32[]{:S(2)}, u32[]{:S(2)}) collective-permute-start(bf16[288,768]{1,0:T(8,128)(2,1)S(1)} %join_two.1.u0), channel_id=1, source_target_pairs={{0,24},{8,16},{16,8},{24,0},{1,25},{9,17},{17,9},{25,1},{2,26},{10... | collective-permute-start | bytes 1327112 | tf_op jit(solution)/shard_map/ppermute | solution.py:561
  239.7 14.1 %collective-permute-start.61 = (bf16[208,384]{1,0:T(8,128)(2,1)S(1)}, bf16[208,384]{1,0:T(8,128)(2,1)S(1)}, u32[]{:S(2)}, u32[]{:S(2)}) collective-permute-start(bf16[208,384]{1,0:T(8,128)(2,1)S(1)} %get-tuple-element.284), channel_id=1, source_target_pairs={{0,4},{1,5},{2,6},{3,7},{4,0},{5,1},{6,2},{7,3},{8,12},{9,13},{10,... | collective-permute-start | bytes 479240 | tf_op jit(solution)/shard_map/ppermute | solution.py:555
  (48 other events, 323.2 us)

commit v5 on v4

--- a/solution.py
+++ b/solution.py
@@ -1147,6 +1147,119 @@
         rows = lax.broadcasted_iota(jnp.int32, total.shape, 0)
         total = jnp.where((rows == at) & (lanes == 0), high, total)
         return jnp.where((rows == at) & (lanes == 1), whole - high, total)
+
+    near_rows = model // 2
+
+    def row_layer_grads(low, mix, low_far, mix_far, mine, got, more):
+        norms_too = len(more) == 1
+        size = near_rows + (0 if norms_too else toks)
+        tail = extra if norms_too else 0
+
+        def row_weight_sums(spot_ref, low_ref, mix_ref, low2_ref, mix2_ref, mine_ref, got_ref, *refs):
+            more_refs, (x_ref, y_ref, a_ref, b_ref) = refs[: len(more)], refs[len(more) : -2]
+            left_ref, right_ref = refs[-2:]
+            left_ref[0, :toks] = low_ref[...]
+            left_ref[0, toks:] = low2_ref[...]
+            left_ref[1, :toks] = mix_ref[...]
+            left_ref[1, toks:] = mix2_ref[...]
+            right_ref[:, :toks] = mine_ref[...]
+            right_ref[:, toks:] = got_ref[...]
+            places = (
+                ((a_ref, 0), (b_ref, 0)),
+                ((x_ref, 0), (b_ref, 1)),
+                ((a_ref, 1), (y_ref, 0)),
+                ((x_ref, 1), (y_ref, 1)),
+            )
+            for step in range(cols_axis):
+                matrix = spot_ref[0] ^ step
+                left = left_ref[matrix // 3]
+                found = dot_tokens(left, right_ref[matrix]).astype(bf16)
+                for part_index, (ref, at) in enumerate(places[step]):
+                    start = at * size
+                    ref[start : start + near_rows] = found[
+                        part_index * near_rows : (part_index + 1) * near_rows
+                    ]
+                    if not norms_too:
+                        lanes = slice(part_index * half, (part_index + 1) * half)
+                        ref[start + near_rows : start + size] = more_refs[step][:, lanes]
+            if norms_too:
+                sums_ref = more_refs[0]
+                line = jnp.concatenate([sums_ref[:, :half], sums_ref[:, half:]], axis=0)
+                line = renew(line, 6).astype(bf16)
+                for ref in (x_ref, a_ref):
+                    ref[2 * size :] = line
+
+        outs = [((2 * size + tail, half), bf16), ((2 * size, half), bf16)] * 2
+        return kernel_call(
+            row_weight_sums,
+            outs,
+            [spot, low, mix, low_far, mix_far, mine, got, *more],
+            smem=(0,),
+            scratch=[
+                pltpu.VMEM((2, 2 * toks, model), bf16),
+                pltpu.VMEM((4, 2 * toks, half), bf16),
+            ],
+        )
+
+    def fold_pairs(parts, got_x, got_y, tail):
+        a_part, b_part = parts[2:]
+        size = b_part.shape[0] // 2
+
+        def pair_sums(a_ref, x_ref, b_ref, y_ref, keep_ref, give_ref, keep2_ref, give2_ref):
+            first = a_ref[...].astype(f32) + x_ref[...].astype(f32)
+            second = b_ref[...].astype(f32) + y_ref[...].astype(f32)
+            keep_ref[:size] = first[:size].astype(bf16)
+            give_ref[:size] = first[size : 2 * size].astype(bf16)
+            keep2_ref[...] = second[:size].astype(bf16)
+            give2_ref[...] = second[size:].astype(bf16)
+            if tail:
+                line = renew(first[2 * size :], 6).astype(bf16)
+                keep_ref[size:] = line
+                give_ref[size:] = line
+
+        return kernel_call(
+            pair_sums,
+            [((size + tail, half), bf16)] * 2 + [((size, half), bf16)] * 2,
+            [a_part, got_x, b_part, got_y],
+        )
+
+    def row_layer_chips(keep, got, keep2, got2, tail, stream, slots):
+        sent_rows = 2 * width * (bool(stream) + bool(slots))
+
+        def layer_parts(spot_ref, a_ref, ga_ref, b_ref, gb_ref, *refs):
+            more, outs, total_ref = refs[: -chips - 1], refs[-chips - 1 : -1], refs[-1]
+            first = a_ref[...].astype(f32) + ga_ref[...].astype(f32)
+            second = b_ref[...].astype(f32) + gb_ref[...].astype(f32)
+            total_ref[:near_rows] = first[:near_rows].astype(bf16)
+            total_ref[near_rows:] = second[:near_rows].astype(bf16)
+            if stream:
+                result = more[0][...] + jnp.concatenate(
+                    [first[near_rows:], second[near_rows:]], axis=1
+                )
+            for hop in range(chips):
+                at = pl.multiple_of((spot_ref[1] ^ hop) * block, block)
+                outs[hop][:block] = total_ref[pl.ds(at, block)]
+                row = block
+                if tail:
+                    outs[hop][row : row + tail] = renew(first[near_rows:], 6).astype(bf16)
+                    row = row + tail
+                sent = []
+                if stream:
+                    sent.append(result[slot_rows(hop)].astype(bf16))
+                if slots:
+                    sent.append(more[hop - chips][...])
+                for slot in sent:
+                    outs[hop][row : row + width] = slot[:, :half]
+                    outs[hop][row + width : row + 2 * width] = slot[:, half:]
+                    row = row + 2 * width
+
+        return kernel_call(
+            layer_parts,
+            [((block + tail + sent_rows, half), bf16)] * chips,
+            [spot, keep, got, keep2, got2, *stream, *slots],
+            smem=(0,),
+            scratch=[pltpu.VMEM((model, half), bf16)],
+        )
 
     def layer_grads(low, mix, low_far, mix_far, mine, got, more):
         rows = model + (extra if len(more) == 1 else 2 * toks)
@@ -1640,7 +1753,7 @@
             ].astype(f32)
             grad_ref[...] = all_ref[source, 2 * shard :].astype(f32)
 
-    row_parts = layer_grads(
+    row_parts = row_layer_grads(
         normed_one,
         row_mix,
         row_low_far,
@@ -1650,8 +1763,11 @@
         [sums],
     )
     row_sends = after(row_parts, col_parts, feed_keep)
-    row_parts = [row_parts[0]] + [along_cols(row_sends[step], step) for step in col_steps]
-    row_slices = split_chips(row_parts, 1, extra)
+    row_x, row_y = along_cols(row_sends[0], 1), along_cols(row_sends[1], 2)
+    keep, give, keep2, give2 = fold_pairs(row_parts, row_x, row_y, extra)
+    row_slices = row_layer_chips(
+        keep, along_cols(give, 2), keep2, along_cols(give2, 1), extra, [], []
+    )
     row_reached = over_chips(row_slices)
     row_keep, row_swap = split_cores(row_reached, 1, extra)
 

time: 271 us -> 270 us (level)
  waiting for transfers between devices: 127 us -> 124 us
    ppermute x16, waiting for transfers between devices: 60.8 us -> 50.9 us  [along_chips(): return lax.ppermute(values, 'seq', [(i, i ^ 2 * step) for i in range(seqs)])]
    ppermute x20 -> x21, waiting for transfers between devices: 30.2 us -> 36.5 us  [along_cols(): lax.ppermute(values, 'col', [(i, i ^ step) for i in range(cols_axis)])]
    ppermute x20 -> x21, starting transfers between devices: 27.9 us -> 29.6 us  [along_cols(): lax.ppermute(values, 'col', [(i, i ^ step) for i in range(cols_axis)])]
    pallas_call x35 -> x36, Pallas kernels: 52 us -> 52.1 us  [kernel_call(): pl.pallas_call(body, grid=(1,) if stream else (), out_shape=out_shapes, i...]
  transfers between devices with their start and end apart: 72 -> 73, of which waited for: 36 -> 36; matrix products, arithmetic and copies ran while one was open for 2% -> 2% of each run, Pallas kernels for 12% -> 12%
where the time goes in v5:
time: 270 us; the launch traced here: 269 us
  waiting for transfers between devices  124 us (46%)
  starting transfers between devices  82.8 us (31%)
  Pallas kernels  52.1 us (19%)
  between operations  4.4 us (2%)
  local copies, waits for them, and re-layouts  3.01 us (1%)
  other arithmetic  2.96 us (1%)
    pallas_call x36, Pallas kernels, kernel_call(): pl.pallas_call(body, grid=(1,) if stream else (), out_shape=out_shapes, i...  52.1 us
    ppermute x16, waiting for transfers between devices, along_chips(): return lax.ppermute(values, 'seq', [(i, i ^ 2 * step) for i in range(seqs)])  50.9 us
    ppermute x21, waiting for transfers between devices, along_cols(): lax.ppermute(values, 'col', [(i, i ^ step) for i in range(cols_axis)])  36.5 us
    ppermute x21, starting transfers between devices, along_cols(): lax.ppermute(values, 'col', [(i, i ^ step) for i in range(cols_axis)])  29.6 us
    ppermute x16, starting transfers between devices, along_chips(): return lax.ppermute(values, 'seq', [(i, i ^ 2 * step) for i in range(seqs)])  29.5 us
    ppermute x28, waiting for transfers between devices, along_core(): return lax.ppermute(values, 'seq', [(i, i ^ 1) for i in range(seqs)])  19.4 us
    ppermute x2, waiting for transfers between devices, to_right(): return lax.ppermute(values, ('col', 'seq'), rightward)  15 us
    ppermute x2, starting transfers between devices, to_right(): return lax.ppermute(values, ('col', 'seq'), rightward)  6.49 us
  transfers between devices with their start and end apart: 73, of which 36 were waited for; matrix products, arithmetic and copies ran while one was open for 2% of the time, Pallas kernels for 12%

profile of v5, /device:TPU:0, one launch (start us, length us, event | category | flops | bytes accessed | tf_op | source)
XLA Modules:
  0.0 269.5 jit_solution(13336146836534676792)
XLA Ops:
  4.1 3.0 %collective-permute-start = (bf16[104,768]{1,0:T(8,128)(2,1)}, bf16[104,768]{1,0:T(8,128)(2,1)S(1)}, u32[]{:S(2)}, u32[]{:S(2)}) collective-permute-start(bf16[104,768]{1,0:T(8,128)(2,1)} %get-tuple-element.173), channel_id=1, source_target_pairs={{0,2},{1,3},{2,0},{3,1},{4,6},{5,7},{6,4},{7,5},{8,10},{9,11},{10,... | collective-permute-start | bytes 479240 | tf_op jit(solution)/shard_map/ppermute | solution.py:555
  7.1 2.6 collective-permute-start.1
  14.1 3.2 %pack_rest.1 = (bf16[2,96,768]{2,1,0:T(8,128)(2,1)}, bf16[384,768]{1,0:T(8,128)(2,1)}, bf16[64,768]{1,0:T(8,128)(2,1)}, bf16[160,768]{1,0:T(8,128)(2,1)}, bf16[1...) custom-call(s32[7]{0:T(128)} %stack.42.spot_ref, bf16[96,768]{1,0:T(8,128)(2,1)} %refs_0_.2, bf16[96,768]{1,0:T(8,128)(2,1)} %refs_1_.2, ...), custom_call_target="tpu_custom_call" | custom-call | flops 1 | bytes 1 | tf_op jit(solution)/shard_map/pack_rest/pallas_call | solution.py:415
  17.3 4.8 %collective-permute-done.1.refs_1_ = bf16[104,768]{1,0:T(8,128)(2,1)S(1)} collective-permute-done((bf16[104,768]{1,0:T(8,128)(2,1)}, bf16[104,768]{1,0:T(8,128)(2,1)S(1)}, u32[]{:S(2)}, u32[]{:S(2)}) %collective-permute-start.1) | collective-permute-done | bytes 159776 | tf_op jit(solution)/shard_map/ppermute | solution.py:555
  27.3 2.6 collective-permute-start.4
  32.5 16.9 %collective-permute-done.9.refs_8_ = bf16[312,768]{1,0:T(8,128)(2,1)S(1)} collective-permute-done((bf16[312,768]{1,0:T(8,128)(2,1)S(1)}, bf16[312,768]{1,0:T(8,128)(2,1)S(1)}, u32[]{:S(2)}, u32[]{:S(2)}) %collective-permute-start.9) | collective-permute-done | bytes 479264 | tf_op jit(solution)/shard_map/ppermute | solution.py:561
  50.7 2.8 %collective-permute-done.7.refs_5_ = bf16[392,768]{1,0:T(8,128)(2,1)S(1)} collective-permute-done((bf16[392,768]{1,0:T(8,128)(2,1)S(1)}, bf16[392,768]{1,0:T(8,128)(2,1)S(1)}, u32[]{:S(2)}, u32[]{:S(2)}) %collective-permute-start.7) | collective-permute-done | bytes 602144 | tf_op jit(solution)/shard_map/ppermute | solution.py:558
  59.7 4.9 %collective-permute-start.20 = (bf16[2,2,96,768]{3,2,1,0:T(8,128)(2,1)S(1)}, bf16[2,2,96,768]{3,2,1,0:T(8,128)(2,1)S(1)}, u32[]{:S(2)}, u32[]{:S(2)}) collective-permute-start(bf16[2,2,96,768]{3,2,1,0:T(8,128)(2,1)S(1)} %pair_feed.1.both_ref), channel_id=1, source_target_pairs={{0,2},{1,5},{2,0},{3,7},{4,6},{5,1},{6,4},{7,3},{8,10},{9,13},{10,... | collective-permute-start | bytes 1769480 | tf_op jit(solution)/shard_map/ppermute | solution.py:573
  67.9 3.5 %collective-permute-start.19 = (bf16[288,768]{1,0:T(8,128)(2,1)S(1)}, bf16[288,768]{1,0:T(8,128)(2,1)S(1)}, u32[]{:S(2)}, u32[]{:S(2)}) collective-permute-start(bf16[288,768]{1,0:T(8,128)(2,1)S(1)} %get-tuple-element.193.near_ref), channel_id=1, source_target_pairs={{0,24},{8,16},{16,8},{24,0},{1,25},{9,17},{17,9},{25,1},{2,26},{10... | collective-permute-start | bytes 1327112 | tf_op jit(solution)/shard_map/ppermute | solution.py:561
  71.4 14.5 %collective-permute-done.13.left_ref = bf16[2,128,768]{2,1,0:T(8,128)(2,1)S(1)} collective-permute-done((bf16[2,128,768]{2,1,0:T(8,128)(2,1)S(1)}, bf16[2,128,768]{2,1,0:T(8,128)(2,1)S(1)}, u32[]{:S(2)}, u32[]{:S(2)}) %collective-permute-start.13) | collective-permute-done | bytes 393248 | tf_op jit(solution)/shard_map/ppermute | solution.py:586
  92.6 2.2 collective-permute-done.16.refs_1_
  105.9 7.2 %collective-permute-done.30.last_ref = bf16[2,96,768]{2,1,0:T(8,128)(2,1)S(1)} collective-permute-done((bf16[2,96,768]{2,1,0:T(8,128)(2,1)S(1)}, bf16[2,96,768]{2,1,0:T(8,128)(2,1)S(1)}, u32[]{:S(2)}, u32[]{:S(2)}) %collective-permute-start.30) | collective-permute-done | bytes 294944 | tf_op jit(solution)/shard_map/ppermute | solution.py:555
  113.1 5.0 %collective-permute-done.27.a1 = bf16[128,768]{1,0:T(8,128)(2,1)S(1)} collective-permute-done((bf16[128,768]{1,0:T(8,128)(2,1)S(1)}, bf16[128,768]{1,0:T(8,128)(2,1)S(1)}, u32[]{:S(2)}, u32[]{:S(2)}) %collective-permute-start.27) | collective-permute-done | bytes 196640 | tf_op jit(solution)/shard_map/ppermute | solution.py:561
  119.0 2.5 collective-permute-done.34.last2_ref
  122.3 3.7 %feed_main.1 = (bf16[4,128,768]{2,1,0:T(8,128)(2,1)S(1)}, bf16[4,128,768]{2,1,0:T(8,128)(2,1)S(1)}, bf16[128,768]{1,0:T(8,128)(2,1)S(1)}, bf16[128,768]{1,0:T(8,...) custom-call(bf16[128,768]{1,0:T(8,128)(2,1)S(1)} %get-tuple-element.205.a0, ...), custom_call_target="tpu_custom_call" | custom-call | flops 1 | bytes 1 | tf_op jit(solution)/shard_map/feed_main/pallas_call | solution.py:415
  129.5 3.0 %feed_weights.1 = (bf16[1536,384]{1,0:T(8,128)(2,1)S(1)}, bf16[1536,384]{1,0:T(8,128)(2,1)S(1)}, bf16[128,768]{1,0:T(8,128)(2,1)S(1)}, bf16[128,768]{1,0:T(8,128...) custom-call(s32[7]{0:T(128)S(1)} %copy-done.3, bf16[128,768]{1,0:T(8,128)(2,1)S(1)} %get-tuple-element.205.a0, ...), custom_call_target="tpu_custom_call" | custom-call | flops 1811939328 | bytes 16777216 | tf_op jit(solution)/shard_map/feed_weights/pallas_call | solution.py:415
  133.8 4.0 %collective-permute-done.37.b2 = bf16[128,768]{1,0:T(8,128)(2,1)S(1)} collective-permute-done((bf16[128,768]{1,0:T(8,128)(2,1)S(1)}, bf16[128,768]{1,0:T(8,128)(2,1)S(1)}, u32[]{:S(2)}, u32[]{:S(2)}) %collective-permute-start.37) | collective-permute-done | bytes 196640 | tf_op jit(solution)/shard_map/ppermute | solution.py:561
  137.8 3.8 %attend_col_back.1 = (f32[128,768]{1,0:T(8,128)S(1)}, bf16[128,768]{1,0:T(8,128)(2,1)S(1)}, bf16[128,768]{1,0:T(8,128)(2,1)S(1)}, f32[2,128,768]{2,1,0:T(8,128)S...) custom-call(s32[7]{0:T(128)S(1)} %copy-done.3, bf16[128,768]{1,0:T(8,128)(2,1)S(1)} %get-tuple-element.221.b0, ...), custom_call_target="tpu_custom_call" | custom-call | flops 1 | bytes 1 | tf_op jit(solution)/shard_map/attend_col_back/pallas_call | solution.py:415
  144.0 3.6 %row_entry_back.1 = (bf16[4,128,384]{2,1,0:T(8,128)(2,1)S(1)}, bf16[4,128,384]{2,1,0:T(8,128)(2,1)S(1)}, f32[128,768]{1,0:T(8,128)S(1)}, bf16[128,768]{1,0:T(8,1...) custom-call(s32[7]{0:T(128)S(1)} %copy-done.3, ...), custom_call_target="tpu_custom_call" | custom-call | flops 1 | bytes 1 | tf_op jit(solution)/shard_map/row_entry_back/pallas_call | solution.py:415
  149.0 2.2 attend_row_back.1
  153.2 4.6 %collective-permute-start.48 = (bf16[2,128,768]{2,1,0:T(8,128)(2,1)S(1)}, bf16[2,128,768]{2,1,0:T(8,128)(2,1)S(1)}, u32[]{:S(2)}, u32[]{:S(2)}) collective-permute-start(bf16[2,128,768]{2,1,0:T(8,128)(2,1)S(1)} %get-tuple-element.253), channel_id=1, source_target_pairs={{0,2},{1,3},{2,4},{3,5},{4,6},{5,7},{6,14},{7,15},{14,12},{15,13},... | collective-permute-start | bytes 1179656 | tf_op jit(solution)/shard_map/ppermute | solution.py:586
  169.4 2.5 collective-permute-start.54
  173.8 12.1 %collective-permute-done.54.refs_1_ = bf16[384,384]{1,0:T(8,128)(2,1)S(1)} collective-permute-done((bf16[384,384]{1,0:T(8,128)(2,1)S(1)}, bf16[384,384]{1,0:T(8,128)(2,1)S(1)}, u32[]{:S(2)}, u32[]{:S(2)}) %collective-permute-start.54) | collective-permute-done | bytes 294944 | tf_op jit(solution)/shard_map/ppermute | solution.py:555
  189.3 7.3 %collective-permute-done.56.refs_3_ = bf16[384,384]{1,0:T(8,128)(2,1)S(1)} collective-permute-done((bf16[384,384]{1,0:T(8,128)(2,1)S(1)}, bf16[384,384]{1,0:T(8,128)(2,1)S(1)}, u32[]{:S(2)}, u32[]{:S(2)}) %collective-permute-start.56) | collective-permute-done | bytes 294944 | tf_op jit(solution)/shard_map/ppermute | solution.py:555
  199.6 2.9 %collective-permute-start.57 = (bf16[784,384]{1,0:T(8,128)(2,1)S(1)}, bf16[784,384]{1,0:T(8,128)(2,1)S(1)}, u32[]{:S(2)}, u32[]{:S(2)}) collective-permute-start(bf16[784,384]{1,0:T(8,128)(2,1)S(1)} %get-tuple-element.282), channel_id=1, source_target_pairs={{0,8},{8,0},{16,24},{24,16},{1,9},{9,1},{17,25},{25,17},{2,10},{10... | collective-permute-start | bytes 1806344 | tf_op jit(solution)/shard_map/ppermute | solution.py:561
  207.9 2.4 collective-permute-start.51
  210.3 6.0 %collective-permute-done.58.y_ref = bf16[768,384]{1,0:T(8,128)(2,1)S(1)} collective-permute-done((bf16[768,384]{1,0:T(8,128)(2,1)S(1)}, bf16[768,384]{1,0:T(8,128)(2,1)S(1)}, u32[]{:S(2)}, u32[]{:S(2)}) %collective-permute-start.58) | collective-permute-done | bytes 589856 | tf_op jit(solution)/shard_map/ppermute | solution.py:561
  220.4 7.1 %collective-permute-done.50.refs_2_ = bf16[320,384]{1,0:T(8,128)(2,1)S(1)} collective-permute-done((bf16[320,384]{1,0:T(8,128)(2,1)S(1)}, bf16[320,384]{1,0:T(8,128)(2,1)S(1)}, u32[]{:S(2)}, u32[]{:S(2)}) %collective-permute-start.50) | collective-permute-done | bytes 245792 | tf_op jit(solution)/shard_map/ppermute | solution.py:555
  234.5 3.7 %collective-permute-start.61 = (bf16[208,384]{1,0:T(8,128)(2,1)S(1)}, bf16[208,384]{1,0:T(8,128)(2,1)S(1)}, u32[]{:S(2)}, u32[]{:S(2)}) collective-permute-start(bf16[208,384]{1,0:T(8,128)(2,1)S(1)} %get-tuple-element.289), channel_id=1, source_target_pairs={{0,2},{1,3},{2,0},{3,1},{4,6},{5,7},{6,4},{7,5},{8,10},{9,11},{10,... | collective-permute-start | bytes 479240 | tf_op jit(solution)/shard_map/ppermute | solution.py:555
  238.7 5.0 %collective-permute-done.61.refs_1_ = bf16[208,384]{1,0:T(8,128)(2,1)S(1)} collective-permute-done((bf16[208,384]{1,0:T(8,128)(2,1)S(1)}, bf16[208,384]{1,0:T(8,128)(2,1)S(1)}, u32[]{:S(2)}, u32[]{:S(2)}) %collective-permute-start.61) | collective-permute-done | bytes 159776 | tf_op jit(solution)/shard_map/ppermute | solution.py:555
  245.7 6.6 %collective-permute-done.62.refs_2_ = bf16[208,384]{1,0:T(8,128)(2,1)S(1)} collective-permute-done((bf16[208,384]{1,0:T(8,128)(2,1)S(1)}, bf16[208,384]{1,0:T(8,128)(2,1)S(1)}, u32[]{:S(2)}, u32[]{:S(2)}) %collective-permute-start.62) | collective-permute-done | bytes 159776 | tf_op jit(solution)/shard_map/ppermute | solution.py:555
  262.6 2.8 %spread_pair.1 = (f32[96,3072]{1,0:T(8,128)}, f32[384,768]{1,0:T(8,128)}, f32[96,768]{1,0:T(8,128)}, f32[96,768]{1,0:T(8,128)}, f32[96,768]{1,0:T(8,128)}, /*index=5*/f32[96,768]{1,0:T(8,128)}) custom-call(s32[7]{0:T(128)S(1)} %copy-done.3, bf16[288,768]{1,0:T(8,128)(2,1)S(1)} %join_two.1.u0, bf16[288,768]{1,0:T(8,128)(2,1)S(1)} %collective-permute-done.67.u1, ...), custom_call_target="tpu_custom_call" | custom-call | flops 1 | bytes 1 | tf_op jit(solution)/shard_map/spread_pair/pallas_call | solution.py:415
  (180 shorter events, 106.0 us)
Async XLA Ops:
  4.1 13.2 %collective-permute-start = (bf16[104,768]{1,0:T(8,128)(2,1)}, bf16[104,768]{1,0:T(8,128)(2,1)S(1)}, u32[]{:S(2)}, u32[]{:S(2)}) collective-permute-start(bf16[104,768]{1,0:T(8,128)(2,1)} %get-tuple-element.173), channel_id=1, source_target_pairs={{0,2},{1,3},{2,0},{3,1},{4,6},{5,7},{6,4},{7,5},{8,10},{9,11},{10,... | collective-permute-start | bytes 479240 | tf_op jit(solution)/shard_map/ppermute | solution.py:555
  7.1 15.0 %collective-permute-start.1 = (bf16[104,768]{1,0:T(8,128)(2,1)}, bf16[104,768]{1,0:T(8,128)(2,1)S(1)}, u32[]{:S(2)}, u32[]{:S(2)}) collective-permute-start(bf16[104,768]{1,0:T(8,128)(2,1)} %get-tuple-element.173), channel_id=1, source_target_pairs={{0,4},{1,5},{2,6},{3,7},{4,0},{5,1},{6,2},{7,3},{8,12},{9,13},{10,... | collective-permute-start | bytes 479240 | tf_op jit(solution)/shard_map/ppermute | solution.py:555
  24.2 25.9 %collective-permute-start.8 = (bf16[624,768]{1,0:T(8,128)(2,1)S(1)}, bf16[624,768]{1,0:T(8,128)(2,1)S(1)}, u32[]{:S(2)}, u32[]{:S(2)}) collective-permute-start(bf16[624,768]{1,0:T(8,128)(2,1)S(1)} %join_cores.2.refs_6_), channel_id=1, source_target_pairs={{0,8},{1,17},{2,10},{3,19},{4,12},{5,21},{6,14},{7,23},{8,0},{9,25... | collective-permute-start | bytes 2875400 | tf_op jit(solution)/shard_map/ppermute | solution.py:569
  25.8 23.6 %collective-permute-start.9 = (bf16[312,768]{1,0:T(8,128)(2,1)S(1)}, bf16[312,768]{1,0:T(8,128)(2,1)S(1)}, u32[]{:S(2)}, u32[]{:S(2)}) collective-permute-start(bf16[312,768]{1,0:T(8,128)(2,1)S(1)} %stack_row.1.near_ref), channel_id=1, source_target_pairs={{0,24},{8,16},{16,8},{24,0},{1,25},{9,17},{17,9},{25,1},{2,26},{10... | collective-permute-start | bytes 1437704 | tf_op jit(solution)/shard_map/ppermute | solution.py:561
  27.3 22.1 %collective-permute-start.4 = (bf16[160,768]{1,0:T(8,128)(2,1)S(1)}, bf16[160,768]{1,0:T(8,128)(2,1)S(1)}, u32[]{:S(2)}, u32[]{:S(2)}) collective-permute-start(bf16[160,768]{1,0:T(8,128)(2,1)S(1)} %copy-done.7), channel_id=1, source_target_pairs={{0,2},{1,3},{2,0},{3,1},{4,6},{5,7},{6,4},{7,5},{8,10},{9,11},{10,... | collective-permute-start | bytes 737288 | tf_op jit(solution)/shard_map/ppermute | solution.py:555
  29.9 20.3 %collective-permute-start.5 = (bf16[160,768]{1,0:T(8,128)(2,1)S(1)}, bf16[160,768]{1,0:T(8,128)(2,1)S(1)}, u32[]{:S(2)}, u32[]{:S(2)}) collective-permute-start(bf16[160,768]{1,0:T(8,128)(2,1)S(1)} %copy-done.6), channel_id=1, source_target_pairs={{0,4},{1,5},{2,6},{3,7},{4,0},{5,1},{6,2},{7,3},{8,12},{9,13},{10,... | collective-permute-start | bytes 737288 | tf_op jit(solution)/shard_map/ppermute | solution.py:555
  31.0 19.2 %collective-permute-start.6 = (bf16[160,768]{1,0:T(8,128)(2,1)S(1)}, bf16[160,768]{1,0:T(8,128)(2,1)S(1)}, u32[]{:S(2)}, u32[]{:S(2)}) collective-permute-start(bf16[160,768]{1,0:T(8,128)(2,1)S(1)} %copy-done.5), channel_id=1, source_target_pairs={{0,6},{1,7},{2,4},{3,5},{4,2},{5,3},{6,0},{7,1},{8,14},{9,15},{10,... | collective-permute-start | bytes 737288 | tf_op jit(solution)/shard_map/ppermute | solution.py:555
  58.1 33.4 %collective-permute-start.18 = (bf16[576,768]{1,0:T(8,128)(2,1)S(1)}, bf16[576,768]{1,0:T(8,128)(2,1)S(1)}, u32[]{:S(2)}, u32[]{:S(2)}) collective-permute-start(bf16[576,768]{1,0:T(8,128)(2,1)S(1)} %join_cores.3.refs_2_), channel_id=1, source_target_pairs={{0,8},{1,17},{2,10},{3,19},{4,12},{5,21},{6,14},{7,23},{8,0},{9,25... | collective-permute-start | bytes 2654216 | tf_op jit(solution)/shard_map/ppermute | solution.py:569
  59.7 31.8 %collective-permute-start.20 = (bf16[2,2,96,768]{3,2,1,0:T(8,128)(2,1)S(1)}, bf16[2,2,96,768]{3,2,1,0:T(8,128)(2,1)S(1)}, u32[]{:S(2)}, u32[]{:S(2)}) collective-permute-start(bf16[2,2,96,768]{3,2,1,0:T(8,128)(2,1)S(1)} %pair_feed.1.both_ref), channel_id=1, source_target_pairs={{0,2},{1,5},{2,0},{3,7},{4,6},{5,1},{6,4},{7,3},{8,10},{9,13},{10,... | collective-permute-start | bytes 1769480 | tf_op jit(solution)/shard_map/ppermute | solution.py:573
  64.5 21.4 %collective-permute-start.13 = (bf16[2,128,768]{2,1,0:T(8,128)(2,1)S(1)}, bf16[2,128,768]{2,1,0:T(8,128)(2,1)S(1)}, u32[]{:S(2)}, u32[]{:S(2)}) collective-permute-start(bf16[2,128,768]{2,1,0:T(8,128)(2,1)S(1)} %get-tuple-element.186.near_ref), channel_id=1, source_target_pairs={{0,2},{1,3},{2,4},{3,5},{4,6},{5,7},{6,14},{7,15},{14,12},{15,13},... | collective-permute-start | bytes 1179656 | tf_op jit(solution)/shard_map/ppermute | solution.py:586
  66.4 20.2 %collective-permute-start.14 = (bf16[2,128,768]{2,1,0:T(8,128)(2,1)S(1)}, bf16[2,128,768]{2,1,0:T(8,128)(2,1)S(1)}, u32[]{:S(2)}, u32[]{:S(2)}) collective-permute-start(bf16[2,128,768]{2,1,0:T(8,128)(2,1)S(1)} %get-tuple-element.186.near_ref), channel_id=1, source_target_pairs={{2,0},{3,1},{4,2},{5,3},{6,4},{7,5},{14,6},{15,7},{12,14},{13,15},... | collective-permute-start | bytes 1179656 | tf_op jit(solution)/shard_map/ppermute | solution.py:589
  67.9 23.5 %collective-permute-start.19 = (bf16[288,768]{1,0:T(8,128)(2,1)S(1)}, bf16[288,768]{1,0:T(8,128)(2,1)S(1)}, u32[]{:S(2)}, u32[]{:S(2)}) collective-permute-start(bf16[288,768]{1,0:T(8,128)(2,1)S(1)} %get-tuple-element.193.near_ref), channel_id=1, source_target_pairs={{0,24},{8,16},{16,8},{24,0},{1,25},{9,17},{17,9},{25,1},{2,26},{10... | collective-permute-start | bytes 1327112 | tf_op jit(solution)/shard_map/ppermute | solution.py:561
  97.6 15.5 %collective-permute-start.32 = (bf16[256,768]{1,0:T(8,128)(2,1)S(1)}, bf16[256,768]{1,0:T(8,128)(2,1)S(1)}, u32[]{:S(2)}, u32[]{:S(2)}) collective-permute-start(bf16[256,768]{1,0:T(8,128)(2,1)S(1)} %join_given.1), channel_id=1, source_target_pairs={{0,8},{1,17},{2,10},{3,19},{4,12},{5,21},{6,14},{7,23},{8,0},{9,25... | collective-permute-start | bytes 1179656 | tf_op jit(solution)/shard_map/ppermute | solution.py:569
  101.0 17.6 %collective-permute-start.29 = (bf16[256,768]{1,0:T(8,128)(2,1)S(1)}, bf16[256,768]{1,0:T(8,128)(2,1)S(1)}, u32[]{:S(2)}, u32[]{:S(2)}) collective-permute-start(bf16[256,768]{1,0:T(8,128)(2,1)S(1)} %get-tuple-element.206), channel_id=1, source_target_pairs={{0,24},{8,16},{16,8},{24,0},{1,25},{9,17},{17,9},{25,1},{2,26},{10... | collective-permute-start | bytes 1179656 | tf_op jit(solution)/shard_map/ppermute | solution.py:561
  104.5 13.6 %collective-permute-start.27 = (bf16[128,768]{1,0:T(8,128)(2,1)S(1)}, bf16[128,768]{1,0:T(8,128)(2,1)S(1)}, u32[]{:S(2)}, u32[]{:S(2)}) collective-permute-start(bf16[128,768]{1,0:T(8,128)(2,1)S(1)} %get-tuple-element.205.a0), channel_id=1, source_target_pairs={{0,8},{8,0},{16,24},{24,16},{1,9},{9,1},{17,25},{25,17},{2,10},{10... | collective-permute-start | bytes 589832 | tf_op jit(solution)/shard_map/ppermute | solution.py:561
  151.3 17.0 %collective-permute-start.53 = (bf16[1536,384]{1,0:T(8,128)(2,1)S(1)}, bf16[1536,384]{1,0:T(8,128)(2,1)S(1)}, u32[]{:S(2)}, u32[]{:S(2)}) collective-permute-start(bf16[1536,384]{1,0:T(8,128)(2,1)S(1)} %get-tuple-element.276), channel_id=1, source_target_pairs={{0,1},{1,0},{2,3},{3,2},{4,5},{5,4},{6,7},{7,6},{8,9},{9,8},{10,11... | collective-permute-start | bytes 3538952 | tf_op jit(solution)/shard_map/ppermute | solution.py:558
  161.2 36.3 %collective-permute-start.44 = (bf16[1024,384]{1,0:T(8,128)(2,1)S(1)}, bf16[1024,384]{1,0:T(8,128)(2,1)S(1)}, u32[]{:S(2)}, u32[]{:S(2)}) collective-permute-start(bf16[1024,384]{1,0:T(8,128)(2,1)S(1)} %get-tuple-element.248), channel_id=1, source_target_pairs={{0,8},{8,0},{16,24},{24,16},{1,9},{9,1},{17,25},{25,17},{2,10},{10... | collective-permute-start | bytes 2359304 | tf_op jit(solution)/shard_map/ppermute | solution.py:561
  163.3 36.3 %collective-permute-start.45 = (bf16[1024,384]{1,0:T(8,128)(2,1)S(1)}, bf16[1024,384]{1,0:T(8,128)(2,1)S(1)}, u32[]{:S(2)}, u32[]{:S(2)}) collective-permute-start(bf16[1024,384]{1,0:T(8,128)(2,1)S(1)} %get-tuple-element.249), channel_id=1, source_target_pairs={{0,16},{8,24},{16,0},{24,8},{1,17},{9,25},{17,1},{25,9},{2,18},{10... | collective-permute-start | bytes 2359304 | tf_op jit(solution)/shard_map/ppermute | solution.py:561
  164.9 34.6 %collective-permute-start.46 = (bf16[1024,384]{1,0:T(8,128)(2,1)S(1)}, bf16[1024,384]{1,0:T(8,128)(2,1)S(1)}, u32[]{:S(2)}, u32[]{:S(2)}) collective-permute-start(bf16[1024,384]{1,0:T(8,128)(2,1)S(1)} %get-tuple-element.250), channel_id=1, source_target_pairs={{0,24},{8,16},{16,8},{24,0},{1,25},{9,17},{17,9},{25,1},{2,26},{10... | collective-permute-start | bytes 2359304 | tf_op jit(solution)/shard_map/ppermute | solution.py:561
  169.4 16.5 %collective-permute-start.54 = (bf16[384,384]{1,0:T(8,128)(2,1)S(1)}, bf16[384,384]{1,0:T(8,128)(2,1)S(1)}, u32[]{:S(2)}, u32[]{:S(2)}) collective-permute-start(bf16[384,384]{1,0:T(8,128)(2,1)S(1)} %get-tuple-element.278), channel_id=1, source_target_pairs={{0,2},{1,3},{2,0},{3,1},{4,6},{5,7},{6,4},{7,5},{8,10},{9,11},{10,... | collective-permute-start | bytes 884744 | tf_op jit(solution)/shard_map/ppermute | solution.py:555
  172.0 17.3 %collective-permute-start.55 = (bf16[384,384]{1,0:T(8,128)(2,1)S(1)}, bf16[384,384]{1,0:T(8,128)(2,1)S(1)}, u32[]{:S(2)}, u32[]{:S(2)}) collective-permute-start(bf16[384,384]{1,0:T(8,128)(2,1)S(1)} %get-tuple-element.279), channel_id=1, source_target_pairs={{0,4},{1,5},{2,6},{3,7},{4,0},{5,1},{6,2},{7,3},{8,12},{9,13},{10,... | collective-permute-start | bytes 884744 | tf_op jit(solution)/shard_map/ppermute | solution.py:555
  199.6 16.8 %collective-permute-start.57 = (bf16[784,384]{1,0:T(8,128)(2,1)S(1)}, bf16[784,384]{1,0:T(8,128)(2,1)S(1)}, u32[]{:S(2)}, u32[]{:S(2)}) collective-permute-start(bf16[784,384]{1,0:T(8,128)(2,1)S(1)} %get-tuple-element.282), channel_id=1, source_target_pairs={{0,8},{8,0},{16,24},{24,16},{1,9},{9,1},{17,25},{25,17},{2,10},{10... | collective-permute-start | bytes 1806344 | tf_op jit(solution)/shard_map/ppermute | solution.py:561
  202.4 13.9 %collective-permute-start.58 = (bf16[768,384]{1,0:T(8,128)(2,1)S(1)}, bf16[768,384]{1,0:T(8,128)(2,1)S(1)}, u32[]{:S(2)}, u32[]{:S(2)}) collective-permute-start(bf16[768,384]{1,0:T(8,128)(2,1)S(1)} %get-tuple-element.283), channel_id=1, source_target_pairs={{0,16},{8,24},{16,0},{24,8},{1,17},{9,25},{17,1},{25,9},{2,18},{10... | collective-permute-start | bytes 1769480 | tf_op jit(solution)/shard_map/ppermute | solution.py:561
  205.8 14.6 %collective-permute-start.49 = (bf16[320,384]{1,0:T(8,128)(2,1)S(1)}, bf16[320,384]{1,0:T(8,128)(2,1)S(1)}, u32[]{:S(2)}, u32[]{:S(2)}) collective-permute-start(bf16[320,384]{1,0:T(8,128)(2,1)S(1)} %get-tuple-element.265), channel_id=1, source_target_pairs={{0,2},{1,3},{2,0},{3,1},{4,6},{5,7},{6,4},{7,5},{8,10},{9,11},{10,... | collective-permute-start | bytes 737288 | tf_op jit(solution)/shard_map/ppermute | solution.py:555
  207.1 20.3 %collective-permute-start.50 = (bf16[320,384]{1,0:T(8,128)(2,1)S(1)}, bf16[320,384]{1,0:T(8,128)(2,1)S(1)}, u32[]{:S(2)}, u32[]{:S(2)}) collective-permute-start(bf16[320,384]{1,0:T(8,128)(2,1)S(1)} %get-tuple-element.266), channel_id=1, source_target_pairs={{0,4},{1,5},{2,6},{3,7},{4,0},{5,1},{6,2},{7,3},{8,12},{9,13},{10,... | collective-permute-start | bytes 737288 | tf_op jit(solution)/shard_map/ppermute | solution.py:555
  207.9 19.6 %collective-permute-start.51 = (bf16[320,384]{1,0:T(8,128)(2,1)S(1)}, bf16[320,384]{1,0:T(8,128)(2,1)S(1)}, u32[]{:S(2)}, u32[]{:S(2)}) collective-permute-start(bf16[320,384]{1,0:T(8,128)(2,1)S(1)} %get-tuple-element.267), channel_id=1, source_target_pairs={{0,6},{1,7},{2,4},{3,5},{4,2},{5,3},{6,0},{7,1},{8,14},{9,15},{10,... | collective-permute-start | bytes 737288 | tf_op jit(solution)/shard_map/ppermute | solution.py:555
  216.8 16.8 %collective-permute-start.59 = (bf16[400,384]{1,0:T(8,128)(2,1)S(1)}, bf16[400,384]{1,0:T(8,128)(2,1)S(1)}, u32[]{:S(2)}, u32[]{:S(2)}) collective-permute-start(bf16[400,384]{1,0:T(8,128)(2,1)S(1)} %get-tuple-element.285), channel_id=1, source_target_pairs={{0,16},{8,24},{16,0},{24,8},{1,17},{9,25},{17,1},{25,9},{2,18},{10... | collective-permute-start | bytes 921608 | tf_op jit(solution)/shard_map/ppermute | solution.py:561
  218.9 14.7 %collective-permute-start.60 = (bf16[384,384]{1,0:T(8,128)(2,1)S(1)}, bf16[384,384]{1,0:T(8,128)(2,1)S(1)}, u32[]{:S(2)}, u32[]{:S(2)}) collective-permute-start(bf16[384,384]{1,0:T(8,128)(2,1)S(1)} %get-tuple-element.287), channel_id=1, source_target_pairs={{0,8},{8,0},{16,24},{24,16},{1,9},{9,1},{17,25},{25,17},{2,10},{10... | collective-permute-start | bytes 884744 | tf_op jit(solution)/shard_map/ppermute | solution.py:561
  230.1 25.8 %collective-permute-start.67 = (bf16[288,768]{1,0:T(8,128)(2,1)S(1)}, bf16[288,768]{1,0:T(8,128)(2,1)S(1)}, u32[]{:S(2)}, u32[]{:S(2)}) collective-permute-start(bf16[288,768]{1,0:T(8,128)(2,1)S(1)} %join_two.1.u0), channel_id=1, source_target_pairs={{0,8},{8,0},{16,24},{24,16},{1,9},{9,1},{17,25},{25,17},{2,10},{10... | collective-permute-start | bytes 1327112 | tf_op jit(solution)/shard_map/ppermute | solution.py:561
  232.1 23.8 %collective-permute-start.68 = (bf16[288,768]{1,0:T(8,128)(2,1)S(1)}, bf16[288,768]{1,0:T(8,128)(2,1)S(1)}, u32[]{:S(2)}, u32[]{:S(2)}) collective-permute-start(bf16[288,768]{1,0:T(8,128)(2,1)S(1)} %join_two.1.u0), channel_id=1, source_target_pairs={{0,16},{8,24},{16,0},{24,8},{1,17},{9,25},{17,1},{25,9},{2,18},{10... | collective-permute-start | bytes 1327112 | tf_op jit(solution)/shard_map/ppermute | solution.py:561
  232.1 23.8 %collective-permute-start.69 = (bf16[288,768]{1,0:T(8,128)(2,1)S(1)}, bf16[288,768]{1,0:T(8,128)(2,1)S(1)}, u32[]{:S(2)}, u32[]{:S(2)}) collective-permute-start(bf16[288,768]{1,0:T(8,128)(2,1)S(1)} %join_two.1.u0), channel_id=1, source_target_pairs={{0,24},{8,16},{16,8},{24,0},{1,25},{9,17},{17,9},{25,1},{2,26},{10... | collective-permute-start | bytes 1327112 | tf_op jit(solution)/shard_map/ppermute | solution.py:561
  238.1 14.1 %collective-permute-start.62 = (bf16[208,384]{1,0:T(8,128)(2,1)S(1)}, bf16[208,384]{1,0:T(8,128)(2,1)S(1)}, u32[]{:S(2)}, u32[]{:S(2)}) collective-permute-start(bf16[208,384]{1,0:T(8,128)(2,1)S(1)} %get-tuple-element.290), channel_id=1, source_target_pairs={{0,4},{1,5},{2,6},{3,7},{4,0},{5,1},{6,2},{7,3},{8,12},{9,13},{10,... | collective-permute-start | bytes 479240 | tf_op jit(solution)/shard_map/ppermute | solution.py:555
  (49 other events, 348.1 us)

commit v6 on v5

--- a/solution.py
+++ b/solution.py
@@ -984,10 +984,10 @@
         lane_heads = head_of_lane(model)
         sides = ((k_ref, v_ref), (k2_ref, v2_ref))
         for slot in range(chips):
-            query = q_ref[slot_rows(slot)].astype(f32)
+            query = q_ref[slot_rows(slot)]
             products = jnp.concatenate(
                 [
-                    query * sides[s // chips][0][slot_rows(s % chips)].astype(f32)
+                    query * sides[s // chips][0][slot_rows(s % chips)]
                     for s in range(seqs)
                 ],
                 axis=0,
@@ -1092,16 +1092,18 @@
 
     def feed_main(a0, a1, a2, a3, given_ref, weight_ref, act_ref, grad_ref, *back_refs):
         up, down = weight_ref[0], weight_ref[1]
-        for step, low_ref in enumerate((a0, a1, a2, a3)):
-            pre = dot(low_ref[:toks], up)
-            bell = 0.5 * (1.0 + lax.erf(pre * (0.5**0.5)))
-            slope = bell + pre * jnp.exp(-0.5 * pre * pre) * ((0.5 / math.pi) ** 0.5)
-            act_ref[step] = (pre * bell).astype(bf16)
-            grad = (slope * dot_back(given_ref[step], down)).astype(bf16)
-            grad_ref[step] = grad
-            back_refs[step][...] = dot_back(grad, up).astype(bf16)
-
-    feed_big = 2.0 * toks * cols_axis * model * hidden
+        rows = cols_axis * toks
+        low = jnp.concatenate([ref[:toks] for ref in (a0, a1, a2, a3)], axis=0)
+        pre = dot(low, up)
+        bell = 0.5 * (1.0 + lax.erf(pre * (0.5**0.5)))
+        slope = bell + pre * jnp.exp(-0.5 * pre * pre) * ((0.5 / math.pi) ** 0.5)
+        act_ref[...] = (pre * bell).astype(bf16).reshape(cols_axis, toks, hidden)
+        grad = (slope * dot_back(given_ref[...].reshape(rows, model), down)).astype(bf16)
+        grad_ref[...] = grad.reshape(cols_axis, toks, hidden)
+        back = dot_back(grad, up).astype(bf16)
+        for step in range(cols_axis):
+            back_refs[step][...] = back[step * toks : (step + 1) * toks]
+
     feed_results = kernel_call(
         feed_main,
         [((cols_axis, toks, hidden), bf16)] * 2 + [((toks, model), bf16)] * cols_axis,
@@ -1391,7 +1393,6 @@
         dkv_ref,
         send_ref,
         sums_ref,
-        wide_ref,
     ):
         lane_heads = head_of_lane(model)
         back = b0[...].astype(f32) + b1[...].astype(f32) + b2[...].astype(f32) + b3[...].astype(f32)
@@ -1401,41 +1402,60 @@
         dtwo_ref[...] = dtwo
         low = dtwo.astype(bf16)
         low_ref[...] = low
-        dmix = dot_back(low, weight_ref[...]).astype(bf16).astype(f32)
-        wide_ref[...] = jnp.zeros_like(wide_ref)
+        dmix_low = dot_back(low, weight_ref[...]).astype(bf16)
+        dmix = dmix_low.astype(f32)
         sides = ((k_ref, v_ref), (k2_ref, v2_ref))
+        rows = seqs * width
+        products = jnp.concatenate(
+            [
+                dmix_low[slot_rows(slot)] * sides[s // chips][1][slot_rows(s % chips)]
+                for slot in range(chips)
+                for s in range(seqs)
+            ],
+            axis=0,
+        )
+        found_all = per_head_sum(products, lane_heads)
+        dscores = []
         for slot in range(chips):
-            dout = dmix[slot_rows(slot)]
-            query = q_ref[slot_rows(slot)].astype(f32)
-            products = jnp.concatenate(
-                [
-                    dout * sides[s // chips][1][slot_rows(s % chips)].astype(f32)
-                    for s in range(seqs)
-                ],
-                axis=0,
-            )
-            found = per_head_sum(products, lane_heads)
+            found = found_all[slot * rows : (slot + 1) * rows]
             weights = probs_ref[slot]
             mean = None
             for s in range(seqs):
-                rows = slice(s * width, (s + 1) * width)
-                term = weights[rows] * found[rows]
+                at = slice(s * width, (s + 1) * width)
+                term = weights[at] * found[at]
                 mean = term if mean is None else mean + term
-            dscores = (weights * (found - jnp.concatenate([mean] * seqs, axis=0))).astype(bf16)
-            wide_d = dot_back(dscores, lane_heads)
-            wide_p = dot_back(weights.astype(bf16), lane_heads)
+            dscores.append(
+                (weights * (found - jnp.concatenate([mean] * seqs, axis=0))).astype(bf16)
+            )
+        wide_d = dot_back(jnp.concatenate(dscores, axis=0), lane_heads)
+        wide_p = dot_back(probs_ref[...].astype(bf16).reshape(chips * rows, 128), lane_heads)
+
+        def piece(wide, slot, s):
+            start = slot * rows + s * width
+            return wide[start : start + width]
+
+        for slot in range(chips):
             dquery = None
             for s in range(seqs):
-                rows = slice(s * width, (s + 1) * width)
-                term = wide_d[rows] * sides[s // chips][0][slot_rows(s % chips)].astype(f32)
+                term = piece(wide_d, slot, s) * sides[s // chips][0][
+                    slot_rows(s % chips)
+                ].astype(f32)
                 dquery = term if dquery is None else dquery + term
-                wide_ref[0, rows] += wide_d[rows] * query
-                wide_ref[1, rows] += wide_p[rows] * dout
             dq_ref[slot_rows(slot)] = (dquery * col_scale).astype(bf16)
-        dkv_ref[0] = wide_ref[0, :toks] * col_scale
-        dkv_ref[1] = wide_ref[1, :toks]
-        send_ref[0] = (wide_ref[0, toks:] * col_scale).astype(bf16)
-        send_ref[1] = wide_ref[1, toks:].astype(bf16)
+        for s in range(seqs):
+            dkey, dvalue = None, None
+            for slot in range(chips):
+                key_term = piece(wide_d, slot, s) * q_ref[slot_rows(slot)].astype(f32)
+                value_term = piece(wide_p, slot, s) * dmix[slot_rows(slot)]
+                dkey = key_term if dkey is None else dkey + key_term
+                dvalue = value_term if dvalue is None else dvalue + value_term
+            at = slot_rows(s % chips)
+            if s < chips:
+                dkv_ref[0, at] = dkey * col_scale
+                dkv_ref[1, at] = dvalue
+            else:
+                send_ref[0, at] = (dkey * col_scale).astype(bf16)
+                send_ref[1, at] = dvalue.astype(bf16)
 
     grad_two, grad_two_low, col_dq, col_dkv, col_send, sums_three = kernel_call(
         attend_col_back,
@@ -1462,7 +1482,7 @@
             col_probs,
         ],
         smem=(0,),
-        scratch=[pltpu.VMEM((2, 2 * toks, model), f32)],
+        room=24,
     )
     row_low_far, row_mix_far = along_core(normed_one), along_core(row_mix)
     col_low_far, col_mix_far = along_core(normed_two), along_core(col_mix)

time: 270 us -> 268 us (level)
  no operation moved by 1% of the time
where the time goes in v6:
time: 268 us
  waiting for transfers between devices  124 us (46%)
  starting transfers between devices  82.5 us (31%)
  Pallas kernels  50.3 us (19%)
  between operations  4.39 us (2%)
  local copies, waits for them, and re-layouts  3.01 us (1%)
  other arithmetic  2.96 us (1%)
    ppermute x16, waiting for transfers between devices, along_chips(): return lax.ppermute(values, 'seq', [(i, i ^ 2 * step) for i in range(seqs)])  51.1 us
    pallas_call x36, Pallas kernels, kernel_call(): pl.pallas_call(body, grid=(1,) if stream else (), out_shape=out_shapes, i...  50.3 us
    ppermute x21, waiting for transfers between devices, along_cols(): lax.ppermute(values, 'col', [(i, i ^ step) for i in range(cols_axis)])  36.5 us
    ppermute x21, starting transfers between devices, along_cols(): lax.ppermute(values, 'col', [(i, i ^ step) for i in range(cols_axis)])  29.6 us
    ppermute x16, starting transfers between devices, along_chips(): return lax.ppermute(values, 'seq', [(i, i ^ 2 * step) for i in range(seqs)])  29.4 us
    ppermute x28, waiting for transfers between devices, along_core(): return lax.ppermute(values, 'seq', [(i, i ^ 1) for i in range(seqs)])  19.4 us
    ppermute x2, waiting for transfers between devices, to_right(): return lax.ppermute(values, ('col', 'seq'), rightward)  15 us
    ppermute x2, starting transfers between devices, to_right(): return lax.ppermute(values, ('col', 'seq'), rightward)  6.49 us
  transfers between devices with their start and end apart: 73, of which 36 were waited for; matrix products, arithmetic and copies ran while one was open for 2% of the time, Pallas kernels for 12%

profile of v6, /device:TPU:0, one launch (start us, length us, event | category | flops | bytes accessed | tf_op | source)
XLA Modules:
  0.0 267.6 jit_solution(844036123473571502)
XLA Ops:
  4.1 3.0 %collective-permute-start = (bf16[104,768]{1,0:T(8,128)(2,1)}, bf16[104,768]{1,0:T(8,128)(2,1)S(1)}, u32[]{:S(2)}, u32[]{:S(2)}) collective-permute-start(bf16[104,768]{1,0:T(8,128)(2,1)} %get-tuple-element.173), channel_id=1, source_target_pairs={{0,2},{1,3},{2,0},{3,1},{4,6},{5,7},{6,4},{7,5},{8,10},{9,11},{10,... | collective-permute-start | bytes 479240 | tf_op jit(solution)/shard_map/ppermute | solution.py:555
  7.1 2.6 collective-permute-start.1
  14.1 3.2 %pack_rest.1 = (bf16[2,96,768]{2,1,0:T(8,128)(2,1)}, bf16[384,768]{1,0:T(8,128)(2,1)}, bf16[64,768]{1,0:T(8,128)(2,1)}, bf16[160,768]{1,0:T(8,128)(2,1)}, bf16[1...) custom-call(s32[7]{0:T(128)} %stack.42.spot_ref, bf16[96,768]{1,0:T(8,128)(2,1)} %refs_0_.2, bf16[96,768]{1,0:T(8,128)(2,1)} %refs_1_.2, ...), custom_call_target="tpu_custom_call" | custom-call | flops 1 | bytes 1 | tf_op jit(solution)/shard_map/pack_rest/pallas_call | solution.py:415
  17.3 4.8 %collective-permute-done.1.refs_1_ = bf16[104,768]{1,0:T(8,128)(2,1)S(1)} collective-permute-done((bf16[104,768]{1,0:T(8,128)(2,1)}, bf16[104,768]{1,0:T(8,128)(2,1)S(1)}, u32[]{:S(2)}, u32[]{:S(2)}) %collective-permute-start.1) | collective-permute-done | bytes 159776 | tf_op jit(solution)/shard_map/ppermute | solution.py:555
  27.3 2.6 collective-permute-start.4
  32.5 16.9 %collective-permute-done.9.refs_8_ = bf16[312,768]{1,0:T(8,128)(2,1)S(1)} collective-permute-done((bf16[312,768]{1,0:T(8,128)(2,1)S(1)}, bf16[312,768]{1,0:T(8,128)(2,1)S(1)}, u32[]{:S(2)}, u32[]{:S(2)}) %collective-permute-start.9) | collective-permute-done | bytes 479264 | tf_op jit(solution)/shard_map/ppermute | solution.py:561
  50.7 2.8 %collective-permute-done.7.refs_5_ = bf16[392,768]{1,0:T(8,128)(2,1)S(1)} collective-permute-done((bf16[392,768]{1,0:T(8,128)(2,1)S(1)}, bf16[392,768]{1,0:T(8,128)(2,1)S(1)}, u32[]{:S(2)}, u32[]{:S(2)}) %collective-permute-start.7) | collective-permute-done | bytes 602144 | tf_op jit(solution)/shard_map/ppermute | solution.py:558
  59.7 4.9 %collective-permute-start.20 = (bf16[2,2,96,768]{3,2,1,0:T(8,128)(2,1)S(1)}, bf16[2,2,96,768]{3,2,1,0:T(8,128)(2,1)S(1)}, u32[]{:S(2)}, u32[]{:S(2)}) collective-permute-start(bf16[2,2,96,768]{3,2,1,0:T(8,128)(2,1)S(1)} %pair_feed.1.both_ref), channel_id=1, source_target_pairs={{0,2},{1,5},{2,0},{3,7},{4,6},{5,1},{6,4},{7,3},{8,10},{9,13},{10,... | collective-permute-start | bytes 1769480 | tf_op jit(solution)/shard_map/ppermute | solution.py:573
  67.9 3.5 %collective-permute-start.19 = (bf16[288,768]{1,0:T(8,128)(2,1)S(1)}, bf16[288,768]{1,0:T(8,128)(2,1)S(1)}, u32[]{:S(2)}, u32[]{:S(2)}) collective-permute-start(bf16[288,768]{1,0:T(8,128)(2,1)S(1)} %get-tuple-element.193.near_ref), channel_id=1, source_target_pairs={{0,24},{8,16},{16,8},{24,0},{1,25},{9,17},{17,9},{25,1},{2,26},{10... | collective-permute-start | bytes 1327112 | tf_op jit(solution)/shard_map/ppermute | solution.py:561
  71.4 14.5 %collective-permute-done.13.left_ref = bf16[2,128,768]{2,1,0:T(8,128)(2,1)S(1)} collective-permute-done((bf16[2,128,768]{2,1,0:T(8,128)(2,1)S(1)}, bf16[2,128,768]{2,1,0:T(8,128)(2,1)S(1)}, u32[]{:S(2)}, u32[]{:S(2)}) %collective-permute-start.13) | collective-permute-done | bytes 393248 | tf_op jit(solution)/shard_map/ppermute | solution.py:586
  92.6 2.2 collective-permute-done.16.refs_1_
  105.8 7.2 %collective-permute-done.30.last_ref = bf16[2,96,768]{2,1,0:T(8,128)(2,1)S(1)} collective-permute-done((bf16[2,96,768]{2,1,0:T(8,128)(2,1)S(1)}, bf16[2,96,768]{2,1,0:T(8,128)(2,1)S(1)}, u32[]{:S(2)}, u32[]{:S(2)}) %collective-permute-start.30) | collective-permute-done | bytes 294944 | tf_op jit(solution)/shard_map/ppermute | solution.py:555
  113.0 5.1 %collective-permute-done.27.a1 = bf16[128,768]{1,0:T(8,128)(2,1)S(1)} collective-permute-done((bf16[128,768]{1,0:T(8,128)(2,1)S(1)}, bf16[128,768]{1,0:T(8,128)(2,1)S(1)}, u32[]{:S(2)}, u32[]{:S(2)}) %collective-permute-start.27) | collective-permute-done | bytes 196640 | tf_op jit(solution)/shard_map/ppermute | solution.py:561
  119.0 2.5 collective-permute-done.34.last2_ref
  122.2 2.2 feed_main.1
  128.0 3.0 %feed_weights.1 = (bf16[1536,384]{1,0:T(8,128)(2,1)S(1)}, bf16[1536,384]{1,0:T(8,128)(2,1)S(1)}, bf16[128,768]{1,0:T(8,128)(2,1)S(1)}, bf16[128,768]{1,0:T(8,128...) custom-call(s32[7]{0:T(128)S(1)} %copy-done.3, bf16[128,768]{1,0:T(8,128)(2,1)S(1)} %get-tuple-element.205.a0, ...), custom_call_target="tpu_custom_call" | custom-call | flops 1811939328 | bytes 16777216 | tf_op jit(solution)/shard_map/feed_weights/pallas_call | solution.py:415
  132.3 4.0 %collective-permute-done.37.b2 = bf16[128,768]{1,0:T(8,128)(2,1)S(1)} collective-permute-done((bf16[128,768]{1,0:T(8,128)(2,1)S(1)}, bf16[128,768]{1,0:T(8,128)(2,1)S(1)}, u32[]{:S(2)}, u32[]{:S(2)}) %collective-permute-start.37) | collective-permute-done | bytes 196640 | tf_op jit(solution)/shard_map/ppermute | solution.py:561
  136.3 3.5 %attend_col_back.1 = (f32[128,768]{1,0:T(8,128)S(1)}, bf16[128,768]{1,0:T(8,128)(2,1)S(1)}, bf16[128,768]{1,0:T(8,128)(2,1)S(1)}, f32[2,128,768]{2,1,0:T(8,128)S...) custom-call(s32[7]{0:T(128)S(1)} %copy-done.3, bf16[128,768]{1,0:T(8,128)(2,1)S(1)} %get-tuple-element.221.b0, ...), custom_call_target="tpu_custom_call" | custom-call | flops 1 | bytes 1 | tf_op jit(solution)/shard_map/attend_col_back/pallas_call | solution.py:415
  142.2 3.6 %row_entry_back.1 = (bf16[4,128,384]{2,1,0:T(8,128)(2,1)S(1)}, bf16[4,128,384]{2,1,0:T(8,128)(2,1)S(1)}, f32[128,768]{1,0:T(8,128)S(1)}, bf16[128,768]{1,0:T(8,1...) custom-call(s32[7]{0:T(128)S(1)} %copy-done.3, ...), custom_call_target="tpu_custom_call" | custom-call | flops 1 | bytes 1 | tf_op jit(solution)/shard_map/row_entry_back/pallas_call | solution.py:415
  147.3 2.2 attend_row_back.1
  151.4 4.6 %collective-permute-start.48 = (bf16[2,128,768]{2,1,0:T(8,128)(2,1)S(1)}, bf16[2,128,768]{2,1,0:T(8,128)(2,1)S(1)}, u32[]{:S(2)}, u32[]{:S(2)}) collective-permute-start(bf16[2,128,768]{2,1,0:T(8,128)(2,1)S(1)} %get-tuple-element.253), channel_id=1, source_target_pairs={{0,2},{1,3},{2,4},{3,5},{4,6},{5,7},{6,14},{7,15},{14,12},{15,13},... | collective-permute-start | bytes 1179656 | tf_op jit(solution)/shard_map/ppermute | solution.py:586
  167.7 2.6 collective-permute-start.54
  171.9 12.2 %collective-permute-done.54.refs_1_ = bf16[384,384]{1,0:T(8,128)(2,1)S(1)} collective-permute-done((bf16[384,384]{1,0:T(8,128)(2,1)S(1)}, bf16[384,384]{1,0:T(8,128)(2,1)S(1)}, u32[]{:S(2)}, u32[]{:S(2)}) %collective-permute-start.54) | collective-permute-done | bytes 294944 | tf_op jit(solution)/shard_map/ppermute | solution.py:555
  187.5 7.4 %collective-permute-done.56.refs_3_ = bf16[384,384]{1,0:T(8,128)(2,1)S(1)} collective-permute-done((bf16[384,384]{1,0:T(8,128)(2,1)S(1)}, bf16[384,384]{1,0:T(8,128)(2,1)S(1)}, u32[]{:S(2)}, u32[]{:S(2)}) %collective-permute-start.56) | collective-permute-done | bytes 294944 | tf_op jit(solution)/shard_map/ppermute | solution.py:555
  197.7 2.9 %collective-permute-start.57 = (bf16[784,384]{1,0:T(8,128)(2,1)S(1)}, bf16[784,384]{1,0:T(8,128)(2,1)S(1)}, u32[]{:S(2)}, u32[]{:S(2)}) collective-permute-start(bf16[784,384]{1,0:T(8,128)(2,1)S(1)} %get-tuple-element.282), channel_id=1, source_target_pairs={{0,8},{8,0},{16,24},{24,16},{1,9},{9,1},{17,25},{25,17},{2,10},{10... | collective-permute-start | bytes 1806344 | tf_op jit(solution)/shard_map/ppermute | solution.py:561
  206.0 2.4 collective-permute-start.51
  208.4 6.1 %collective-permute-done.58.y_ref = bf16[768,384]{1,0:T(8,128)(2,1)S(1)} collective-permute-done((bf16[768,384]{1,0:T(8,128)(2,1)S(1)}, bf16[768,384]{1,0:T(8,128)(2,1)S(1)}, u32[]{:S(2)}, u32[]{:S(2)}) %collective-permute-start.58) | collective-permute-done | bytes 589856 | tf_op jit(solution)/shard_map/ppermute | solution.py:561
  218.6 7.1 %collective-permute-done.50.refs_2_ = bf16[320,384]{1,0:T(8,128)(2,1)S(1)} collective-permute-done((bf16[320,384]{1,0:T(8,128)(2,1)S(1)}, bf16[320,384]{1,0:T(8,128)(2,1)S(1)}, u32[]{:S(2)}, u32[]{:S(2)}) %collective-permute-start.50) | collective-permute-done | bytes 245792 | tf_op jit(solution)/shard_map/ppermute | solution.py:555
  232.6 3.7 %collective-permute-start.61 = (bf16[208,384]{1,0:T(8,128)(2,1)S(1)}, bf16[208,384]{1,0:T(8,128)(2,1)S(1)}, u32[]{:S(2)}, u32[]{:S(2)}) collective-permute-start(bf16[208,384]{1,0:T(8,128)(2,1)S(1)} %get-tuple-element.289), channel_id=1, source_target_pairs={{0,2},{1,3},{2,0},{3,1},{4,6},{5,7},{6,4},{7,5},{8,10},{9,11},{10,... | collective-permute-start | bytes 479240 | tf_op jit(solution)/shard_map/ppermute | solution.py:555
  236.9 5.0 %collective-permute-done.61.refs_1_ = bf16[208,384]{1,0:T(8,128)(2,1)S(1)} collective-permute-done((bf16[208,384]{1,0:T(8,128)(2,1)S(1)}, bf16[208,384]{1,0:T(8,128)(2,1)S(1)}, u32[]{:S(2)}, u32[]{:S(2)}) %collective-permute-start.61) | collective-permute-done | bytes 159776 | tf_op jit(solution)/shard_map/ppermute | solution.py:555
  243.8 6.6 %collective-permute-done.62.refs_2_ = bf16[208,384]{1,0:T(8,128)(2,1)S(1)} collective-permute-done((bf16[208,384]{1,0:T(8,128)(2,1)S(1)}, bf16[208,384]{1,0:T(8,128)(2,1)S(1)}, u32[]{:S(2)}, u32[]{:S(2)}) %collective-permute-start.62) | collective-permute-done | bytes 159776 | tf_op jit(solution)/shard_map/ppermute | solution.py:555
  260.8 2.8 %spread_pair.1 = (f32[96,3072]{1,0:T(8,128)}, f32[384,768]{1,0:T(8,128)}, f32[96,768]{1,0:T(8,128)}, f32[96,768]{1,0:T(8,128)}, f32[96,768]{1,0:T(8,128)}, /*index=5*/f32[96,768]{1,0:T(8,128)}) custom-call(s32[7]{0:T(128)S(1)} %copy-done.3, bf16[288,768]{1,0:T(8,128)(2,1)S(1)} %join_two.1.u0, bf16[288,768]{1,0:T(8,128)(2,1)S(1)} %collective-permute-done.67.u1, ...), custom_call_target="tpu_custom_call" | custom-call | flops 1 | bytes 1 | tf_op jit(solution)/shard_map/spread_pair/pallas_call | solution.py:415
  (180 shorter events, 105.5 us)
Async XLA Ops:
  4.1 13.2 %collective-permute-start = (bf16[104,768]{1,0:T(8,128)(2,1)}, bf16[104,768]{1,0:T(8,128)(2,1)S(1)}, u32[]{:S(2)}, u32[]{:S(2)}) collective-permute-start(bf16[104,768]{1,0:T(8,128)(2,1)} %get-tuple-element.173), channel_id=1, source_target_pairs={{0,2},{1,3},{2,0},{3,1},{4,6},{5,7},{6,4},{7,5},{8,10},{9,11},{10,... | collective-permute-start | bytes 479240 | tf_op jit(solution)/shard_map/ppermute | solution.py:555
  7.1 15.0 %collective-permute-start.1 = (bf16[104,768]{1,0:T(8,128)(2,1)}, bf16[104,768]{1,0:T(8,128)(2,1)S(1)}, u32[]{:S(2)}, u32[]{:S(2)}) collective-permute-start(bf16[104,768]{1,0:T(8,128)(2,1)} %get-tuple-element.173), channel_id=1, source_target_pairs={{0,4},{1,5},{2,6},{3,7},{4,0},{5,1},{6,2},{7,3},{8,12},{9,13},{10,... | collective-permute-start | bytes 479240 | tf_op jit(solution)/shard_map/ppermute | solution.py:555
  24.2 25.9 %collective-permute-start.8 = (bf16[624,768]{1,0:T(8,128)(2,1)S(1)}, bf16[624,768]{1,0:T(8,128)(2,1)S(1)}, u32[]{:S(2)}, u32[]{:S(2)}) collective-permute-start(bf16[624,768]{1,0:T(8,128)(2,1)S(1)} %join_cores.2.refs_6_), channel_id=1, source_target_pairs={{0,8},{1,17},{2,10},{3,19},{4,12},{5,21},{6,14},{7,23},{8,0},{9,25... | collective-permute-start | bytes 2875400 | tf_op jit(solution)/shard_map/ppermute | solution.py:569
  25.8 23.6 %collective-permute-start.9 = (bf16[312,768]{1,0:T(8,128)(2,1)S(1)}, bf16[312,768]{1,0:T(8,128)(2,1)S(1)}, u32[]{:S(2)}, u32[]{:S(2)}) collective-permute-start(bf16[312,768]{1,0:T(8,128)(2,1)S(1)} %stack_row.1.near_ref), channel_id=1, source_target_pairs={{0,24},{8,16},{16,8},{24,0},{1,25},{9,17},{17,9},{25,1},{2,26},{10... | collective-permute-start | bytes 1437704 | tf_op jit(solution)/shard_map/ppermute | solution.py:561
  27.3 22.1 %collective-permute-start.4 = (bf16[160,768]{1,0:T(8,128)(2,1)S(1)}, bf16[160,768]{1,0:T(8,128)(2,1)S(1)}, u32[]{:S(2)}, u32[]{:S(2)}) collective-permute-start(bf16[160,768]{1,0:T(8,128)(2,1)S(1)} %copy-done.7), channel_id=1, source_target_pairs={{0,2},{1,3},{2,0},{3,1},{4,6},{5,7},{6,4},{7,5},{8,10},{9,11},{10,... | collective-permute-start | bytes 737288 | tf_op jit(solution)/shard_map/ppermute | solution.py:555
  29.9 20.3 %collective-permute-start.5 = (bf16[160,768]{1,0:T(8,128)(2,1)S(1)}, bf16[160,768]{1,0:T(8,128)(2,1)S(1)}, u32[]{:S(2)}, u32[]{:S(2)}) collective-permute-start(bf16[160,768]{1,0:T(8,128)(2,1)S(1)} %copy-done.6), channel_id=1, source_target_pairs={{0,4},{1,5},{2,6},{3,7},{4,0},{5,1},{6,2},{7,3},{8,12},{9,13},{10,... | collective-permute-start | bytes 737288 | tf_op jit(solution)/shard_map/ppermute | solution.py:555
  31.0 19.2 %collective-permute-start.6 = (bf16[160,768]{1,0:T(8,128)(2,1)S(1)}, bf16[160,768]{1,0:T(8,128)(2,1)S(1)}, u32[]{:S(2)}, u32[]{:S(2)}) collective-permute-start(bf16[160,768]{1,0:T(8,128)(2,1)S(1)} %copy-done.5), channel_id=1, source_target_pairs={{0,6},{1,7},{2,4},{3,5},{4,2},{5,3},{6,0},{7,1},{8,14},{9,15},{10,... | collective-permute-start | bytes 737288 | tf_op jit(solution)/shard_map/ppermute | solution.py:555
  58.1 33.4 %collective-permute-start.18 = (bf16[576,768]{1,0:T(8,128)(2,1)S(1)}, bf16[576,768]{1,0:T(8,128)(2,1)S(1)}, u32[]{:S(2)}, u32[]{:S(2)}) collective-permute-start(bf16[576,768]{1,0:T(8,128)(2,1)S(1)} %join_cores.3.refs_2_), channel_id=1, source_target_pairs={{0,8},{1,17},{2,10},{3,19},{4,12},{5,21},{6,14},{7,23},{8,0},{9,25... | collective-permute-start | bytes 2654216 | tf_op jit(solution)/shard_map/ppermute | solution.py:569
  59.7 31.8 %collective-permute-start.20 = (bf16[2,2,96,768]{3,2,1,0:T(8,128)(2,1)S(1)}, bf16[2,2,96,768]{3,2,1,0:T(8,128)(2,1)S(1)}, u32[]{:S(2)}, u32[]{:S(2)}) collective-permute-start(bf16[2,2,96,768]{3,2,1,0:T(8,128)(2,1)S(1)} %pair_feed.1.both_ref), channel_id=1, source_target_pairs={{0,2},{1,5},{2,0},{3,7},{4,6},{5,1},{6,4},{7,3},{8,10},{9,13},{10,... | collective-permute-start | bytes 1769480 | tf_op jit(solution)/shard_map/ppermute | solution.py:573
  64.5 21.4 %collective-permute-start.13 = (bf16[2,128,768]{2,1,0:T(8,128)(2,1)S(1)}, bf16[2,128,768]{2,1,0:T(8,128)(2,1)S(1)}, u32[]{:S(2)}, u32[]{:S(2)}) collective-permute-start(bf16[2,128,768]{2,1,0:T(8,128)(2,1)S(1)} %get-tuple-element.186.near_ref), channel_id=1, source_target_pairs={{0,2},{1,3},{2,4},{3,5},{4,6},{5,7},{6,14},{7,15},{14,12},{15,13},... | collective-permute-start | bytes 1179656 | tf_op jit(solution)/shard_map/ppermute | solution.py:586
  66.4 20.2 %collective-permute-start.14 = (bf16[2,128,768]{2,1,0:T(8,128)(2,1)S(1)}, bf16[2,128,768]{2,1,0:T(8,128)(2,1)S(1)}, u32[]{:S(2)}, u32[]{:S(2)}) collective-permute-start(bf16[2,128,768]{2,1,0:T(8,128)(2,1)S(1)} %get-tuple-element.186.near_ref), channel_id=1, source_target_pairs={{2,0},{3,1},{4,2},{5,3},{6,4},{7,5},{14,6},{15,7},{12,14},{13,15},... | collective-permute-start | bytes 1179656 | tf_op jit(solution)/shard_map/ppermute | solution.py:589
  67.9 23.5 %collective-permute-start.19 = (bf16[288,768]{1,0:T(8,128)(2,1)S(1)}, bf16[288,768]{1,0:T(8,128)(2,1)S(1)}, u32[]{:S(2)}, u32[]{:S(2)}) collective-permute-start(bf16[288,768]{1,0:T(8,128)(2,1)S(1)} %get-tuple-element.193.near_ref), channel_id=1, source_target_pairs={{0,24},{8,16},{16,8},{24,0},{1,25},{9,17},{17,9},{25,1},{2,26},{10... | collective-permute-start | bytes 1327112 | tf_op jit(solution)/shard_map/ppermute | solution.py:561
  97.6 15.4 %collective-permute-start.32 = (bf16[256,768]{1,0:T(8,128)(2,1)S(1)}, bf16[256,768]{1,0:T(8,128)(2,1)S(1)}, u32[]{:S(2)}, u32[]{:S(2)}) collective-permute-start(bf16[256,768]{1,0:T(8,128)(2,1)S(1)} %join_given.1), channel_id=1, source_target_pairs={{0,8},{1,17},{2,10},{3,19},{4,12},{5,21},{6,14},{7,23},{8,0},{9,25... | collective-permute-start | bytes 1179656 | tf_op jit(solution)/shard_map/ppermute | solution.py:569
  100.9 17.6 %collective-permute-start.29 = (bf16[256,768]{1,0:T(8,128)(2,1)S(1)}, bf16[256,768]{1,0:T(8,128)(2,1)S(1)}, u32[]{:S(2)}, u32[]{:S(2)}) collective-permute-start(bf16[256,768]{1,0:T(8,128)(2,1)S(1)} %get-tuple-element.206), channel_id=1, source_target_pairs={{0,24},{8,16},{16,8},{24,0},{1,25},{9,17},{17,9},{25,1},{2,26},{10... | collective-permute-start | bytes 1179656 | tf_op jit(solution)/shard_map/ppermute | solution.py:561
  104.4 13.7 %collective-permute-start.27 = (bf16[128,768]{1,0:T(8,128)(2,1)S(1)}, bf16[128,768]{1,0:T(8,128)(2,1)S(1)}, u32[]{:S(2)}, u32[]{:S(2)}) collective-permute-start(bf16[128,768]{1,0:T(8,128)(2,1)S(1)} %get-tuple-element.205.a0), channel_id=1, source_target_pairs={{0,8},{8,0},{16,24},{24,16},{1,9},{9,1},{17,25},{25,17},{2,10},{10... | collective-permute-start | bytes 589832 | tf_op jit(solution)/shard_map/ppermute | solution.py:561
  149.5 17.0 %collective-permute-start.53 = (bf16[1536,384]{1,0:T(8,128)(2,1)S(1)}, bf16[1536,384]{1,0:T(8,128)(2,1)S(1)}, u32[]{:S(2)}, u32[]{:S(2)}) collective-permute-start(bf16[1536,384]{1,0:T(8,128)(2,1)S(1)} %get-tuple-element.276), channel_id=1, source_target_pairs={{0,1},{1,0},{2,3},{3,2},{4,5},{5,4},{6,7},{7,6},{8,9},{9,8},{10,11... | collective-permute-start | bytes 3538952 | tf_op jit(solution)/shard_map/ppermute | solution.py:558
  159.4 36.3 %collective-permute-start.44 = (bf16[1024,384]{1,0:T(8,128)(2,1)S(1)}, bf16[1024,384]{1,0:T(8,128)(2,1)S(1)}, u32[]{:S(2)}, u32[]{:S(2)}) collective-permute-start(bf16[1024,384]{1,0:T(8,128)(2,1)S(1)} %get-tuple-element.248), channel_id=1, source_target_pairs={{0,8},{8,0},{16,24},{24,16},{1,9},{9,1},{17,25},{25,17},{2,10},{10... | collective-permute-start | bytes 2359304 | tf_op jit(solution)/shard_map/ppermute | solution.py:561
  161.5 36.3 %collective-permute-start.45 = (bf16[1024,384]{1,0:T(8,128)(2,1)S(1)}, bf16[1024,384]{1,0:T(8,128)(2,1)S(1)}, u32[]{:S(2)}, u32[]{:S(2)}) collective-permute-start(bf16[1024,384]{1,0:T(8,128)(2,1)S(1)} %get-tuple-element.249), channel_id=1, source_target_pairs={{0,16},{8,24},{16,0},{24,8},{1,17},{9,25},{17,1},{25,9},{2,18},{10... | collective-permute-start | bytes 2359304 | tf_op jit(solution)/shard_map/ppermute | solution.py:561
  163.2 34.6 %collective-permute-start.46 = (bf16[1024,384]{1,0:T(8,128)(2,1)S(1)}, bf16[1024,384]{1,0:T(8,128)(2,1)S(1)}, u32[]{:S(2)}, u32[]{:S(2)}) collective-permute-start(bf16[1024,384]{1,0:T(8,128)(2,1)S(1)} %get-tuple-element.250), channel_id=1, source_target_pairs={{0,24},{8,16},{16,8},{24,0},{1,25},{9,17},{17,9},{25,1},{2,26},{10... | collective-permute-start | bytes 2359304 | tf_op jit(solution)/shard_map/ppermute | solution.py:561
  167.7 16.5 %collective-permute-start.54 = (bf16[384,384]{1,0:T(8,128)(2,1)S(1)}, bf16[384,384]{1,0:T(8,128)(2,1)S(1)}, u32[]{:S(2)}, u32[]{:S(2)}) collective-permute-start(bf16[384,384]{1,0:T(8,128)(2,1)S(1)} %get-tuple-element.278), channel_id=1, source_target_pairs={{0,2},{1,3},{2,0},{3,1},{4,6},{5,7},{6,4},{7,5},{8,10},{9,11},{10,... | collective-permute-start | bytes 884744 | tf_op jit(solution)/shard_map/ppermute | solution.py:555
  170.2 17.2 %collective-permute-start.55 = (bf16[384,384]{1,0:T(8,128)(2,1)S(1)}, bf16[384,384]{1,0:T(8,128)(2,1)S(1)}, u32[]{:S(2)}, u32[]{:S(2)}) collective-permute-start(bf16[384,384]{1,0:T(8,128)(2,1)S(1)} %get-tuple-element.279), channel_id=1, source_target_pairs={{0,4},{1,5},{2,6},{3,7},{4,0},{5,1},{6,2},{7,3},{8,12},{9,13},{10,... | collective-permute-start | bytes 884744 | tf_op jit(solution)/shard_map/ppermute | solution.py:555
  197.7 16.7 %collective-permute-start.57 = (bf16[784,384]{1,0:T(8,128)(2,1)S(1)}, bf16[784,384]{1,0:T(8,128)(2,1)S(1)}, u32[]{:S(2)}, u32[]{:S(2)}) collective-permute-start(bf16[784,384]{1,0:T(8,128)(2,1)S(1)} %get-tuple-element.282), channel_id=1, source_target_pairs={{0,8},{8,0},{16,24},{24,16},{1,9},{9,1},{17,25},{25,17},{2,10},{10... | collective-permute-start | bytes 1806344 | tf_op jit(solution)/shard_map/ppermute | solution.py:561
  200.6 13.9 %collective-permute-start.58 = (bf16[768,384]{1,0:T(8,128)(2,1)S(1)}, bf16[768,384]{1,0:T(8,128)(2,1)S(1)}, u32[]{:S(2)}, u32[]{:S(2)}) collective-permute-start(bf16[768,384]{1,0:T(8,128)(2,1)S(1)} %get-tuple-element.283), channel_id=1, source_target_pairs={{0,16},{8,24},{16,0},{24,8},{1,17},{9,25},{17,1},{25,9},{2,18},{10... | collective-permute-start | bytes 1769480 | tf_op jit(solution)/shard_map/ppermute | solution.py:561
  204.0 14.6 %collective-permute-start.49 = (bf16[320,384]{1,0:T(8,128)(2,1)S(1)}, bf16[320,384]{1,0:T(8,128)(2,1)S(1)}, u32[]{:S(2)}, u32[]{:S(2)}) collective-permute-start(bf16[320,384]{1,0:T(8,128)(2,1)S(1)} %get-tuple-element.265), channel_id=1, source_target_pairs={{0,2},{1,3},{2,0},{3,1},{4,6},{5,7},{6,4},{7,5},{8,10},{9,11},{10,... | collective-permute-start | bytes 737288 | tf_op jit(solution)/shard_map/ppermute | solution.py:555
  205.3 20.3 %collective-permute-start.50 = (bf16[320,384]{1,0:T(8,128)(2,1)S(1)}, bf16[320,384]{1,0:T(8,128)(2,1)S(1)}, u32[]{:S(2)}, u32[]{:S(2)}) collective-permute-start(bf16[320,384]{1,0:T(8,128)(2,1)S(1)} %get-tuple-element.266), channel_id=1, source_target_pairs={{0,4},{1,5},{2,6},{3,7},{4,0},{5,1},{6,2},{7,3},{8,12},{9,13},{10,... | collective-permute-start | bytes 737288 | tf_op jit(solution)/shard_map/ppermute | solution.py:555
  206.0 19.7 %collective-permute-start.51 = (bf16[320,384]{1,0:T(8,128)(2,1)S(1)}, bf16[320,384]{1,0:T(8,128)(2,1)S(1)}, u32[]{:S(2)}, u32[]{:S(2)}) collective-permute-start(bf16[320,384]{1,0:T(8,128)(2,1)S(1)} %get-tuple-element.267), channel_id=1, source_target_pairs={{0,6},{1,7},{2,4},{3,5},{4,2},{5,3},{6,0},{7,1},{8,14},{9,15},{10,... | collective-permute-start | bytes 737288 | tf_op jit(solution)/shard_map/ppermute | solution.py:555
  215.0 16.8 %collective-permute-start.59 = (bf16[400,384]{1,0:T(8,128)(2,1)S(1)}, bf16[400,384]{1,0:T(8,128)(2,1)S(1)}, u32[]{:S(2)}, u32[]{:S(2)}) collective-permute-start(bf16[400,384]{1,0:T(8,128)(2,1)S(1)} %get-tuple-element.285), channel_id=1, source_target_pairs={{0,16},{8,24},{16,0},{24,8},{1,17},{9,25},{17,1},{25,9},{2,18},{10... | collective-permute-start | bytes 921608 | tf_op jit(solution)/shard_map/ppermute | solution.py:561
  217.1 14.7 %collective-permute-start.60 = (bf16[384,384]{1,0:T(8,128)(2,1)S(1)}, bf16[384,384]{1,0:T(8,128)(2,1)S(1)}, u32[]{:S(2)}, u32[]{:S(2)}) collective-permute-start(bf16[384,384]{1,0:T(8,128)(2,1)S(1)} %get-tuple-element.287), channel_id=1, source_target_pairs={{0,8},{8,0},{16,24},{24,16},{1,9},{9,1},{17,25},{25,17},{2,10},{10... | collective-permute-start | bytes 884744 | tf_op jit(solution)/shard_map/ppermute | solution.py:561
  228.2 25.8 %collective-permute-start.67 = (bf16[288,768]{1,0:T(8,128)(2,1)S(1)}, bf16[288,768]{1,0:T(8,128)(2,1)S(1)}, u32[]{:S(2)}, u32[]{:S(2)}) collective-permute-start(bf16[288,768]{1,0:T(8,128)(2,1)S(1)} %join_two.1.u0), channel_id=1, source_target_pairs={{0,8},{8,0},{16,24},{24,16},{1,9},{9,1},{17,25},{25,17},{2,10},{10... | collective-permute-start | bytes 1327112 | tf_op jit(solution)/shard_map/ppermute | solution.py:561
  230.3 23.8 %collective-permute-start.68 = (bf16[288,768]{1,0:T(8,128)(2,1)S(1)}, bf16[288,768]{1,0:T(8,128)(2,1)S(1)}, u32[]{:S(2)}, u32[]{:S(2)}) collective-permute-start(bf16[288,768]{1,0:T(8,128)(2,1)S(1)} %join_two.1.u0), channel_id=1, source_target_pairs={{0,16},{8,24},{16,0},{24,8},{1,17},{9,25},{17,1},{25,9},{2,18},{10... | collective-permute-start | bytes 1327112 | tf_op jit(solution)/shard_map/ppermute | solution.py:561
  230.3 23.8 %collective-permute-start.69 = (bf16[288,768]{1,0:T(8,128)(2,1)S(1)}, bf16[288,768]{1,0:T(8,128)(2,1)S(1)}, u32[]{:S(2)}, u32[]{:S(2)}) collective-permute-start(bf16[288,768]{1,0:T(8,128)(2,1)S(1)} %join_two.1.u0), channel_id=1, source_target_pairs={{0,24},{8,16},{16,8},{24,0},{1,25},{9,17},{17,9},{25,1},{2,26},{10... | collective-permute-start | bytes 1327112 | tf_op jit(solution)/shard_map/ppermute | solution.py:561
  236.3 14.1 %collective-permute-start.62 = (bf16[208,384]{1,0:T(8,128)(2,1)S(1)}, bf16[208,384]{1,0:T(8,128)(2,1)S(1)}, u32[]{:S(2)}, u32[]{:S(2)}) collective-permute-start(bf16[208,384]{1,0:T(8,128)(2,1)S(1)} %get-tuple-element.290), channel_id=1, source_target_pairs={{0,4},{1,5},{2,6},{3,7},{4,0},{5,1},{6,2},{7,3},{8,12},{9,13},{10,... | collective-permute-start | bytes 479240 | tf_op jit(solution)/shard_map/ppermute | solution.py:555
  (49 other events, 348.2 us)

commit v7 on v6

--- a/solution.py
+++ b/solution.py
@@ -983,17 +983,22 @@
     ):
         lane_heads = head_of_lane(model)
         sides = ((k_ref, v_ref), (k2_ref, v2_ref))
+        rows = seqs * width
+        products = jnp.concatenate(
+            [
+                q_ref[slot_rows(slot)] * sides[s // chips][0][slot_rows(s % chips)]
+                for slot in range(chips)
+                for s in range(seqs)
+            ],
+            axis=0,
+        )
+        found_all = per_head_sum(products, lane_heads) * col_scale
+        weights_all = []
         for slot in range(chips):
-            query = q_ref[slot_rows(slot)]
-            products = jnp.concatenate(
-                [
-                    query * sides[s // chips][0][slot_rows(s % chips)]
-                    for s in range(seqs)
-                ],
-                axis=0,
-            )
-            found = per_head_sum(products, lane_heads) * col_scale
-            parts = [found[s * width : (s + 1) * width] for s in range(seqs)]
+            start = slot * rows
+            parts = [
+                found_all[start + s * width : start + (s + 1) * width] for s in range(seqs)
+            ]
             largest = parts[0]
             for item in parts[1:]:
                 largest = jnp.maximum(largest, item)
@@ -1003,10 +1008,13 @@
                 total = total + item
             weights = jnp.concatenate([item / total for item in powers], axis=0)
             probs_ref[slot] = weights
-            wide = dot_back(weights.astype(bf16), lane_heads)
+            weights_all.append(weights.astype(bf16))
+        wide = dot_back(jnp.concatenate(weights_all, axis=0), lane_heads)
+        for slot in range(chips):
             mixed = None
             for s in range(seqs):
-                term = wide[s * width : (s + 1) * width] * sides[s // chips][1][
+                start = slot * rows + s * width
+                term = wide[start : start + width] * sides[s // chips][1][
                     slot_rows(s % chips)
                 ].astype(f32)
                 mixed = term if mixed is None else mixed + term
@@ -1789,10 +1797,20 @@
         keep, along_cols(give, 2), keep2, along_cols(give2, 1), extra, [], []
     )
     row_reached = over_chips(row_slices)
-    row_keep, row_swap = split_cores(row_reached, 1, extra)
-
-    def join_row(spot_ref, keep_ref, got_ref, out_ref, norm_ref, entropy_ref):
+    result = order_rows(col_reached, block)
+    grad_in = order_rows(col_reached, block + 2 * width)
+    row_keep, row_swap = split_cores(after(row_reached, result, grad_in), 1, extra)
+
+    row_got_back = along_core(row_swap)
+
+    def join_row(spot_ref, keep_ref, got_ref, out_ref):
         out_ref[...] = join_halves(spot_ref, keep_ref[:shard], got_ref[:shard])
+
+    (row_join,) = kernel_call(
+        join_row, [((shard, model), bf16)], [spot, row_keep, row_got_back], smem=(0,)
+    )
+
+    def pick_norms(spot_ref, keep_ref, got_ref, norm_ref, entropy_ref):
         total = keep_ref[shard:].astype(f32) + got_ref[shard:].astype(f32)
         line = total[6:7]
         entropy_ref[...] = line[:, 0:1] + line[:, 1:2]
@@ -1804,15 +1822,13 @@
             found = jnp.where(at == index, here, found)
         norm_ref[...] = found
 
-    row_join, norm_here, entropy_sum = kernel_call(
-        join_row,
-        [((shard, model), bf16), ((lines, shard), f32), ((1, 1), f32)],
-        [spot, row_keep, along_core(row_swap)],
+    norm_here, entropy_sum = kernel_call(
+        pick_norms,
+        [((lines, shard), f32), ((1, 1), f32)],
+        [spot, row_keep, after(row_got_back, row_join)],
         smem=(0,),
     )
     row_ends = over_cols(after(row_join, pair_ends))
-    result = order_rows(after(col_reached, row_join), block)
-    grad_in = order_rows(after(col_reached, row_join), block + 2 * width)
     grad_feed_in, grad_feed_out, *col_grads = kernel_call(
         spread_pair,
         [(feed_in.shape, f32), (feed_out.shape, f32)] + [((shard, model), f32)] * cols_axis,

time: 268 us -> 267 us (level)
    pallas_call x36 -> x37, Pallas kernels: 50.3 us -> 50.9 us  [kernel_call(): pl.pallas_call(body, grid=(1,) if stream else (), out_shape=out_shapes, i...]
where the time goes in v7:
time: 267 us
  waiting for transfers between devices  123 us (46%)
  starting transfers between devices  82.6 us (31%)
  Pallas kernels  50.9 us (19%)
  between operations  4.42 us (2%)
  local copies, waits for them, and re-layouts  3.01 us (1%)
  other arithmetic  2.96 us (1%)
    pallas_call x37, Pallas kernels, kernel_call(): pl.pallas_call(body, grid=(1,) if stream else (), out_shape=out_shapes, i...  50.9 us
    ppermute x16, waiting for transfers between devices, along_chips(): return lax.ppermute(values, 'seq', [(i, i ^ 2 * step) for i in range(seqs)])  48.6 us
    ppermute x21, waiting for transfers between devices, along_cols(): lax.ppermute(values, 'col', [(i, i ^ step) for i in range(cols_axis)])  37.5 us
    ppermute x21, starting transfers between devices, along_cols(): lax.ppermute(values, 'col', [(i, i ^ step) for i in range(cols_axis)])  29.6 us
    ppermute x16, starting transfers between devices, along_chips(): return lax.ppermute(values, 'seq', [(i, i ^ 2 * step) for i in range(seqs)])  29.4 us
    ppermute x28, waiting for transfers between devices, along_core(): return lax.ppermute(values, 'seq', [(i, i ^ 1) for i in range(seqs)])  19.4 us
    ppermute x2, waiting for transfers between devices, to_right(): return lax.ppermute(values, ('col', 'seq'), rightward)  15 us
    ppermute x2, starting transfers between devices, to_right(): return lax.ppermute(values, ('col', 'seq'), rightward)  6.49 us
  transfers between devices with their start and end apart: 73, of which 36 were waited for; matrix products, arithmetic and copies ran while one was open for 2% of the time, Pallas kernels for 12%

profile of v7, /device:TPU:0, one launch (start us, length us, event | category | flops | bytes accessed | tf_op | source)
XLA Modules:
  0.0 266.7 jit_solution(12899143955992826076)
XLA Ops:
  4.1 3.0 %collective-permute-start = (bf16[104,768]{1,0:T(8,128)(2,1)}, bf16[104,768]{1,0:T(8,128)(2,1)S(1)}, u32[]{:S(2)}, u32[]{:S(2)}) collective-permute-start(bf16[104,768]{1,0:T(8,128)(2,1)} %get-tuple-element.173), channel_id=1, source_target_pairs={{0,2},{1,3},{2,0},{3,1},{4,6},{5,7},{6,4},{7,5},{8,10},{9,11},{10,... | collective-permute-start | bytes 479240 | tf_op jit(solution)/shard_map/ppermute | solution.py:555
  7.1 2.6 collective-permute-start.1
  14.1 3.2 %pack_rest.1 = (bf16[2,96,768]{2,1,0:T(8,128)(2,1)}, bf16[384,768]{1,0:T(8,128)(2,1)}, bf16[64,768]{1,0:T(8,128)(2,1)}, bf16[160,768]{1,0:T(8,128)(2,1)}, bf16[1...) custom-call(s32[7]{0:T(128)} %stack.42.spot_ref, bf16[96,768]{1,0:T(8,128)(2,1)} %refs_0_.2, bf16[96,768]{1,0:T(8,128)(2,1)} %refs_1_.2, ...), custom_call_target="tpu_custom_call" | custom-call | flops 1 | bytes 1 | tf_op jit(solution)/shard_map/pack_rest/pallas_call | solution.py:415
  17.3 4.8 %collective-permute-done.1.refs_1_ = bf16[104,768]{1,0:T(8,128)(2,1)S(1)} collective-permute-done((bf16[104,768]{1,0:T(8,128)(2,1)}, bf16[104,768]{1,0:T(8,128)(2,1)S(1)}, u32[]{:S(2)}, u32[]{:S(2)}) %collective-permute-start.1) | collective-permute-done | bytes 159776 | tf_op jit(solution)/shard_map/ppermute | solution.py:555
  27.3 2.6 collective-permute-start.4
  32.5 16.9 %collective-permute-done.9.refs_8_ = bf16[312,768]{1,0:T(8,128)(2,1)S(1)} collective-permute-done((bf16[312,768]{1,0:T(8,128)(2,1)S(1)}, bf16[312,768]{1,0:T(8,128)(2,1)S(1)}, u32[]{:S(2)}, u32[]{:S(2)}) %collective-permute-start.9) | collective-permute-done | bytes 479264 | tf_op jit(solution)/shard_map/ppermute | solution.py:561
  50.7 2.8 %collective-permute-done.7.refs_5_ = bf16[392,768]{1,0:T(8,128)(2,1)S(1)} collective-permute-done((bf16[392,768]{1,0:T(8,128)(2,1)S(1)}, bf16[392,768]{1,0:T(8,128)(2,1)S(1)}, u32[]{:S(2)}, u32[]{:S(2)}) %collective-permute-start.7) | collective-permute-done | bytes 602144 | tf_op jit(solution)/shard_map/ppermute | solution.py:558
  59.7 4.9 %collective-permute-start.20 = (bf16[2,2,96,768]{3,2,1,0:T(8,128)(2,1)S(1)}, bf16[2,2,96,768]{3,2,1,0:T(8,128)(2,1)S(1)}, u32[]{:S(2)}, u32[]{:S(2)}) collective-permute-start(bf16[2,2,96,768]{3,2,1,0:T(8,128)(2,1)S(1)} %pair_feed.1.both_ref), channel_id=1, source_target_pairs={{0,2},{1,5},{2,0},{3,7},{4,6},{5,1},{6,4},{7,3},{8,10},{9,13},{10,... | collective-permute-start | bytes 1769480 | tf_op jit(solution)/shard_map/ppermute | solution.py:573
  67.9 3.5 %collective-permute-start.19 = (bf16[288,768]{1,0:T(8,128)(2,1)S(1)}, bf16[288,768]{1,0:T(8,128)(2,1)S(1)}, u32[]{:S(2)}, u32[]{:S(2)}) collective-permute-start(bf16[288,768]{1,0:T(8,128)(2,1)S(1)} %get-tuple-element.193.near_ref), channel_id=1, source_target_pairs={{0,24},{8,16},{16,8},{24,0},{1,25},{9,17},{17,9},{25,1},{2,26},{10... | collective-permute-start | bytes 1327112 | tf_op jit(solution)/shard_map/ppermute | solution.py:561
  71.4 14.5 %collective-permute-done.13.left_ref = bf16[2,128,768]{2,1,0:T(8,128)(2,1)S(1)} collective-permute-done((bf16[2,128,768]{2,1,0:T(8,128)(2,1)S(1)}, bf16[2,128,768]{2,1,0:T(8,128)(2,1)S(1)}, u32[]{:S(2)}, u32[]{:S(2)}) %collective-permute-start.13) | collective-permute-done | bytes 393248 | tf_op jit(solution)/shard_map/ppermute | solution.py:586
  92.6 2.2 collective-permute-done.16.refs_1_
  105.9 7.2 %collective-permute-done.30.last_ref = bf16[2,96,768]{2,1,0:T(8,128)(2,1)S(1)} collective-permute-done((bf16[2,96,768]{2,1,0:T(8,128)(2,1)S(1)}, bf16[2,96,768]{2,1,0:T(8,128)(2,1)S(1)}, u32[]{:S(2)}, u32[]{:S(2)}) %collective-permute-start.30) | collective-permute-done | bytes 294944 | tf_op jit(solution)/shard_map/ppermute | solution.py:555
  113.0 5.1 %collective-permute-done.27.a1 = bf16[128,768]{1,0:T(8,128)(2,1)S(1)} collective-permute-done((bf16[128,768]{1,0:T(8,128)(2,1)S(1)}, bf16[128,768]{1,0:T(8,128)(2,1)S(1)}, u32[]{:S(2)}, u32[]{:S(2)}) %collective-permute-start.27) | collective-permute-done | bytes 196640 | tf_op jit(solution)/shard_map/ppermute | solution.py:561
  119.0 2.5 collective-permute-done.34.last2_ref
  122.2 2.2 feed_main.1
  128.0 3.0 %feed_weights.1 = (bf16[1536,384]{1,0:T(8,128)(2,1)S(1)}, bf16[1536,384]{1,0:T(8,128)(2,1)S(1)}, bf16[128,768]{1,0:T(8,128)(2,1)S(1)}, bf16[128,768]{1,0:T(8,128...) custom-call(s32[7]{0:T(128)S(1)} %copy-done.3, bf16[128,768]{1,0:T(8,128)(2,1)S(1)} %get-tuple-element.205.a0, ...), custom_call_target="tpu_custom_call" | custom-call | flops 1811939328 | bytes 16777216 | tf_op jit(solution)/shard_map/feed_weights/pallas_call | solution.py:415
  132.3 4.0 %collective-permute-done.37.b2 = bf16[128,768]{1,0:T(8,128)(2,1)S(1)} collective-permute-done((bf16[128,768]{1,0:T(8,128)(2,1)S(1)}, bf16[128,768]{1,0:T(8,128)(2,1)S(1)}, u32[]{:S(2)}, u32[]{:S(2)}) %collective-permute-start.37) | collective-permute-done | bytes 196640 | tf_op jit(solution)/shard_map/ppermute | solution.py:561
  136.3 3.5 %attend_col_back.1 = (f32[128,768]{1,0:T(8,128)S(1)}, bf16[128,768]{1,0:T(8,128)(2,1)S(1)}, bf16[128,768]{1,0:T(8,128)(2,1)S(1)}, f32[2,128,768]{2,1,0:T(8,128)S...) custom-call(s32[7]{0:T(128)S(1)} %copy-done.3, bf16[128,768]{1,0:T(8,128)(2,1)S(1)} %get-tuple-element.221.b0, ...), custom_call_target="tpu_custom_call" | custom-call | flops 1 | bytes 1 | tf_op jit(solution)/shard_map/attend_col_back/pallas_call | solution.py:415
  142.2 3.6 %row_entry_back.1 = (bf16[4,128,384]{2,1,0:T(8,128)(2,1)S(1)}, bf16[4,128,384]{2,1,0:T(8,128)(2,1)S(1)}, f32[128,768]{1,0:T(8,128)S(1)}, bf16[128,768]{1,0:T(8,1...) custom-call(s32[7]{0:T(128)S(1)} %copy-done.3, ...), custom_call_target="tpu_custom_call" | custom-call | flops 1 | bytes 1 | tf_op jit(solution)/shard_map/row_entry_back/pallas_call | solution.py:415
  147.3 2.2 attend_row_back.1
  151.4 4.6 %collective-permute-start.48 = (bf16[2,128,768]{2,1,0:T(8,128)(2,1)S(1)}, bf16[2,128,768]{2,1,0:T(8,128)(2,1)S(1)}, u32[]{:S(2)}, u32[]{:S(2)}) collective-permute-start(bf16[2,128,768]{2,1,0:T(8,128)(2,1)S(1)} %get-tuple-element.253), channel_id=1, source_target_pairs={{0,2},{1,3},{2,4},{3,5},{4,6},{5,7},{6,14},{7,15},{14,12},{15,13},... | collective-permute-start | bytes 1179656 | tf_op jit(solution)/shard_map/ppermute | solution.py:586
  167.7 2.6 collective-permute-start.54
  172.0 12.2 %collective-permute-done.54.refs_1_ = bf16[384,384]{1,0:T(8,128)(2,1)S(1)} collective-permute-done((bf16[384,384]{1,0:T(8,128)(2,1)S(1)}, bf16[384,384]{1,0:T(8,128)(2,1)S(1)}, u32[]{:S(2)}, u32[]{:S(2)}) %collective-permute-start.54) | collective-permute-done | bytes 294944 | tf_op jit(solution)/shard_map/ppermute | solution.py:555
  187.5 7.4 %collective-permute-done.56.refs_3_ = bf16[384,384]{1,0:T(8,128)(2,1)S(1)} collective-permute-done((bf16[384,384]{1,0:T(8,128)(2,1)S(1)}, bf16[384,384]{1,0:T(8,128)(2,1)S(1)}, u32[]{:S(2)}, u32[]{:S(2)}) %collective-permute-start.56) | collective-permute-done | bytes 294944 | tf_op jit(solution)/shard_map/ppermute | solution.py:555
  197.8 2.9 %collective-permute-start.57 = (bf16[784,384]{1,0:T(8,128)(2,1)S(1)}, bf16[784,384]{1,0:T(8,128)(2,1)S(1)}, u32[]{:S(2)}, u32[]{:S(2)}) collective-permute-start(bf16[784,384]{1,0:T(8,128)(2,1)S(1)} %get-tuple-element.282), channel_id=1, source_target_pairs={{0,8},{8,0},{16,24},{24,16},{1,9},{9,1},{17,25},{25,17},{2,10},{10... | collective-permute-start | bytes 1806344 | tf_op jit(solution)/shard_map/ppermute | solution.py:561
  206.0 2.5 collective-permute-start.51
  208.5 6.1 %collective-permute-done.58.y_ref = bf16[768,384]{1,0:T(8,128)(2,1)S(1)} collective-permute-done((bf16[768,384]{1,0:T(8,128)(2,1)S(1)}, bf16[768,384]{1,0:T(8,128)(2,1)S(1)}, u32[]{:S(2)}, u32[]{:S(2)}) %collective-permute-start.58) | collective-permute-done | bytes 589856 | tf_op jit(solution)/shard_map/ppermute | solution.py:561
  218.6 7.1 %collective-permute-done.50.refs_2_ = bf16[320,384]{1,0:T(8,128)(2,1)S(1)} collective-permute-done((bf16[320,384]{1,0:T(8,128)(2,1)S(1)}, bf16[320,384]{1,0:T(8,128)(2,1)S(1)}, u32[]{:S(2)}, u32[]{:S(2)}) %collective-permute-start.50) | collective-permute-done | bytes 245792 | tf_op jit(solution)/shard_map/ppermute | solution.py:555
  232.7 3.7 %collective-permute-start.61 = (bf16[208,384]{1,0:T(8,128)(2,1)S(1)}, bf16[208,384]{1,0:T(8,128)(2,1)S(1)}, u32[]{:S(2)}, u32[]{:S(2)}) collective-permute-start(bf16[208,384]{1,0:T(8,128)(2,1)S(1)} %get-tuple-element.289), channel_id=1, source_target_pairs={{0,2},{1,3},{2,0},{3,1},{4,6},{5,7},{6,4},{7,5},{8,10},{9,11},{10,... | collective-permute-start | bytes 479240 | tf_op jit(solution)/shard_map/ppermute | solution.py:555
  236.9 5.0 %collective-permute-done.61.refs_1_ = bf16[208,384]{1,0:T(8,128)(2,1)S(1)} collective-permute-done((bf16[208,384]{1,0:T(8,128)(2,1)S(1)}, bf16[208,384]{1,0:T(8,128)(2,1)S(1)}, u32[]{:S(2)}, u32[]{:S(2)}) %collective-permute-start.61) | collective-permute-done | bytes 159776 | tf_op jit(solution)/shard_map/ppermute | solution.py:555
  246.3 4.1 %collective-permute-done.62.refs_2_ = bf16[208,384]{1,0:T(8,128)(2,1)S(1)} collective-permute-done((bf16[208,384]{1,0:T(8,128)(2,1)S(1)}, bf16[208,384]{1,0:T(8,128)(2,1)S(1)}, u32[]{:S(2)}, u32[]{:S(2)}) %collective-permute-start.62) | collective-permute-done | bytes 159776 | tf_op jit(solution)/shard_map/ppermute | solution.py:555
  258.9 2.8 %spread_pair.1 = (f32[96,3072]{1,0:T(8,128)}, f32[384,768]{1,0:T(8,128)}, f32[96,768]{1,0:T(8,128)}, f32[96,768]{1,0:T(8,128)}, f32[96,768]{1,0:T(8,128)}, /*index=5*/f32[96,768]{1,0:T(8,128)}) custom-call(s32[7]{0:T(128)S(1)} %copy-done.3, bf16[288,768]{1,0:T(8,128)(2,1)S(1)} %join_two.1.u0, bf16[288,768]{1,0:T(8,128)(2,1)S(1)} %collective-permute-done.67.u1, ...), custom_call_target="tpu_custom_call" | custom-call | flops 1 | bytes 1 | tf_op jit(solution)/shard_map/spread_pair/pallas_call | solution.py:415
  (181 shorter events, 107.2 us)
Async XLA Ops:
  4.1 13.2 %collective-permute-start = (bf16[104,768]{1,0:T(8,128)(2,1)}, bf16[104,768]{1,0:T(8,128)(2,1)S(1)}, u32[]{:S(2)}, u32[]{:S(2)}) collective-permute-start(bf16[104,768]{1,0:T(8,128)(2,1)} %get-tuple-element.173), channel_id=1, source_target_pairs={{0,2},{1,3},{2,0},{3,1},{4,6},{5,7},{6,4},{7,5},{8,10},{9,11},{10,... | collective-permute-start | bytes 479240 | tf_op jit(solution)/shard_map/ppermute | solution.py:555
  7.1 15.0 %collective-permute-start.1 = (bf16[104,768]{1,0:T(8,128)(2,1)}, bf16[104,768]{1,0:T(8,128)(2,1)S(1)}, u32[]{:S(2)}, u32[]{:S(2)}) collective-permute-start(bf16[104,768]{1,0:T(8,128)(2,1)} %get-tuple-element.173), channel_id=1, source_target_pairs={{0,4},{1,5},{2,6},{3,7},{4,0},{5,1},{6,2},{7,3},{8,12},{9,13},{10,... | collective-permute-start | bytes 479240 | tf_op jit(solution)/shard_map/ppermute | solution.py:555
  24.2 25.9 %collective-permute-start.8 = (bf16[624,768]{1,0:T(8,128)(2,1)S(1)}, bf16[624,768]{1,0:T(8,128)(2,1)S(1)}, u32[]{:S(2)}, u32[]{:S(2)}) collective-permute-start(bf16[624,768]{1,0:T(8,128)(2,1)S(1)} %join_cores.2.refs_6_), channel_id=1, source_target_pairs={{0,8},{1,17},{2,10},{3,19},{4,12},{5,21},{6,14},{7,23},{8,0},{9,25... | collective-permute-start | bytes 2875400 | tf_op jit(solution)/shard_map/ppermute | solution.py:569
  25.8 23.6 %collective-permute-start.9 = (bf16[312,768]{1,0:T(8,128)(2,1)S(1)}, bf16[312,768]{1,0:T(8,128)(2,1)S(1)}, u32[]{:S(2)}, u32[]{:S(2)}) collective-permute-start(bf16[312,768]{1,0:T(8,128)(2,1)S(1)} %stack_row.1.near_ref), channel_id=1, source_target_pairs={{0,24},{8,16},{16,8},{24,0},{1,25},{9,17},{17,9},{25,1},{2,26},{10... | collective-permute-start | bytes 1437704 | tf_op jit(solution)/shard_map/ppermute | solution.py:561
  27.3 22.1 %collective-permute-start.4 = (bf16[160,768]{1,0:T(8,128)(2,1)S(1)}, bf16[160,768]{1,0:T(8,128)(2,1)S(1)}, u32[]{:S(2)}, u32[]{:S(2)}) collective-permute-start(bf16[160,768]{1,0:T(8,128)(2,1)S(1)} %copy-done.7), channel_id=1, source_target_pairs={{0,2},{1,3},{2,0},{3,1},{4,6},{5,7},{6,4},{7,5},{8,10},{9,11},{10,... | collective-permute-start | bytes 737288 | tf_op jit(solution)/shard_map/ppermute | solution.py:555
  29.9 20.3 %collective-permute-start.5 = (bf16[160,768]{1,0:T(8,128)(2,1)S(1)}, bf16[160,768]{1,0:T(8,128)(2,1)S(1)}, u32[]{:S(2)}, u32[]{:S(2)}) collective-permute-start(bf16[160,768]{1,0:T(8,128)(2,1)S(1)} %copy-done.6), channel_id=1, source_target_pairs={{0,4},{1,5},{2,6},{3,7},{4,0},{5,1},{6,2},{7,3},{8,12},{9,13},{10,... | collective-permute-start | bytes 737288 | tf_op jit(solution)/shard_map/ppermute | solution.py:555
  31.0 19.2 %collective-permute-start.6 = (bf16[160,768]{1,0:T(8,128)(2,1)S(1)}, bf16[160,768]{1,0:T(8,128)(2,1)S(1)}, u32[]{:S(2)}, u32[]{:S(2)}) collective-permute-start(bf16[160,768]{1,0:T(8,128)(2,1)S(1)} %copy-done.5), channel_id=1, source_target_pairs={{0,6},{1,7},{2,4},{3,5},{4,2},{5,3},{6,0},{7,1},{8,14},{9,15},{10,... | collective-permute-start | bytes 737288 | tf_op jit(solution)/shard_map/ppermute | solution.py:555
  58.1 33.4 %collective-permute-start.18 = (bf16[576,768]{1,0:T(8,128)(2,1)S(1)}, bf16[576,768]{1,0:T(8,128)(2,1)S(1)}, u32[]{:S(2)}, u32[]{:S(2)}) collective-permute-start(bf16[576,768]{1,0:T(8,128)(2,1)S(1)} %join_cores.3.refs_2_), channel_id=1, source_target_pairs={{0,8},{1,17},{2,10},{3,19},{4,12},{5,21},{6,14},{7,23},{8,0},{9,25... | collective-permute-start | bytes 2654216 | tf_op jit(solution)/shard_map/ppermute | solution.py:569
  59.7 31.8 %collective-permute-start.20 = (bf16[2,2,96,768]{3,2,1,0:T(8,128)(2,1)S(1)}, bf16[2,2,96,768]{3,2,1,0:T(8,128)(2,1)S(1)}, u32[]{:S(2)}, u32[]{:S(2)}) collective-permute-start(bf16[2,2,96,768]{3,2,1,0:T(8,128)(2,1)S(1)} %pair_feed.1.both_ref), channel_id=1, source_target_pairs={{0,2},{1,5},{2,0},{3,7},{4,6},{5,1},{6,4},{7,3},{8,10},{9,13},{10,... | collective-permute-start | bytes 1769480 | tf_op jit(solution)/shard_map/ppermute | solution.py:573
  64.5 21.4 %collective-permute-start.13 = (bf16[2,128,768]{2,1,0:T(8,128)(2,1)S(1)}, bf16[2,128,768]{2,1,0:T(8,128)(2,1)S(1)}, u32[]{:S(2)}, u32[]{:S(2)}) collective-permute-start(bf16[2,128,768]{2,1,0:T(8,128)(2,1)S(1)} %get-tuple-element.186.near_ref), channel_id=1, source_target_pairs={{0,2},{1,3},{2,4},{3,5},{4,6},{5,7},{6,14},{7,15},{14,12},{15,13},... | collective-permute-start | bytes 1179656 | tf_op jit(solution)/shard_map/ppermute | solution.py:586
  66.4 20.2 %collective-permute-start.14 = (bf16[2,128,768]{2,1,0:T(8,128)(2,1)S(1)}, bf16[2,128,768]{2,1,0:T(8,128)(2,1)S(1)}, u32[]{:S(2)}, u32[]{:S(2)}) collective-permute-start(bf16[2,128,768]{2,1,0:T(8,128)(2,1)S(1)} %get-tuple-element.186.near_ref), channel_id=1, source_target_pairs={{2,0},{3,1},{4,2},{5,3},{6,4},{7,5},{14,6},{15,7},{12,14},{13,15},... | collective-permute-start | bytes 1179656 | tf_op jit(solution)/shard_map/ppermute | solution.py:589
  67.9 23.5 %collective-permute-start.19 = (bf16[288,768]{1,0:T(8,128)(2,1)S(1)}, bf16[288,768]{1,0:T(8,128)(2,1)S(1)}, u32[]{:S(2)}, u32[]{:S(2)}) collective-permute-start(bf16[288,768]{1,0:T(8,128)(2,1)S(1)} %get-tuple-element.193.near_ref), channel_id=1, source_target_pairs={{0,24},{8,16},{16,8},{24,0},{1,25},{9,17},{17,9},{25,1},{2,26},{10... | collective-permute-start | bytes 1327112 | tf_op jit(solution)/shard_map/ppermute | solution.py:561
  97.6 15.4 %collective-permute-start.32 = (bf16[256,768]{1,0:T(8,128)(2,1)S(1)}, bf16[256,768]{1,0:T(8,128)(2,1)S(1)}, u32[]{:S(2)}, u32[]{:S(2)}) collective-permute-start(bf16[256,768]{1,0:T(8,128)(2,1)S(1)} %join_given.1), channel_id=1, source_target_pairs={{0,8},{1,17},{2,10},{3,19},{4,12},{5,21},{6,14},{7,23},{8,0},{9,25... | collective-permute-start | bytes 1179656 | tf_op jit(solution)/shard_map/ppermute | solution.py:569
  100.9 17.6 %collective-permute-start.29 = (bf16[256,768]{1,0:T(8,128)(2,1)S(1)}, bf16[256,768]{1,0:T(8,128)(2,1)S(1)}, u32[]{:S(2)}, u32[]{:S(2)}) collective-permute-start(bf16[256,768]{1,0:T(8,128)(2,1)S(1)} %get-tuple-element.206), channel_id=1, source_target_pairs={{0,24},{8,16},{16,8},{24,0},{1,25},{9,17},{17,9},{25,1},{2,26},{10... | collective-permute-start | bytes 1179656 | tf_op jit(solution)/shard_map/ppermute | solution.py:561
  104.4 13.7 %collective-permute-start.27 = (bf16[128,768]{1,0:T(8,128)(2,1)S(1)}, bf16[128,768]{1,0:T(8,128)(2,1)S(1)}, u32[]{:S(2)}, u32[]{:S(2)}) collective-permute-start(bf16[128,768]{1,0:T(8,128)(2,1)S(1)} %get-tuple-element.205.a0), channel_id=1, source_target_pairs={{0,8},{8,0},{16,24},{24,16},{1,9},{9,1},{17,25},{25,17},{2,10},{10... | collective-permute-start | bytes 589832 | tf_op jit(solution)/shard_map/ppermute | solution.py:561
  149.5 17.0 %collective-permute-start.53 = (bf16[1536,384]{1,0:T(8,128)(2,1)S(1)}, bf16[1536,384]{1,0:T(8,128)(2,1)S(1)}, u32[]{:S(2)}, u32[]{:S(2)}) collective-permute-start(bf16[1536,384]{1,0:T(8,128)(2,1)S(1)} %get-tuple-element.276), channel_id=1, source_target_pairs={{0,1},{1,0},{2,3},{3,2},{4,5},{5,4},{6,7},{7,6},{8,9},{9,8},{10,11... | collective-permute-start | bytes 3538952 | tf_op jit(solution)/shard_map/ppermute | solution.py:558
  159.4 36.3 %collective-permute-start.44 = (bf16[1024,384]{1,0:T(8,128)(2,1)S(1)}, bf16[1024,384]{1,0:T(8,128)(2,1)S(1)}, u32[]{:S(2)}, u32[]{:S(2)}) collective-permute-start(bf16[1024,384]{1,0:T(8,128)(2,1)S(1)} %get-tuple-element.248), channel_id=1, source_target_pairs={{0,8},{8,0},{16,24},{24,16},{1,9},{9,1},{17,25},{25,17},{2,10},{10... | collective-permute-start | bytes 2359304 | tf_op jit(solution)/shard_map/ppermute | solution.py:561
  161.5 36.3 %collective-permute-start.45 = (bf16[1024,384]{1,0:T(8,128)(2,1)S(1)}, bf16[1024,384]{1,0:T(8,128)(2,1)S(1)}, u32[]{:S(2)}, u32[]{:S(2)}) collective-permute-start(bf16[1024,384]{1,0:T(8,128)(2,1)S(1)} %get-tuple-element.249), channel_id=1, source_target_pairs={{0,16},{8,24},{16,0},{24,8},{1,17},{9,25},{17,1},{25,9},{2,18},{10... | collective-permute-start | bytes 2359304 | tf_op jit(solution)/shard_map/ppermute | solution.py:561
  163.2 34.6 %collective-permute-start.46 = (bf16[1024,384]{1,0:T(8,128)(2,1)S(1)}, bf16[1024,384]{1,0:T(8,128)(2,1)S(1)}, u32[]{:S(2)}, u32[]{:S(2)}) collective-permute-start(bf16[1024,384]{1,0:T(8,128)(2,1)S(1)} %get-tuple-element.250), channel_id=1, source_target_pairs={{0,24},{8,16},{16,8},{24,0},{1,25},{9,17},{17,9},{25,1},{2,26},{10... | collective-permute-start | bytes 2359304 | tf_op jit(solution)/shard_map/ppermute | solution.py:561
  167.7 16.5 %collective-permute-start.54 = (bf16[384,384]{1,0:T(8,128)(2,1)S(1)}, bf16[384,384]{1,0:T(8,128)(2,1)S(1)}, u32[]{:S(2)}, u32[]{:S(2)}) collective-permute-start(bf16[384,384]{1,0:T(8,128)(2,1)S(1)} %get-tuple-element.278), channel_id=1, source_target_pairs={{0,2},{1,3},{2,0},{3,1},{4,6},{5,7},{6,4},{7,5},{8,10},{9,11},{10,... | collective-permute-start | bytes 884744 | tf_op jit(solution)/shard_map/ppermute | solution.py:555
  170.2 17.2 %collective-permute-start.55 = (bf16[384,384]{1,0:T(8,128)(2,1)S(1)}, bf16[384,384]{1,0:T(8,128)(2,1)S(1)}, u32[]{:S(2)}, u32[]{:S(2)}) collective-permute-start(bf16[384,384]{1,0:T(8,128)(2,1)S(1)} %get-tuple-element.279), channel_id=1, source_target_pairs={{0,4},{1,5},{2,6},{3,7},{4,0},{5,1},{6,2},{7,3},{8,12},{9,13},{10,... | collective-permute-start | bytes 884744 | tf_op jit(solution)/shard_map/ppermute | solution.py:555
  197.8 16.7 %collective-permute-start.57 = (bf16[784,384]{1,0:T(8,128)(2,1)S(1)}, bf16[784,384]{1,0:T(8,128)(2,1)S(1)}, u32[]{:S(2)}, u32[]{:S(2)}) collective-permute-start(bf16[784,384]{1,0:T(8,128)(2,1)S(1)} %get-tuple-element.282), channel_id=1, source_target_pairs={{0,8},{8,0},{16,24},{24,16},{1,9},{9,1},{17,25},{25,17},{2,10},{10... | collective-permute-start | bytes 1806344 | tf_op jit(solution)/shard_map/ppermute | solution.py:561
  200.7 13.9 %collective-permute-start.58 = (bf16[768,384]{1,0:T(8,128)(2,1)S(1)}, bf16[768,384]{1,0:T(8,128)(2,1)S(1)}, u32[]{:S(2)}, u32[]{:S(2)}) collective-permute-start(bf16[768,384]{1,0:T(8,128)(2,1)S(1)} %get-tuple-element.283), channel_id=1, source_target_pairs={{0,16},{8,24},{16,0},{24,8},{1,17},{9,25},{17,1},{25,9},{2,18},{10... | collective-permute-start | bytes 1769480 | tf_op jit(solution)/shard_map/ppermute | solution.py:561
  204.0 14.6 %collective-permute-start.49 = (bf16[320,384]{1,0:T(8,128)(2,1)S(1)}, bf16[320,384]{1,0:T(8,128)(2,1)S(1)}, u32[]{:S(2)}, u32[]{:S(2)}) collective-permute-start(bf16[320,384]{1,0:T(8,128)(2,1)S(1)} %get-tuple-element.265), channel_id=1, source_target_pairs={{0,2},{1,3},{2,0},{3,1},{4,6},{5,7},{6,4},{7,5},{8,10},{9,11},{10,... | collective-permute-start | bytes 737288 | tf_op jit(solution)/shard_map/ppermute | solution.py:555
  205.3 20.3 %collective-permute-start.50 = (bf16[320,384]{1,0:T(8,128)(2,1)S(1)}, bf16[320,384]{1,0:T(8,128)(2,1)S(1)}, u32[]{:S(2)}, u32[]{:S(2)}) collective-permute-start(bf16[320,384]{1,0:T(8,128)(2,1)S(1)} %get-tuple-element.266), channel_id=1, source_target_pairs={{0,4},{1,5},{2,6},{3,7},{4,0},{5,1},{6,2},{7,3},{8,12},{9,13},{10,... | collective-permute-start | bytes 737288 | tf_op jit(solution)/shard_map/ppermute | solution.py:555
  206.0 19.7 %collective-permute-start.51 = (bf16[320,384]{1,0:T(8,128)(2,1)S(1)}, bf16[320,384]{1,0:T(8,128)(2,1)S(1)}, u32[]{:S(2)}, u32[]{:S(2)}) collective-permute-start(bf16[320,384]{1,0:T(8,128)(2,1)S(1)} %get-tuple-element.267), channel_id=1, source_target_pairs={{0,6},{1,7},{2,4},{3,5},{4,2},{5,3},{6,0},{7,1},{8,14},{9,15},{10,... | collective-permute-start | bytes 737288 | tf_op jit(solution)/shard_map/ppermute | solution.py:555
  215.0 16.8 %collective-permute-start.59 = (bf16[400,384]{1,0:T(8,128)(2,1)S(1)}, bf16[400,384]{1,0:T(8,128)(2,1)S(1)}, u32[]{:S(2)}, u32[]{:S(2)}) collective-permute-start(bf16[400,384]{1,0:T(8,128)(2,1)S(1)} %get-tuple-element.285), channel_id=1, source_target_pairs={{0,16},{8,24},{16,0},{24,8},{1,17},{9,25},{17,1},{25,9},{2,18},{10... | collective-permute-start | bytes 921608 | tf_op jit(solution)/shard_map/ppermute | solution.py:561
  217.1 14.7 %collective-permute-start.60 = (bf16[384,384]{1,0:T(8,128)(2,1)S(1)}, bf16[384,384]{1,0:T(8,128)(2,1)S(1)}, u32[]{:S(2)}, u32[]{:S(2)}) collective-permute-start(bf16[384,384]{1,0:T(8,128)(2,1)S(1)} %get-tuple-element.287), channel_id=1, source_target_pairs={{0,8},{8,0},{16,24},{24,16},{1,9},{9,1},{17,25},{25,17},{2,10},{10... | collective-permute-start | bytes 884744 | tf_op jit(solution)/shard_map/ppermute | solution.py:561
  228.3 24.9 %collective-permute-start.67 = (bf16[288,768]{1,0:T(8,128)(2,1)S(1)}, bf16[288,768]{1,0:T(8,128)(2,1)S(1)}, u32[]{:S(2)}, u32[]{:S(2)}) collective-permute-start(bf16[288,768]{1,0:T(8,128)(2,1)S(1)} %join_two.1.u0), channel_id=1, source_target_pairs={{0,8},{8,0},{16,24},{24,16},{1,9},{9,1},{17,25},{25,17},{2,10},{10... | collective-permute-start | bytes 1327112 | tf_op jit(solution)/shard_map/ppermute | solution.py:561
  230.3 22.9 %collective-permute-start.68 = (bf16[288,768]{1,0:T(8,128)(2,1)S(1)}, bf16[288,768]{1,0:T(8,128)(2,1)S(1)}, u32[]{:S(2)}, u32[]{:S(2)}) collective-permute-start(bf16[288,768]{1,0:T(8,128)(2,1)S(1)} %join_two.1.u0), channel_id=1, source_target_pairs={{0,16},{8,24},{16,0},{24,8},{1,17},{9,25},{17,1},{25,9},{2,18},{10... | collective-permute-start | bytes 1327112 | tf_op jit(solution)/shard_map/ppermute | solution.py:561
  230.3 22.9 %collective-permute-start.69 = (bf16[288,768]{1,0:T(8,128)(2,1)S(1)}, bf16[288,768]{1,0:T(8,128)(2,1)S(1)}, u32[]{:S(2)}, u32[]{:S(2)}) collective-permute-start(bf16[288,768]{1,0:T(8,128)(2,1)S(1)} %join_two.1.u0), channel_id=1, source_target_pairs={{0,24},{8,16},{16,8},{24,0},{1,25},{9,17},{17,9},{25,1},{2,26},{10... | collective-permute-start | bytes 1327112 | tf_op jit(solution)/shard_map/ppermute | solution.py:561
  236.3 14.1 %collective-permute-start.62 = (bf16[208,384]{1,0:T(8,128)(2,1)S(1)}, bf16[208,384]{1,0:T(8,128)(2,1)S(1)}, u32[]{:S(2)}, u32[]{:S(2)}) collective-permute-start(bf16[208,384]{1,0:T(8,128)(2,1)S(1)} %get-tuple-element.290), channel_id=1, source_target_pairs={{0,4},{1,5},{2,6},{3,7},{4,0},{5,1},{6,2},{7,3},{8,12},{9,13},{10,... | collective-permute-start | bytes 479240 | tf_op jit(solution)/shard_map/ppermute | solution.py:555
  (49 other events, 347.3 us)
